TPU v7x, 32 devices: a whole 2x2x4 slice. The times are simulated.
32 devices in a mesh: row: 4 (over z), col: 8 (over y, x, core).
Axes of the slice: x: 2, y: 2, z: 4, core: 2. Of those that a mesh axis runs over, the one named last changes fastest.
Arguments:
- load: float32 [4, 8, 640, 128], P('row', 'col'), may hold values from -16 to 16
- schur: float32 [4, 8, 640, 640], P('row', 'col'), may hold values from -0.090915483 to 4.0909155, as said below
- local_inverse: float32 [4, 8, 640, 640], P('row', 'col'), may hold values from -0.0059292706 to 0.30592927, as said below
- iface_index: int32 [4, 8, 640], P('row', 'col'), may hold values from 0 to 639, each once within a row
- face_link: int32 [4, 8, 4], P('row', 'col'), may hold values from 0 to 1, as said below
- coarse_basis: float32 [4, 8, 640, 48], P('row', 'col'), may hold values from -0.25 to 0.25
- coarse_inverse: float32 [8, 192, 192], P('col', 'row'), may hold values from -0.0036084392 to 0.06360844, as said below
- coarse_map: float32 [8, 192, 48], P('col', 'row'), may hold values from -0.875 to 0.875
- top_inverse: float32 [384, 384], P('col'), may hold values from -0.00025515518 to 0.006255155, as said below
Outputs:
- solution: float32 [4, 8, 640, 128], P('row', 'col')
- residual: float32 [4, 8, 640, 128], P('row', 'col')
Inputs may be any that keep to these rules, and one draw needn't show every extreme that they name: `iface_index`: position j of face k of a subdomain and position j of the opposite face of its neighbour across face k are the same unknown. `face_link`: equal on the two sides of every face; 0 on faces on the outside of the grid of subdomains. `schur`: each matrix is symmetric. `local_inverse`: each matrix is symmetric. `coarse_inverse`: each matrix is symmetric. `top_inverse`: Symmetric.
All inputs are finite; a program needn't handle non-finite values.
Results may differ from a plain program's by a relative error of at most 0.0003.
Values sent between devices are 32-bit elements; how exact they have to be, the bound alone decides.
No kernel may reach another device: no remote copies, remote signals or barrier semaphores. Data moves between devices by JAX's collectives and lax.ppermute only.
A program may use at most 64 MiB of HBM per device.

v0:
```python
import math

import jax
import jax.numpy as jnp
from jax import lax
from jax.sharding import PartitionSpec as P

DEGREE = 2
STEPS = 4


def extended(cells, sides, width):
    for axis, dim in sides:
        count = lax.axis_size(axis)
        ends = count - 1
        head = lax.slice_in_dim(cells, 0, width, axis=dim)
        tail = lax.slice_in_dim(cells, cells.shape[dim] - width, cells.shape[dim], axis=dim)
        cells = jnp.concatenate(
            [
                lax.ppermute(tail, axis, [(i, (i + 1) % count) for i in range(ends)]),
                cells,
                lax.ppermute(head, axis, [((i + 1) % count, i) for i in range(ends)]),
            ],
            axis=dim,
        )
    return cells


def product(left, right):
    return jnp.dot(left, right, precision=lax.Precision.HIGHEST, preferred_element_type=jnp.float32)


def shards(
    load,
    schur,
    local_inverse,
    iface_index,
    face_link,
    coarse_basis,
    coarse_inverse,
    coarse_map,
    top_inverse,
):
    highest = lax.Precision.HIGHEST
    loads = load[0, 0]
    schur_block = schur[0, 0]
    inverse_block = local_inverse[0, 0]
    index_list = iface_index[0, 0]
    link_mask = face_link[0, 0].astype(jnp.float32)
    basis = coarse_basis[0, 0]
    level_inverse = coarse_inverse[0]
    map_block = coarse_map[0]
    interface_size = index_list.shape[0]
    face_size = interface_size // 4
    columns = loads.shape[1]
    inverse_list = (
        jnp.zeros_like(index_list).at[index_list].set(jnp.arange(interface_size, dtype=jnp.int32))
    )

    def assemble(field):
        face_rows = jnp.take(field, index_list, axis=0).reshape(4, face_size, columns)
        across = extended(face_rows[0:2], (("col", 0),), 1)
        upward = extended(face_rows[2:4], (("row", 0),), 1)
        received = (
            jnp.stack([across[0], across[3], upward[0], upward[3]]) * link_mask[:, None, None]
        )
        return field + jnp.take(received.reshape(interface_size, columns), inverse_list, axis=0)

    map_all = lax.all_gather(map_block, "row", axis=0, tiled=True)
    assembled = assemble(loads)
    solution = jnp.zeros_like(loads)
    for step_index in range(STEPS):
        phase = step_index % DEGREE
        weight_step = 1.0 / (1.4 - math.cos(math.pi * (2 * phase + 1) / (2 * DEGREE)))
        if step_index == 0:
            current = assembled
        else:
            current = assembled - assemble(product(schur_block, solution))
        coeffs = jnp.einsum("gk,gr->kr", basis, current, precision=highest)
        piece = lax.all_gather(coeffs, "row", axis=0, tiled=True)
        level_two = product(level_inverse, piece)
        level_three = jnp.einsum("kt,kr->tr", map_all, piece, precision=highest)
        top = product(top_inverse, lax.all_gather(level_three, "col", axis=0, tiled=True))
        group = level_two + product(map_block, top)
        update = assemble(product(inverse_block, current) + product(basis, group))
        solution = solution + weight_step * update
    residual = assembled - assemble(product(schur_block, solution))
    return (solution[None, None], residual[None, None])


def solution(mesh):
    return jax.shard_map(
        shards,
        mesh=mesh,
        in_specs=(
            P("row", "col", None, None),
            P("row", "col", None, None),
            P("row", "col", None, None),
            P("row", "col", None),
            P("row", "col", None),
            P("row", "col", None, None),
            P("col", "row", None),
            P("col", "row", None),
            P("col", None),
        ),
        out_specs=(P("row", "col", None, None), P("row", "col", None, None)),
        check_vma=False,
    )
```

profile of v0, /device:TPU:1, one launch (start us, length us, event | category | flops | bytes accessed | tf_op | source)
XLA Modules:
  0.0 309.5 jit_solution(12108482244012460377)
XLA Ops:
  1.6 2.7 gather_fusion
  4.5 4.5 %collective-permute-start = (f32[1,160,128]{2,1,0:T(8,128)S(1)}, f32[1,160,128]{2,1,0:T(8,128)S(1)}, u32[]{:S(2)}, u32[]{:S(2)}) collective-permute-start(f32[1,160,128]{2,1,0:T(8,128)S(1)} %get-tuple-element.41), channel_id=1, source_target_pairs={{0,1},{1,2},{2,3},{3,4},{4,5},{5,6},{6,7},{8,9},{9,10},{10,11},{11... | collective-permute-start | bytes 245768 | tf_op jit(solution)/shard_map/ppermute | solution.py:20
  10.3 4.0 %collective-permute-start.2 = (f32[1,160,128]{2,1,0:T(8,128)S(1)}, f32[1,160,128]{2,1,0:T(8,128)S(1)}, u32[]{:S(2)}, u32[]{:S(2)}) collective-permute-start(f32[1,160,128]{2,1,0:T(8,128)S(1)} %get-tuple-element.43), channel_id=1, source_target_pairs={{0,8},{8,16},{16,24},{1,9},{9,17},{17,25},{2,10},{10,18},{18,26},{... | collective-permute-start | bytes 245768 | tf_op jit(solution)/shard_map/ppermute | solution.py:20
  14.3 1.9 collective-permute-start.1
  16.2 4.1 %scatter_custom_fusion = s32[640]{0:T(1024)S(1)} fusion(s32[640]{0:T(1024)S(1)} %fusion.69, s32[640]{0:T(1024)S(1)} %iota.3, s32[]{:T(128)} %constant.0.clone.1), kind=kCustom, calls=%fused_computation.175 | custom fusion | bytes 2564 | tf_op jit(solution)/shard_map/scatter | solution.py:57
  20.7 11.0 %all-gather = f32[1,192,48]{2,1,0:T(8,128)S(1)} all-gather(f32[1,48,48]{2,1,0:T(8,128)S(1)} %copy-done.25), channel_id=2, replica_groups=mesh['row'=4,'col'=8] {'row'}, dimensions={1}, use_global_device_ids=true | all-gather | bytes 46080 | tf_op jit(solution)/shard_map/all_gather | solution.py:69
  34.3 10.4 %all_gather.27 = f32[192,128]{1,0:T(8,128)S(1)} all-gather(f32[48,128]{1,0:T(8,128)S(1)} %convolution_bitcast_fusion.7), channel_id=1, replica_groups=mesh['row'=4,'col'=8] {'row'}, dimensions={0}, use_global_device_ids=true | all-gather | bytes 122880 | tf_op jit(solution)/shard_map/all_gather | solution.py:80
  45.4 15.9 %all_gather.29 = f32[384,128]{1,0:T(8,128)S(1)} all-gather(f32[48,128]{1,0:T(8,128)S(1)} %convolution_bitcast_fusion.3), channel_id=1, replica_groups=mesh['row'=4,'col'=8] {'col'}, dimensions={0}, use_global_device_ids=true | all-gather | bytes 221184 | tf_op jit(solution)/shard_map/all_gather | solution.py:83
  61.3 1.7 fusion.14
  65.9 2.3 collective-permute-start.4
  69.5 4.0 %collective-permute-start.6 = (f32[1,160,128]{2,1,0:T(8,128)S(1)}, f32[1,160,128]{2,1,0:T(8,128)S(1)}, u32[]{:S(2)}, u32[]{:S(2)}) collective-permute-start(f32[1,160,128]{2,1,0:T(8,128)S(1)} %get-tuple-element.39), channel_id=1, source_target_pairs={{0,8},{8,16},{16,24},{1,9},{9,17},{17,25},{2,10},{10,18},{18,26},{... | collective-permute-start | bytes 245768 | tf_op jit(solution)/shard_map/ppermute | solution.py:20
  73.5 2.6 collective-permute-start.5
  76.2 3.1 %collective-permute-done.5 = f32[1,160,128]{2,1,0:T(8,128)S(1)} collective-permute-done((f32[1,160,128]{2,1,0:T(8,128)S(1)}, f32[1,160,128]{2,1,0:T(8,128)S(1)}, u32[]{:S(2)}, u32[]{:S(2)}) %collective-permute-start.5) | collective-permute-done | bytes 81952 | tf_op jit(solution)/shard_map/ppermute | solution.py:22
  79.5 1.7 gather_fusion.3
  81.3 3.2 %fusion.20 = f32[640,128]{0,1:T(8,128)S(1)} fusion(f32[1,1,640,640]{3,2,1,0:T(8,128)} %param.12, f32[640,128]{0,1:T(8,128)S(1)} %fusion.19, f32[640,128]{0,1:T(8,128)S(1)} %copy.57, pred[640]{0:T(1024)(128)(4,1)S(1)} %compare_and_fusion), kind=kOutput, calls=%fused_computation.43 | convolution fusion | flops 629391360 | bytes 2622080 | tf_op jit(solution)/shard_map/dot_general | solution.py:30
  84.7 2.3 gather_fusion.4
  88.1 1.9 collective-permute-start.8
  91.3 4.0 %collective-permute-start.10 = (f32[1,160,128]{2,1,0:T(8,128)S(1)}, f32[1,160,128]{2,1,0:T(8,128)S(1)}, u32[]{:S(2)}, u32[]{:S(2)}) collective-permute-start(f32[1,160,128]{2,1,0:T(8,128)S(1)} %get-tuple-element.35), channel_id=1, source_target_pairs={{0,8},{8,16},{16,24},{1,9},{9,17},{17,25},{2,10},{10,18},{18,26},{... | collective-permute-start | bytes 245768 | tf_op jit(solution)/shard_map/ppermute | solution.py:20
  95.3 3.1 %collective-permute-start.9 = (f32[1,160,128]{2,1,0:T(8,128)S(1)}, f32[1,160,128]{2,1,0:T(8,128)S(1)}, u32[]{:S(2)}, u32[]{:S(2)}) collective-permute-start(f32[1,160,128]{2,1,0:T(8,128)S(1)} %get-tuple-element.36), channel_id=1, source_target_pairs={{1,0},{2,1},{3,2},{4,3},{5,4},{6,5},{7,6},{9,8},{10,9},{11,10},{12... | collective-permute-start | bytes 245768 | tf_op jit(solution)/shard_map/ppermute | solution.py:22
  98.5 3.9 %collective-permute-done.9 = f32[1,160,128]{2,1,0:T(8,128)S(1)} collective-permute-done((f32[1,160,128]{2,1,0:T(8,128)S(1)}, f32[1,160,128]{2,1,0:T(8,128)S(1)}, u32[]{:S(2)}, u32[]{:S(2)}) %collective-permute-start.9) | collective-permute-done | bytes 81952 | tf_op jit(solution)/shard_map/ppermute | solution.py:22
  105.6 1.7 fusion.12
  107.3 10.3 %all_gather.30 = f32[192,128]{1,0:T(8,128)S(1)} all-gather(f32[48,128]{1,0:T(8,128)S(1)} %convolution_bitcast_fusion.6), channel_id=1, replica_groups=mesh['row'=4,'col'=8] {'row'}, dimensions={0}, use_global_device_ids=true | all-gather | bytes 122880 | tf_op jit(solution)/shard_map/all_gather | solution.py:80
  118.2 11.5 %all_gather.31 = f32[384,128]{1,0:T(8,128)S(1)} all-gather(f32[48,128]{1,0:T(8,128)S(1)} %convolution_bitcast_fusion.2), channel_id=1, replica_groups=mesh['row'=4,'col'=8] {'col'}, dimensions={0}, use_global_device_ids=true | all-gather | bytes 221184 | tf_op jit(solution)/shard_map/all_gather | solution.py:83
  132.6 1.9 collective-permute-start.12
  135.9 4.0 %collective-permute-start.14 = (f32[1,160,128]{2,1,0:T(8,128)S(1)}, f32[1,160,128]{2,1,0:T(8,128)S(1)}, u32[]{:S(2)}, u32[]{:S(2)}) collective-permute-start(f32[1,160,128]{2,1,0:T(8,128)S(1)} %get-tuple-element.31), channel_id=1, source_target_pairs={{0,8},{8,16},{16,24},{1,9},{9,17},{17,25},{2,10},{10,18},{18,26},{... | collective-permute-start | bytes 245768 | tf_op jit(solution)/shard_map/ppermute | solution.py:20
  139.9 3.0 collective-permute-start.13
  142.9 2.8 collective-permute-done.13
  145.8 2.2 gather_fusion.7
  148.1 2.0 copy.61
  152.2 2.4 fusion.23
  155.7 1.9 gather_fusion.8
  157.9 1.9 collective-permute-start.16
  161.1 4.0 %collective-permute-start.18 = (f32[1,160,128]{2,1,0:T(8,128)S(1)}, f32[1,160,128]{2,1,0:T(8,128)S(1)}, u32[]{:S(2)}, u32[]{:S(2)}) collective-permute-start(f32[1,160,128]{2,1,0:T(8,128)S(1)} %get-tuple-element.27), channel_id=1, source_target_pairs={{0,8},{8,16},{16,24},{1,9},{9,17},{17,25},{2,10},{10,18},{18,26},{... | collective-permute-start | bytes 245768 | tf_op jit(solution)/shard_map/ppermute | solution.py:20
  165.1 3.0 collective-permute-start.17
  168.1 3.8 %collective-permute-done.17 = f32[1,160,128]{2,1,0:T(8,128)S(1)} collective-permute-done((f32[1,160,128]{2,1,0:T(8,128)S(1)}, f32[1,160,128]{2,1,0:T(8,128)S(1)}, u32[]{:S(2)}, u32[]{:S(2)}) %collective-permute-start.17) | collective-permute-done | bytes 81952 | tf_op jit(solution)/shard_map/ppermute | solution.py:22
  172.1 1.7 gather_fusion.9
  175.2 1.7 fusion.10
  176.9 10.4 %all_gather.32 = f32[192,128]{1,0:T(8,128)S(1)} all-gather(f32[48,128]{1,0:T(8,128)S(1)} %convolution_bitcast_fusion.5), channel_id=1, replica_groups=mesh['row'=4,'col'=8] {'row'}, dimensions={0}, use_global_device_ids=true | all-gather | bytes 122880 | tf_op jit(solution)/shard_map/all_gather | solution.py:80
  187.8 11.5 %all_gather.33 = f32[384,128]{1,0:T(8,128)S(1)} all-gather(f32[48,128]{1,0:T(8,128)S(1)} %convolution_bitcast_fusion.1), channel_id=1, replica_groups=mesh['row'=4,'col'=8] {'col'}, dimensions={0}, use_global_device_ids=true | all-gather | bytes 221184 | tf_op jit(solution)/shard_map/all_gather | solution.py:83
  200.4 1.7 gather_fusion.10
  202.3 1.9 collective-permute-start.20
  205.5 4.0 %collective-permute-start.22 = (f32[1,160,128]{2,1,0:T(8,128)S(1)}, f32[1,160,128]{2,1,0:T(8,128)S(1)}, u32[]{:S(2)}, u32[]{:S(2)}) collective-permute-start(f32[1,160,128]{2,1,0:T(8,128)S(1)} %get-tuple-element.23), channel_id=1, source_target_pairs={{0,8},{8,16},{16,24},{1,9},{9,17},{17,25},{2,10},{10,18},{18,26},{... | collective-permute-start | bytes 245768 | tf_op jit(solution)/shard_map/ppermute | solution.py:20
  209.5 3.0 collective-permute-start.21
  212.5 2.8 collective-permute-done.21
  217.3 3.2 %fusion.26 = f32[640,128]{0,1:T(8,128)S(1)} fusion(f32[1,1,640,640]{3,2,1,0:T(8,128)} %param.12, f32[640,128]{0,1:T(8,128)S(1)} %copy-done.11, f32[640,128]{0,1:T(8,128)S(1)} %fusion.17, f32[640,128]{0,1:T(8,128)S(1)} %copy.65, pred[640]{0:T(1024)(128)(4,1)} %copy-done.39), kind=kOutput, calls=%fused_computation.45 | convolution fusion | flops 629473280 | bytes 2949760 | tf_op jit(solution)/shard_map/dot_general | solution.py:30
  220.7 1.9 gather_fusion.12
  223.5 1.9 collective-permute-start.24
  226.8 4.0 %collective-permute-start.26 = (f32[1,160,128]{2,1,0:T(8,128)S(1)}, f32[1,160,128]{2,1,0:T(8,128)S(1)}, u32[]{:S(2)}, u32[]{:S(2)}) collective-permute-start(f32[1,160,128]{2,1,0:T(8,128)S(1)} %get-tuple-element.19), channel_id=1, source_target_pairs={{0,8},{8,16},{16,24},{1,9},{9,17},{17,25},{2,10},{10,18},{18,26},{... | collective-permute-start | bytes 245768 | tf_op jit(solution)/shard_map/ppermute | solution.py:20
  230.8 3.0 collective-permute-start.25
  233.8 4.0 %collective-permute-done.25 = f32[1,160,128]{2,1,0:T(8,128)S(1)} collective-permute-done((f32[1,160,128]{2,1,0:T(8,128)S(1)}, f32[1,160,128]{2,1,0:T(8,128)S(1)}, u32[]{:S(2)}, u32[]{:S(2)}) %collective-permute-start.25) | collective-permute-done | bytes 81952 | tf_op jit(solution)/shard_map/ppermute | solution.py:22
  240.4 1.7 fusion.8
  242.1 10.3 %all_gather.34 = f32[192,128]{1,0:T(8,128)S(1)} all-gather(f32[48,128]{1,0:T(8,128)S(1)} %convolution_bitcast_fusion.4), channel_id=1, replica_groups=mesh['row'=4,'col'=8] {'row'}, dimensions={0}, use_global_device_ids=true | all-gather | bytes 122880 | tf_op jit(solution)/shard_map/all_gather | solution.py:80
  253.0 11.4 %all_gather.35 = f32[384,128]{1,0:T(8,128)S(1)} all-gather(f32[48,128]{1,0:T(8,128)S(1)} %convolution_bitcast_fusion), channel_id=1, replica_groups=mesh['row'=4,'col'=8] {'col'}, dimensions={0}, use_global_device_ids=true | all-gather | bytes 221184 | tf_op jit(solution)/shard_map/all_gather | solution.py:83
  267.4 1.9 collective-permute-start.28
  270.6 4.0 %collective-permute-start.30 = (f32[1,160,128]{2,1,0:T(8,128)S(1)}, f32[1,160,128]{2,1,0:T(8,128)S(1)}, u32[]{:S(2)}, u32[]{:S(2)}) collective-permute-start(f32[1,160,128]{2,1,0:T(8,128)S(1)} %get-tuple-element.15), channel_id=1, source_target_pairs={{0,8},{8,16},{16,24},{1,9},{9,17},{17,25},{2,10},{10,18},{18,26},{... | collective-permute-start | bytes 245768 | tf_op jit(solution)/shard_map/ppermute | solution.py:20
  274.6 3.2 %collective-permute-start.29 = (f32[1,160,128]{2,1,0:T(8,128)S(1)}, f32[1,160,128]{2,1,0:T(8,128)S(1)}, u32[]{:S(2)}, u32[]{:S(2)}) collective-permute-start(f32[1,160,128]{2,1,0:T(8,128)S(1)} %get-tuple-element.16), channel_id=1, source_target_pairs={{1,0},{2,1},{3,2},{4,3},{5,4},{6,5},{7,6},{9,8},{10,9},{11,10},{12... | collective-permute-start | bytes 245768 | tf_op jit(solution)/shard_map/ppermute | solution.py:22
  277.9 2.5 collective-permute-done.29
  280.6 2.2 gather_fusion.15
  282.8 2.0 copy.69
  287.0 2.4 fusion.29
  292.4 1.9 collective-permute-start.32
  295.7 4.0 %collective-permute-start.34 = (f32[1,160,128]{2,1,0:T(8,128)S(1)}, f32[1,160,128]{2,1,0:T(8,128)S(1)}, u32[]{:S(2)}, u32[]{:S(2)}) collective-permute-start(f32[1,160,128]{2,1,0:T(8,128)S(1)} %get-tuple-element.11), channel_id=1, source_target_pairs={{0,8},{8,16},{16,24},{1,9},{9,17},{17,25},{2,10},{10,18},{18,26},{... | collective-permute-start | bytes 245768 | tf_op jit(solution)/shard_map/ppermute | solution.py:20
  299.7 3.0 collective-permute-start.33
  303.6 3.0 collective-permute-done.33
  (231 shorter events, 52.4 us)
Async XLA Ops:
  0.6 60.7 %copy-start = (f32[1,1,640,640]{3,2,1,0:T(8,128)S(1)}, f32[1,1,640,640]{3,2,1,0:T(8,128)}, u32[]{:S(2)}) copy-start(f32[1,1,640,640]{3,2,1,0:T(8,128)} %param.13) | copy-start | bytes 4915204
  1.5 64.3 %copy-start.34 = (pred[640]{0:T(1024)(128)(4,1)}, pred[640]{0:T(1024)(128)(4,1)S(1)}, u32[]{:S(2)}) copy-start(pred[640]{0:T(1024)(128)(4,1)S(1)} %compare_and_fusion.1) | copy-start | bytes 1924
  1.5 83.2 %copy-start.29 = (s32[1024]{0:T(1024)}, s32[1024]{0:T(1024)S(1)}, u32[]{:S(2)}) copy-start(s32[1024]{0:T(1024)S(1)} %pad_clamp_fusion.1) | copy-start | bytes 12292
  1.5 14.7 %copy-start.42 = (s32[1,1,640]{2,1,0:T(1,128)S(1)}, s32[1,1,640]{2,1,0:T(1,128)}, u32[]{:S(2)}) copy-start(s32[1,1,640]{2,1,0:T(1,128)} %param.14) | copy-start | bytes 7684
  1.5 18.8 %copy-start.1 = (f32[1,1,640,128]{3,2,1,0:T(8,128)S(1)}, f32[1,1,640,128]{3,2,1,0:T(8,128)}, u32[]{:S(2)}) copy-start(f32[1,1,640,128]{3,2,1,0:T(8,128)} %param.11) | copy-start | bytes 983044
  4.2 16.3 %copy-start.43 = (s32[1,1,4]{2,1,0:T(1,128)S(1)}, s32[1,1,4]{2,1,0:T(1,128)}, u32[]{:S(2)}) copy-start(s32[1,1,4]{2,1,0:T(1,128)} %param.15) | copy-start | bytes 52
  4.3 16.5 %copy-start.25 = (f32[1,48,48]{2,1,0:T(8,128)S(1)}, f32[1,48,48]{2,1,0:T(8,128)}, u32[]{:S(2)}) copy-start(f32[1,48,48]{2,1,0:T(8,128)} %param.18) | copy-start | bytes 27652
  4.5 27.2 %collective-permute-start = (f32[1,160,128]{2,1,0:T(8,128)S(1)}, f32[1,160,128]{2,1,0:T(8,128)S(1)}, u32[]{:S(2)}, u32[]{:S(2)}) collective-permute-start(f32[1,160,128]{2,1,0:T(8,128)S(1)} %get-tuple-element.41), channel_id=1, source_target_pairs={{0,1},{1,2},{2,3},{3,4},{4,5},{5,6},{6,7},{8,9},{9,10},{10,11},{11... | collective-permute-start | bytes 245768 | tf_op jit(solution)/shard_map/ppermute | solution.py:20
  9.0 22.7 %collective-permute-start.3 = (f32[1,160,128]{2,1,0:T(8,128)S(1)}, f32[1,160,128]{2,1,0:T(8,128)S(1)}, u32[]{:S(2)}, u32[]{:S(2)}) collective-permute-start(f32[1,160,128]{2,1,0:T(8,128)S(1)} %get-tuple-element.42), channel_id=1, source_target_pairs={{8,0},{16,8},{24,16},{9,1},{17,9},{25,17},{10,2},{18,10},{26,18},{... | collective-permute-start | bytes 245768 | tf_op jit(solution)/shard_map/ppermute | solution.py:22
  10.3 21.4 %collective-permute-start.2 = (f32[1,160,128]{2,1,0:T(8,128)S(1)}, f32[1,160,128]{2,1,0:T(8,128)S(1)}, u32[]{:S(2)}, u32[]{:S(2)}) collective-permute-start(f32[1,160,128]{2,1,0:T(8,128)S(1)} %get-tuple-element.43), channel_id=1, source_target_pairs={{0,8},{8,16},{16,24},{1,9},{9,17},{17,25},{2,10},{10,18},{18,26},{... | collective-permute-start | bytes 245768 | tf_op jit(solution)/shard_map/ppermute | solution.py:20
  14.3 17.5 %collective-permute-start.1 = (f32[1,160,128]{2,1,0:T(8,128)S(1)}, f32[1,160,128]{2,1,0:T(8,128)S(1)}, u32[]{:S(2)}, u32[]{:S(2)}) collective-permute-start(f32[1,160,128]{2,1,0:T(8,128)S(1)} %get-tuple-element.44), channel_id=1, source_target_pairs={{1,0},{2,1},{3,2},{4,3},{5,4},{6,5},{7,6},{9,8},{10,9},{11,10},{12... | collective-permute-start | bytes 245768 | tf_op jit(solution)/shard_map/ppermute | solution.py:22
  20.4 60.9 %copy-start.39 = (pred[640]{0:T(1024)(128)(4,1)}, pred[640]{0:T(1024)(128)(4,1)S(1)}, u32[]{:S(2)}) copy-start(pred[640]{0:T(1024)(128)(4,1)S(1)} %compare_and_fusion) | copy-start | bytes 1924
  33.6 11.5 %copy-start.24 = (f32[1,48,192]{2,1,0:T(8,128)S(1)}, f32[1,48,192]{2,1,0:T(8,128)}, u32[]{:S(2)}) copy-start(f32[1,48,192]{2,1,0:T(8,128)} %param.17) | copy-start | bytes 110596
  33.8 70.6 %copy-start.4 = (f32[640,128]{0,1:T(8,128)}, f32[640,128]{0,1:T(8,128)S(1)}, u32[]{:S(2)}) copy-start(f32[640,128]{0,1:T(8,128)S(1)} %bitcast_add_fusion) | copy-start | bytes 983044
  33.8 29.1 %copy-start.20 = (f32[48,384]{1,0:T(8,128)S(1)}, f32[48,384]{1,0:T(8,128)}, u32[]{:S(2)}) copy-start(f32[48,384]{1,0:T(8,128)} %param.19) | copy-start | bytes 221188
  63.9 17.4 %copy-start.9 = (f32[640,128]{0,1:T(8,128)}, f32[640,128]{0,1:T(8,128)S(1)}, u32[]{:S(2)}) copy-start(f32[640,128]{0,1:T(8,128)S(1)} %fusion.19) | copy-start | bytes 983044
  65.9 10.2 %collective-permute-start.4 = (f32[1,160,128]{2,1,0:T(8,128)S(1)}, f32[1,160,128]{2,1,0:T(8,128)S(1)}, u32[]{:S(2)}, u32[]{:S(2)}) collective-permute-start(f32[1,160,128]{2,1,0:T(8,128)S(1)} %get-tuple-element.37), channel_id=1, source_target_pairs={{0,1},{1,2},{2,3},{3,4},{4,5},{5,6},{6,7},{8,9},{9,10},{10,11},{11... | collective-permute-start | bytes 245768 | tf_op jit(solution)/shard_map/ppermute | solution.py:20
  68.2 7.9 %collective-permute-start.7 = (f32[1,160,128]{2,1,0:T(8,128)S(1)}, f32[1,160,128]{2,1,0:T(8,128)S(1)}, u32[]{:S(2)}, u32[]{:S(2)}) collective-permute-start(f32[1,160,128]{2,1,0:T(8,128)S(1)} %get-tuple-element.38), channel_id=1, source_target_pairs={{8,0},{16,8},{24,16},{9,1},{17,9},{25,17},{10,2},{18,10},{26,18},{... | collective-permute-start | bytes 245768 | tf_op jit(solution)/shard_map/ppermute | solution.py:22
  69.5 6.6 %collective-permute-start.6 = (f32[1,160,128]{2,1,0:T(8,128)S(1)}, f32[1,160,128]{2,1,0:T(8,128)S(1)}, u32[]{:S(2)}, u32[]{:S(2)}) collective-permute-start(f32[1,160,128]{2,1,0:T(8,128)S(1)} %get-tuple-element.39), channel_id=1, source_target_pairs={{0,8},{8,16},{16,24},{1,9},{9,17},{17,25},{2,10},{10,18},{18,26},{... | collective-permute-start | bytes 245768 | tf_op jit(solution)/shard_map/ppermute | solution.py:20
  73.5 5.8 %collective-permute-start.5 = (f32[1,160,128]{2,1,0:T(8,128)S(1)}, f32[1,160,128]{2,1,0:T(8,128)S(1)}, u32[]{:S(2)}, u32[]{:S(2)}) collective-permute-start(f32[1,160,128]{2,1,0:T(8,128)S(1)} %get-tuple-element.40), channel_id=1, source_target_pairs={{1,0},{2,1},{3,2},{4,3},{5,4},{6,5},{7,6},{9,8},{10,9},{11,10},{12... | collective-permute-start | bytes 245768 | tf_op jit(solution)/shard_map/ppermute | solution.py:22
  88.1 10.4 %collective-permute-start.8 = (f32[1,160,128]{2,1,0:T(8,128)S(1)}, f32[1,160,128]{2,1,0:T(8,128)S(1)}, u32[]{:S(2)}, u32[]{:S(2)}) collective-permute-start(f32[1,160,128]{2,1,0:T(8,128)S(1)} %get-tuple-element.33), channel_id=1, source_target_pairs={{0,1},{1,2},{2,3},{3,4},{4,5},{5,6},{6,7},{8,9},{9,10},{10,11},{11... | collective-permute-start | bytes 245768 | tf_op jit(solution)/shard_map/ppermute | solution.py:20
  90.0 8.5 %collective-permute-start.11 = (f32[1,160,128]{2,1,0:T(8,128)S(1)}, f32[1,160,128]{2,1,0:T(8,128)S(1)}, u32[]{:S(2)}, u32[]{:S(2)}) collective-permute-start(f32[1,160,128]{2,1,0:T(8,128)S(1)} %get-tuple-element.34), channel_id=1, source_target_pairs={{8,0},{16,8},{24,16},{9,1},{17,9},{25,17},{10,2},{18,10},{26,18},{... | collective-permute-start | bytes 245768 | tf_op jit(solution)/shard_map/ppermute | solution.py:22
  91.3 7.2 %collective-permute-start.10 = (f32[1,160,128]{2,1,0:T(8,128)S(1)}, f32[1,160,128]{2,1,0:T(8,128)S(1)}, u32[]{:S(2)}, u32[]{:S(2)}) collective-permute-start(f32[1,160,128]{2,1,0:T(8,128)S(1)} %get-tuple-element.35), channel_id=1, source_target_pairs={{0,8},{8,16},{16,24},{1,9},{9,17},{17,25},{2,10},{10,18},{18,26},{... | collective-permute-start | bytes 245768 | tf_op jit(solution)/shard_map/ppermute | solution.py:20
  95.3 7.0 %collective-permute-start.9 = (f32[1,160,128]{2,1,0:T(8,128)S(1)}, f32[1,160,128]{2,1,0:T(8,128)S(1)}, u32[]{:S(2)}, u32[]{:S(2)}) collective-permute-start(f32[1,160,128]{2,1,0:T(8,128)S(1)} %get-tuple-element.36), channel_id=1, source_target_pairs={{1,0},{2,1},{3,2},{4,3},{5,4},{6,5},{7,6},{9,8},{10,9},{11,10},{12... | collective-permute-start | bytes 245768 | tf_op jit(solution)/shard_map/ppermute | solution.py:22
  105.1 24.6 %copy-start.21 = (f32[48,384]{1,0:T(8,128)S(1)}, f32[48,384]{1,0:T(8,128)}, u32[]{:S(2)}) copy-start(f32[48,384]{1,0:T(8,128)} %param.19) | copy-start | bytes 221188
  105.6 24.3 %copy-start.26 = (f32[1,48,48]{2,1,0:T(8,128)S(1)}, f32[1,48,48]{2,1,0:T(8,128)}, u32[]{:S(2)}) copy-start(f32[1,48,48]{2,1,0:T(8,128)} %param.18) | copy-start | bytes 27652
  107.3 23.5 %copy-start.30 = (s32[1024]{0:T(1024)S(1)}, s32[1024]{0:T(1024)}, u32[]{:S(2)}) copy-start(s32[1024]{0:T(1024)} %copy-done.29) | copy-start | bytes 12292
  132.6 10.2 %collective-permute-start.12 = (f32[1,160,128]{2,1,0:T(8,128)S(1)}, f32[1,160,128]{2,1,0:T(8,128)S(1)}, u32[]{:S(2)}, u32[]{:S(2)}) collective-permute-start(f32[1,160,128]{2,1,0:T(8,128)S(1)} %get-tuple-element.29), channel_id=1, source_target_pairs={{0,1},{1,2},{2,3},{3,4},{4,5},{5,6},{6,7},{8,9},{9,10},{10,11},{11... | collective-permute-start | bytes 245768 | tf_op jit(solution)/shard_map/ppermute | solution.py:20
  134.6 8.3 %collective-permute-start.15 = (f32[1,160,128]{2,1,0:T(8,128)S(1)}, f32[1,160,128]{2,1,0:T(8,128)S(1)}, u32[]{:S(2)}, u32[]{:S(2)}) collective-permute-start(f32[1,160,128]{2,1,0:T(8,128)S(1)} %get-tuple-element.30), channel_id=1, source_target_pairs={{8,0},{16,8},{24,16},{9,1},{17,9},{25,17},{10,2},{18,10},{26,18},{... | collective-permute-start | bytes 245768 | tf_op jit(solution)/shard_map/ppermute | solution.py:22
  135.9 7.0 %collective-permute-start.14 = (f32[1,160,128]{2,1,0:T(8,128)S(1)}, f32[1,160,128]{2,1,0:T(8,128)S(1)}, u32[]{:S(2)}, u32[]{:S(2)}) collective-permute-start(f32[1,160,128]{2,1,0:T(8,128)S(1)} %get-tuple-element.31), channel_id=1, source_target_pairs={{0,8},{8,16},{16,24},{1,9},{9,17},{17,25},{2,10},{10,18},{18,26},{... | collective-permute-start | bytes 245768 | tf_op jit(solution)/shard_map/ppermute | solution.py:20
  139.9 5.8 %collective-permute-start.13 = (f32[1,160,128]{2,1,0:T(8,128)S(1)}, f32[1,160,128]{2,1,0:T(8,128)S(1)}, u32[]{:S(2)}, u32[]{:S(2)}) collective-permute-start(f32[1,160,128]{2,1,0:T(8,128)S(1)} %get-tuple-element.32), channel_id=1, source_target_pairs={{1,0},{2,1},{3,2},{4,3},{5,4},{6,5},{7,6},{9,8},{10,9},{11,10},{12... | collective-permute-start | bytes 245768 | tf_op jit(solution)/shard_map/ppermute | solution.py:22
  148.1 4.1 %copy-start.2 = (f32[1,1,640,640]{3,2,1,0:T(8,128)S(1)}, f32[1,1,640,640]{3,2,1,0:T(8,128)}, u32[]{:S(2)}) copy-start(f32[1,1,640,640]{3,2,1,0:T(8,128)} %param.12) | copy-start | bytes 4915204
  157.9 10.2 %collective-permute-start.16 = (f32[1,160,128]{2,1,0:T(8,128)S(1)}, f32[1,160,128]{2,1,0:T(8,128)S(1)}, u32[]{:S(2)}, u32[]{:S(2)}) collective-permute-start(f32[1,160,128]{2,1,0:T(8,128)S(1)} %get-tuple-element.25), channel_id=1, source_target_pairs={{0,1},{1,2},{2,3},{3,4},{4,5},{5,6},{6,7},{8,9},{9,10},{10,11},{11... | collective-permute-start | bytes 245768 | tf_op jit(solution)/shard_map/ppermute | solution.py:20
  159.8 8.3 %collective-permute-start.19 = (f32[1,160,128]{2,1,0:T(8,128)S(1)}, f32[1,160,128]{2,1,0:T(8,128)S(1)}, u32[]{:S(2)}, u32[]{:S(2)}) collective-permute-start(f32[1,160,128]{2,1,0:T(8,128)S(1)} %get-tuple-element.26), channel_id=1, source_target_pairs={{8,0},{16,8},{24,16},{9,1},{17,9},{25,17},{10,2},{18,10},{26,18},{... | collective-permute-start | bytes 245768 | tf_op jit(solution)/shard_map/ppermute | solution.py:22
  161.1 7.0 %collective-permute-start.18 = (f32[1,160,128]{2,1,0:T(8,128)S(1)}, f32[1,160,128]{2,1,0:T(8,128)S(1)}, u32[]{:S(2)}, u32[]{:S(2)}) collective-permute-start(f32[1,160,128]{2,1,0:T(8,128)S(1)} %get-tuple-element.27), channel_id=1, source_target_pairs={{0,8},{8,16},{16,24},{1,9},{9,17},{17,25},{2,10},{10,18},{18,26},{... | collective-permute-start | bytes 245768 | tf_op jit(solution)/shard_map/ppermute | solution.py:20
  165.1 6.9 %collective-permute-start.17 = (f32[1,160,128]{2,1,0:T(8,128)S(1)}, f32[1,160,128]{2,1,0:T(8,128)S(1)}, u32[]{:S(2)}, u32[]{:S(2)}) collective-permute-start(f32[1,160,128]{2,1,0:T(8,128)S(1)} %get-tuple-element.28), channel_id=1, source_target_pairs={{1,0},{2,1},{3,2},{4,3},{5,4},{6,5},{7,6},{9,8},{10,9},{11,10},{12... | collective-permute-start | bytes 245768 | tf_op jit(solution)/shard_map/ppermute | solution.py:22
  174.7 24.7 %copy-start.22 = (f32[48,384]{1,0:T(8,128)S(1)}, f32[48,384]{1,0:T(8,128)}, u32[]{:S(2)}) copy-start(f32[48,384]{1,0:T(8,128)} %param.19) | copy-start | bytes 221188
  175.2 24.4 %copy-start.27 = (f32[1,48,48]{2,1,0:T(8,128)S(1)}, f32[1,48,48]{2,1,0:T(8,128)}, u32[]{:S(2)}) copy-start(f32[1,48,48]{2,1,0:T(8,128)} %param.18) | copy-start | bytes 27652
  176.9 23.6 %copy-start.31 = (s32[1024]{0:T(1024)S(1)}, s32[1024]{0:T(1024)}, u32[]{:S(2)}) copy-start(s32[1024]{0:T(1024)} %copy-done.29) | copy-start | bytes 12292
  200.2 17.1 %copy-start.8 = (f32[640,128]{0,1:T(8,128)}, f32[640,128]{0,1:T(8,128)S(1)}, u32[]{:S(2)}) copy-start(f32[640,128]{0,1:T(8,128)S(1)} %fusion.17) | copy-start | bytes 983044
  202.3 10.2 %collective-permute-start.20 = (f32[1,160,128]{2,1,0:T(8,128)S(1)}, f32[1,160,128]{2,1,0:T(8,128)S(1)}, u32[]{:S(2)}, u32[]{:S(2)}) collective-permute-start(f32[1,160,128]{2,1,0:T(8,128)S(1)} %get-tuple-element.21), channel_id=1, source_target_pairs={{0,1},{1,2},{2,3},{3,4},{4,5},{5,6},{6,7},{8,9},{9,10},{10,11},{11... | collective-permute-start | bytes 245768 | tf_op jit(solution)/shard_map/ppermute | solution.py:20
  204.2 8.3 %collective-permute-start.23 = (f32[1,160,128]{2,1,0:T(8,128)S(1)}, f32[1,160,128]{2,1,0:T(8,128)S(1)}, u32[]{:S(2)}, u32[]{:S(2)}) collective-permute-start(f32[1,160,128]{2,1,0:T(8,128)S(1)} %get-tuple-element.22), channel_id=1, source_target_pairs={{8,0},{16,8},{24,16},{9,1},{17,9},{25,17},{10,2},{18,10},{26,18},{... | collective-permute-start | bytes 245768 | tf_op jit(solution)/shard_map/ppermute | solution.py:22
  205.5 7.0 %collective-permute-start.22 = (f32[1,160,128]{2,1,0:T(8,128)S(1)}, f32[1,160,128]{2,1,0:T(8,128)S(1)}, u32[]{:S(2)}, u32[]{:S(2)}) collective-permute-start(f32[1,160,128]{2,1,0:T(8,128)S(1)} %get-tuple-element.23), channel_id=1, source_target_pairs={{0,8},{8,16},{16,24},{1,9},{9,17},{17,25},{2,10},{10,18},{18,26},{... | collective-permute-start | bytes 245768 | tf_op jit(solution)/shard_map/ppermute | solution.py:20
  209.5 5.8 %collective-permute-start.21 = (f32[1,160,128]{2,1,0:T(8,128)S(1)}, f32[1,160,128]{2,1,0:T(8,128)S(1)}, u32[]{:S(2)}, u32[]{:S(2)}) collective-permute-start(f32[1,160,128]{2,1,0:T(8,128)S(1)} %get-tuple-element.24), channel_id=1, source_target_pairs={{1,0},{2,1},{3,2},{4,3},{5,4},{6,5},{7,6},{9,8},{10,9},{11,10},{12... | collective-permute-start | bytes 245768 | tf_op jit(solution)/shard_map/ppermute | solution.py:22
  217.3 3.4 %copy-start.19 = (f32[640,128]{0,1:T(8,128)}, f32[640,128]{0,1:T(8,128)S(1)}, u32[]{:S(2)}) copy-start(f32[640,128]{0,1:T(8,128)S(1)} %copy.65) | copy-start | bytes 983044
  223.5 10.2 %collective-permute-start.24 = (f32[1,160,128]{2,1,0:T(8,128)S(1)}, f32[1,160,128]{2,1,0:T(8,128)S(1)}, u32[]{:S(2)}, u32[]{:S(2)}) collective-permute-start(f32[1,160,128]{2,1,0:T(8,128)S(1)} %get-tuple-element.17), channel_id=1, source_target_pairs={{0,1},{1,2},{2,3},{3,4},{4,5},{5,6},{6,7},{8,9},{9,10},{10,11},{11... | collective-permute-start | bytes 245768 | tf_op jit(solution)/shard_map/ppermute | solution.py:20
  225.5 8.3 %collective-permute-start.27 = (f32[1,160,128]{2,1,0:T(8,128)S(1)}, f32[1,160,128]{2,1,0:T(8,128)S(1)}, u32[]{:S(2)}, u32[]{:S(2)}) collective-permute-start(f32[1,160,128]{2,1,0:T(8,128)S(1)} %get-tuple-element.18), channel_id=1, source_target_pairs={{8,0},{16,8},{24,16},{9,1},{17,9},{25,17},{10,2},{18,10},{26,18},{... | collective-permute-start | bytes 245768 | tf_op jit(solution)/shard_map/ppermute | solution.py:22
  226.8 7.0 %collective-permute-start.26 = (f32[1,160,128]{2,1,0:T(8,128)S(1)}, f32[1,160,128]{2,1,0:T(8,128)S(1)}, u32[]{:S(2)}, u32[]{:S(2)}) collective-permute-start(f32[1,160,128]{2,1,0:T(8,128)S(1)} %get-tuple-element.19), channel_id=1, source_target_pairs={{0,8},{8,16},{16,24},{1,9},{9,17},{17,25},{2,10},{10,18},{18,26},{... | collective-permute-start | bytes 245768 | tf_op jit(solution)/shard_map/ppermute | solution.py:20
  230.8 7.0 %collective-permute-start.25 = (f32[1,160,128]{2,1,0:T(8,128)S(1)}, f32[1,160,128]{2,1,0:T(8,128)S(1)}, u32[]{:S(2)}, u32[]{:S(2)}) collective-permute-start(f32[1,160,128]{2,1,0:T(8,128)S(1)} %get-tuple-element.20), channel_id=1, source_target_pairs={{1,0},{2,1},{3,2},{4,3},{5,4},{6,5},{7,6},{9,8},{10,9},{11,10},{12... | collective-permute-start | bytes 245768 | tf_op jit(solution)/shard_map/ppermute | solution.py:22
  239.9 24.5 %copy-start.23 = (f32[48,384]{1,0:T(8,128)S(1)}, f32[48,384]{1,0:T(8,128)}, u32[]{:S(2)}) copy-start(f32[48,384]{1,0:T(8,128)} %param.19) | copy-start | bytes 221188
  240.4 24.3 %copy-start.28 = (f32[1,48,48]{2,1,0:T(8,128)S(1)}, f32[1,48,48]{2,1,0:T(8,128)}, u32[]{:S(2)}) copy-start(f32[1,48,48]{2,1,0:T(8,128)} %param.18) | copy-start | bytes 27652
  242.1 23.4 %copy-start.32 = (s32[1024]{0:T(1024)S(1)}, s32[1024]{0:T(1024)}, u32[]{:S(2)}) copy-start(s32[1024]{0:T(1024)} %copy-done.29) | copy-start | bytes 12292
  267.4 10.5 %collective-permute-start.28 = (f32[1,160,128]{2,1,0:T(8,128)S(1)}, f32[1,160,128]{2,1,0:T(8,128)S(1)}, u32[]{:S(2)}, u32[]{:S(2)}) collective-permute-start(f32[1,160,128]{2,1,0:T(8,128)S(1)} %get-tuple-element.13), channel_id=1, source_target_pairs={{0,1},{1,2},{2,3},{3,4},{4,5},{5,6},{6,7},{8,9},{9,10},{10,11},{11... | collective-permute-start | bytes 245768 | tf_op jit(solution)/shard_map/ppermute | solution.py:20
  269.3 8.5 %collective-permute-start.31 = (f32[1,160,128]{2,1,0:T(8,128)S(1)}, f32[1,160,128]{2,1,0:T(8,128)S(1)}, u32[]{:S(2)}, u32[]{:S(2)}) collective-permute-start(f32[1,160,128]{2,1,0:T(8,128)S(1)} %get-tuple-element.14), channel_id=1, source_target_pairs={{8,0},{16,8},{24,16},{9,1},{17,9},{25,17},{10,2},{18,10},{26,18},{... | collective-permute-start | bytes 245768 | tf_op jit(solution)/shard_map/ppermute | solution.py:22
  270.6 7.3 %collective-permute-start.30 = (f32[1,160,128]{2,1,0:T(8,128)S(1)}, f32[1,160,128]{2,1,0:T(8,128)S(1)}, u32[]{:S(2)}, u32[]{:S(2)}) collective-permute-start(f32[1,160,128]{2,1,0:T(8,128)S(1)} %get-tuple-element.15), channel_id=1, source_target_pairs={{0,8},{8,16},{16,24},{1,9},{9,17},{17,25},{2,10},{10,18},{18,26},{... | collective-permute-start | bytes 245768 | tf_op jit(solution)/shard_map/ppermute | solution.py:20
  274.6 5.8 %collective-permute-start.29 = (f32[1,160,128]{2,1,0:T(8,128)S(1)}, f32[1,160,128]{2,1,0:T(8,128)S(1)}, u32[]{:S(2)}, u32[]{:S(2)}) collective-permute-start(f32[1,160,128]{2,1,0:T(8,128)S(1)} %get-tuple-element.16), channel_id=1, source_target_pairs={{1,0},{2,1},{3,2},{4,3},{5,4},{6,5},{7,6},{9,8},{10,9},{11,10},{12... | collective-permute-start | bytes 245768 | tf_op jit(solution)/shard_map/ppermute | solution.py:22
  280.6 4.2 %copy-start.41 = (pred[640]{0:T(1024)(128)(4,1)S(1)}, pred[640]{0:T(1024)(128)(4,1)}, u32[]{:S(2)}) copy-start(pred[640]{0:T(1024)(128)(4,1)} %copy-done.39) | copy-start | bytes 1924
  282.8 4.2 %copy-start.3 = (f32[1,1,640,640]{3,2,1,0:T(8,128)S(1)}, f32[1,1,640,640]{3,2,1,0:T(8,128)}, u32[]{:S(2)}) copy-start(f32[1,1,640,640]{3,2,1,0:T(8,128)} %param.12) | copy-start | bytes 4915204
  287.0 3.5 %copy-start.33 = (s32[1024]{0:T(1024)S(1)}, s32[1024]{0:T(1024)}, u32[]{:S(2)}) copy-start(s32[1024]{0:T(1024)} %copy-done.29) | copy-start | bytes 12292
  290.6 12.1 %copy-start.14 = (f32[640,128]{0,1:T(8,128)S(1)}, f32[640,128]{0,1:T(8,128)}, u32[]{:S(2)}) copy-start(f32[640,128]{0,1:T(8,128)} %copy-done.13) | copy-start | bytes 983044
  292.4 11.1 %collective-permute-start.32 = (f32[1,160,128]{2,1,0:T(8,128)S(1)}, f32[1,160,128]{2,1,0:T(8,128)S(1)}, u32[]{:S(2)}, u32[]{:S(2)}) collective-permute-start(f32[1,160,128]{2,1,0:T(8,128)S(1)} %get-tuple-element.9), channel_id=1, source_target_pairs={{0,1},{1,2},{2,3},{3,4},{4,5},{5,6},{6,7},{8,9},{9,10},{10,11},{11... | collective-permute-start | bytes 245768 | tf_op jit(solution)/shard_map/ppermute | solution.py:20
  294.4 9.2 %collective-permute-start.35 = (f32[1,160,128]{2,1,0:T(8,128)S(1)}, f32[1,160,128]{2,1,0:T(8,128)S(1)}, u32[]{:S(2)}, u32[]{:S(2)}) collective-permute-start(f32[1,160,128]{2,1,0:T(8,128)S(1)} %get-tuple-element.10), channel_id=1, source_target_pairs={{8,0},{16,8},{24,16},{9,1},{17,9},{25,17},{10,2},{18,10},{26,18},{... | collective-permute-start | bytes 245768 | tf_op jit(solution)/shard_map/ppermute | solution.py:22
  295.7 7.9 %collective-permute-start.34 = (f32[1,160,128]{2,1,0:T(8,128)S(1)}, f32[1,160,128]{2,1,0:T(8,128)S(1)}, u32[]{:S(2)}, u32[]{:S(2)}) collective-permute-start(f32[1,160,128]{2,1,0:T(8,128)S(1)} %get-tuple-element.11), channel_id=1, source_target_pairs={{0,8},{8,16},{16,24},{1,9},{9,17},{17,25},{2,10},{10,18},{18,26},{... | collective-permute-start | bytes 245768 | tf_op jit(solution)/shard_map/ppermute | solution.py:20
  299.7 6.8 %collective-permute-start.33 = (f32[1,160,128]{2,1,0:T(8,128)S(1)}, f32[1,160,128]{2,1,0:T(8,128)S(1)}, u32[]{:S(2)}, u32[]{:S(2)}) collective-permute-start(f32[1,160,128]{2,1,0:T(8,128)S(1)} %get-tuple-element.12), channel_id=1, source_target_pairs={{1,0},{2,1},{3,2},{4,3},{5,4},{6,5},{7,6},{9,8},{10,9},{11,10},{12... | collective-permute-start | bytes 245768 | tf_op jit(solution)/shard_map/ppermute | solution.py:22
  (16 other events, 28.6 us)
where the time goes:
time: 311 us; the launch traced here: 310 us
  blocking collectives  103 us (33%)
  starting transfers between devices  93.5 us (30%)
  local copies, waits for them, and re-layouts  49.7 us (16%)
  waiting for transfers between devices  25.9 us (8%)
  matrix products  25.6 us (8%)
  other arithmetic  9.68 us (3%)
    ppermute x18, starting transfers between devices, extended(): lax.ppermute(tail, axis, [(i, (i + 1) % count) for i in range(ends)])  56.1 us
    all_gather x4, blocking collectives, shards(): lax.all_gather(level_three, 'col', axis=0, tiled=True)  50.3 us
    all_gather x4, blocking collectives, shards(): piece = lax.all_gather(coeffs, 'row', axis=0, tiled=True)  41.5 us
    ppermute x18, starting transfers between devices, extended(): lax.ppermute(head, axis, [((i + 1) % count, i) for i in range(ends)])  37.4 us
    ppermute x18, waiting for transfers between devices, extended(): lax.ppermute(head, axis, [((i + 1) % count, i) for i in range(ends)])  25.8 us
    dot_general x24, matrix products, product(): jnp.dot(left, right, precision=lax.Precision.HIGHEST, preferred_element_t...  22.4 us
    gather x18, local copies, waits for them, and re-layouts, assemble(): jnp.take(received.reshape(interface_size, columns), inverse_list, axis=0)  21.2 us
    gather x9, local copies, waits for them, and re-layouts, assemble(): jnp.take(field, index_list, axis=0).reshape(4, face_size, columns)  17.1 us
  transfers between devices with their start and end apart: 36, of which 8 were waited for; matrix products, arithmetic and copies ran while one was open for 2% of the time, Pallas kernels for 0%

commit v1 on v0

v1 whole, which is shorter than its diff:
```python
import functools
import math

import jax
import jax.numpy as jnp
from jax import lax
from jax.experimental import pallas as pl
from jax.experimental.pallas import tpu as pltpu
from jax.sharding import PartitionSpec as P

DEGREE = 2
STEPS = 4
LANES = 128
INTERPRET = False
F32 = jnp.float32
BF16 = jnp.bfloat16


def split(x, parts):
    pieces = []
    for _ in range(parts - 1):
        piece = x.astype(BF16)
        pieces.append(piece)
        x = x - piece.astype(F32)
    pieces.append(x.astype(BF16))
    return pieces


def stack_split(x):
    return jnp.concatenate(split(x, 2), axis=0)


def dot(left, right):
    return jnp.dot(left, right, preferred_element_type=F32)


def product_parts(left2, right_parts):
    rows = left2.shape[0] // 2
    n = right_parts[0].shape[1]
    out = dot(left2, jnp.concatenate(right_parts, axis=1))
    out = out[:rows] + out[rows:]
    return out[:, :n] + out[:, n:]


def product(left2, right):
    return product_parts(left2, split(right, 2))


def permuted(onehot, x, parts=3):
    n = x.shape[1]
    out = dot(onehot, jnp.concatenate(split(x, parts), axis=1))
    total = out[:, (parts - 1) * n :]
    for i in reversed(range(parts - 1)):
        total = out[:, i * n : (i + 1) * n] + total
    return total


def call(body, out_shapes, scalars, arrays, flops=0, scratch=()):
    smem = pl.BlockSpec(memory_space=pltpu.SMEM)
    vmem = pl.BlockSpec(memory_space=pltpu.VMEM)
    moved = sum(a.size * a.dtype.itemsize for a in arrays)
    return pl.pallas_call(
        body,
        out_shape=[jax.ShapeDtypeStruct(s, d) for s, d in out_shapes],
        in_specs=[smem] * len(scalars) + [vmem] * len(arrays),
        out_specs=[vmem] * len(out_shapes),
        scratch_shapes=[pltpu.VMEM(shape, F32) for shape in scratch],
        compiler_params=pltpu.CompilerParams(vmem_limit_bytes=24 * 2**20),
        cost_estimate=pl.CostEstimate(flops=flops, bytes_accessed=moved, transcendentals=0),
        interpret=INTERPRET,
    )(*scalars, *arrays)


def start_kernel(row_ref, col_ref, load_ref, basis_ref, map_ref, perm_ref, back_ref, load_out, basis_out, coarse_out):
    size = perm_ref.shape[0]
    perm = jnp.where(row_ref[...] == lax.broadcasted_iota(jnp.int32, (size, size), 1), 1.0, 0.0).astype(BF16)
    back_ref[...] = jnp.where(
        col_ref[...] == lax.broadcasted_iota(jnp.int32, (size, size), 0), 1.0, 0.0
    ).astype(BF16)
    perm_ref[...] = perm
    load_out[...] = permuted(perm, load_ref[...])
    basis = permuted(perm, basis_ref[...])
    basis_out[...] = basis
    coarse_out[...] = product(stack_split(basis), map_ref[...])


def split_kernel(*refs):
    half = len(refs) // 2
    for x_ref, o_ref in zip(refs[:half], refs[half:]):
        o_ref[...] = stack_split(x_ref[...])


def stacked(*arrays):
    return call(split_kernel, [((2 * a.shape[0], a.shape[1]), BF16) for a in arrays], [], arrays)


def level_kernel(
    face,
    link_ref,
    basis_ref,
    inverse_ref,
    map_top_ref,
    top_ref,
    basis_g_ref,
    basis_h_ref,
    inverse_g_ref,
    inverse_h_ref,
    map_g_ref,
    map_h_ref,
    coarse_e_ref,
    coarse_f_ref,
    top_e_ref,
    top_f_ref,
    two_ref,
    top_out_ref,
):
    coarse = map_top_ref[...]
    basis = basis_ref[...]
    top = top_ref[...]
    link = [link_ref[i].astype(F32) for i in range(4)]
    basis_g, basis_h = basis_g_ref[...] * link[2], basis_h_ref[...] * link[3]
    two = product(stack_split(basis), inverse_ref[...])
    two_g = product(stack_split(basis_g), inverse_g_ref[...])
    two_h = product(stack_split(basis_h), inverse_h_ref[...])
    two = jnp.concatenate([two[: 2 * face], two[2 * face : 3 * face] + two_g, two[3 * face :] + two_h], axis=0)
    two_ref[...] = stack_split(two)
    coarse_g = product(stack_split(basis_g), map_g_ref[...])
    coarse_h = product(stack_split(basis_h), map_h_ref[...])
    coarse = jnp.concatenate(
        [coarse[: 2 * face], coarse[2 * face : 3 * face] + coarse_g, coarse[3 * face :] + coarse_h], axis=0
    )
    out = product(stack_split(coarse), top)
    out_e = product(stack_split(coarse_e_ref[...] * link[0]), top_e_ref[...])
    out_f = product(stack_split(coarse_f_ref[...] * link[1]), top_f_ref[...])
    out = jnp.concatenate([out[:face] + out_e, out[face : 2 * face] + out_f, out[2 * face :]], axis=0)
    top_out_ref[...] = stack_split(out)


def received(link_ref, refs):
    return jnp.concatenate([r[...] * link_ref[i].astype(F32) for i, r in enumerate(refs)], axis=0)


def assemble_kernel(link_ref, load_ref, r0, r1, r2, r3, out_ref):
    out_ref[...] = load_ref[...] + received(link_ref, (r0, r1, r2, r3))


def current_kernel(first, face, *refs):
    if first:
        asm_ref, basis_ref, map_ref, inverse_ref, perm_ref, back_ref = refs[:6]
        outs = refs[6:]
        current = asm_ref[...]
    else:
        link_ref = refs[0]
        f_ref, r0, r1, r2, r3, asm_ref, basis_ref, map_ref, inverse_ref, perm_ref, back_ref = refs[1:12]
        outs = refs[12:]
        current = asm_ref[...] - (f_ref[...] + received(link_ref, (r0, r1, r2, r3)))
    y_ref, g_ref, h_ref, c_ref = outs
    coarse = basis_ref.shape[0] // 2
    parts = split(current, 2)
    coeffs = product_parts(basis_ref[...], parts)
    moved = dot(back_ref[...], jnp.concatenate(parts, axis=1)).astype(BF16)
    n = current.shape[1]
    y = product_parts(inverse_ref[...], [moved[:, :n], moved[:, n:]])
    y = permuted(perm_ref[...], y)
    y_ref[...] = y
    third = product(map_ref[...], coeffs)
    c_ref[:coarse] = coeffs
    c_ref[coarse:] = third
    for ref, k in ((g_ref, 2), (h_ref, 3)):
        ref[:face] = y[k * face : (k + 1) * face]
        ref[face : face + coarse] = coeffs
        ref[face + coarse :] = third


def group_kernel(face, pieces, coarse, link_ref, order_ref, y_ref, g_ref, h_ref, two_ref, *refs):
    cs = refs[:pieces]
    y2_ref, e_ref, third_ref, stack_ref = refs[pieces:]
    third = None
    for i, c in enumerate(cs):
        start = c.shape[0] - 2 * coarse
        offset = pl.multiple_of(order_ref[i], 8)
        stack_ref[pl.ds(offset, coarse)] = c[start : start + coarse]
        part = c[start + coarse :]
        third = part if third is None else third + part
    y = y_ref[...] + product(two_ref[...], stack_ref[...])
    y2_ref[: 2 * face] = y[: 2 * face]
    y2_ref[2 * face : 3 * face] = y[2 * face : 3 * face] + g_ref[:face] * link_ref[2].astype(F32)
    y2_ref[3 * face :] = y[3 * face :] + h_ref[:face] * link_ref[3].astype(F32)
    e_ref[:face] = y[:face]
    e_ref[face:] = third
    third_ref[...] = third


def update_kernel(weight, first, face, starts, top, link_ref, order_ref, y2_ref, e_ref, f_ref, top_ref, perm_ref, back_ref, schur_ref, *refs):
    if not first:
        old_ref, refs = refs[0], refs[1:]
    x_ref, out_ref, stack_ref = refs[len(starts) :]
    slot = 0
    for ref, first_row in zip(refs, starts):
        for start in range(first_row, ref.shape[0], top):
            offset = pl.multiple_of(order_ref[slot], 8)
            stack_ref[pl.ds(offset, top)] = ref[start : start + top]
            slot += 1
    y2 = y2_ref[...] + product(top_ref[...], stack_ref[...])
    update = jnp.concatenate(
        [
            y2[:face] + e_ref[:face] * link_ref[0].astype(F32),
            y2[face : 2 * face] + f_ref[...] * link_ref[1].astype(F32),
            y2[2 * face :],
        ],
        axis=0,
    )
    x = weight * permuted(back_ref[...], update)
    if not first:
        x = old_ref[...] + x
    x_ref[...] = x
    out_ref[...] = permuted(perm_ref[...], product(schur_ref[...], x))


def residual_kernel(link_ref, f_ref, r0, r1, r2, r3, asm_ref, back_ref, out_ref):
    current = asm_ref[...] - (f_ref[...] + received(link_ref, (r0, r1, r2, r3)))
    out_ref[...] = permuted(back_ref[...], current)


def xor_pairs(count, bits):
    return [(i, i ^ bits) for i in range(count) if i ^ bits < count]


def odd_pairs(count):
    return [(i, i + 1 if i % 2 else i - 1) for i in range(count) if 0 <= (i + 1 if i % 2 else i - 1) < count]


def swap(x, axis, pairs):
    return lax.ppermute(x, axis, pairs)


def lanes(x):
    width = -(-x.shape[1] // LANES) * LANES
    x = jnp.pad(x, ((0, 0), (0, width - x.shape[1])))
    return jnp.concatenate([x[:, i : i + LANES] for i in range(0, width, LANES)], axis=0)


def unlanes(x, rows, columns):
    parts = [x[i : i + rows] for i in range(0, x.shape[0], rows)]
    return jnp.concatenate(parts, axis=1)[:, :columns]


def shards(
    load,
    schur,
    local_inverse,
    iface_index,
    face_link,
    coarse_basis,
    coarse_inverse,
    coarse_map,
    top_inverse,
):
    loads, basis = load[0, 0], coarse_basis[0, 0]
    inverse_rows, map_block = coarse_inverse[0], coarse_map[0]
    size, columns = loads.shape
    face = size // 4
    coarse, top = basis.shape[1], map_block.shape[1]
    rows, cols = lax.axis_size("row"), lax.axis_size("col")
    row, col = lax.axis_index("row"), lax.axis_index("col")
    width = top_inverse.shape[1]

    def by_partner(x):
        west, east, south, north = x
        even_col, even_row = col % 2 == 0, row % 2 == 0
        return [
            jnp.where(even_col, east, west),
            jnp.where(even_col, west, east),
            jnp.where(even_row, north, south),
            jnp.where(even_row, south, north),
        ]

    index = jnp.concatenate(by_partner(iface_index[0, 0].reshape(4, face)))
    link = jnp.stack(by_partner(face_link[0, 0]))

    col_even, col_odd = xor_pairs(cols, 1), odd_pairs(cols)
    row_even, row_odd = xor_pairs(rows, 1), odd_pairs(rows)
    ring = rows == 4
    if ring:
        row_odd = xor_pairs(rows, 3)
    doubling = cols & (cols - 1) == 0

    def exchange(parts):
        return [
            swap(parts[0], "col", col_even),
            swap(parts[1], "col", col_odd),
            swap(parts[2], "row", row_even),
            swap(parts[3], "row", row_odd),
        ]

    def faces(x):
        return [x[i * face : (i + 1) * face] for i in range(4)]

    n = (size, columns)
    perm, back, load_f, basis_f, coarse_f = call(
        start_kernel,
        [((size, size), BF16), ((size, size), BF16), (n, F32), ((size, coarse), F32), ((size, top), F32)],
        [],
        [index.reshape(size, 1), index.reshape(1, size), loads, basis, map_block],
        flops=4 * size**2 * columns,
    )
    schur2, inverse2 = stacked(schur[0, 0], local_inverse[0, 0])
    basis2, map2 = stacked(basis_f.T, map_block.T)

    along_col = lanes(top_inverse)
    along_row = jnp.concatenate([lanes(inverse_rows), lanes(map_block)])
    got = exchange(
        [jnp.concatenate([x, lanes(y), along_col]) for x, y in zip(faces(load_f)[:2], faces(coarse_f)[:2])]
        + [jnp.concatenate([x, lanes(y), along_row]) for x, y in zip(faces(load_f)[2:], faces(basis_f)[2:])]
    )
    assembled = call(assemble_kernel, [(n, F32)], [link], [load_f] + [g[:face] for g in got])[0]
    second = [g[face : 2 * face] for g in got]
    rest = [g[2 * face :] for g in got]
    split_at = lanes(inverse_rows).shape[0]
    total = rows * coarse
    two2, top2 = call(
        functools.partial(level_kernel, face),
        [((2 * size, total), BF16), ((2 * size, width), BF16)],
        [link],
        [basis_f, inverse_rows, coarse_f, top_inverse]
        + [second[2][:, :coarse], second[3][:, :coarse]]
        + [unlanes(rest[k][:split_at], coarse, total) for k in (2, 3)]
        + [unlanes(rest[k][split_at:], coarse, top) for k in (2, 3)]
        + [second[0][:, :top], second[1][:, :top]]
        + [unlanes(rest[k], top, width) for k in (0, 1)],
    )

    if ring:
        row_order = jnp.stack([(row ^ i) * coarse for i in range(rows)])
    else:
        row_order = jnp.arange(rows, dtype=jnp.int32) * coarse
    if doubling:
        col_order = jnp.stack([(col ^ i) * top for i in range(cols)])
    else:
        col_order = jnp.arange(cols, dtype=jnp.int32) * top

    solution, field = None, None
    square = 8 * size * size * columns
    for step_index in range(STEPS):
        phase = step_index % DEGREE
        weight = 1.0 / (1.4 - math.cos(math.pi * (2 * phase + 1) / (2 * DEGREE)))
        first = step_index == 0
        stationary = [assembled, basis2, map2, inverse2, perm, back]
        if first:
            head, scalars = [], []
        else:
            head, scalars = [field] + exchange(faces(field)), [link]
        y, pay_g, pay_h, coeffs = call(
            functools.partial(current_kernel, first, face),
            [
                (n, F32),
                ((face + coarse + top, columns), F32),
                ((face + coarse + top, columns), F32),
                ((coarse + top, columns), F32),
            ],
            scalars,
            head + stationary,
            flops=2 * square,
        )
        got_g = swap(pay_g, "row", row_even)
        got_h = swap(pay_h, "row", row_odd)
        if ring:
            got_r = swap(coeffs, "row", xor_pairs(rows, 2))
            pieces = [coeffs, got_g, got_r, got_h]
        else:
            everyone = lax.all_gather(coeffs, "row", axis=0)
            pieces = [everyone[i] for i in range(rows)]
        y2, pay_e, third = call(
            functools.partial(group_kernel, face, len(pieces), coarse),
            [(n, F32), ((face + top, columns), F32), ((top, columns), F32)],
            [link, row_order],
            [y, got_g, got_h, two2] + pieces,
            scratch=[(total, columns)],
        )
        got_e = swap(pay_e, "col", col_even)
        got_f = swap(y2[face : 2 * face], "col", col_odd)
        starts = [0]
        if doubling:
            tops = [third, got_e]
            starts = [0, face]
            known = jnp.concatenate([third, got_e[face:]])
            bits = 2
            while bits < cols:
                more = swap(known, "col", xor_pairs(cols, bits))
                tops.append(more)
                starts.append(0)
                known = jnp.concatenate([known, more])
                bits *= 2
        else:
            tops = [lax.all_gather(third, "col", axis=0, tiled=True)]
        solution, field = call(
            functools.partial(update_kernel, weight, first, face, starts, top),
            [(n, F32), (n, F32)],
            [link, col_order],
            [y2, got_e, got_f, top2, perm, back, schur2] + ([] if first else [solution]) + tops,
            flops=2 * square,
            scratch=[(width, columns)],
        )
    residual = call(
        residual_kernel,
        [(n, F32)],
        [link],
        [field] + exchange(faces(field)) + [assembled, back],
    )[0]
    return (solution[None, None], residual[None, None])


def solution(mesh):
    return jax.shard_map(
        shards,
        mesh=mesh,
        in_specs=(
            P("row", "col", None, None),
            P("row", "col", None, None),
            P("row", "col", None, None),
            P("row", "col", None),
            P("row", "col", None),
            P("row", "col", None, None),
            P("col", "row", None),
            P("col", "row", None),
            P("col", None),
        ),
        out_specs=(P("row", "col", None, None), P("row", "col", None, None)),
        check_vma=False,
    )
```

time: 311 us -> 213 us (0.68)
  blocking collectives: 103 us -> 0 us
  Pallas kernels: 0 us -> 39.4 us
  waiting for transfers between devices: 25.9 us -> 52.8 us
  matrix products: 25.6 us -> 0 us
  starting transfers between devices: 93.5 us -> 75.2 us
  local copies, waits for them, and re-layouts: 49.7 us -> 34.3 us
  other arithmetic: 9.68 us -> 1.83 us
  between operations: 2.41 us -> 6.43 us
    all_gather x9 -> x0, blocking collectives: 103 us -> none  [the longest x4 50.3 us: shards(): lax.all_gather(level_three, 'col', axis=0, tiled=True)]
    pallas_call x0 -> x18, Pallas kernels: none -> 39.4 us  [call(): pl.pallas_call(body, out_shape=[jax.ShapeDtypeStruct(s, d) for s, d in ou...]
    gather x27 -> x0, local copies, waits for them, and re-layouts: 38.4 us -> none  [the longest x18 21.2 us: assemble(): jnp.take(received.reshape(interface_size, columns), inverse_list, axis=0)]
    ppermute x36 -> x48, waiting for transfers between devices: 25.9 us -> 52.8 us  [swap(): return lax.ppermute(x, axis, pairs)]
    dot_general x32 -> x0, matrix products: 25.6 us -> none  [the longest x24 22.4 us: product(): jnp.dot(left, right, precision=lax.Precision.HIGHEST, preferred_element_t...]
    ppermute x36 -> x48, starting transfers between devices: 93.5 us -> 75.2 us  [swap(): return lax.ppermute(x, axis, pairs)]
    unnamed x91 -> x76, local copies, waits for them, and re-layouts: 3.61 us -> 18.3 us
    slice x9 -> x27, local copies, waits for them, and re-layouts: 0.22 us -> 12.6 us  [the longest x4 3.69 us: shards(): g[:face]]
  transfers between devices with their start and end apart: 36 -> 48, of which waited for: 8 -> 27; matrix products, arithmetic and copies ran while one was open for 2% -> 8% of each run, Pallas kernels for 0% -> 1%
where the time goes in v1:
time: 213 us; the launch traced here: 210 us
  starting transfers between devices  75.2 us (35%)
  waiting for transfers between devices  52.8 us (25%)
  Pallas kernels  39.4 us (18%)
  local copies, waits for them, and re-layouts  34.3 us (16%)
  between operations  6.43 us (3%)
    ppermute x48, starting transfers between devices, swap(): return lax.ppermute(x, axis, pairs)  75.2 us
    ppermute x48, waiting for transfers between devices, swap(): return lax.ppermute(x, axis, pairs)  52.8 us
    pallas_call x18, Pallas kernels, call(): pl.pallas_call(body, out_shape=[jax.ShapeDtypeStruct(s, d) for s, d in ou...  39.4 us
    unnamed x76, local copies, waits for them, and re-layouts  18.3 us
  transfers between devices with their start and end apart: 48, of which 27 were waited for; matrix products, arithmetic and copies ran while one was open for 8% of the time, Pallas kernels for 1%

profile of v1, /device:TPU:1, one launch (start us, length us, event | category | flops | bytes accessed | tf_op | source)
XLA Modules:
  0.0 210.1 jit_solution(16302295769919623845)
XLA Ops:
  1.8 1.1 copy.14
  2.8 1.0 copy-done.20
  4.6 2.0 shard_map.104
  11.9 4.5 %collective-permute-start.1 = (f32[464,128]{1,0:T(8,128)}, f32[464,128]{1,0:T(8,128)}, u32[]{:S(2)}, u32[]{:S(2)}) collective-permute-start(f32[464,128]{1,0:T(8,128)} %get-tuple-element.130), channel_id=1, source_target_pairs={{1,2},{2,1},{3,4},{4,3},{5,6},{6,5},{9,10},{10,9},{11,12},{12,11},... | collective-permute-start | bytes 712712 | tf_op jit(solution)/shard_map/ppermute | solution.py:234
  19.5 3.3 %collective-permute-start.3 = (f32[464,128]{1,0:T(8,128)}, f32[464,128]{1,0:T(8,128)}, u32[]{:S(2)}, u32[]{:S(2)}) collective-permute-start(f32[464,128]{1,0:T(8,128)} %get-tuple-element.138), channel_id=1, source_target_pairs={{0,24},{8,16},{16,8},{24,0},{1,25},{9,17},{17,9},{25,1},{2,26},{10... | collective-permute-start | bytes 712712 | tf_op jit(solution)/shard_map/ppermute | solution.py:234
  29.0 1.4 copy-done.11
  30.4 1.4 copy-done.12
  32.5 1.0 slice.277.r0
  36.8 2.4 %shard_map.108 = (f32[640,128]{1,0:T(8,128)S(1)}, f32[256,128]{1,0:T(8,128)S(1)}, f32[256,128]{1,0:T(8,128)S(1)}, f32[96,128]{1,0:T(8,128)S(1)}) custom-call(f32[640,128]{1,0:T(8,128)S(1)} %shard_map.105.refs_0_.refs_6_.asm_ref, bf16[96,640]{1,0:T(8,128)(2,1)S(1)} %get-tuple-element.52.refs_1_.refs_7_, bf16[96,48]{1,0:T(8,128)(2,1)S(1)} %get-tuple-element.53.refs_2_.refs_8_, ...), custom_call_target="tpu_custom_call" | custom-call | flops 838860800 | bytes 3736576 | tf_op jit(solution)/shard_map/pallas_call | solution.py:62
  39.6 1.3 collective-permute-start.4
  40.9 2.0 collective-permute-start.5
  51.1 2.1 shard_map.109
  53.2 1.0 copy-done.2
  55.9 1.3 collective-permute-done.7.e_ref.refs_1_
  57.2 1.5 collective-permute-start.9
  58.8 1.5 collective-permute-done.9.refs_2_
  60.9 2.4 %collective-permute-start.10 = (f32[192,128]{1,0:T(8,128)}, f32[192,128]{1,0:T(8,128)}, u32[]{:S(2)}, u32[]{:S(2)}) collective-permute-start(f32[192,128]{1,0:T(8,128)} %pad_maximum_fusion), channel_id=1, source_target_pairs={{0,4},{1,5},{2,6},{3,7},{4,0},{5,1},{6,2},{7,3},{8,12},{9,13},{10,... | collective-permute-start | bytes 294920 | tf_op jit(solution)/shard_map/ppermute | solution.py:234
  63.9 3.9 %collective-permute-start.8 = (f32[160,128]{1,0:T(8,128)}, f32[160,128]{1,0:T(8,128)}, u32[]{:S(2)}, u32[]{:S(2)}) collective-permute-start(f32[160,128]{1,0:T(8,128)} %slice.253), channel_id=1, source_target_pairs={{1,2},{2,1},{3,4},{4,3},{5,6},{6,5},{9,10},{10,9},{11,12},{12,11},... | collective-permute-start | bytes 245768 | tf_op jit(solution)/shard_map/ppermute | solution.py:234
  68.5 2.4 %collective-permute-done.8.f_ref = f32[160,128]{1,0:T(8,128)} collective-permute-done((f32[160,128]{1,0:T(8,128)}, f32[160,128]{1,0:T(8,128)}, u32[]{:S(2)}, u32[]{:S(2)}) %collective-permute-start.8) | collective-permute-done | bytes 81952 | tf_op jit(solution)/shard_map/ppermute | solution.py:234
  70.9 1.2 copy-done.3
  72.1 1.0 copy-done.19
  75.1 4.8 %shard_map.111 = (f32[640,128]{1,0:T(8,128)S(1)}, f32[640,128]{1,0:T(8,128)S(1)}) custom-call(s32[4]{0:T(128)S(1)} %copy-done.27, s32[8]{0:T(128)S(1)} %copy-done.30, f32[640,128]{1,0:T(8,128)S(1)} %copy-done.19, f32[208,128]{1,0:T(8,128)S(1)} %collective-permute-done.7.e_ref.refs_1_, f32[160,128]{1,0:T(8,128)} %collective-permute-done.8.f_ref, ...), custom_call_target="tpu_custom_call" | custom-call | flops 838860800 | bytes 5054464 | tf_op jit(solution)/shard_map/pallas_call | solution.py:62
  79.9 1.3 collective-permute-start.14
  81.2 3.3 %collective-permute-start.12 = (f32[160,128]{1,0:T(8,128)S(1)}, f32[160,128]{1,0:T(8,128)S(1)}, u32[]{:S(2)}, u32[]{:S(2)}) collective-permute-start(f32[160,128]{1,0:T(8,128)S(1)} %get-tuple-element.110), channel_id=1, source_target_pairs={{1,2},{2,1},{3,4},{4,3},{5,6},{6,5},{9,10},{10,9},{11,12},{12,11},... | collective-permute-start | bytes 245768 | tf_op jit(solution)/shard_map/ppermute | solution.py:234
  85.4 1.6 collective-permute-done.12.refs_3_
  87.0 3.0 %shard_map.112 = (f32[640,128]{1,0:T(8,128)S(1)}, f32[256,128]{1,0:T(8,128)S(1)}, f32[256,128]{1,0:T(8,128)S(1)}, f32[96,128]{1,0:T(8,128)S(1)}) custom-call(s32[4]{0:T(128)S(1)} %copy-done.27, f32[640,128]{1,0:T(8,128)S(1)} %get-tuple-element.67.refs_1_, f32[160,128]{1,0:T(8,128)S(1)} %collective-permute-done.11.refs_2_, ...), custom_call_target="tpu_custom_call" | custom-call | flops 838860800 | bytes 4391936 | tf_op jit(solution)/shard_map/pallas_call | solution.py:62
  90.0 1.5 collective-permute-start.15
  91.5 2.0 collective-permute-start.16
  93.5 8.3 %collective-permute-done.17.refs_2_ = f32[96,128]{1,0:T(8,128)S(1)} collective-permute-done((f32[96,128]{1,0:T(8,128)S(1)}, f32[96,128]{1,0:T(8,128)S(1)}, u32[]{:S(2)}, u32[]{:S(2)}) %collective-permute-start.17) | collective-permute-done | bytes 49184 | tf_op jit(solution)/shard_map/ppermute | solution.py:234
  104.4 2.5 %collective-permute-start.20 = (f32[96,128]{1,0:T(8,128)S(1)}, f32[96,128]{1,0:T(8,128)S(1)}, u32[]{:S(2)}, u32[]{:S(2)}) collective-permute-start(f32[96,128]{1,0:T(8,128)S(1)} %pad_maximum_fusion.9), channel_id=1, source_target_pairs={{0,2},{1,3},{2,0},{3,1},{4,6},{5,7},{6,4},{7,5},{8,10},{9,11},{10,... | collective-permute-start | bytes 147464 | tf_op jit(solution)/shard_map/ppermute | solution.py:234
  106.9 1.5 collective-permute-done.20.refs_3_
  108.8 4.7 %collective-permute-start.19 = (f32[160,128]{1,0:T(8,128)S(1)}, f32[160,128]{1,0:T(8,128)S(1)}, u32[]{:S(2)}, u32[]{:S(2)}) collective-permute-start(f32[160,128]{1,0:T(8,128)S(1)} %slice.259), channel_id=1, source_target_pairs={{1,2},{2,1},{3,4},{4,3},{5,6},{6,5},{9,10},{10,9},{11,12},{12,11},... | collective-permute-start | bytes 245768 | tf_op jit(solution)/shard_map/ppermute | solution.py:234
  113.5 2.0 collective-permute-done.19.f_ref
  115.5 4.3 %shard_map.114 = (f32[640,128]{1,0:T(8,128)S(1)}, f32[640,128]{1,0:T(8,128)S(1)}) custom-call(s32[4]{0:T(128)S(1)} %copy-done.27, s32[8]{0:T(128)S(1)} %copy-done.31, f32[640,128]{1,0:T(8,128)S(1)} %get-tuple-element.72.y2_ref, f32[208,128]{1,0:T(8,128)S(1)} %collective-permute-done.18.e_ref.refs_2_, f32[160,128]{1,0:T(8,128)S(1)} %collective-permute-done.19.f_ref, ...), custom_call_target="tpu_custom_call" | custom-call | flops 838860800 | bytes 5382144 | tf_op jit(solution)/shard_map/pallas_call | solution.py:62
  119.7 1.5 collective-permute-start.25
  121.2 3.9 %collective-permute-start.23 = (f32[160,128]{1,0:T(8,128)S(1)}, f32[160,128]{1,0:T(8,128)S(1)}, u32[]{:S(2)}, u32[]{:S(2)}) collective-permute-start(f32[160,128]{1,0:T(8,128)S(1)} %get-tuple-element.106), channel_id=1, source_target_pairs={{1,2},{2,1},{3,4},{4,3},{5,6},{6,5},{9,10},{10,9},{11,12},{12,11},... | collective-permute-start | bytes 245768 | tf_op jit(solution)/shard_map/ppermute | solution.py:234
  125.8 1.1 collective-permute-done.24.refs_4_
  127.2 3.0 %shard_map.115 = (f32[640,128]{1,0:T(8,128)S(1)}, f32[256,128]{1,0:T(8,128)S(1)}, f32[256,128]{1,0:T(8,128)S(1)}, f32[96,128]{1,0:T(8,128)S(1)}) custom-call(s32[4]{0:T(128)S(1)} %copy-done.27, f32[640,128]{1,0:T(8,128)S(1)} %get-tuple-element.76.refs_1_, f32[160,128]{1,0:T(8,128)S(1)} %collective-permute-done.22.refs_2_, ...), custom_call_target="tpu_custom_call" | custom-call | flops 838860800 | bytes 4391936 | tf_op jit(solution)/shard_map/pallas_call | solution.py:62
  130.2 1.8 collective-permute-start.26
  132.0 1.9 collective-permute-start.27
  133.9 8.3 %collective-permute-done.28.refs_2_ = f32[96,128]{1,0:T(8,128)S(1)} collective-permute-done((f32[96,128]{1,0:T(8,128)S(1)}, f32[96,128]{1,0:T(8,128)S(1)}, u32[]{:S(2)}, u32[]{:S(2)}) %collective-permute-start.28) | collective-permute-done | bytes 49184 | tf_op jit(solution)/shard_map/ppermute | solution.py:234
  144.7 2.5 %collective-permute-start.31 = (f32[96,128]{1,0:T(8,128)S(1)}, f32[96,128]{1,0:T(8,128)S(1)}, u32[]{:S(2)}, u32[]{:S(2)}) collective-permute-start(f32[96,128]{1,0:T(8,128)S(1)} %pad_maximum_fusion.10), channel_id=1, source_target_pairs={{0,2},{1,3},{2,0},{3,1},{4,6},{5,7},{6,4},{7,5},{8,10},{9,11},{10,... | collective-permute-start | bytes 147464 | tf_op jit(solution)/shard_map/ppermute | solution.py:234
  147.2 1.5 collective-permute-done.31.refs_3_
  148.7 1.2 collective-permute-start.32
  149.9 3.7 %collective-permute-start.30 = (f32[160,128]{1,0:T(8,128)S(1)}, f32[160,128]{1,0:T(8,128)S(1)}, u32[]{:S(2)}, u32[]{:S(2)}) collective-permute-start(f32[160,128]{1,0:T(8,128)S(1)} %slice.265), channel_id=1, source_target_pairs={{1,2},{2,1},{3,4},{4,3},{5,6},{6,5},{9,10},{10,9},{11,12},{12,11},... | collective-permute-start | bytes 245768 | tf_op jit(solution)/shard_map/ppermute | solution.py:234
  153.6 2.1 %collective-permute-done.30.f_ref = f32[160,128]{1,0:T(8,128)S(1)} collective-permute-done((f32[160,128]{1,0:T(8,128)S(1)}, f32[160,128]{1,0:T(8,128)S(1)}, u32[]{:S(2)}, u32[]{:S(2)}) %collective-permute-start.30) | collective-permute-done | bytes 81952 | tf_op jit(solution)/shard_map/ppermute | solution.py:234
  155.7 4.3 %shard_map.117 = (f32[640,128]{1,0:T(8,128)S(1)}, f32[640,128]{1,0:T(8,128)S(1)}) custom-call(s32[4]{0:T(128)S(1)} %copy-done.27, s32[8]{0:T(128)S(1)} %copy-done.31, f32[640,128]{1,0:T(8,128)S(1)} %get-tuple-element.81.y2_ref, f32[208,128]{1,0:T(8,128)S(1)} %collective-permute-done.29.e_ref.refs_2_, f32[160,128]{1,0:T(8,128)S(1)} %collective-permute-done.30.f_ref, ...), custom_call_target="tpu_custom_call" | custom-call | flops 838860800 | bytes 5382144 | tf_op jit(solution)/shard_map/pallas_call | solution.py:62
  160.0 2.1 %collective-permute-start.36 = (f32[160,128]{1,0:T(8,128)S(1)}, f32[160,128]{1,0:T(8,128)S(1)}, u32[]{:S(2)}, u32[]{:S(2)}) collective-permute-start(f32[160,128]{1,0:T(8,128)S(1)} %get-tuple-element.100), channel_id=1, source_target_pairs={{0,24},{8,16},{16,8},{24,0},{1,25},{9,17},{17,9},{25,1},{2,26},{10... | collective-permute-start | bytes 245768 | tf_op jit(solution)/shard_map/ppermute | solution.py:234
  162.2 3.4 %collective-permute-start.34 = (f32[160,128]{1,0:T(8,128)S(1)}, f32[160,128]{1,0:T(8,128)S(1)}, u32[]{:S(2)}, u32[]{:S(2)}) collective-permute-start(f32[160,128]{1,0:T(8,128)S(1)} %get-tuple-element.102), channel_id=1, source_target_pairs={{1,2},{2,1},{3,4},{4,3},{5,6},{6,5},{9,10},{10,9},{11,12},{12,11},... | collective-permute-start | bytes 245768 | tf_op jit(solution)/shard_map/ppermute | solution.py:234
  166.0 1.3 collective-permute-done.35.refs_4_
  167.9 3.0 %shard_map.118 = (f32[640,128]{1,0:T(8,128)S(1)}, f32[256,128]{1,0:T(8,128)S(1)}, f32[256,128]{1,0:T(8,128)S(1)}, f32[96,128]{1,0:T(8,128)S(1)}) custom-call(s32[4]{0:T(128)S(1)} %copy-done.27, f32[640,128]{1,0:T(8,128)S(1)} %get-tuple-element.85.refs_1_, f32[160,128]{1,0:T(8,128)S(1)} %collective-permute-done.33.refs_2_, ...), custom_call_target="tpu_custom_call" | custom-call | flops 838860800 | bytes 4391936 | tf_op jit(solution)/shard_map/pallas_call | solution.py:62
  170.9 1.6 collective-permute-start.37
  172.4 1.7 collective-permute-start.38
  174.1 8.3 %collective-permute-done.39.refs_2_ = f32[96,128]{1,0:T(8,128)S(1)} collective-permute-done((f32[96,128]{1,0:T(8,128)S(1)}, f32[96,128]{1,0:T(8,128)S(1)}, u32[]{:S(2)}, u32[]{:S(2)}) %collective-permute-start.39) | collective-permute-done | bytes 49184 | tf_op jit(solution)/shard_map/ppermute | solution.py:234
  185.0 2.5 %collective-permute-start.42 = (f32[96,128]{1,0:T(8,128)S(1)}, f32[96,128]{1,0:T(8,128)S(1)}, u32[]{:S(2)}, u32[]{:S(2)}) collective-permute-start(f32[96,128]{1,0:T(8,128)S(1)} %pad_maximum_fusion.11), channel_id=1, source_target_pairs={{0,2},{1,3},{2,0},{3,1},{4,6},{5,7},{6,4},{7,5},{8,10},{9,11},{10,... | collective-permute-start | bytes 147464 | tf_op jit(solution)/shard_map/ppermute | solution.py:234
  187.4 1.5 collective-permute-done.42.refs_3_
  188.9 1.4 collective-permute-start.43
  190.3 3.5 %collective-permute-start.41 = (f32[160,128]{1,0:T(8,128)S(1)}, f32[160,128]{1,0:T(8,128)S(1)}, u32[]{:S(2)}, u32[]{:S(2)}) collective-permute-start(f32[160,128]{1,0:T(8,128)S(1)} %slice.271), channel_id=1, source_target_pairs={{1,2},{2,1},{3,4},{4,3},{5,6},{6,5},{9,10},{10,9},{11,12},{12,11},... | collective-permute-start | bytes 245768 | tf_op jit(solution)/shard_map/ppermute | solution.py:234
  193.8 2.4 %collective-permute-done.41.f_ref = f32[160,128]{1,0:T(8,128)S(1)} collective-permute-done((f32[160,128]{1,0:T(8,128)S(1)}, f32[160,128]{1,0:T(8,128)S(1)}, u32[]{:S(2)}, u32[]{:S(2)}) %collective-permute-start.41) | collective-permute-done | bytes 81952 | tf_op jit(solution)/shard_map/ppermute | solution.py:234
  196.3 4.3 %shard_map.120 = (f32[640,128]{1,0:T(8,128)}, f32[640,128]{1,0:T(8,128)S(1)}) custom-call(s32[4]{0:T(128)S(1)} %copy-done.27, s32[8]{0:T(128)S(1)} %copy-done.31, f32[640,128]{1,0:T(8,128)S(1)} %get-tuple-element.90.y2_ref, f32[208,128]{1,0:T(8,128)S(1)} %collective-permute-done.40.e_ref.refs_2_, f32[160,128]{1,0:T(8,128)S(1)} %collective-permute-done.41.f_ref, ...), custom_call_target="tpu_custom_call" | custom-call | flops 838860800 | bytes 5382144 | tf_op jit(solution)/shard_map/pallas_call | solution.py:62
  200.6 1.9 collective-permute-start.47
  202.4 3.4 %collective-permute-start.45 = (f32[160,128]{1,0:T(8,128)S(1)}, f32[160,128]{1,0:T(8,128)S(1)}, u32[]{:S(2)}, u32[]{:S(2)}) collective-permute-start(f32[160,128]{1,0:T(8,128)S(1)} %get-tuple-element.98), channel_id=1, source_target_pairs={{1,2},{2,1},{3,4},{4,3},{5,6},{6,5},{9,10},{10,9},{11,12},{12,11},... | collective-permute-start | bytes 245768 | tf_op jit(solution)/shard_map/ppermute | solution.py:234
  206.6 1.1 collective-permute-done.46.r2
  208.2 1.9 shard_map.121
  (178 shorter events, 41.7 us)
Async XLA Ops:
  1.6 7.1 %copy-start.17 = (f32[48,384]{1,0:T(8,128)S(1)}, f32[48,384]{1,0:T(8,128)}, u32[]{:S(2)}) copy-start(f32[48,384]{1,0:T(8,128)} %top_ref.1) | copy-start | bytes 221188
  4.5 13.1 %copy-start.21 = (f32[1,48,192]{2,1,0:T(8,128)S(1)}, f32[1,48,192]{2,1,0:T(8,128)}, u32[]{:S(2)}) copy-start(f32[1,48,192]{2,1,0:T(8,128)} %param.15) | copy-start | bytes 110596
  4.6 18.3 %copy-start.32 = (s32[1,1,4]{2,1,0:T(1,128)S(1)}, s32[1,1,4]{2,1,0:T(1,128)}, u32[]{:S(2)}) copy-start(s32[1,1,4]{2,1,0:T(1,128)} %param.13) | copy-start | bytes 52
  6.5 22.4 %copy-start.9 = (f32[640,48]{1,0:T(8,128)}, f32[640,48]{1,0:T(8,128)S(1)}, u32[]{:S(2)}) copy-start(f32[640,48]{1,0:T(8,128)S(1)} %get-tuple-element.51.basis_ref) | copy-start | bytes 368644
  11.8 20.7 %collective-permute-start = (f32[464,128]{1,0:T(8,128)}, f32[464,128]{1,0:T(8,128)}, u32[]{:S(2)}, u32[]{:S(2)}) collective-permute-start(f32[464,128]{1,0:T(8,128)} %constant_dynamic-update-slice_fusion), channel_id=1, source_target_pairs={{0,1},{1,0},{2,3},{3,2},{4,5},{5,4},{6,7},{7,6},{8,9},{9,8},{10,11... | collective-permute-start | bytes 712712 | tf_op jit(solution)/shard_map/ppermute | solution.py:234
  11.9 21.6 %collective-permute-start.1 = (f32[464,128]{1,0:T(8,128)}, f32[464,128]{1,0:T(8,128)}, u32[]{:S(2)}, u32[]{:S(2)}) collective-permute-start(f32[464,128]{1,0:T(8,128)} %get-tuple-element.130), channel_id=1, source_target_pairs={{1,2},{2,1},{3,4},{4,3},{5,6},{6,5},{9,10},{10,9},{11,12},{12,11},... | collective-permute-start | bytes 712712 | tf_op jit(solution)/shard_map/ppermute | solution.py:234
  19.5 14.9 %collective-permute-start.3 = (f32[464,128]{1,0:T(8,128)}, f32[464,128]{1,0:T(8,128)}, u32[]{:S(2)}, u32[]{:S(2)}) collective-permute-start(f32[464,128]{1,0:T(8,128)} %get-tuple-element.138), channel_id=1, source_target_pairs={{0,24},{8,16},{16,8},{24,0},{1,25},{9,17},{17,9},{25,1},{2,26},{10... | collective-permute-start | bytes 712712 | tf_op jit(solution)/shard_map/ppermute | solution.py:234
  22.8 12.5 %collective-permute-start.2 = (f32[464,128]{1,0:T(8,128)}, f32[464,128]{1,0:T(8,128)}, u32[]{:S(2)}, u32[]{:S(2)}) collective-permute-start(f32[464,128]{1,0:T(8,128)} %get-tuple-element.139), channel_id=1, source_target_pairs={{0,8},{8,0},{16,24},{24,16},{1,9},{9,1},{17,25},{25,17},{2,10},{10... | collective-permute-start | bytes 712712 | tf_op jit(solution)/shard_map/ppermute | solution.py:234
  32.4 21.7 %copy-start.28 = (s32[4]{0:T(128)}, s32[4]{0:T(128)S(1)}, u32[]{:S(2)}) copy-start(s32[4]{0:T(128)S(1)} %pad_add_fusion.2.order_ref) | copy-start | bytes 52
  32.5 21.7 %copy-start.26 = (s32[4]{0:T(128)}, s32[4]{0:T(128)S(1)}, u32[]{:S(2)}) copy-start(s32[4]{0:T(128)S(1)} %pad_add_fusion.1.link_ref.refs_0_) | copy-start | bytes 52
  39.2 11.8 %copy-start.10 = (f32[640,48]{1,0:T(8,128)S(1)}, f32[640,48]{1,0:T(8,128)}, u32[]{:S(2)}) copy-start(f32[640,48]{1,0:T(8,128)} %copy-done.9) | copy-start | bytes 368644
  39.3 11.8 %copy-start.16 = (f32[640,48]{1,0:T(8,128)S(1)}, f32[640,48]{1,0:T(8,128)}, u32[]{:S(2)}) copy-start(f32[640,48]{1,0:T(8,128)} %copy-done.15) | copy-start | bytes 368644
  39.3 11.8 %copy-start.22 = (f32[1,48,192]{2,1,0:T(8,128)S(1)}, f32[1,48,192]{2,1,0:T(8,128)}, u32[]{:S(2)}) copy-start(f32[1,48,192]{2,1,0:T(8,128)} %param.15) | copy-start | bytes 110596
  39.3 14.9 %collective-permute-start.6 = (f32[96,128]{1,0:T(8,128)S(1)}, f32[96,128]{1,0:T(8,128)S(1)}, u32[]{:S(2)}, u32[]{:S(2)}) collective-permute-start(f32[96,128]{1,0:T(8,128)S(1)} %get-tuple-element.61.refs_0_), channel_id=1, source_target_pairs={{0,16},{8,24},{16,0},{24,8},{1,17},{9,25},{17,1},{25,9},{2,18},{10... | collective-permute-start | bytes 147464 | tf_op jit(solution)/shard_map/ppermute | solution.py:234
  39.6 14.5 %collective-permute-start.4 = (f32[256,128]{1,0:T(8,128)S(1)}, f32[256,128]{1,0:T(8,128)S(1)}, u32[]{:S(2)}, u32[]{:S(2)}) collective-permute-start(f32[256,128]{1,0:T(8,128)S(1)} %get-tuple-element.58), channel_id=1, source_target_pairs={{0,8},{8,0},{16,24},{24,16},{1,9},{9,1},{17,25},{25,17},{2,10},{10... | collective-permute-start | bytes 393224 | tf_op jit(solution)/shard_map/ppermute | solution.py:234
  40.9 13.3 %collective-permute-start.5 = (f32[256,128]{1,0:T(8,128)S(1)}, f32[256,128]{1,0:T(8,128)S(1)}, u32[]{:S(2)}, u32[]{:S(2)}) collective-permute-start(f32[256,128]{1,0:T(8,128)S(1)} %get-tuple-element.59), channel_id=1, source_target_pairs={{0,24},{8,16},{16,8},{24,0},{1,25},{9,17},{17,9},{25,1},{2,26},{10... | collective-permute-start | bytes 393224 | tf_op jit(solution)/shard_map/ppermute | solution.py:234
  55.9 7.4 %copy-start.18 = (f32[640,128]{1,0:T(8,128)}, f32[640,128]{1,0:T(8,128)S(1)}, u32[]{:S(2)}) copy-start(f32[640,128]{1,0:T(8,128)S(1)} %get-tuple-element.62.y2_ref) | copy-start | bytes 983044
  55.9 1.3 collective-permute-start.7
  57.2 3.0 %collective-permute-start.9 = (f32[96,128]{1,0:T(8,128)S(1)}, f32[96,128]{1,0:T(8,128)S(1)}, u32[]{:S(2)}, u32[]{:S(2)}) collective-permute-start(f32[96,128]{1,0:T(8,128)S(1)} %pad_maximum_fusion.8), channel_id=1, source_target_pairs={{0,2},{1,3},{2,0},{3,1},{4,6},{5,7},{6,4},{7,5},{8,10},{9,11},{10,... | collective-permute-start | bytes 147464 | tf_op jit(solution)/shard_map/ppermute | solution.py:234
  60.9 10.0 %collective-permute-start.10 = (f32[192,128]{1,0:T(8,128)}, f32[192,128]{1,0:T(8,128)}, u32[]{:S(2)}, u32[]{:S(2)}) collective-permute-start(f32[192,128]{1,0:T(8,128)} %pad_maximum_fusion), channel_id=1, source_target_pairs={{0,4},{1,5},{2,6},{3,7},{4,0},{5,1},{6,2},{7,3},{8,12},{9,13},{10,... | collective-permute-start | bytes 294920 | tf_op jit(solution)/shard_map/ppermute | solution.py:234
  63.9 7.0 %collective-permute-start.8 = (f32[160,128]{1,0:T(8,128)}, f32[160,128]{1,0:T(8,128)}, u32[]{:S(2)}, u32[]{:S(2)}) collective-permute-start(f32[160,128]{1,0:T(8,128)} %slice.253), channel_id=1, source_target_pairs={{1,2},{2,1},{3,4},{4,3},{5,6},{6,5},{9,10},{10,9},{11,12},{12,11},... | collective-permute-start | bytes 245768 | tf_op jit(solution)/shard_map/ppermute | solution.py:234
  75.1 11.9 %copy-start.1 = (bf16[1280,640]{1,0:T(8,128)(2,1)S(1)}, bf16[1280,640]{1,0:T(8,128)(2,1)}, u32[]{:S(2)}) copy-start(bf16[1280,640]{1,0:T(8,128)(2,1)} %copy-done) | copy-start | bytes 4915204
  75.1 11.9 %copy-start.6 = (f32[640,128]{1,0:T(8,128)S(1)}, f32[640,128]{1,0:T(8,128)}, u32[]{:S(2)}) copy-start(f32[640,128]{1,0:T(8,128)} %copy-done.5) | copy-start | bytes 983044
  79.9 5.3 %collective-permute-start.14 = (f32[160,128]{1,0:T(8,128)S(1)}, f32[160,128]{1,0:T(8,128)S(1)}, u32[]{:S(2)}, u32[]{:S(2)}) collective-permute-start(f32[160,128]{1,0:T(8,128)S(1)} %get-tuple-element.108), channel_id=1, source_target_pairs={{0,24},{8,16},{16,8},{24,0},{1,25},{9,17},{17,9},{25,1},{2,26},{10... | collective-permute-start | bytes 245768 | tf_op jit(solution)/shard_map/ppermute | solution.py:234
  81.2 4.2 %collective-permute-start.13 = (f32[160,128]{1,0:T(8,128)S(1)}, f32[160,128]{1,0:T(8,128)S(1)}, u32[]{:S(2)}, u32[]{:S(2)}) collective-permute-start(f32[160,128]{1,0:T(8,128)S(1)} %get-tuple-element.109), channel_id=1, source_target_pairs={{0,8},{8,0},{16,24},{24,16},{1,9},{9,1},{17,25},{25,17},{2,10},{10... | collective-permute-start | bytes 245768 | tf_op jit(solution)/shard_map/ppermute | solution.py:234
  81.2 5.7 %collective-permute-start.12 = (f32[160,128]{1,0:T(8,128)S(1)}, f32[160,128]{1,0:T(8,128)S(1)}, u32[]{:S(2)}, u32[]{:S(2)}) collective-permute-start(f32[160,128]{1,0:T(8,128)S(1)} %get-tuple-element.110), channel_id=1, source_target_pairs={{1,2},{2,1},{3,4},{4,3},{5,6},{6,5},{9,10},{10,9},{11,12},{12,11},... | collective-permute-start | bytes 245768 | tf_op jit(solution)/shard_map/ppermute | solution.py:234
  84.6 17.3 %copy-start.8 = (bf16[1280,192]{1,0:T(8,128)(2,1)S(1)}, bf16[1280,192]{1,0:T(8,128)(2,1)}, u32[]{:S(2)}) copy-start(bf16[1280,192]{1,0:T(8,128)(2,1)} %copy-done.7) | copy-start | bytes 1474564
  84.6 17.2 %copy-start.29 = (s32[4]{0:T(128)S(1)}, s32[4]{0:T(128)}, u32[]{:S(2)}) copy-start(s32[4]{0:T(128)} %copy-done.28) | copy-start | bytes 52
  84.6 2.4 %collective-permute-start.11 = (f32[160,128]{1,0:T(8,128)S(1)}, f32[160,128]{1,0:T(8,128)S(1)}, u32[]{:S(2)}, u32[]{:S(2)}) collective-permute-start(f32[160,128]{1,0:T(8,128)S(1)} %get-tuple-element.111), channel_id=1, source_target_pairs={{0,1},{1,0},{2,3},{3,2},{4,5},{5,4},{6,7},{7,6},{8,9},{9,8},{10,11... | collective-permute-start | bytes 245768 | tf_op jit(solution)/shard_map/ppermute | solution.py:234
  90.0 25.5 %copy-start.4 = (bf16[1280,384]{1,0:T(8,128)(2,1)S(1)}, bf16[1280,384]{1,0:T(8,128)(2,1)}, u32[]{:S(2)}) copy-start(bf16[1280,384]{1,0:T(8,128)(2,1)} %copy-done.2) | copy-start | bytes 2949124
  90.0 25.5 %copy-start.31 = (s32[8]{0:T(128)S(1)}, s32[8]{0:T(128)}, u32[]{:S(2)}) copy-start(s32[8]{0:T(128)} %stack.70.order_ref) | copy-start | bytes 100
  90.0 11.8 %collective-permute-start.15 = (f32[256,128]{1,0:T(8,128)S(1)}, f32[256,128]{1,0:T(8,128)S(1)}, u32[]{:S(2)}, u32[]{:S(2)}) collective-permute-start(f32[256,128]{1,0:T(8,128)S(1)} %get-tuple-element.69), channel_id=1, source_target_pairs={{0,8},{8,0},{16,24},{24,16},{1,9},{9,1},{17,25},{25,17},{2,10},{10... | collective-permute-start | bytes 393224 | tf_op jit(solution)/shard_map/ppermute | solution.py:234
  91.5 10.3 %collective-permute-start.16 = (f32[256,128]{1,0:T(8,128)S(1)}, f32[256,128]{1,0:T(8,128)S(1)}, u32[]{:S(2)}, u32[]{:S(2)}) collective-permute-start(f32[256,128]{1,0:T(8,128)S(1)} %get-tuple-element.70), channel_id=1, source_target_pairs={{0,24},{8,16},{16,8},{24,0},{1,25},{9,17},{17,9},{25,1},{2,26},{10... | collective-permute-start | bytes 393224 | tf_op jit(solution)/shard_map/ppermute | solution.py:234
  93.5 8.3 %collective-permute-start.17 = (f32[96,128]{1,0:T(8,128)S(1)}, f32[96,128]{1,0:T(8,128)S(1)}, u32[]{:S(2)}, u32[]{:S(2)}) collective-permute-start(f32[96,128]{1,0:T(8,128)S(1)} %get-tuple-element.71.refs_0_), channel_id=1, source_target_pairs={{0,16},{8,24},{16,0},{24,8},{1,17},{9,25},{17,1},{25,9},{2,18},{10... | collective-permute-start | bytes 147464 | tf_op jit(solution)/shard_map/ppermute | solution.py:234
  102.7 1.7 collective-permute-start.18
  104.4 4.0 %collective-permute-start.20 = (f32[96,128]{1,0:T(8,128)S(1)}, f32[96,128]{1,0:T(8,128)S(1)}, u32[]{:S(2)}, u32[]{:S(2)}) collective-permute-start(f32[96,128]{1,0:T(8,128)S(1)} %pad_maximum_fusion.9), channel_id=1, source_target_pairs={{0,2},{1,3},{2,0},{3,1},{4,6},{5,7},{6,4},{7,5},{8,10},{9,11},{10,... | collective-permute-start | bytes 147464 | tf_op jit(solution)/shard_map/ppermute | solution.py:234
  108.4 7.0 %collective-permute-start.21 = (f32[192,128]{1,0:T(8,128)S(1)}, f32[192,128]{1,0:T(8,128)S(1)}, u32[]{:S(2)}, u32[]{:S(2)}) collective-permute-start(f32[192,128]{1,0:T(8,128)S(1)} %pad_maximum_fusion.1), channel_id=1, source_target_pairs={{0,4},{1,5},{2,6},{3,7},{4,0},{5,1},{6,2},{7,3},{8,12},{9,13},{10,... | collective-permute-start | bytes 294920 | tf_op jit(solution)/shard_map/ppermute | solution.py:234
  108.8 6.6 %collective-permute-start.19 = (f32[160,128]{1,0:T(8,128)S(1)}, f32[160,128]{1,0:T(8,128)S(1)}, u32[]{:S(2)}, u32[]{:S(2)}) collective-permute-start(f32[160,128]{1,0:T(8,128)S(1)} %slice.259), channel_id=1, source_target_pairs={{1,2},{2,1},{3,4},{4,3},{5,6},{6,5},{9,10},{10,9},{11,12},{12,11},... | collective-permute-start | bytes 245768 | tf_op jit(solution)/shard_map/ppermute | solution.py:234
  119.7 6.0 %collective-permute-start.25 = (f32[160,128]{1,0:T(8,128)S(1)}, f32[160,128]{1,0:T(8,128)S(1)}, u32[]{:S(2)}, u32[]{:S(2)}) collective-permute-start(f32[160,128]{1,0:T(8,128)S(1)} %get-tuple-element.104), channel_id=1, source_target_pairs={{0,24},{8,16},{16,8},{24,0},{1,25},{9,17},{17,9},{25,1},{2,26},{10... | collective-permute-start | bytes 245768 | tf_op jit(solution)/shard_map/ppermute | solution.py:234
  121.2 5.6 %collective-permute-start.24 = (f32[160,128]{1,0:T(8,128)S(1)}, f32[160,128]{1,0:T(8,128)S(1)}, u32[]{:S(2)}, u32[]{:S(2)}) collective-permute-start(f32[160,128]{1,0:T(8,128)S(1)} %get-tuple-element.105), channel_id=1, source_target_pairs={{0,8},{8,0},{16,24},{24,16},{1,9},{9,1},{17,25},{25,17},{2,10},{10... | collective-permute-start | bytes 245768 | tf_op jit(solution)/shard_map/ppermute | solution.py:234
  121.2 6.0 %collective-permute-start.23 = (f32[160,128]{1,0:T(8,128)S(1)}, f32[160,128]{1,0:T(8,128)S(1)}, u32[]{:S(2)}, u32[]{:S(2)}) collective-permute-start(f32[160,128]{1,0:T(8,128)S(1)} %get-tuple-element.106), channel_id=1, source_target_pairs={{1,2},{2,1},{3,4},{4,3},{5,6},{6,5},{9,10},{10,9},{11,12},{12,11},... | collective-permute-start | bytes 245768 | tf_op jit(solution)/shard_map/ppermute | solution.py:234
  125.1 2.1 %collective-permute-start.22 = (f32[160,128]{1,0:T(8,128)S(1)}, f32[160,128]{1,0:T(8,128)S(1)}, u32[]{:S(2)}, u32[]{:S(2)}) collective-permute-start(f32[160,128]{1,0:T(8,128)S(1)} %get-tuple-element.107), channel_id=1, source_target_pairs={{0,1},{1,0},{2,3},{3,2},{4,5},{5,4},{6,7},{7,6},{8,9},{9,8},{10,11... | collective-permute-start | bytes 245768 | tf_op jit(solution)/shard_map/ppermute | solution.py:234
  130.2 11.9 %collective-permute-start.26 = (f32[256,128]{1,0:T(8,128)S(1)}, f32[256,128]{1,0:T(8,128)S(1)}, u32[]{:S(2)}, u32[]{:S(2)}) collective-permute-start(f32[256,128]{1,0:T(8,128)S(1)} %get-tuple-element.78), channel_id=1, source_target_pairs={{0,8},{8,0},{16,24},{24,16},{1,9},{9,1},{17,25},{25,17},{2,10},{10... | collective-permute-start | bytes 393224 | tf_op jit(solution)/shard_map/ppermute | solution.py:234
  132.0 10.1 %collective-permute-start.27 = (f32[256,128]{1,0:T(8,128)S(1)}, f32[256,128]{1,0:T(8,128)S(1)}, u32[]{:S(2)}, u32[]{:S(2)}) collective-permute-start(f32[256,128]{1,0:T(8,128)S(1)} %get-tuple-element.79), channel_id=1, source_target_pairs={{0,24},{8,16},{16,8},{24,0},{1,25},{9,17},{17,9},{25,1},{2,26},{10... | collective-permute-start | bytes 393224 | tf_op jit(solution)/shard_map/ppermute | solution.py:234
  133.9 8.3 %collective-permute-start.28 = (f32[96,128]{1,0:T(8,128)S(1)}, f32[96,128]{1,0:T(8,128)S(1)}, u32[]{:S(2)}, u32[]{:S(2)}) collective-permute-start(f32[96,128]{1,0:T(8,128)S(1)} %get-tuple-element.80.refs_0_), channel_id=1, source_target_pairs={{0,16},{8,24},{16,0},{24,8},{1,17},{9,25},{17,1},{25,9},{2,18},{10... | collective-permute-start | bytes 147464 | tf_op jit(solution)/shard_map/ppermute | solution.py:234
  143.0 1.7 collective-permute-start.29
  144.7 4.0 %collective-permute-start.31 = (f32[96,128]{1,0:T(8,128)S(1)}, f32[96,128]{1,0:T(8,128)S(1)}, u32[]{:S(2)}, u32[]{:S(2)}) collective-permute-start(f32[96,128]{1,0:T(8,128)S(1)} %pad_maximum_fusion.10), channel_id=1, source_target_pairs={{0,2},{1,3},{2,0},{3,1},{4,6},{5,7},{6,4},{7,5},{8,10},{9,11},{10,... | collective-permute-start | bytes 147464 | tf_op jit(solution)/shard_map/ppermute | solution.py:234
  148.7 7.0 %collective-permute-start.32 = (f32[192,128]{1,0:T(8,128)S(1)}, f32[192,128]{1,0:T(8,128)S(1)}, u32[]{:S(2)}, u32[]{:S(2)}) collective-permute-start(f32[192,128]{1,0:T(8,128)S(1)} %pad_maximum_fusion.2), channel_id=1, source_target_pairs={{0,4},{1,5},{2,6},{3,7},{4,0},{5,1},{6,2},{7,3},{8,12},{9,13},{10,... | collective-permute-start | bytes 294920 | tf_op jit(solution)/shard_map/ppermute | solution.py:234
  149.9 5.8 %collective-permute-start.30 = (f32[160,128]{1,0:T(8,128)S(1)}, f32[160,128]{1,0:T(8,128)S(1)}, u32[]{:S(2)}, u32[]{:S(2)}) collective-permute-start(f32[160,128]{1,0:T(8,128)S(1)} %slice.265), channel_id=1, source_target_pairs={{1,2},{2,1},{3,4},{4,3},{5,6},{6,5},{9,10},{10,9},{11,12},{12,11},... | collective-permute-start | bytes 245768 | tf_op jit(solution)/shard_map/ppermute | solution.py:234
  160.0 6.0 %collective-permute-start.36 = (f32[160,128]{1,0:T(8,128)S(1)}, f32[160,128]{1,0:T(8,128)S(1)}, u32[]{:S(2)}, u32[]{:S(2)}) collective-permute-start(f32[160,128]{1,0:T(8,128)S(1)} %get-tuple-element.100), channel_id=1, source_target_pairs={{0,24},{8,16},{16,8},{24,0},{1,25},{9,17},{17,9},{25,1},{2,26},{10... | collective-permute-start | bytes 245768 | tf_op jit(solution)/shard_map/ppermute | solution.py:234
  162.2 5.2 %collective-permute-start.35 = (f32[160,128]{1,0:T(8,128)S(1)}, f32[160,128]{1,0:T(8,128)S(1)}, u32[]{:S(2)}, u32[]{:S(2)}) collective-permute-start(f32[160,128]{1,0:T(8,128)S(1)} %get-tuple-element.101), channel_id=1, source_target_pairs={{0,8},{8,0},{16,24},{24,16},{1,9},{9,1},{17,25},{25,17},{2,10},{10... | collective-permute-start | bytes 245768 | tf_op jit(solution)/shard_map/ppermute | solution.py:234
  162.2 5.7 %collective-permute-start.34 = (f32[160,128]{1,0:T(8,128)S(1)}, f32[160,128]{1,0:T(8,128)S(1)}, u32[]{:S(2)}, u32[]{:S(2)}) collective-permute-start(f32[160,128]{1,0:T(8,128)S(1)} %get-tuple-element.102), channel_id=1, source_target_pairs={{1,2},{2,1},{3,4},{4,3},{5,6},{6,5},{9,10},{10,9},{11,12},{12,11},... | collective-permute-start | bytes 245768 | tf_op jit(solution)/shard_map/ppermute | solution.py:234
  165.5 2.4 %collective-permute-start.33 = (f32[160,128]{1,0:T(8,128)S(1)}, f32[160,128]{1,0:T(8,128)S(1)}, u32[]{:S(2)}, u32[]{:S(2)}) collective-permute-start(f32[160,128]{1,0:T(8,128)S(1)} %get-tuple-element.103), channel_id=1, source_target_pairs={{0,1},{1,0},{2,3},{3,2},{4,5},{5,4},{6,7},{7,6},{8,9},{9,8},{10,11... | collective-permute-start | bytes 245768 | tf_op jit(solution)/shard_map/ppermute | solution.py:234
  170.9 11.5 %collective-permute-start.37 = (f32[256,128]{1,0:T(8,128)S(1)}, f32[256,128]{1,0:T(8,128)S(1)}, u32[]{:S(2)}, u32[]{:S(2)}) collective-permute-start(f32[256,128]{1,0:T(8,128)S(1)} %get-tuple-element.87), channel_id=1, source_target_pairs={{0,8},{8,0},{16,24},{24,16},{1,9},{9,1},{17,25},{25,17},{2,10},{10... | collective-permute-start | bytes 393224 | tf_op jit(solution)/shard_map/ppermute | solution.py:234
  172.4 10.0 %collective-permute-start.38 = (f32[256,128]{1,0:T(8,128)S(1)}, f32[256,128]{1,0:T(8,128)S(1)}, u32[]{:S(2)}, u32[]{:S(2)}) collective-permute-start(f32[256,128]{1,0:T(8,128)S(1)} %get-tuple-element.88), channel_id=1, source_target_pairs={{0,24},{8,16},{16,8},{24,0},{1,25},{9,17},{17,9},{25,1},{2,26},{10... | collective-permute-start | bytes 393224 | tf_op jit(solution)/shard_map/ppermute | solution.py:234
  174.1 8.3 %collective-permute-start.39 = (f32[96,128]{1,0:T(8,128)S(1)}, f32[96,128]{1,0:T(8,128)S(1)}, u32[]{:S(2)}, u32[]{:S(2)}) collective-permute-start(f32[96,128]{1,0:T(8,128)S(1)} %get-tuple-element.89.refs_0_), channel_id=1, source_target_pairs={{0,16},{8,24},{16,0},{24,8},{1,17},{9,25},{17,1},{25,9},{2,18},{10... | collective-permute-start | bytes 147464 | tf_op jit(solution)/shard_map/ppermute | solution.py:234
  183.3 1.7 collective-permute-start.40
  185.0 3.9 %collective-permute-start.42 = (f32[96,128]{1,0:T(8,128)S(1)}, f32[96,128]{1,0:T(8,128)S(1)}, u32[]{:S(2)}, u32[]{:S(2)}) collective-permute-start(f32[96,128]{1,0:T(8,128)S(1)} %pad_maximum_fusion.11), channel_id=1, source_target_pairs={{0,2},{1,3},{2,0},{3,1},{4,6},{5,7},{6,4},{7,5},{8,10},{9,11},{10,... | collective-permute-start | bytes 147464 | tf_op jit(solution)/shard_map/ppermute | solution.py:234
  188.9 7.3 %collective-permute-start.43 = (f32[192,128]{1,0:T(8,128)S(1)}, f32[192,128]{1,0:T(8,128)S(1)}, u32[]{:S(2)}, u32[]{:S(2)}) collective-permute-start(f32[192,128]{1,0:T(8,128)S(1)} %pad_maximum_fusion.3), channel_id=1, source_target_pairs={{0,4},{1,5},{2,6},{3,7},{4,0},{5,1},{6,2},{7,3},{8,12},{9,13},{10,... | collective-permute-start | bytes 294920 | tf_op jit(solution)/shard_map/ppermute | solution.py:234
  190.3 5.9 %collective-permute-start.41 = (f32[160,128]{1,0:T(8,128)S(1)}, f32[160,128]{1,0:T(8,128)S(1)}, u32[]{:S(2)}, u32[]{:S(2)}) collective-permute-start(f32[160,128]{1,0:T(8,128)S(1)} %slice.271), channel_id=1, source_target_pairs={{1,2},{2,1},{3,4},{4,3},{5,6},{6,5},{9,10},{10,9},{11,12},{12,11},... | collective-permute-start | bytes 245768 | tf_op jit(solution)/shard_map/ppermute | solution.py:234
  200.6 6.0 %collective-permute-start.47 = (f32[160,128]{1,0:T(8,128)S(1)}, f32[160,128]{1,0:T(8,128)S(1)}, u32[]{:S(2)}, u32[]{:S(2)}) collective-permute-start(f32[160,128]{1,0:T(8,128)S(1)} %get-tuple-element.96), channel_id=1, source_target_pairs={{0,24},{8,16},{16,8},{24,0},{1,25},{9,17},{17,9},{25,1},{2,26},{10... | collective-permute-start | bytes 245768 | tf_op jit(solution)/shard_map/ppermute | solution.py:234
  202.4 5.2 %collective-permute-start.46 = (f32[160,128]{1,0:T(8,128)S(1)}, f32[160,128]{1,0:T(8,128)S(1)}, u32[]{:S(2)}, u32[]{:S(2)}) collective-permute-start(f32[160,128]{1,0:T(8,128)S(1)} %get-tuple-element.97), channel_id=1, source_target_pairs={{0,8},{8,0},{16,24},{24,16},{1,9},{9,1},{17,25},{25,17},{2,10},{10... | collective-permute-start | bytes 245768 | tf_op jit(solution)/shard_map/ppermute | solution.py:234
  202.4 5.7 %collective-permute-start.45 = (f32[160,128]{1,0:T(8,128)S(1)}, f32[160,128]{1,0:T(8,128)S(1)}, u32[]{:S(2)}, u32[]{:S(2)}) collective-permute-start(f32[160,128]{1,0:T(8,128)S(1)} %get-tuple-element.98), channel_id=1, source_target_pairs={{1,2},{2,1},{3,4},{4,3},{5,6},{6,5},{9,10},{10,9},{11,12},{12,11},... | collective-permute-start | bytes 245768 | tf_op jit(solution)/shard_map/ppermute | solution.py:234
  205.8 2.4 %collective-permute-start.44 = (f32[160,128]{1,0:T(8,128)S(1)}, f32[160,128]{1,0:T(8,128)S(1)}, u32[]{:S(2)}, u32[]{:S(2)}) collective-permute-start(f32[160,128]{1,0:T(8,128)S(1)} %get-tuple-element.99), channel_id=1, source_target_pairs={{0,1},{1,0},{2,3},{3,2},{4,5},{5,4},{6,7},{7,6},{8,9},{9,8},{10,11... | collective-permute-start | bytes 245768 | tf_op jit(solution)/shard_map/ppermute | solution.py:234
  (17 other events, 30.2 us)

commit v2 on v0

v2 whole, which is shorter than its diff:
```python
import functools
import math

import jax
import jax.numpy as jnp
from jax import lax
from jax.experimental import pallas as pl
from jax.experimental.pallas import tpu as pltpu
from jax.sharding import PartitionSpec as P


DEGREE = 2
STEPS = 4
LANES = 128
INTERPRET = False
VMEM_LIMIT = 16 * 2**20
F32 = jnp.float32
BF16 = jnp.bfloat16


def split(x, parts):
    pieces = []
    for _ in range(parts - 1):
        piece = x.astype(BF16)
        pieces.append(piece)
        x = x - piece.astype(F32)
    pieces.append(x.astype(BF16))
    return pieces


def stack_split(x):
    return jnp.concatenate(split(x, 2), axis=0)


def dot(left, right):
    return jnp.dot(left, right, preferred_element_type=F32)


def product_parts(left2, right_parts):
    rows = left2.shape[0] // 2
    n = right_parts[0].shape[1]
    out = dot(left2, jnp.concatenate(right_parts, axis=1))
    out = out[:rows] + out[rows:]
    return out[:, :n] + out[:, n:]


def product(left2, right):
    return product_parts(left2, split(right, 2))


def permuted(onehot, x, parts=2):
    n = x.shape[1]
    out = dot(onehot, jnp.concatenate(split(x, parts), axis=1))
    total = out[:, (parts - 1) * n :]
    for i in reversed(range(parts - 1)):
        total = out[:, i * n : (i + 1) * n] + total
    return total


def call(body, out_shapes, scalars, arrays, flops=0, scratch=(), space=pltpu.VMEM):
    smem = pl.BlockSpec(memory_space=pltpu.SMEM)
    vmem = pl.BlockSpec(memory_space=pltpu.VMEM)
    moved = sum(a.size * a.dtype.itemsize for a in arrays)
    return pl.pallas_call(
        body,
        out_shape=[jax.ShapeDtypeStruct(s, d) for s, d in out_shapes],
        in_specs=[smem] * len(scalars) + [pl.BlockSpec(memory_space=space)] * len(arrays),
        out_specs=[vmem] * len(out_shapes),
        scratch_shapes=[pltpu.VMEM(shape, F32) if isinstance(shape, tuple) else shape for shape in scratch],
        compiler_params=pltpu.CompilerParams(vmem_limit_bytes=VMEM_LIMIT),
        cost_estimate=pl.CostEstimate(flops=flops, bytes_accessed=moved, transcendentals=0),
        interpret=INTERPRET,
    )(*scalars, *arrays)


def pack(ref, start, x):
    rows, width = x.shape
    for i in range(0, width, LANES):
        w = min(LANES, width - i)
        ref[start : start + rows, :w] = x[:, i : i + w]
        start += rows
    return start


def unpack(ref, start, rows, width):
    parts = []
    for i in range(0, width, LANES):
        parts.append(ref[start : start + rows, : min(LANES, width - i)])
        start += rows
    return jnp.concatenate(parts, axis=1) if len(parts) > 1 else parts[0]


def blocks(width):
    return -(-width // LANES)


def pack_halves(ref, start, x):
    half = x.shape[0] // 2
    ref[start : start + half, : x.shape[1]] = x[:half]
    ref[start : start + half, LANES // 2 : LANES // 2 + x.shape[1]] = x[half:]


def unpack_halves(ref, start, rows, width):
    x = ref[start : start + rows // 2, :]
    return jnp.concatenate([x[:, :width], x[:, LANES // 2 : LANES // 2 + width]], axis=0)


def transposed(x, pad_ref):
    rows, width = x.shape
    pad_ref[...] = jnp.zeros_like(pad_ref)
    pad_ref[:rows, :width] = x
    return pad_ref[...].T[:width, :rows]


def start_kernel(
    face,
    place_ref,
    index_hbm,
    load_hbm,
    basis_hbm,
    map_hbm,
    inverse_hbm,
    top_hbm,
    perm_ref,
    back_ref,
    load_out,
    basis_out,
    coarse_out,
    basis2_ref,
    map2_ref,
    map_t_ref,
    e_ref,
    f_ref,
    g_ref,
    h_ref,
    index_ref,
    load_ref,
    basis_ref,
    map_ref,
    inverse_ref,
    top_ref,
    tall_ref,
    small_ref,
    sems,
):
    sources = (index_hbm, load_hbm, basis_hbm, map_hbm, inverse_hbm, top_hbm)
    targets = (index_ref, load_ref, basis_ref, map_ref, inverse_ref, top_ref)
    copies = [pltpu.make_async_copy(a, b, sems.at[i]) for i, (a, b) in enumerate(zip(sources, targets))]
    for copy in copies:
        copy.start()
    size = perm_ref.shape[0]
    coarse = basis_ref.shape[1]
    for ref in (e_ref, f_ref, g_ref, h_ref):
        ref[face:] = jnp.zeros((ref.shape[0] - face, ref.shape[1]), F32)
    copies[0].wait()
    raw = index_ref[...].astype(F32)
    west, east, south, north = [raw[:, k * face : (k + 1) * face] for k in range(4)]
    even_row, even_col = place_ref[0] % 2 == 0, place_ref[1] % 2 == 0
    index = jnp.concatenate(
        [
            jnp.where(even_col, east, west),
            jnp.where(even_col, west, east),
            jnp.where(even_row, north, south),
            jnp.where(even_row, south, north),
        ],
        axis=1,
    )
    tall = jnp.broadcast_to(index, (LANES, size)).T
    lane = lax.broadcasted_iota(jnp.int32, (size, LANES), 1).astype(F32)
    for i in range(0, size, LANES):
        perm_ref[:, i : i + LANES] = jnp.where(tall == lane + float(i), 1.0, 0.0).astype(BF16)
    perm = perm_ref[...]
    copies[1].wait()
    load = permuted(perm, load_ref[...])
    load_out[...] = load
    for copy in copies[2:]:
        copy.wait()
    basis = permuted(perm, basis_ref[...])
    basis_out[...] = basis
    product_map = product(stack_split(basis), map_ref[...])
    coarse_out[...] = product_map
    level = jnp.concatenate([inverse_ref[...], map_ref[...]], axis=1)
    for k, ref in enumerate((e_ref, f_ref, g_ref, h_ref)):
        rows = slice(k * face, (k + 1) * face)
        ref[:face] = load[rows]
        pack_halves(ref, face, product_map[rows] if k < 2 else basis[rows])
        pack(ref, face + face // 2, top_ref[...] if k < 2 else level)
    down = lax.broadcasted_iota(jnp.int32, (size, size), 0).astype(F32)
    back_ref[...] = jnp.where(index == down, 1.0, 0.0).astype(BF16)
    basis2_ref[...] = stack_split(transposed(basis, tall_ref))
    map_t = transposed(map_ref[...], small_ref)
    map2_ref[...] = stack_split(map_t)
    map_t_ref[...] = jnp.zeros_like(map_t_ref)
    map_t_ref[:, :coarse] = map_t


def split_kernel(x_ref, o_ref):
    o_ref[...] = stack_split(x_ref[...])


def level_kernel(
    face, link_ref, basis_ref, inverse_ref, coarse_ref, top_ref, e_ref, f_ref, g_ref, h_ref, two_ref, top_out_ref
):
    coarse, total = inverse_ref.shape
    top, width = top_ref.shape
    start = face + face // 2
    link = [link_ref[i].astype(F32) for i in range(4)]
    two = product(stack_split(basis_ref[...]), inverse_ref[...])
    third = coarse_ref[...]
    twos, thirds = [two[: 2 * face]], [third[: 2 * face]]
    for k, ref in ((2, g_ref), (3, h_ref)):
        rows = slice(k * face, (k + 1) * face)
        basis = stack_split(unpack_halves(ref, face, face, coarse) * link[k])
        level = product(basis, unpack(ref, start, coarse, total + top))
        twos.append(two[rows] + level[:, :total])
        thirds.append(third[rows] + level[:, total:])
    two_ref[...] = stack_split(jnp.concatenate(twos, axis=0))
    out = product(stack_split(jnp.concatenate(thirds, axis=0)), top_ref[...])
    outs = []
    for k, ref in ((0, e_ref), (1, f_ref)):
        rows = slice(k * face, (k + 1) * face)
        near = stack_split(unpack_halves(ref, face, face, top) * link[k])
        outs.append(out[rows] + product(near, unpack(ref, start, top, width)))
    top_out_ref[...] = stack_split(jnp.concatenate(outs + [out[2 * face :]], axis=0))


def received(face, link_ref, refs):
    return jnp.concatenate([r[:face] * link_ref[i].astype(F32) for i, r in enumerate(refs)], axis=0)


def coeffs_kernel(first, face, link_ref, f_ref, r0, r1, r2, r3, *refs):
    field = f_ref[...] + received(face, link_ref, (r0, r1, r2, r3))
    if first:
        basis_ref, current_ref, c_ref = refs
        current = field
    else:
        asm_ref, basis_ref, current_ref, c_ref = refs
        current = asm_ref[...] - field
    current_ref[...] = current
    c_ref[...] = product(basis_ref[...], current)


def local_kernel(face, current_ref, inverse_ref, perm_ref, back_ref, y_ref, g_ref, h_ref):
    n = current_ref.shape[1]
    moved = dot(back_ref[...], jnp.concatenate(split(current_ref[...], 2), axis=1)).astype(BF16)
    y = permuted(perm_ref[...], product_parts(inverse_ref[...], [moved[:, :n], moved[:, n:]]))
    y_ref[...] = y
    g_ref[...] = y[2 * face : 3 * face]
    h_ref[...] = y[3 * face :]


def maps_kernel(coarse, starts, *refs):
    out_ref = refs[-1]
    slot = 0
    for ref, spans in zip(refs, starts):
        for start in spans:
            part = stack_split(ref[start : start + coarse, :coarse])
            out_ref[slot * part.shape[0] : (slot + 1) * part.shape[0]] = part
            slot += 1


def third_kernel(starts, coarse, maps_ref, *refs):
    third, slot = None, 0
    rows = maps_ref.shape[0] // sum(len(spans) for spans in starts)
    for ref, spans in zip(refs, starts):
        for start in spans:
            part = product(maps_ref[slot * rows : (slot + 1) * rows], ref[start : start + coarse])
            third = part if third is None else third + part
            slot += 1
    refs[-1][...] = third


def group_kernel(face, starts, coarse, link_ref, order_ref, y_ref, g_ref, h_ref, two_ref, *refs):
    y2_ref, stack_ref = refs[len(starts) :]
    slot = 0
    for ref, spans in zip(refs, starts):
        for start in spans:
            offset = pl.multiple_of(order_ref[slot], 8)
            stack_ref[pl.ds(offset, coarse)] = ref[start : start + coarse]
            slot += 1
    y = y_ref[...] + product(two_ref[...], stack_ref[...])
    y2_ref[: 2 * face] = y[: 2 * face]
    y2_ref[2 * face : 3 * face] = y[2 * face : 3 * face] + g_ref[:face] * link_ref[2].astype(F32)
    y2_ref[3 * face :] = y[3 * face :] + h_ref[:face] * link_ref[3].astype(F32)


def update_kernel(
    weight, first, face, starts, top, link_ref, order_ref, y2_ref, e_ref, f_ref, top_ref, perm_ref, back_ref, schur_ref, *refs
):
    if not first:
        old_ref, refs = refs[0], refs[1:]
    x_ref, out_ref, stack_ref = refs[len(starts) :]
    slot = 0
    for ref, first_row in zip(refs, starts):
        for start in range(first_row, ref.shape[0], top):
            stack_ref[pl.ds(pl.multiple_of(order_ref[slot], 8), top)] = ref[start : start + top]
            slot += 1
    y2 = y2_ref[...] + product(top_ref[...], stack_ref[...])
    update = jnp.concatenate(
        [
            y2[:face] + e_ref[:face] * link_ref[0].astype(F32),
            y2[face : 2 * face] + f_ref[:face] * link_ref[1].astype(F32),
            y2[2 * face :],
        ],
        axis=0,
    )
    x = weight * permuted(back_ref[...], update)
    if not first:
        x = old_ref[...] + x
    x_ref[...] = x
    out_ref[...] = permuted(perm_ref[...], product(schur_ref[...], x))


def residual_kernel(face, link_ref, f_ref, r0, r1, r2, r3, asm_ref, back_ref, out_ref):
    current = asm_ref[...] - (f_ref[...] + received(face, link_ref, (r0, r1, r2, r3)))
    out_ref[...] = permuted(back_ref[...], current, 3)


def swap_pairs(rows, cols, partner):
    pairs = []
    for r in range(rows):
        for c in range(cols):
            a, b = partner(r, c)
            if not (0 <= a < rows and 0 <= b < cols):
                a, b = (r, c ^ 1) if not 0 <= a < rows else (r ^ 1, c)
            if a < rows and b < cols:
                pairs.append((r * cols + c, a * cols + b))
    return pairs


def odd_neighbour(i):
    return i + 1 if i % 2 else i - 1


def shards(
    load,
    schur,
    local_inverse,
    iface_index,
    face_link,
    coarse_basis,
    coarse_inverse,
    coarse_map,
    top_inverse,
):
    loads, basis = load[0, 0], coarse_basis[0, 0]
    inverse_rows, map_block = coarse_inverse[0], coarse_map[0]
    size, columns = loads.shape
    face = size // 4
    coarse, top = basis.shape[1], map_block.shape[1]
    rows, cols = lax.axis_size("row"), lax.axis_size("col")
    row, col = lax.axis_index("row"), lax.axis_index("col")
    total, width = inverse_rows.shape[1], top_inverse.shape[1]

    place = jnp.stack([row, col])
    side = jnp.arange(4, dtype=jnp.int32)
    parity = jnp.where(side < 2, col, row) & 1
    facing = jnp.where(side < 2, 0, 2) + ((side & 1) ^ parity ^ 1)
    link = jnp.sum(jnp.where(facing[:, None] == side[None, :], face_link[0, 0][None, :], 0), axis=1)

    def swap(x, partner):
        return lax.ppermute(x, ("row", "col"), swap_pairs(rows, cols, partner))

    def swap_even_col(x):
        return swap(x, lambda r, c: (r, c ^ 1))

    def swap_odd_col(x):
        return swap(x, lambda r, c: (r, odd_neighbour(c)))

    def swap_even_row(x):
        return swap(x, lambda r, c: (r ^ 1, c))

    def swap_odd_row(x):
        return swap(x, lambda r, c: (odd_neighbour(r), c))

    def exchange(parts):
        got_f = swap_odd_col(parts[1])
        got_g = swap_even_row(parts[2])
        got_h = swap_odd_row(parts[3])
        got_e = swap_even_col(parts[0])
        return [got_e, got_f, got_g, got_h]

    row_pairs = rows == 4

    def faces(x):
        return [x[i * face : (i + 1) * face] for i in range(4)]

    n = (size, columns)
    common = face + face // 2
    payloads = [common + blocks(width) * top] * 2 + [common + blocks(total + top) * coarse] * 2
    perm, back, load_f, basis_f, coarse_f, basis2, map2, map_t, *sent = call(
        functools.partial(start_kernel, face),
        [((size, size), BF16), ((size, size), BF16), (n, F32), ((size, coarse), F32), ((size, top), F32)]
        + [((2 * coarse, size), BF16), ((2 * top, coarse), BF16), ((top, columns), F32)]
        + [((p, columns), F32) for p in payloads],
        [place],
        [iface_index[0], loads, basis, map_block, inverse_rows, top_inverse],
        flops=4 * size**2 * columns,
        scratch=[pltpu.VMEM((1, size), jnp.int32), n, basis.shape, map_block.shape, inverse_rows.shape]
        + [top_inverse.shape, (size, LANES), (LANES, LANES), pltpu.SemaphoreType.DMA((6,))],
        space=pltpu.HBM,
    )
    schur2 = call(split_kernel, [((2 * size, size), BF16)], [], [schur[0, 0]])[0]
    inverse2 = call(split_kernel, [((2 * size, size), BF16)], [], [local_inverse[0, 0]])[0]

    got = exchange(sent)
    two2, top2 = call(
        functools.partial(level_kernel, face),
        [((2 * size, total), BF16), ((2 * size, width), BF16)],
        [link],
        [basis_f, inverse_rows, coarse_f, top_inverse] + got,
    )

    doubling = cols & (cols - 1) == 0
    col_order = jnp.arange(cols, dtype=jnp.int32)
    if doubling:
        col_order = col_order ^ col
    col_order = col_order * top
    row_order = jnp.arange(rows, dtype=jnp.int32)
    if row_pairs:
        row_order = row ^ ((row_order & 1) * 2 + row_order // 2)
    row_order = row_order * coarse

    solution, field, assembled, maps = load_f, load_f, None, None
    square = 8 * size * size * columns
    for step_index in range(STEPS):
        phase = step_index % DEGREE
        weight = 1.0 / (1.4 - math.cos(math.pi * (2 * phase + 1) / (2 * DEGREE)))
        first = step_index == 0
        if first:
            operands = [load_f] + got + [basis2]
        else:
            operands = [field] + exchange(faces(field)) + [assembled, basis2]
        current, coeffs = call(
            functools.partial(coeffs_kernel, first, face), [(n, F32), ((coarse, columns), F32)], [link], operands
        )
        if first:
            assembled = current

        known = jnp.concatenate([coeffs, map_t]) if first else coeffs
        if row_pairs:
            got_r = swap(known, lambda r, c: (r ^ 2, c))
        y, face_g, face_h = call(
            functools.partial(local_kernel, face),
            [(n, F32), ((face, columns), F32), ((face, columns), F32)],
            [],
            [current, inverse2, perm, back],
            flops=2 * square,
        )
        got_h = swap_odd_row(face_h)
        if row_pairs:
            got_g = swap_even_row(jnp.concatenate([face_g, known, got_r]))
            more = face + known.shape[0]
            pieces, starts = [coeffs, got_r, got_g], ((0,), (0,), (face, more))
            map_starts = ((0,), (coarse,), (face + coarse, more + coarse))
            sources = [map_t, got_r, got_g]
        else:
            got_g = swap_even_row(face_g)
            spans = tuple(range(0, total, coarse))
            pieces, starts = [lax.all_gather(coeffs, "row", axis=0, tiled=True)], (spans,)
            map_starts = starts
            sources = [lax.all_gather(map_t, "row", axis=0, tiled=True)] if first else None
        if first:
            maps = call(
                functools.partial(maps_kernel, coarse, map_starts), [((2 * rows * top, coarse), BF16)], [], sources
            )[0]
        third = call(functools.partial(third_kernel, starts, coarse), [((top, columns), F32)], [], [maps] + pieces)[0]

        if doubling:
            more = swap(third, lambda r, c: (r, c ^ 1))
        y2 = call(
            functools.partial(group_kernel, face, starts, coarse),
            [(n, F32)],
            [link, row_order],
            [y, got_g, got_h, two2] + pieces,
            scratch=[(total, columns)],
        )[0]
        got_f = swap_odd_col(y2[face : 2 * face])
        got_e = swap_even_col(y2[:face])
        if doubling:
            tops, bits = [third, more], 2
            known = jnp.concatenate([third, more])
            while bits < cols:
                more = swap(known, lambda r, c: (r, c ^ bits))
                tops.append(more)
                known = jnp.concatenate([known, more])
                bits *= 2
        else:
            tops = [lax.all_gather(third, "col", axis=0, tiled=True)]
        starts = (0,) * len(tops)
        solution, field = call(
            functools.partial(update_kernel, weight, first, face, starts, top),
            [(n, F32), (n, F32)],
            [link, col_order],
            [y2, got_e, got_f, top2, perm, back, schur2] + ([] if first else [solution]) + tops,
            flops=2 * square,
            scratch=[(width, columns)],
        )
    residual = call(
        functools.partial(residual_kernel, face),
        [(n, F32)],
        [link],
        [field] + exchange(faces(field)) + [assembled, back],
    )[0]
    return (solution[None, None], residual[None, None])


def solution(mesh):
    return jax.shard_map(
        shards,
        mesh=mesh,
        in_specs=(
            P("row", "col", None, None),
            P("row", "col", None, None),
            P("row", "col", None, None),
            P("row", "col", None),
            P("row", "col", None),
            P("row", "col", None, None),
            P("col", "row", None),
            P("col", "row", None),
            P("col", None),
        ),
        out_specs=(P("row", "col", None, None), P("row", "col", None, None)),
        check_vma=False,
    )
```

time: 311 us -> 157 us (0.50)
  blocking collectives: 103 us -> 0 us
  local copies, waits for them, and re-layouts: 49.7 us -> 7.75 us
  Pallas kernels: 0 us -> 38.5 us
  starting transfers between devices: 93.5 us -> 65.6 us
  matrix products: 25.6 us -> 0 us
  waiting for transfers between devices: 25.9 us -> 41.9 us
  other arithmetic: 9.68 us -> 0.38 us
    all_gather x9 -> x0, blocking collectives: 103 us -> none  [the longest x4 50.3 us: shards(): lax.all_gather(level_three, 'col', axis=0, tiled=True)]
    pallas_call x0 -> x26, Pallas kernels: none -> 38.5 us  [call(): pl.pallas_call(body, out_shape=[jax.ShapeDtypeStruct(s, d) for s, d in ou...]
    gather x27 -> x0, local copies, waits for them, and re-layouts: 38.4 us -> none  [the longest x18 21.2 us: assemble(): jnp.take(received.reshape(interface_size, columns), inverse_list, axis=0)]
    ppermute x36 -> x52, starting transfers between devices: 93.5 us -> 65.6 us  [swap(): return lax.ppermute(x, ('row', 'col'), swap_pairs(rows, cols, partner))]
    dot_general x32 -> x0, matrix products: 25.6 us -> none  [the longest x24 22.4 us: product(): jnp.dot(left, right, precision=lax.Precision.HIGHEST, preferred_element_t...]
    ppermute x36 -> x52, waiting for transfers between devices: 25.9 us -> 41.9 us  [swap(): return lax.ppermute(x, ('row', 'col'), swap_pairs(rows, cols, partner))]
    scatter x1 -> x0, local copies, waits for them, and re-layouts: 4.1 us -> none  [shards(): jnp.zeros_like(index_list).at[index_list]]
    unnamed x91 -> x19, local copies, waits for them, and re-layouts: 3.61 us -> 7.6 us
  transfers between devices with their start and end apart: 36 -> 52, of which waited for: 8 -> 27; matrix products, arithmetic and copies ran while one was open for 2% -> 0% of each run, Pallas kernels for 0% -> 10%
where the time goes in v2:
time: 157 us; the launch traced here: 155 us
  starting transfers between devices  65.6 us (42%)
  waiting for transfers between devices  41.9 us (27%)
  Pallas kernels  38.5 us (25%)
  local copies, waits for them, and re-layouts  7.75 us (5%)
    ppermute x52, starting transfers between devices, swap(): return lax.ppermute(x, ('row', 'col'), swap_pairs(rows, cols, partner))  65.6 us
    ppermute x52, waiting for transfers between devices, swap(): return lax.ppermute(x, ('row', 'col'), swap_pairs(rows, cols, partner))  41.9 us
    pallas_call x26, Pallas kernels, call(): pl.pallas_call(body, out_shape=[jax.ShapeDtypeStruct(s, d) for s, d in ou...  38.5 us
    unnamed x19, local copies, waits for them, and re-layouts  7.6 us
  transfers between devices with their start and end apart: 52, of which 27 were waited for; matrix products, arithmetic and copies ran while one was open for 0% of the time, Pallas kernels for 10%

profile of v2, /device:TPU:1, one launch (start us, length us, event | category | flops | bytes accessed | tf_op | source)
XLA Modules:
  0.0 155.2 jit_solution(1644829433839730121)
XLA Ops:
  0.6 1.1 copy.12
  1.8 1.0 copy-done.2
  5.9 4.0 %shard_map.104 = (bf16[640,640]{1,0:T(8,128)(2,1)S(1)}, bf16[640,640]{1,0:T(8,128)(2,1)S(1)}, f32[640,128]{1,0:T(8,128)S(1)}, f32[640,48]{1,0:T(8,128)S(1)}, f32...) custom-call(s32[2]{0:T(128)S(1)} %pad_add_fusion.place_ref, ...), custom_call_target="tpu_custom_call" | custom-call | flops 209715200 | bytes 572928 | tf_op jit(solution)/shard_map/pallas_call | solution.py:64
  9.9 2.2 %collective-permute-start.2 = (f32[336,128]{1,0:T(8,128)S(1)}, f32[336,128]{1,0:T(8,128)S(1)}, u32[]{:S(2)}, u32[]{:S(2)}) collective-permute-start(f32[336,128]{1,0:T(8,128)S(1)} %get-tuple-element.46), channel_id=1, source_target_pairs={{0,8},{1,9},{2,10},{3,11},{4,12},{5,13},{6,14},{7,15},{8,0},{9,1},... | collective-permute-start | bytes 516104 | tf_op jit(solution)/shard_map/ppermute | solution.py:362
  12.1 1.0 collective-permute-start.3
  13.1 1.6 %collective-permute-start.1 = (f32[384,128]{1,0:T(8,128)S(1)}, f32[384,128]{1,0:T(8,128)S(1)}, u32[]{:S(2)}, u32[]{:S(2)}) collective-permute-start(f32[384,128]{1,0:T(8,128)S(1)} %get-tuple-element.45), channel_id=1, source_target_pairs={{0,8},{1,2},{2,1},{3,4},{4,3},{5,6},{6,5},{7,15},{8,0},{9,10},{10,... | collective-permute-start | bytes 589832 | tf_op jit(solution)/shard_map/ppermute | solution.py:362
  14.7 1.4 copy-done
  16.9 2.5 %collective-permute-done.1.r1.f_ref = f32[384,128]{1,0:T(8,128)S(1)} collective-permute-done((f32[384,128]{1,0:T(8,128)S(1)}, f32[384,128]{1,0:T(8,128)S(1)}, u32[]{:S(2)}, u32[]{:S(2)}) %collective-permute-start.1) | collective-permute-done | bytes 196640 | tf_op jit(solution)/shard_map/ppermute | solution.py:362
  20.3 2.9 %collective-permute-start.4 = (f32[96,128]{1,0:T(8,128)S(1)}, f32[96,128]{1,0:T(8,128)S(1)}, u32[]{:S(2)}, u32[]{:S(2)}) collective-permute-start(f32[96,128]{1,0:T(8,128)S(1)} %pad_maximum_fusion.8), channel_id=1, source_target_pairs={{0,16},{1,17},{2,18},{3,19},{4,20},{5,21},{6,22},{7,23},{8,24},{9,... | collective-permute-start | bytes 147464 | tf_op jit(solution)/shard_map/ppermute | solution.py:362
  23.1 2.2 %shard_map.107 = (f32[640,128]{1,0:T(8,128)S(1)}, f32[160,128]{1,0:T(8,128)S(1)}, f32[160,128]{1,0:T(8,128)S(1)}) custom-call(f32[640,128]{1,0:T(8,128)S(1)} %get-tuple-element.49.current_ref.refs_0_.asm_ref, bf16[1280,640]{1,0:T(8,128)(2,1)S(1)} %shard_map.106.inverse_ref, bf16[640,640]{1,0:T(8,128)(2,1)S(1)} %get-tuple-element.50.perm_ref, ...), custom_call_target="tpu_custom_call" | custom-call | flops 838860800 | bytes 3604480 | tf_op jit(solution)/shard_map/pallas_call | solution.py:64
  25.4 2.2 %collective-permute-start.5 = (f32[352,128]{1,0:T(8,128)S(1)}, f32[352,128]{1,0:T(8,128)S(1)}, u32[]{:S(2)}, u32[]{:S(2)}) collective-permute-start(f32[352,128]{1,0:T(8,128)S(1)} %pad_maximum_fusion), channel_id=1, source_target_pairs={{0,8},{1,9},{2,10},{3,11},{4,12},{5,13},{6,14},{7,15},{8,0},{9,1},... | collective-permute-start | bytes 540680 | tf_op jit(solution)/shard_map/ppermute | solution.py:362
  27.8 4.7 %collective-permute-done.5.g_ref.refs_2_ = f32[352,128]{1,0:T(8,128)S(1)} collective-permute-done((f32[352,128]{1,0:T(8,128)S(1)}, f32[352,128]{1,0:T(8,128)S(1)}, u32[]{:S(2)}, u32[]{:S(2)}) %collective-permute-start.5) | collective-permute-done | bytes 180256 | tf_op jit(solution)/shard_map/ppermute | solution.py:362
  34.3 2.2 %shard_map.108 = (bf16[1280,192]{1,0:T(8,128)(2,1)S(1)}, bf16[1280,384]{1,0:T(8,128)(2,1)S(1)}) custom-call(s32[4]{0:T(128)S(1)} %select_reduce_fusion.link_ref, f32[640,48]{1,0:T(8,128)S(1)} %get-tuple-element.57.basis_ref, f32[48,192]{1,0:T(8,128)S(1)} %bitcast.17, f32[640,48]{1,0:T(8,128)S(1)} %get-tuple-element.58.coarse_ref, f32[48,384]{1,0:T(8,128)S(1)} %copy-done.4, ...), custom_call_target="tpu_custom_call" | custom-call | bytes 1093632 | tf_op jit(solution)/shard_map/pallas_call | solution.py:64
  36.5 0.9 shard_map.109.y2_ref
  38.3 0.9 collective-permute-start.8
  39.2 1.8 %collective-permute-start.7 = (f32[160,128]{1,0:T(8,128)S(1)}, f32[160,128]{1,0:T(8,128)S(1)}, u32[]{:S(2)}, u32[]{:S(2)}) collective-permute-start(f32[160,128]{1,0:T(8,128)S(1)} %get-tuple-element.107), channel_id=1, source_target_pairs={{0,1},{1,0},{2,3},{3,2},{4,5},{5,4},{6,7},{7,6},{8,9},{9,8},{10,11... | collective-permute-start | bytes 245768 | tf_op jit(solution)/shard_map/ppermute | solution.py:362
  41.1 1.8 %collective-permute-start.11 = (f32[192,128]{1,0:T(8,128)S(1)}, f32[192,128]{1,0:T(8,128)S(1)}, u32[]{:S(2)}, u32[]{:S(2)}) collective-permute-start(f32[192,128]{1,0:T(8,128)S(1)} %pad_maximum_fusion.4), channel_id=1, source_target_pairs={{0,4},{1,5},{2,6},{3,7},{4,0},{5,1},{6,2},{7,3},{8,12},{9,13},{10,... | collective-permute-start | bytes 294920 | tf_op jit(solution)/shard_map/ppermute | solution.py:362
  43.0 1.8 %collective-permute-done.11.refs_3_ = f32[192,128]{1,0:T(8,128)S(1)} collective-permute-done((f32[192,128]{1,0:T(8,128)S(1)}, f32[192,128]{1,0:T(8,128)S(1)}, u32[]{:S(2)}, u32[]{:S(2)}) %collective-permute-start.11) | collective-permute-done | bytes 98336 | tf_op jit(solution)/shard_map/ppermute | solution.py:362
  44.9 3.4 %shard_map.113 = (f32[640,128]{1,0:T(8,128)S(1)}, f32[640,128]{1,0:T(8,128)S(1)}) custom-call(s32[4]{0:T(128)S(1)} %select_reduce_fusion.link_ref, s32[8]{0:T(128)S(1)} %xor_multiply_fusion.1.order_ref, f32[640,128]{1,0:T(8,128)S(1)} %shard_map.109.y2_ref, f32[160,128]{1,0:T(8,128)S(1)} %collective-permute-done.7.e_ref, ...), custom_call_target="tpu_custom_call" | custom-call | flops 838860800 | bytes 4947968 | tf_op jit(solution)/shard_map/pallas_call | solution.py:64
  48.3 1.8 %collective-permute-start.15 = (f32[160,128]{1,0:T(8,128)S(1)}, f32[160,128]{1,0:T(8,128)S(1)}, u32[]{:S(2)}, u32[]{:S(2)}) collective-permute-start(f32[160,128]{1,0:T(8,128)S(1)} %get-tuple-element.102), channel_id=1, source_target_pairs={{0,1},{1,0},{2,3},{3,2},{4,5},{5,4},{6,7},{7,6},{8,16},{9,17},{10,... | collective-permute-start | bytes 245768 | tf_op jit(solution)/shard_map/ppermute | solution.py:362
  50.2 3.4 %collective-permute-start.13 = (f32[160,128]{1,0:T(8,128)S(1)}, f32[160,128]{1,0:T(8,128)S(1)}, u32[]{:S(2)}, u32[]{:S(2)}) collective-permute-start(f32[160,128]{1,0:T(8,128)S(1)} %get-tuple-element.104), channel_id=1, source_target_pairs={{0,8},{1,2},{2,1},{3,4},{4,3},{5,6},{6,5},{7,15},{8,0},{9,10},{10,... | collective-permute-start | bytes 245768 | tf_op jit(solution)/shard_map/ppermute | solution.py:362
  54.0 2.0 %collective-permute-done.13.r1 = f32[160,128]{1,0:T(8,128)S(1)} collective-permute-done((f32[160,128]{1,0:T(8,128)S(1)}, f32[160,128]{1,0:T(8,128)S(1)}, u32[]{:S(2)}, u32[]{:S(2)}) %collective-permute-start.13) | collective-permute-done | bytes 81952 | tf_op jit(solution)/shard_map/ppermute | solution.py:362
  56.8 1.0 collective-permute-start.16
  57.8 2.2 %shard_map.115 = (f32[640,128]{1,0:T(8,128)S(1)}, f32[160,128]{1,0:T(8,128)S(1)}, f32[160,128]{1,0:T(8,128)S(1)}) custom-call(f32[640,128]{1,0:T(8,128)S(1)} %get-tuple-element.62.current_ref, bf16[1280,640]{1,0:T(8,128)(2,1)S(1)} %shard_map.106.inverse_ref, bf16[640,640]{1,0:T(8,128)(2,1)S(1)} %get-tuple-element.50.perm_ref, ...), custom_call_target="tpu_custom_call" | custom-call | flops 838860800 | bytes 3604480 | tf_op jit(solution)/shard_map/pallas_call | solution.py:64
  60.7 1.2 collective-permute-start.17
  61.9 2.7 %collective-permute-done.17.g_ref.refs_2_ = f32[256,128]{1,0:T(8,128)S(1)} collective-permute-done((f32[256,128]{1,0:T(8,128)S(1)}, f32[256,128]{1,0:T(8,128)S(1)}, u32[]{:S(2)}, u32[]{:S(2)}) %collective-permute-start.17) | collective-permute-done | bytes 131104 | tf_op jit(solution)/shard_map/ppermute | solution.py:362
  64.8 2.8 %collective-permute-start.21 = (f32[48,128]{1,0:T(8,128)S(1)}, f32[48,128]{1,0:T(8,128)S(1)}, u32[]{:S(2)}, u32[]{:S(2)}) collective-permute-start(f32[48,128]{1,0:T(8,128)S(1)} %shard_map.117.refs_1_), channel_id=1, source_target_pairs={{0,1},{1,0},{2,3},{3,2},{4,5},{5,4},{6,7},{7,6},{8,9},{9,8},{10,11... | collective-permute-start | bytes 73736 | tf_op jit(solution)/shard_map/ppermute | solution.py:362
  68.4 1.3 collective-permute-start.22
  71.4 2.3 %collective-permute-start.23 = (f32[192,128]{1,0:T(8,128)S(1)}, f32[192,128]{1,0:T(8,128)S(1)}, u32[]{:S(2)}, u32[]{:S(2)}) collective-permute-start(f32[192,128]{1,0:T(8,128)S(1)} %pad_maximum_fusion.5), channel_id=1, source_target_pairs={{0,4},{1,5},{2,6},{3,7},{4,0},{5,1},{6,2},{7,3},{8,12},{9,13},{10,... | collective-permute-start | bytes 294920 | tf_op jit(solution)/shard_map/ppermute | solution.py:362
  73.7 2.1 %collective-permute-start.20 = (f32[160,128]{1,0:T(8,128)S(1)}, f32[160,128]{1,0:T(8,128)S(1)}, u32[]{:S(2)}, u32[]{:S(2)}) collective-permute-start(f32[160,128]{1,0:T(8,128)S(1)} %get-tuple-element.100), channel_id=1, source_target_pairs={{0,8},{1,2},{2,1},{3,4},{4,3},{5,6},{6,5},{7,15},{8,0},{9,10},{10,... | collective-permute-start | bytes 245768 | tf_op jit(solution)/shard_map/ppermute | solution.py:362
  75.7 1.0 collective-permute-start.19
  76.7 2.0 %collective-permute-done.20.f_ref = f32[160,128]{1,0:T(8,128)S(1)} collective-permute-done((f32[160,128]{1,0:T(8,128)S(1)}, f32[160,128]{1,0:T(8,128)S(1)}, u32[]{:S(2)}, u32[]{:S(2)}) %collective-permute-start.20) | collective-permute-done | bytes 81952 | tf_op jit(solution)/shard_map/ppermute | solution.py:362
  78.7 3.4 %shard_map.118 = (f32[640,128]{1,0:T(8,128)S(1)}, f32[640,128]{1,0:T(8,128)S(1)}) custom-call(s32[4]{0:T(128)S(1)} %select_reduce_fusion.link_ref, s32[8]{0:T(128)S(1)} %xor_multiply_fusion.1.order_ref, f32[640,128]{1,0:T(8,128)S(1)} %shard_map.116.y2_ref, f32[160,128]{1,0:T(8,128)S(1)} %collective-permute-done.19.e_ref, ...), custom_call_target="tpu_custom_call" | custom-call | flops 838860800 | bytes 5275648 | tf_op jit(solution)/shard_map/pallas_call | solution.py:64
  82.2 1.3 collective-permute-start.27
  84.2 1.6 %collective-permute-start.25 = (f32[160,128]{1,0:T(8,128)S(1)}, f32[160,128]{1,0:T(8,128)S(1)}, u32[]{:S(2)}, u32[]{:S(2)}) collective-permute-start(f32[160,128]{1,0:T(8,128)S(1)} %get-tuple-element.98), channel_id=1, source_target_pairs={{0,8},{1,2},{2,1},{3,4},{4,3},{5,6},{6,5},{7,15},{8,0},{9,10},{10,... | collective-permute-start | bytes 245768 | tf_op jit(solution)/shard_map/ppermute | solution.py:362
  85.8 1.3 collective-permute-done.26.r2
  87.1 0.9 collective-permute-done.25.r1
  88.8 2.9 %collective-permute-start.28 = (f32[48,128]{1,0:T(8,128)S(1)}, f32[48,128]{1,0:T(8,128)S(1)}, u32[]{:S(2)}, u32[]{:S(2)}) collective-permute-start(f32[48,128]{1,0:T(8,128)S(1)} %get-tuple-element.72.refs_0_), channel_id=1, source_target_pairs={{0,16},{1,17},{2,18},{3,19},{4,20},{5,21},{6,22},{7,23},{8,24},{9,... | collective-permute-start | bytes 73736 | tf_op jit(solution)/shard_map/ppermute | solution.py:362
  91.8 2.4 %shard_map.120 = (f32[640,128]{1,0:T(8,128)S(1)}, f32[160,128]{1,0:T(8,128)S(1)}, f32[160,128]{1,0:T(8,128)S(1)}) custom-call(f32[640,128]{1,0:T(8,128)S(1)} %get-tuple-element.69.current_ref, bf16[1280,640]{1,0:T(8,128)(2,1)S(1)} %shard_map.106.inverse_ref, bf16[640,640]{1,0:T(8,128)(2,1)S(1)} %get-tuple-element.50.perm_ref, ...), custom_call_target="tpu_custom_call" | custom-call | flops 838860800 | bytes 3604480 | tf_op jit(solution)/shard_map/pallas_call | solution.py:64
  94.3 3.8 %collective-permute-done.29.g_ref.refs_2_ = f32[256,128]{1,0:T(8,128)S(1)} collective-permute-done((f32[256,128]{1,0:T(8,128)S(1)}, f32[256,128]{1,0:T(8,128)S(1)}, u32[]{:S(2)}, u32[]{:S(2)}) %collective-permute-start.29) | collective-permute-done | bytes 131104 | tf_op jit(solution)/shard_map/ppermute | solution.py:362
  98.3 2.9 %collective-permute-start.33 = (f32[48,128]{1,0:T(8,128)S(1)}, f32[48,128]{1,0:T(8,128)S(1)}, u32[]{:S(2)}, u32[]{:S(2)}) collective-permute-start(f32[48,128]{1,0:T(8,128)S(1)} %shard_map.122.refs_1_), channel_id=1, source_target_pairs={{0,1},{1,0},{2,3},{3,2},{4,5},{5,4},{6,7},{7,6},{8,9},{9,8},{10,11... | collective-permute-start | bytes 73736 | tf_op jit(solution)/shard_map/ppermute | solution.py:362
  102.7 0.9 shard_map.121.y2_ref
  103.6 1.3 collective-permute-done.34.refs_3_
  104.9 1.3 collective-permute-start.35
  106.3 2.2 %collective-permute-start.32 = (f32[160,128]{1,0:T(8,128)S(1)}, f32[160,128]{1,0:T(8,128)S(1)}, u32[]{:S(2)}, u32[]{:S(2)}) collective-permute-start(f32[160,128]{1,0:T(8,128)S(1)} %get-tuple-element.94), channel_id=1, source_target_pairs={{0,8},{1,2},{2,1},{3,4},{4,3},{5,6},{6,5},{7,15},{8,0},{9,10},{10,... | collective-permute-start | bytes 245768 | tf_op jit(solution)/shard_map/ppermute | solution.py:362
  109.2 1.7 %collective-permute-done.32.f_ref = f32[160,128]{1,0:T(8,128)S(1)} collective-permute-done((f32[160,128]{1,0:T(8,128)S(1)}, f32[160,128]{1,0:T(8,128)S(1)}, u32[]{:S(2)}, u32[]{:S(2)}) %collective-permute-start.32) | collective-permute-done | bytes 81952 | tf_op jit(solution)/shard_map/ppermute | solution.py:362
  111.0 3.4 %shard_map.123 = (f32[640,128]{1,0:T(8,128)S(1)}, f32[640,128]{1,0:T(8,128)S(1)}) custom-call(s32[4]{0:T(128)S(1)} %select_reduce_fusion.link_ref, s32[8]{0:T(128)S(1)} %xor_multiply_fusion.1.order_ref, f32[640,128]{1,0:T(8,128)S(1)} %shard_map.121.y2_ref, f32[160,128]{1,0:T(8,128)S(1)} %collective-permute-done.31.e_ref, ...), custom_call_target="tpu_custom_call" | custom-call | flops 838860800 | bytes 5275648 | tf_op jit(solution)/shard_map/pallas_call | solution.py:64
  114.4 1.7 %collective-permute-start.39 = (f32[160,128]{1,0:T(8,128)S(1)}, f32[160,128]{1,0:T(8,128)S(1)}, u32[]{:S(2)}, u32[]{:S(2)}) collective-permute-start(f32[160,128]{1,0:T(8,128)S(1)} %get-tuple-element.90), channel_id=1, source_target_pairs={{0,1},{1,0},{2,3},{3,2},{4,5},{5,4},{6,7},{7,6},{8,16},{9,17},{10,... | collective-permute-start | bytes 245768 | tf_op jit(solution)/shard_map/ppermute | solution.py:362
  116.1 1.5 collective-permute-start.38
  117.5 1.1 collective-permute-start.37
  119.4 2.0 %collective-permute-done.37.r1 = f32[160,128]{1,0:T(8,128)S(1)} collective-permute-done((f32[160,128]{1,0:T(8,128)S(1)}, f32[160,128]{1,0:T(8,128)S(1)}, u32[]{:S(2)}, u32[]{:S(2)}) %collective-permute-start.37) | collective-permute-done | bytes 81952 | tf_op jit(solution)/shard_map/ppermute | solution.py:362
  122.2 1.2 collective-permute-start.40
  123.4 2.2 %shard_map.125 = (f32[640,128]{1,0:T(8,128)S(1)}, f32[160,128]{1,0:T(8,128)S(1)}, f32[160,128]{1,0:T(8,128)S(1)}) custom-call(f32[640,128]{1,0:T(8,128)S(1)} %get-tuple-element.76.current_ref, bf16[1280,640]{1,0:T(8,128)(2,1)S(1)} %shard_map.106.inverse_ref, bf16[640,640]{1,0:T(8,128)(2,1)S(1)} %get-tuple-element.50.perm_ref, ...), custom_call_target="tpu_custom_call" | custom-call | flops 838860800 | bytes 3604480 | tf_op jit(solution)/shard_map/pallas_call | solution.py:64
  126.3 3.7 %collective-permute-done.41.g_ref.refs_2_ = f32[256,128]{1,0:T(8,128)S(1)} collective-permute-done((f32[256,128]{1,0:T(8,128)S(1)}, f32[256,128]{1,0:T(8,128)S(1)}, u32[]{:S(2)}, u32[]{:S(2)}) %collective-permute-start.41) | collective-permute-done | bytes 131104 | tf_op jit(solution)/shard_map/ppermute | solution.py:362
  130.2 3.9 %collective-permute-start.45 = (f32[48,128]{1,0:T(8,128)S(1)}, f32[48,128]{1,0:T(8,128)S(1)}, u32[]{:S(2)}, u32[]{:S(2)}) collective-permute-start(f32[48,128]{1,0:T(8,128)S(1)} %shard_map.127.refs_1_), channel_id=1, source_target_pairs={{0,1},{1,0},{2,3},{3,2},{4,5},{5,4},{6,7},{7,6},{8,9},{9,8},{10,11... | collective-permute-start | bytes 73736 | tf_op jit(solution)/shard_map/ppermute | solution.py:362
  136.2 1.6 %collective-permute-done.46.refs_3_ = f32[96,128]{1,0:T(8,128)S(1)} collective-permute-done((f32[96,128]{1,0:T(8,128)S(1)}, f32[96,128]{1,0:T(8,128)S(1)}, u32[]{:S(2)}, u32[]{:S(2)}) %collective-permute-start.46) | collective-permute-done | bytes 49184 | tf_op jit(solution)/shard_map/ppermute | solution.py:362
  137.8 1.5 collective-permute-start.47
  139.3 1.4 collective-permute-start.44
  141.6 1.9 %collective-permute-done.44.f_ref = f32[160,128]{1,0:T(8,128)S(1)} collective-permute-done((f32[160,128]{1,0:T(8,128)S(1)}, f32[160,128]{1,0:T(8,128)S(1)}, u32[]{:S(2)}, u32[]{:S(2)}) %collective-permute-start.44) | collective-permute-done | bytes 81952 | tf_op jit(solution)/shard_map/ppermute | solution.py:362
  143.5 3.4 %shard_map.128 = (f32[640,128]{1,0:T(8,128)}, f32[640,128]{1,0:T(8,128)S(1)}) custom-call(s32[4]{0:T(128)S(1)} %select_reduce_fusion.link_ref, s32[8]{0:T(128)S(1)} %xor_multiply_fusion.1.order_ref, f32[640,128]{1,0:T(8,128)S(1)} %shard_map.126.y2_ref, f32[160,128]{1,0:T(8,128)S(1)} %collective-permute-done.43.e_ref, ...), custom_call_target="tpu_custom_call" | custom-call | flops 838860800 | bytes 5275648 | tf_op jit(solution)/shard_map/pallas_call | solution.py:64
  147.0 2.1 %collective-permute-start.51 = (f32[160,128]{1,0:T(8,128)S(1)}, f32[160,128]{1,0:T(8,128)S(1)}, u32[]{:S(2)}, u32[]{:S(2)}) collective-permute-start(f32[160,128]{1,0:T(8,128)S(1)} %get-tuple-element.84), channel_id=1, source_target_pairs={{0,1},{1,0},{2,3},{3,2},{4,5},{5,4},{6,7},{7,6},{8,16},{9,17},{10,... | collective-permute-start | bytes 245768 | tf_op jit(solution)/shard_map/ppermute | solution.py:362
  149.2 2.0 %collective-permute-start.48 = (f32[160,128]{1,0:T(8,128)S(1)}, f32[160,128]{1,0:T(8,128)S(1)}, u32[]{:S(2)}, u32[]{:S(2)}) collective-permute-start(f32[160,128]{1,0:T(8,128)S(1)} %get-tuple-element.87), channel_id=1, source_target_pairs={{0,1},{1,0},{2,3},{3,2},{4,5},{5,4},{6,7},{7,6},{8,9},{9,8},{10,11... | collective-permute-start | bytes 245768 | tf_op jit(solution)/shard_map/ppermute | solution.py:362
  151.2 1.8 %collective-permute-done.50.r2 = f32[160,128]{1,0:T(8,128)S(1)} collective-permute-done((f32[160,128]{1,0:T(8,128)S(1)}, f32[160,128]{1,0:T(8,128)S(1)}, u32[]{:S(2)}, u32[]{:S(2)}) %collective-permute-start.50) | collective-permute-done | bytes 81952 | tf_op jit(solution)/shard_map/ppermute | solution.py:362
  153.3 1.9 %shard_map.129 = f32[640,128]{1,0:T(8,128)} custom-call(s32[4]{0:T(128)S(1)} %select_reduce_fusion.link_ref, f32[640,128]{1,0:T(8,128)S(1)} %get-tuple-element.83.f_ref, f32[160,128]{1,0:T(8,128)S(1)} %collective-permute-done.48.r0, f32[160,128]{1,0:T(8,128)S(1)} %collective-permute-done.49.r1, f32[160,128]{1,0:T(8,128)S(1)} %collective-permute-done.50.r2, ...), custom_call_target="tpu_custom_call" | custom-call | bytes 1802240 | tf_op jit(solution)/shard_map/pallas_call | solution.py:64
  (111 shorter events, 22.6 us)
Async XLA Ops:
  1.8 1.0 copy-start.2
  2.8 0.9 copy-start.3
  3.6 0.8 copy-start.5
  4.4 0.7 copy-start.6
  5.2 0.7 copy-start.7
  9.9 7.0 %collective-permute-start.2 = (f32[336,128]{1,0:T(8,128)S(1)}, f32[336,128]{1,0:T(8,128)S(1)}, u32[]{:S(2)}, u32[]{:S(2)}) collective-permute-start(f32[336,128]{1,0:T(8,128)S(1)} %get-tuple-element.46), channel_id=1, source_target_pairs={{0,8},{1,9},{2,10},{3,11},{4,12},{5,13},{6,14},{7,15},{8,0},{9,1},... | collective-permute-start | bytes 516104 | tf_op jit(solution)/shard_map/ppermute | solution.py:362
  12.1 4.8 %collective-permute-start.3 = (f32[336,128]{1,0:T(8,128)S(1)}, f32[336,128]{1,0:T(8,128)S(1)}, u32[]{:S(2)}, u32[]{:S(2)}) collective-permute-start(f32[336,128]{1,0:T(8,128)S(1)} %get-tuple-element.47), channel_id=1, source_target_pairs={{0,1},{1,0},{2,3},{3,2},{4,5},{5,4},{6,7},{7,6},{8,16},{9,17},{10,... | collective-permute-start | bytes 516104 | tf_op jit(solution)/shard_map/ppermute | solution.py:362
  13.1 3.9 %collective-permute-start = (f32[384,128]{1,0:T(8,128)S(1)}, f32[384,128]{1,0:T(8,128)S(1)}, u32[]{:S(2)}, u32[]{:S(2)}) collective-permute-start(f32[384,128]{1,0:T(8,128)S(1)} %get-tuple-element.44), channel_id=1, source_target_pairs={{0,1},{1,0},{2,3},{3,2},{4,5},{5,4},{6,7},{7,6},{8,9},{9,8},{10,11... | collective-permute-start | bytes 589832 | tf_op jit(solution)/shard_map/ppermute | solution.py:362
  13.1 6.4 %collective-permute-start.1 = (f32[384,128]{1,0:T(8,128)S(1)}, f32[384,128]{1,0:T(8,128)S(1)}, u32[]{:S(2)}, u32[]{:S(2)}) collective-permute-start(f32[384,128]{1,0:T(8,128)S(1)} %get-tuple-element.45), channel_id=1, source_target_pairs={{0,8},{1,2},{2,1},{3,4},{4,3},{5,6},{6,5},{7,15},{8,0},{9,10},{10,... | collective-permute-start | bytes 589832 | tf_op jit(solution)/shard_map/ppermute | solution.py:362
  14.7 1.4 copy-start
  16.1 0.7 copy-start.8
  20.3 5.1 %collective-permute-start.4 = (f32[96,128]{1,0:T(8,128)S(1)}, f32[96,128]{1,0:T(8,128)S(1)}, u32[]{:S(2)}, u32[]{:S(2)}) collective-permute-start(f32[96,128]{1,0:T(8,128)S(1)} %pad_maximum_fusion.8), channel_id=1, source_target_pairs={{0,16},{1,17},{2,18},{3,19},{4,20},{5,21},{6,22},{7,23},{8,24},{9,... | collective-permute-start | bytes 147464 | tf_op jit(solution)/shard_map/ppermute | solution.py:362
  23.1 10.3 %copy-start.1 = (f32[1,1,640,640]{3,2,1,0:T(8,128)S(1)}, f32[1,1,640,640]{3,2,1,0:T(8,128)}, u32[]{:S(2)}) copy-start(f32[1,1,640,640]{3,2,1,0:T(8,128)} %param.10) | copy-start | bytes 4915204
  25.4 7.1 %collective-permute-start.5 = (f32[352,128]{1,0:T(8,128)S(1)}, f32[352,128]{1,0:T(8,128)S(1)}, u32[]{:S(2)}, u32[]{:S(2)}) collective-permute-start(f32[352,128]{1,0:T(8,128)S(1)} %pad_maximum_fusion), channel_id=1, source_target_pairs={{0,8},{1,9},{2,10},{3,11},{4,12},{5,13},{6,14},{7,15},{8,0},{9,1},... | collective-permute-start | bytes 540680 | tf_op jit(solution)/shard_map/ppermute | solution.py:362
  27.6 8.9 %collective-permute-start.6 = (f32[160,128]{1,0:T(8,128)S(1)}, f32[160,128]{1,0:T(8,128)S(1)}, u32[]{:S(2)}, u32[]{:S(2)}) collective-permute-start(f32[160,128]{1,0:T(8,128)S(1)} %get-tuple-element.56), channel_id=1, source_target_pairs={{0,1},{1,0},{2,3},{3,2},{4,5},{5,4},{6,7},{7,6},{8,16},{9,17},{10,... | collective-permute-start | bytes 245768 | tf_op jit(solution)/shard_map/ppermute | solution.py:362
  32.7 4.6 %collective-permute-start.9 = (f32[48,128]{1,0:T(8,128)S(1)}, f32[48,128]{1,0:T(8,128)S(1)}, u32[]{:S(2)}, u32[]{:S(2)}) collective-permute-start(f32[48,128]{1,0:T(8,128)S(1)} %shard_map.112.refs_0_), channel_id=1, source_target_pairs={{0,1},{1,0},{2,3},{3,2},{4,5},{5,4},{6,7},{7,6},{8,9},{9,8},{10,11... | collective-permute-start | bytes 73736 | tf_op jit(solution)/shard_map/ppermute | solution.py:362
  33.4 0.9 copy-start.4
  37.4 3.7 %collective-permute-start.10 = (f32[96,128]{1,0:T(8,128)S(1)}, f32[96,128]{1,0:T(8,128)S(1)}, u32[]{:S(2)}, u32[]{:S(2)}) collective-permute-start(f32[96,128]{1,0:T(8,128)S(1)} %pad_maximum_fusion.9), channel_id=1, source_target_pairs={{0,2},{1,3},{2,0},{3,1},{4,6},{5,7},{6,4},{7,5},{8,10},{9,11},{10,... | collective-permute-start | bytes 147464 | tf_op jit(solution)/shard_map/ppermute | solution.py:362
  38.3 4.8 %collective-permute-start.8 = (f32[160,128]{1,0:T(8,128)S(1)}, f32[160,128]{1,0:T(8,128)S(1)}, u32[]{:S(2)}, u32[]{:S(2)}) collective-permute-start(f32[160,128]{1,0:T(8,128)S(1)} %get-tuple-element.106), channel_id=1, source_target_pairs={{0,8},{1,2},{2,1},{3,4},{4,3},{5,6},{6,5},{7,15},{8,0},{9,10},{10,... | collective-permute-start | bytes 245768 | tf_op jit(solution)/shard_map/ppermute | solution.py:362
  39.2 3.9 %collective-permute-start.7 = (f32[160,128]{1,0:T(8,128)S(1)}, f32[160,128]{1,0:T(8,128)S(1)}, u32[]{:S(2)}, u32[]{:S(2)}) collective-permute-start(f32[160,128]{1,0:T(8,128)S(1)} %get-tuple-element.107), channel_id=1, source_target_pairs={{0,1},{1,0},{2,3},{3,2},{4,5},{5,4},{6,7},{7,6},{8,9},{9,8},{10,11... | collective-permute-start | bytes 245768 | tf_op jit(solution)/shard_map/ppermute | solution.py:362
  41.1 3.8 %collective-permute-start.11 = (f32[192,128]{1,0:T(8,128)S(1)}, f32[192,128]{1,0:T(8,128)S(1)}, u32[]{:S(2)}, u32[]{:S(2)}) collective-permute-start(f32[192,128]{1,0:T(8,128)S(1)} %pad_maximum_fusion.4), channel_id=1, source_target_pairs={{0,4},{1,5},{2,6},{3,7},{4,0},{5,1},{6,2},{7,3},{8,12},{9,13},{10,... | collective-permute-start | bytes 294920 | tf_op jit(solution)/shard_map/ppermute | solution.py:362
  48.3 5.3 %collective-permute-start.15 = (f32[160,128]{1,0:T(8,128)S(1)}, f32[160,128]{1,0:T(8,128)S(1)}, u32[]{:S(2)}, u32[]{:S(2)}) collective-permute-start(f32[160,128]{1,0:T(8,128)S(1)} %get-tuple-element.102), channel_id=1, source_target_pairs={{0,1},{1,0},{2,3},{3,2},{4,5},{5,4},{6,7},{7,6},{8,16},{9,17},{10,... | collective-permute-start | bytes 245768 | tf_op jit(solution)/shard_map/ppermute | solution.py:362
  50.1 3.9 %collective-permute-start.14 = (f32[160,128]{1,0:T(8,128)S(1)}, f32[160,128]{1,0:T(8,128)S(1)}, u32[]{:S(2)}, u32[]{:S(2)}) collective-permute-start(f32[160,128]{1,0:T(8,128)S(1)} %get-tuple-element.103), channel_id=1, source_target_pairs={{0,8},{1,9},{2,10},{3,11},{4,12},{5,13},{6,14},{7,15},{8,0},{9,1},... | collective-permute-start | bytes 245768 | tf_op jit(solution)/shard_map/ppermute | solution.py:362
  50.2 5.8 %collective-permute-start.13 = (f32[160,128]{1,0:T(8,128)S(1)}, f32[160,128]{1,0:T(8,128)S(1)}, u32[]{:S(2)}, u32[]{:S(2)}) collective-permute-start(f32[160,128]{1,0:T(8,128)S(1)} %get-tuple-element.104), channel_id=1, source_target_pairs={{0,8},{1,2},{2,1},{3,4},{4,3},{5,6},{6,5},{7,15},{8,0},{9,10},{10,... | collective-permute-start | bytes 245768 | tf_op jit(solution)/shard_map/ppermute | solution.py:362
  53.6 2.4 %collective-permute-start.12 = (f32[160,128]{1,0:T(8,128)S(1)}, f32[160,128]{1,0:T(8,128)S(1)}, u32[]{:S(2)}, u32[]{:S(2)}) collective-permute-start(f32[160,128]{1,0:T(8,128)S(1)} %get-tuple-element.105), channel_id=1, source_target_pairs={{0,1},{1,0},{2,3},{3,2},{4,5},{5,4},{6,7},{7,6},{8,9},{9,8},{10,11... | collective-permute-start | bytes 245768 | tf_op jit(solution)/shard_map/ppermute | solution.py:362
  56.8 3.9 %collective-permute-start.16 = (f32[48,128]{1,0:T(8,128)S(1)}, f32[48,128]{1,0:T(8,128)S(1)}, u32[]{:S(2)}, u32[]{:S(2)}) collective-permute-start(f32[48,128]{1,0:T(8,128)S(1)} %get-tuple-element.65.refs_0_), channel_id=1, source_target_pairs={{0,16},{1,17},{2,18},{3,19},{4,20},{5,21},{6,22},{7,23},{8,24},{9,... | collective-permute-start | bytes 73736 | tf_op jit(solution)/shard_map/ppermute | solution.py:362
  60.7 3.9 %collective-permute-start.17 = (f32[256,128]{1,0:T(8,128)S(1)}, f32[256,128]{1,0:T(8,128)S(1)}, u32[]{:S(2)}, u32[]{:S(2)}) collective-permute-start(f32[256,128]{1,0:T(8,128)S(1)} %pad_maximum_fusion.1), channel_id=1, source_target_pairs={{0,8},{1,9},{2,10},{3,11},{4,12},{5,13},{6,14},{7,15},{8,0},{9,1},... | collective-permute-start | bytes 393224 | tf_op jit(solution)/shard_map/ppermute | solution.py:362
  64.8 3.6 %collective-permute-start.21 = (f32[48,128]{1,0:T(8,128)S(1)}, f32[48,128]{1,0:T(8,128)S(1)}, u32[]{:S(2)}, u32[]{:S(2)}) collective-permute-start(f32[48,128]{1,0:T(8,128)S(1)} %shard_map.117.refs_1_), channel_id=1, source_target_pairs={{0,1},{1,0},{2,3},{3,2},{4,5},{5,4},{6,7},{7,6},{8,9},{9,8},{10,11... | collective-permute-start | bytes 73736 | tf_op jit(solution)/shard_map/ppermute | solution.py:362
  67.5 2.2 %collective-permute-start.18 = (f32[160,128]{1,0:T(8,128)S(1)}, f32[160,128]{1,0:T(8,128)S(1)}, u32[]{:S(2)}, u32[]{:S(2)}) collective-permute-start(f32[160,128]{1,0:T(8,128)S(1)} %get-tuple-element.66), channel_id=1, source_target_pairs={{0,1},{1,0},{2,3},{3,2},{4,5},{5,4},{6,7},{7,6},{8,16},{9,17},{10,... | collective-permute-start | bytes 245768 | tf_op jit(solution)/shard_map/ppermute | solution.py:362
  68.4 2.9 %collective-permute-start.22 = (f32[96,128]{1,0:T(8,128)S(1)}, f32[96,128]{1,0:T(8,128)S(1)}, u32[]{:S(2)}, u32[]{:S(2)}) collective-permute-start(f32[96,128]{1,0:T(8,128)S(1)} %pad_maximum_fusion.10), channel_id=1, source_target_pairs={{0,2},{1,3},{2,0},{3,1},{4,6},{5,7},{6,4},{7,5},{8,10},{9,11},{10,... | collective-permute-start | bytes 147464 | tf_op jit(solution)/shard_map/ppermute | solution.py:362
  71.4 7.4 %collective-permute-start.23 = (f32[192,128]{1,0:T(8,128)S(1)}, f32[192,128]{1,0:T(8,128)S(1)}, u32[]{:S(2)}, u32[]{:S(2)}) collective-permute-start(f32[192,128]{1,0:T(8,128)S(1)} %pad_maximum_fusion.5), channel_id=1, source_target_pairs={{0,4},{1,5},{2,6},{3,7},{4,0},{5,1},{6,2},{7,3},{8,12},{9,13},{10,... | collective-permute-start | bytes 294920 | tf_op jit(solution)/shard_map/ppermute | solution.py:362
  73.7 5.1 %collective-permute-start.20 = (f32[160,128]{1,0:T(8,128)S(1)}, f32[160,128]{1,0:T(8,128)S(1)}, u32[]{:S(2)}, u32[]{:S(2)}) collective-permute-start(f32[160,128]{1,0:T(8,128)S(1)} %get-tuple-element.100), channel_id=1, source_target_pairs={{0,8},{1,2},{2,1},{3,4},{4,3},{5,6},{6,5},{7,15},{8,0},{9,10},{10,... | collective-permute-start | bytes 245768 | tf_op jit(solution)/shard_map/ppermute | solution.py:362
  75.7 3.0 %collective-permute-start.19 = (f32[160,128]{1,0:T(8,128)S(1)}, f32[160,128]{1,0:T(8,128)S(1)}, u32[]{:S(2)}, u32[]{:S(2)}) collective-permute-start(f32[160,128]{1,0:T(8,128)S(1)} %get-tuple-element.101), channel_id=1, source_target_pairs={{0,1},{1,0},{2,3},{3,2},{4,5},{5,4},{6,7},{7,6},{8,9},{9,8},{10,11... | collective-permute-start | bytes 245768 | tf_op jit(solution)/shard_map/ppermute | solution.py:362
  82.2 3.7 %collective-permute-start.27 = (f32[160,128]{1,0:T(8,128)S(1)}, f32[160,128]{1,0:T(8,128)S(1)}, u32[]{:S(2)}, u32[]{:S(2)}) collective-permute-start(f32[160,128]{1,0:T(8,128)S(1)} %get-tuple-element.96), channel_id=1, source_target_pairs={{0,1},{1,0},{2,3},{3,2},{4,5},{5,4},{6,7},{7,6},{8,16},{9,17},{10,... | collective-permute-start | bytes 245768 | tf_op jit(solution)/shard_map/ppermute | solution.py:362
  83.5 3.7 %collective-permute-start.26 = (f32[160,128]{1,0:T(8,128)S(1)}, f32[160,128]{1,0:T(8,128)S(1)}, u32[]{:S(2)}, u32[]{:S(2)}) collective-permute-start(f32[160,128]{1,0:T(8,128)S(1)} %get-tuple-element.97), channel_id=1, source_target_pairs={{0,8},{1,9},{2,10},{3,11},{4,12},{5,13},{6,14},{7,15},{8,0},{9,1},... | collective-permute-start | bytes 245768 | tf_op jit(solution)/shard_map/ppermute | solution.py:362
  84.2 3.9 %collective-permute-start.25 = (f32[160,128]{1,0:T(8,128)S(1)}, f32[160,128]{1,0:T(8,128)S(1)}, u32[]{:S(2)}, u32[]{:S(2)}) collective-permute-start(f32[160,128]{1,0:T(8,128)S(1)} %get-tuple-element.98), channel_id=1, source_target_pairs={{0,8},{1,2},{2,1},{3,4},{4,3},{5,6},{6,5},{7,15},{8,0},{9,10},{10,... | collective-permute-start | bytes 245768 | tf_op jit(solution)/shard_map/ppermute | solution.py:362
  85.8 2.3 %collective-permute-start.24 = (f32[160,128]{1,0:T(8,128)S(1)}, f32[160,128]{1,0:T(8,128)S(1)}, u32[]{:S(2)}, u32[]{:S(2)}) collective-permute-start(f32[160,128]{1,0:T(8,128)S(1)} %get-tuple-element.99), channel_id=1, source_target_pairs={{0,1},{1,0},{2,3},{3,2},{4,5},{5,4},{6,7},{7,6},{8,9},{9,8},{10,11... | collective-permute-start | bytes 245768 | tf_op jit(solution)/shard_map/ppermute | solution.py:362
  88.8 5.3 %collective-permute-start.28 = (f32[48,128]{1,0:T(8,128)S(1)}, f32[48,128]{1,0:T(8,128)S(1)}, u32[]{:S(2)}, u32[]{:S(2)}) collective-permute-start(f32[48,128]{1,0:T(8,128)S(1)} %get-tuple-element.72.refs_0_), channel_id=1, source_target_pairs={{0,16},{1,17},{2,18},{3,19},{4,20},{5,21},{6,22},{7,23},{8,24},{9,... | collective-permute-start | bytes 73736 | tf_op jit(solution)/shard_map/ppermute | solution.py:362
  94.2 3.9 %collective-permute-start.29 = (f32[256,128]{1,0:T(8,128)S(1)}, f32[256,128]{1,0:T(8,128)S(1)}, u32[]{:S(2)}, u32[]{:S(2)}) collective-permute-start(f32[256,128]{1,0:T(8,128)S(1)} %pad_maximum_fusion.2), channel_id=1, source_target_pairs={{0,8},{1,9},{2,10},{3,11},{4,12},{5,13},{6,14},{7,15},{8,0},{9,1},... | collective-permute-start | bytes 393224 | tf_op jit(solution)/shard_map/ppermute | solution.py:362
  98.3 3.7 %collective-permute-start.33 = (f32[48,128]{1,0:T(8,128)S(1)}, f32[48,128]{1,0:T(8,128)S(1)}, u32[]{:S(2)}, u32[]{:S(2)}) collective-permute-start(f32[48,128]{1,0:T(8,128)S(1)} %shard_map.122.refs_1_), channel_id=1, source_target_pairs={{0,1},{1,0},{2,3},{3,2},{4,5},{5,4},{6,7},{7,6},{8,9},{9,8},{10,11... | collective-permute-start | bytes 73736 | tf_op jit(solution)/shard_map/ppermute | solution.py:362
  101.1 1.6 %collective-permute-start.30 = (f32[160,128]{1,0:T(8,128)S(1)}, f32[160,128]{1,0:T(8,128)S(1)}, u32[]{:S(2)}, u32[]{:S(2)}) collective-permute-start(f32[160,128]{1,0:T(8,128)S(1)} %get-tuple-element.73), channel_id=1, source_target_pairs={{0,1},{1,0},{2,3},{3,2},{4,5},{5,4},{6,7},{7,6},{8,16},{9,17},{10,... | collective-permute-start | bytes 245768 | tf_op jit(solution)/shard_map/ppermute | solution.py:362
  102.0 2.9 %collective-permute-start.34 = (f32[96,128]{1,0:T(8,128)S(1)}, f32[96,128]{1,0:T(8,128)S(1)}, u32[]{:S(2)}, u32[]{:S(2)}) collective-permute-start(f32[96,128]{1,0:T(8,128)S(1)} %pad_maximum_fusion.11), channel_id=1, source_target_pairs={{0,2},{1,3},{2,0},{3,1},{4,6},{5,7},{6,4},{7,5},{8,10},{9,11},{10,... | collective-permute-start | bytes 147464 | tf_op jit(solution)/shard_map/ppermute | solution.py:362
  104.9 6.0 %collective-permute-start.35 = (f32[192,128]{1,0:T(8,128)S(1)}, f32[192,128]{1,0:T(8,128)S(1)}, u32[]{:S(2)}, u32[]{:S(2)}) collective-permute-start(f32[192,128]{1,0:T(8,128)S(1)} %pad_maximum_fusion.6), channel_id=1, source_target_pairs={{0,4},{1,5},{2,6},{3,7},{4,0},{5,1},{6,2},{7,3},{8,12},{9,13},{10,... | collective-permute-start | bytes 294920 | tf_op jit(solution)/shard_map/ppermute | solution.py:362
  106.3 4.7 %collective-permute-start.32 = (f32[160,128]{1,0:T(8,128)S(1)}, f32[160,128]{1,0:T(8,128)S(1)}, u32[]{:S(2)}, u32[]{:S(2)}) collective-permute-start(f32[160,128]{1,0:T(8,128)S(1)} %get-tuple-element.94), channel_id=1, source_target_pairs={{0,8},{1,2},{2,1},{3,4},{4,3},{5,6},{6,5},{7,15},{8,0},{9,10},{10,... | collective-permute-start | bytes 245768 | tf_op jit(solution)/shard_map/ppermute | solution.py:362
  108.5 2.4 %collective-permute-start.31 = (f32[160,128]{1,0:T(8,128)S(1)}, f32[160,128]{1,0:T(8,128)S(1)}, u32[]{:S(2)}, u32[]{:S(2)}) collective-permute-start(f32[160,128]{1,0:T(8,128)S(1)} %get-tuple-element.95), channel_id=1, source_target_pairs={{0,1},{1,0},{2,3},{3,2},{4,5},{5,4},{6,7},{7,6},{8,9},{9,8},{10,11... | collective-permute-start | bytes 245768 | tf_op jit(solution)/shard_map/ppermute | solution.py:362
  114.4 4.4 %collective-permute-start.39 = (f32[160,128]{1,0:T(8,128)S(1)}, f32[160,128]{1,0:T(8,128)S(1)}, u32[]{:S(2)}, u32[]{:S(2)}) collective-permute-start(f32[160,128]{1,0:T(8,128)S(1)} %get-tuple-element.90), channel_id=1, source_target_pairs={{0,1},{1,0},{2,3},{3,2},{4,5},{5,4},{6,7},{7,6},{8,16},{9,17},{10,... | collective-permute-start | bytes 245768 | tf_op jit(solution)/shard_map/ppermute | solution.py:362
  116.1 3.3 %collective-permute-start.38 = (f32[160,128]{1,0:T(8,128)S(1)}, f32[160,128]{1,0:T(8,128)S(1)}, u32[]{:S(2)}, u32[]{:S(2)}) collective-permute-start(f32[160,128]{1,0:T(8,128)S(1)} %get-tuple-element.91), channel_id=1, source_target_pairs={{0,8},{1,9},{2,10},{3,11},{4,12},{5,13},{6,14},{7,15},{8,0},{9,1},... | collective-permute-start | bytes 245768 | tf_op jit(solution)/shard_map/ppermute | solution.py:362
  117.5 3.9 %collective-permute-start.37 = (f32[160,128]{1,0:T(8,128)S(1)}, f32[160,128]{1,0:T(8,128)S(1)}, u32[]{:S(2)}, u32[]{:S(2)}) collective-permute-start(f32[160,128]{1,0:T(8,128)S(1)} %get-tuple-element.92), channel_id=1, source_target_pairs={{0,8},{1,2},{2,1},{3,4},{4,3},{5,6},{6,5},{7,15},{8,0},{9,10},{10,... | collective-permute-start | bytes 245768 | tf_op jit(solution)/shard_map/ppermute | solution.py:362
  118.6 2.8 %collective-permute-start.36 = (f32[160,128]{1,0:T(8,128)S(1)}, f32[160,128]{1,0:T(8,128)S(1)}, u32[]{:S(2)}, u32[]{:S(2)}) collective-permute-start(f32[160,128]{1,0:T(8,128)S(1)} %get-tuple-element.93), channel_id=1, source_target_pairs={{0,1},{1,0},{2,3},{3,2},{4,5},{5,4},{6,7},{7,6},{8,9},{9,8},{10,11... | collective-permute-start | bytes 245768 | tf_op jit(solution)/shard_map/ppermute | solution.py:362
  122.2 3.9 %collective-permute-start.40 = (f32[48,128]{1,0:T(8,128)S(1)}, f32[48,128]{1,0:T(8,128)S(1)}, u32[]{:S(2)}, u32[]{:S(2)}) collective-permute-start(f32[48,128]{1,0:T(8,128)S(1)} %get-tuple-element.79.refs_0_), channel_id=1, source_target_pairs={{0,16},{1,17},{2,18},{3,19},{4,20},{5,21},{6,22},{7,23},{8,24},{9,... | collective-permute-start | bytes 73736 | tf_op jit(solution)/shard_map/ppermute | solution.py:362
  126.1 3.9 %collective-permute-start.41 = (f32[256,128]{1,0:T(8,128)S(1)}, f32[256,128]{1,0:T(8,128)S(1)}, u32[]{:S(2)}, u32[]{:S(2)}) collective-permute-start(f32[256,128]{1,0:T(8,128)S(1)} %pad_maximum_fusion.3), channel_id=1, source_target_pairs={{0,8},{1,9},{2,10},{3,11},{4,12},{5,13},{6,14},{7,15},{8,0},{9,1},... | collective-permute-start | bytes 393224 | tf_op jit(solution)/shard_map/ppermute | solution.py:362
  130.2 4.7 %collective-permute-start.45 = (f32[48,128]{1,0:T(8,128)S(1)}, f32[48,128]{1,0:T(8,128)S(1)}, u32[]{:S(2)}, u32[]{:S(2)}) collective-permute-start(f32[48,128]{1,0:T(8,128)S(1)} %shard_map.127.refs_1_), channel_id=1, source_target_pairs={{0,1},{1,0},{2,3},{3,2},{4,5},{5,4},{6,7},{7,6},{8,9},{9,8},{10,11... | collective-permute-start | bytes 73736 | tf_op jit(solution)/shard_map/ppermute | solution.py:362
  134.0 1.3 collective-permute-start.42
  134.9 2.9 %collective-permute-start.46 = (f32[96,128]{1,0:T(8,128)S(1)}, f32[96,128]{1,0:T(8,128)S(1)}, u32[]{:S(2)}, u32[]{:S(2)}) collective-permute-start(f32[96,128]{1,0:T(8,128)S(1)} %pad_maximum_fusion.12), channel_id=1, source_target_pairs={{0,2},{1,3},{2,0},{3,1},{4,6},{5,7},{6,4},{7,5},{8,10},{9,11},{10,... | collective-permute-start | bytes 147464 | tf_op jit(solution)/shard_map/ppermute | solution.py:362
  137.8 5.7 %collective-permute-start.47 = (f32[192,128]{1,0:T(8,128)S(1)}, f32[192,128]{1,0:T(8,128)S(1)}, u32[]{:S(2)}, u32[]{:S(2)}) collective-permute-start(f32[192,128]{1,0:T(8,128)S(1)} %pad_maximum_fusion.7), channel_id=1, source_target_pairs={{0,4},{1,5},{2,6},{3,7},{4,0},{5,1},{6,2},{7,3},{8,12},{9,13},{10,... | collective-permute-start | bytes 294920 | tf_op jit(solution)/shard_map/ppermute | solution.py:362
  139.3 4.2 %collective-permute-start.44 = (f32[160,128]{1,0:T(8,128)S(1)}, f32[160,128]{1,0:T(8,128)S(1)}, u32[]{:S(2)}, u32[]{:S(2)}) collective-permute-start(f32[160,128]{1,0:T(8,128)S(1)} %get-tuple-element.88), channel_id=1, source_target_pairs={{0,8},{1,2},{2,1},{3,4},{4,3},{5,6},{6,5},{7,15},{8,0},{9,10},{10,... | collective-permute-start | bytes 245768 | tf_op jit(solution)/shard_map/ppermute | solution.py:362
  140.8 2.8 %collective-permute-start.43 = (f32[160,128]{1,0:T(8,128)S(1)}, f32[160,128]{1,0:T(8,128)S(1)}, u32[]{:S(2)}, u32[]{:S(2)}) collective-permute-start(f32[160,128]{1,0:T(8,128)S(1)} %get-tuple-element.89), channel_id=1, source_target_pairs={{0,1},{1,0},{2,3},{3,2},{4,5},{5,4},{6,7},{7,6},{8,9},{9,8},{10,11... | collective-permute-start | bytes 245768 | tf_op jit(solution)/shard_map/ppermute | solution.py:362
  147.0 4.2 %collective-permute-start.51 = (f32[160,128]{1,0:T(8,128)S(1)}, f32[160,128]{1,0:T(8,128)S(1)}, u32[]{:S(2)}, u32[]{:S(2)}) collective-permute-start(f32[160,128]{1,0:T(8,128)S(1)} %get-tuple-element.84), channel_id=1, source_target_pairs={{0,1},{1,0},{2,3},{3,2},{4,5},{5,4},{6,7},{7,6},{8,16},{9,17},{10,... | collective-permute-start | bytes 245768 | tf_op jit(solution)/shard_map/ppermute | solution.py:362
  149.1 3.9 %collective-permute-start.50 = (f32[160,128]{1,0:T(8,128)S(1)}, f32[160,128]{1,0:T(8,128)S(1)}, u32[]{:S(2)}, u32[]{:S(2)}) collective-permute-start(f32[160,128]{1,0:T(8,128)S(1)} %get-tuple-element.85), channel_id=1, source_target_pairs={{0,8},{1,9},{2,10},{3,11},{4,12},{5,13},{6,14},{7,15},{8,0},{9,1},... | collective-permute-start | bytes 245768 | tf_op jit(solution)/shard_map/ppermute | solution.py:362
  149.1 4.2 %collective-permute-start.49 = (f32[160,128]{1,0:T(8,128)S(1)}, f32[160,128]{1,0:T(8,128)S(1)}, u32[]{:S(2)}, u32[]{:S(2)}) collective-permute-start(f32[160,128]{1,0:T(8,128)S(1)} %get-tuple-element.86), channel_id=1, source_target_pairs={{0,8},{1,2},{2,1},{3,4},{4,3},{5,6},{6,5},{7,15},{8,0},{9,10},{10,... | collective-permute-start | bytes 245768 | tf_op jit(solution)/shard_map/ppermute | solution.py:362
  149.2 4.0 %collective-permute-start.48 = (f32[160,128]{1,0:T(8,128)S(1)}, f32[160,128]{1,0:T(8,128)S(1)}, u32[]{:S(2)}, u32[]{:S(2)}) collective-permute-start(f32[160,128]{1,0:T(8,128)S(1)} %get-tuple-element.87), channel_id=1, source_target_pairs={{0,1},{1,0},{2,3},{3,2},{4,5},{5,4},{6,7},{7,6},{8,9},{9,8},{10,11... | collective-permute-start | bytes 245768 | tf_op jit(solution)/shard_map/ppermute | solution.py:362

commit v3 on v2

--- a/solution.py
+++ b/solution.py
@@ -57,16 +57,16 @@
     return total
 
 
-def call(body, out_shapes, scalars, arrays, flops=0, scratch=(), space=pltpu.VMEM):
+def call(body, out_shapes, scalars, arrays, flops=0, scratch=()):
     smem = pl.BlockSpec(memory_space=pltpu.SMEM)
     vmem = pl.BlockSpec(memory_space=pltpu.VMEM)
     moved = sum(a.size * a.dtype.itemsize for a in arrays)
     return pl.pallas_call(
         body,
         out_shape=[jax.ShapeDtypeStruct(s, d) for s, d in out_shapes],
-        in_specs=[smem] * len(scalars) + [pl.BlockSpec(memory_space=space)] * len(arrays),
+        in_specs=[smem] * len(scalars) + [vmem] * len(arrays),
         out_specs=[vmem] * len(out_shapes),
-        scratch_shapes=[pltpu.VMEM(shape, F32) if isinstance(shape, tuple) else shape for shape in scratch],
+        scratch_shapes=[pltpu.VMEM(shape, F32) for shape in scratch],
         compiler_params=pltpu.CompilerParams(vmem_limit_bytes=VMEM_LIMIT),
         cost_estimate=pl.CostEstimate(flops=flops, bytes_accessed=moved, transcendentals=0),
         interpret=INTERPRET,
@@ -112,47 +112,8 @@
     return pad_ref[...].T[:width, :rows]
 
 
-def start_kernel(
-    face,
-    place_ref,
-    index_hbm,
-    load_hbm,
-    basis_hbm,
-    map_hbm,
-    inverse_hbm,
-    top_hbm,
-    perm_ref,
-    back_ref,
-    load_out,
-    basis_out,
-    coarse_out,
-    basis2_ref,
-    map2_ref,
-    map_t_ref,
-    e_ref,
-    f_ref,
-    g_ref,
-    h_ref,
-    index_ref,
-    load_ref,
-    basis_ref,
-    map_ref,
-    inverse_ref,
-    top_ref,
-    tall_ref,
-    small_ref,
-    sems,
-):
-    sources = (index_hbm, load_hbm, basis_hbm, map_hbm, inverse_hbm, top_hbm)
-    targets = (index_ref, load_ref, basis_ref, map_ref, inverse_ref, top_ref)
-    copies = [pltpu.make_async_copy(a, b, sems.at[i]) for i, (a, b) in enumerate(zip(sources, targets))]
-    for copy in copies:
-        copy.start()
+def index_kernel(face, columns, place_ref, index_ref, load_ref, perm_ref, back_ref, load_out):
     size = perm_ref.shape[0]
-    coarse = basis_ref.shape[1]
-    for ref in (e_ref, f_ref, g_ref, h_ref):
-        ref[face:] = jnp.zeros((ref.shape[0] - face, ref.shape[1]), F32)
-    copies[0].wait()
     raw = index_ref[...].astype(F32)
     west, east, south, north = [raw[:, k * face : (k + 1) * face] for k in range(4)]
     even_row, even_col = place_ref[0] % 2 == 0, place_ref[1] % 2 == 0
@@ -169,29 +130,50 @@
     lane = lax.broadcasted_iota(jnp.int32, (size, LANES), 1).astype(F32)
     for i in range(0, size, LANES):
         perm_ref[:, i : i + LANES] = jnp.where(tall == lane + float(i), 1.0, 0.0).astype(BF16)
-    perm = perm_ref[...]
-    copies[1].wait()
-    load = permuted(perm, load_ref[...])
-    load_out[...] = load
-    for copy in copies[2:]:
-        copy.wait()
-    basis = permuted(perm, basis_ref[...])
+    down = lax.broadcasted_iota(jnp.int32, (size, size), 0).astype(F32)
+    back_ref[...] = jnp.where(index == down, 1.0, 0.0).astype(BF16)
+    load_out[...] = permuted(perm_ref[...], load_ref[:, :columns])
+
+
+def start_kernel(
+    face,
+    shapes,
+    perm_ref,
+    load_ref,
+    basis_ref,
+    small_in_ref,
+    basis_out,
+    coarse_out,
+    basis2_ref,
+    map_t_ref,
+    inverse_out,
+    top_out,
+    e_ref,
+    f_ref,
+    g_ref,
+    h_ref,
+    tall_ref,
+    small_ref,
+):
+    coarse, total, top, _ = shapes
+    columns = load_ref.shape[1]
+    level = small_in_ref[:, : total + top]
+    inverse, mapped, tops = level[:, :total], level[:, total:], small_in_ref[:, blocks(total + top) * LANES :]
+    basis = permuted(perm_ref[...], basis_ref[:, columns : columns + coarse])
     basis_out[...] = basis
-    product_map = product(stack_split(basis), map_ref[...])
+    product_map = product(stack_split(basis), mapped)
     coarse_out[...] = product_map
-    level = jnp.concatenate([inverse_ref[...], map_ref[...]], axis=1)
+    inverse_out[...] = inverse
+    top_out[...] = tops
     for k, ref in enumerate((e_ref, f_ref, g_ref, h_ref)):
         rows = slice(k * face, (k + 1) * face)
-        ref[:face] = load[rows]
+        ref[:face] = load_ref[rows]
+        ref[face:] = jnp.zeros((ref.shape[0] - face, ref.shape[1]), F32)
         pack_halves(ref, face, product_map[rows] if k < 2 else basis[rows])
-        pack(ref, face + face // 2, top_ref[...] if k < 2 else level)
-    down = lax.broadcasted_iota(jnp.int32, (size, size), 0).astype(F32)
-    back_ref[...] = jnp.where(index == down, 1.0, 0.0).astype(BF16)
+        pack(ref, face + face // 2, tops if k < 2 else level)
     basis2_ref[...] = stack_split(transposed(basis, tall_ref))
-    map_t = transposed(map_ref[...], small_ref)
-    map2_ref[...] = stack_split(map_t)
     map_t_ref[...] = jnp.zeros_like(map_t_ref)
-    map_t_ref[:, :coarse] = map_t
+    map_t_ref[:, :coarse] = transposed(mapped, small_ref)
 
 
 def split_kernel(x_ref, o_ref):
@@ -313,7 +295,7 @@
 
 def residual_kernel(face, link_ref, f_ref, r0, r1, r2, r3, asm_ref, back_ref, out_ref):
     current = asm_ref[...] - (f_ref[...] + received(face, link_ref, (r0, r1, r2, r3)))
-    out_ref[...] = permuted(back_ref[...], current, 3)
+    out_ref[...] = permuted(back_ref[...], current)
 
 
 def swap_pairs(rows, cols, partner):
@@ -388,17 +370,25 @@
     n = (size, columns)
     common = face + face // 2
     payloads = [common + blocks(width) * top] * 2 + [common + blocks(total + top) * coarse] * 2
-    perm, back, load_f, basis_f, coarse_f, basis2, map2, map_t, *sent = call(
-        functools.partial(start_kernel, face),
-        [((size, size), BF16), ((size, size), BF16), (n, F32), ((size, coarse), F32), ((size, top), F32)]
-        + [((2 * coarse, size), BF16), ((2 * top, coarse), BF16), ((top, columns), F32)]
+    wide = jnp.concatenate([loads, basis], axis=1)
+    gap = jnp.zeros((coarse, blocks(total + top) * LANES - total - top), F32)
+    small = jnp.concatenate([inverse_rows, map_block, gap, top_inverse], axis=1)
+    perm, back, load_f = call(
+        functools.partial(index_kernel, face, columns),
+        [((size, size), BF16), ((size, size), BF16), (n, F32)],
+        [place],
+        [iface_index[0], wide],
+        flops=4 * size**2 * columns,
+    )
+    basis_f, coarse_f, basis2, map_t, inverse_rows, top_inverse, *sent = call(
+        functools.partial(start_kernel, face, (coarse, total, top, width)),
+        [((size, coarse), F32), ((size, top), F32), ((2 * coarse, size), BF16), ((top, columns), F32)]
+        + [(inverse_rows.shape, F32), (top_inverse.shape, F32)]
         + [((p, columns), F32) for p in payloads],
-        [place],
-        [iface_index[0], loads, basis, map_block, inverse_rows, top_inverse],
+        [],
+        [perm, load_f, wide, small],
         flops=4 * size**2 * columns,
-        scratch=[pltpu.VMEM((1, size), jnp.int32), n, basis.shape, map_block.shape, inverse_rows.shape]
-        + [top_inverse.shape, (size, LANES), (LANES, LANES), pltpu.SemaphoreType.DMA((6,))],
-        space=pltpu.HBM,
+        scratch=[(size, LANES), (LANES, LANES)],
     )
     schur2 = call(split_kernel, [((2 * size, size), BF16)], [], [schur[0, 0]])[0]
     inverse2 = call(split_kernel, [((2 * size, size), BF16)], [], [local_inverse[0, 0]])[0]
@@ -414,7 +404,8 @@
     doubling = cols & (cols - 1) == 0
     col_order = jnp.arange(cols, dtype=jnp.int32)
     if doubling:
-        col_order = col_order ^ col
+        rest = sum((col_order >> i & 1) for i in range(1, cols.bit_length() - 1))
+        col_order = col ^ col_order ^ (rest & 1)
     col_order = col_order * top
     row_order = jnp.arange(rows, dtype=jnp.int32)
     if row_pairs:
@@ -481,7 +472,7 @@
             tops, bits = [third, more], 2
             known = jnp.concatenate([third, more])
             while bits < cols:
-                more = swap(known, lambda r, c: (r, c ^ bits))
+                more = swap(known, lambda r, c: (r, c ^ bits ^ 1))
                 tops.append(more)
                 known = jnp.concatenate([known, more])
                 bits *= 2

time: 157 us -> 150 us (0.955)
  waiting for transfers between devices: 41.9 us -> 52.9 us
  starting transfers between devices: 65.6 us -> 54.9 us
  local copies, waits for them, and re-layouts: 7.75 us -> 1.74 us
  Pallas kernels: 38.5 us -> 36.7 us
    ppermute x52, waiting for transfers between devices: 41.9 us -> 52.9 us  [swap(): return lax.ppermute(x, ('row', 'col'), swap_pairs(rows, cols, partner))]
    ppermute x52, starting transfers between devices: 65.6 us -> 54.9 us  [swap(): return lax.ppermute(x, ('row', 'col'), swap_pairs(rows, cols, partner))]
    unnamed x19 -> x15, local copies, waits for them, and re-layouts: 7.6 us -> 1.52 us
    pallas_call x26 -> x27, Pallas kernels: 38.5 us -> 36.7 us  [call(): pl.pallas_call(body, out_shape=[jax.ShapeDtypeStruct(s, d) for s, d in ou...]
  transfers between devices with their start and end apart: 52 -> 52, of which waited for: 27 -> 28; matrix products, arithmetic and copies ran while one was open for 0% -> 0% of each run, Pallas kernels for 10% -> 10%
where the time goes in v3:
time: 150 us; the launch traced here: 149 us
  starting transfers between devices  54.9 us (37%)
  waiting for transfers between devices  52.9 us (35%)
  Pallas kernels  36.7 us (24%)
  local copies, waits for them, and re-layouts  1.74 us (1%)
  other arithmetic  1.53 us (1%)
    ppermute x52, starting transfers between devices, swap(): return lax.ppermute(x, ('row', 'col'), swap_pairs(rows, cols, partner))  54.9 us
    ppermute x52, waiting for transfers between devices, swap(): return lax.ppermute(x, ('row', 'col'), swap_pairs(rows, cols, partner))  52.9 us
    pallas_call x27, Pallas kernels, call(): pl.pallas_call(body, out_shape=[jax.ShapeDtypeStruct(s, d) for s, d in ou...  36.7 us
  transfers between devices with their start and end apart: 52, of which 28 were waited for; matrix products, arithmetic and copies ran while one was open for 0% of the time, Pallas kernels for 10%

profile of v3, /device:TPU:1, one launch (start us, length us, event | category | flops | bytes accessed | tf_op | source)
XLA Modules:
  0.0 148.8 jit_solution(5723296994681997016)
XLA Ops:
  0.7 1.1 copy.12
  1.9 1.1 pad_maximum_fusion.load_ref.basis_ref
  3.0 1.3 shard_map.104
  4.5 1.0 shard_map.105
  5.5 2.2 %collective-permute-start.2 = (f32[336,128]{1,0:T(8,128)S(1)}, f32[336,128]{1,0:T(8,128)S(1)}, u32[]{:S(2)}, u32[]{:S(2)}) collective-permute-start(f32[336,128]{1,0:T(8,128)S(1)} %get-tuple-element.49), channel_id=1, source_target_pairs={{0,8},{1,9},{2,10},{3,11},{4,12},{5,13},{6,14},{7,15},{8,0},{9,1},... | collective-permute-start | bytes 516104 | tf_op jit(solution)/shard_map/ppermute | solution.py:344
  7.7 1.0 collective-permute-start.3
  8.6 1.6 %collective-permute-start.1 = (f32[384,128]{1,0:T(8,128)S(1)}, f32[384,128]{1,0:T(8,128)S(1)}, u32[]{:S(2)}, u32[]{:S(2)}) collective-permute-start(f32[384,128]{1,0:T(8,128)S(1)} %get-tuple-element.48), channel_id=1, source_target_pairs={{0,8},{1,2},{2,1},{3,4},{4,3},{5,6},{6,5},{7,15},{8,0},{9,10},{10,... | collective-permute-start | bytes 589832 | tf_op jit(solution)/shard_map/ppermute | solution.py:344
  11.7 3.3 %collective-permute-done.1.r1.f_ref = f32[384,128]{1,0:T(8,128)S(1)} collective-permute-done((f32[384,128]{1,0:T(8,128)S(1)}, f32[384,128]{1,0:T(8,128)S(1)}, u32[]{:S(2)}, u32[]{:S(2)}) %collective-permute-start.1) | collective-permute-done | bytes 196640 | tf_op jit(solution)/shard_map/ppermute | solution.py:344
  15.8 2.9 %collective-permute-start.4 = (f32[96,128]{1,0:T(8,128)S(1)}, f32[96,128]{1,0:T(8,128)S(1)}, u32[]{:S(2)}, u32[]{:S(2)}) collective-permute-start(f32[96,128]{1,0:T(8,128)S(1)} %pad_maximum_fusion.10), channel_id=1, source_target_pairs={{0,16},{1,17},{2,18},{3,19},{4,20},{5,21},{6,22},{7,23},{8,24},{9,... | collective-permute-start | bytes 147464 | tf_op jit(solution)/shard_map/ppermute | solution.py:344
  18.7 2.2 %shard_map.108 = (f32[640,128]{1,0:T(8,128)S(1)}, f32[160,128]{1,0:T(8,128)S(1)}, f32[160,128]{1,0:T(8,128)S(1)}) custom-call(f32[640,128]{1,0:T(8,128)S(1)} %get-tuple-element.52.current_ref.refs_0_.asm_ref, bf16[1280,640]{1,0:T(8,128)(2,1)S(1)} %shard_map.107.inverse_ref, bf16[640,640]{1,0:T(8,128)(2,1)S(1)} %get-tuple-element.46.perm_ref, ...), custom_call_target="tpu_custom_call" | custom-call | flops 838860800 | bytes 3604480 | tf_op jit(solution)/shard_map/pallas_call | solution.py:64
  20.9 2.2 %collective-permute-start.5 = (f32[352,128]{1,0:T(8,128)S(1)}, f32[352,128]{1,0:T(8,128)S(1)}, u32[]{:S(2)}, u32[]{:S(2)}) collective-permute-start(f32[352,128]{1,0:T(8,128)S(1)} %pad_maximum_fusion.1), channel_id=1, source_target_pairs={{0,8},{1,9},{2,10},{3,11},{4,12},{5,13},{6,14},{7,15},{8,0},{9,1},... | collective-permute-start | bytes 540680 | tf_op jit(solution)/shard_map/ppermute | solution.py:344
  23.4 4.7 %collective-permute-done.5.g_ref.refs_2_ = f32[352,128]{1,0:T(8,128)S(1)} collective-permute-done((f32[352,128]{1,0:T(8,128)S(1)}, f32[352,128]{1,0:T(8,128)S(1)}, u32[]{:S(2)}, u32[]{:S(2)}) %collective-permute-start.5) | collective-permute-done | bytes 180256 | tf_op jit(solution)/shard_map/ppermute | solution.py:344
  29.2 2.2 %shard_map.109 = (bf16[1280,192]{1,0:T(8,128)(2,1)S(1)}, bf16[1280,384]{1,0:T(8,128)(2,1)S(1)}) custom-call(s32[4]{0:T(128)S(1)} %select_reduce_fusion.link_ref, f32[640,48]{1,0:T(8,128)S(1)} %get-tuple-element.59.basis_ref, f32[48,192]{1,0:T(8,128)S(1)} %get-tuple-element.60.inverse_ref, f32[640,48]{1,0:T(8,128)S(1)} %get-tuple-element.61.coarse_ref, ...), custom_call_target="tpu_custom_call" | custom-call | bytes 1093632 | tf_op jit(solution)/shard_map/pallas_call | solution.py:64
  31.4 0.9 shard_map.110.y2_ref
  32.3 1.1 collective-permute-start.10
  34.2 1.8 %collective-permute-start.7 = (f32[160,128]{1,0:T(8,128)S(1)}, f32[160,128]{1,0:T(8,128)S(1)}, u32[]{:S(2)}, u32[]{:S(2)}) collective-permute-start(f32[160,128]{1,0:T(8,128)S(1)} %get-tuple-element.111), channel_id=1, source_target_pairs={{0,1},{1,0},{2,3},{3,2},{4,5},{5,4},{6,7},{7,6},{8,9},{9,8},{10,11... | collective-permute-start | bytes 245768 | tf_op jit(solution)/shard_map/ppermute | solution.py:344
  36.0 2.0 %collective-permute-start.11 = (f32[192,128]{1,0:T(8,128)S(1)}, f32[192,128]{1,0:T(8,128)S(1)}, u32[]{:S(2)}, u32[]{:S(2)}) collective-permute-start(f32[192,128]{1,0:T(8,128)S(1)} %pad_maximum_fusion.6), channel_id=1, source_target_pairs={{0,5},{1,4},{2,7},{3,6},{4,1},{5,0},{6,3},{7,2},{8,13},{9,12},{10,... | collective-permute-start | bytes 294920 | tf_op jit(solution)/shard_map/ppermute | solution.py:344
  38.1 3.5 %collective-permute-done.11.refs_3_ = f32[192,128]{1,0:T(8,128)S(1)} collective-permute-done((f32[192,128]{1,0:T(8,128)S(1)}, f32[192,128]{1,0:T(8,128)S(1)}, u32[]{:S(2)}, u32[]{:S(2)}) %collective-permute-start.11) | collective-permute-done | bytes 98336 | tf_op jit(solution)/shard_map/ppermute | solution.py:344
  41.5 3.4 %shard_map.114 = (f32[640,128]{1,0:T(8,128)S(1)}, f32[640,128]{1,0:T(8,128)S(1)}) custom-call(s32[4]{0:T(128)S(1)} %select_reduce_fusion.link_ref, s32[8]{0:T(128)S(1)} %fusion.9.order_ref, f32[640,128]{1,0:T(8,128)S(1)} %shard_map.110.y2_ref, f32[160,128]{1,0:T(8,128)S(1)} %collective-permute-done.7.e_ref, f32[160,128]{1,0:T(8,128)S(1)} %collective-permute-done.8.f_ref, ...), custom_call_target="tpu_custom_call" | custom-call | flops 838860800 | bytes 4947968 | tf_op jit(solution)/shard_map/pallas_call | solution.py:64
  45.5 1.3 collective-permute-start.14
  46.8 1.0 collective-permute-start.13
  47.9 1.5 %collective-permute-done.14.r2 = f32[160,128]{1,0:T(8,128)S(1)} collective-permute-done((f32[160,128]{1,0:T(8,128)S(1)}, f32[160,128]{1,0:T(8,128)S(1)}, u32[]{:S(2)}, u32[]{:S(2)}) %collective-permute-start.14) | collective-permute-done | bytes 81952 | tf_op jit(solution)/shard_map/ppermute | solution.py:344
  49.4 2.2 %collective-permute-done.13.r1 = f32[160,128]{1,0:T(8,128)S(1)} collective-permute-done((f32[160,128]{1,0:T(8,128)S(1)}, f32[160,128]{1,0:T(8,128)S(1)}, u32[]{:S(2)}, u32[]{:S(2)}) %collective-permute-start.13) | collective-permute-done | bytes 81952 | tf_op jit(solution)/shard_map/ppermute | solution.py:344
  52.4 1.3 collective-permute-start.16
  53.7 2.2 %shard_map.116 = (f32[640,128]{1,0:T(8,128)S(1)}, f32[160,128]{1,0:T(8,128)S(1)}, f32[160,128]{1,0:T(8,128)S(1)}) custom-call(f32[640,128]{1,0:T(8,128)S(1)} %get-tuple-element.66.current_ref, bf16[1280,640]{1,0:T(8,128)(2,1)S(1)} %shard_map.107.inverse_ref, bf16[640,640]{1,0:T(8,128)(2,1)S(1)} %get-tuple-element.46.perm_ref, ...), custom_call_target="tpu_custom_call" | custom-call | flops 838860800 | bytes 3604480 | tf_op jit(solution)/shard_map/pallas_call | solution.py:64
  56.2 1.1 collective-permute-start.17
  57.3 2.8 %collective-permute-done.17.g_ref.refs_2_ = f32[256,128]{1,0:T(8,128)S(1)} collective-permute-done((f32[256,128]{1,0:T(8,128)S(1)}, f32[256,128]{1,0:T(8,128)S(1)}, u32[]{:S(2)}, u32[]{:S(2)}) %collective-permute-start.17) | collective-permute-done | bytes 131104 | tf_op jit(solution)/shard_map/ppermute | solution.py:344
  60.3 2.6 %collective-permute-start.21 = (f32[48,128]{1,0:T(8,128)S(1)}, f32[48,128]{1,0:T(8,128)S(1)}, u32[]{:S(2)}, u32[]{:S(2)}) collective-permute-start(f32[48,128]{1,0:T(8,128)S(1)} %shard_map.118.refs_1_), channel_id=1, source_target_pairs={{0,1},{1,0},{2,3},{3,2},{4,5},{5,4},{6,7},{7,6},{8,9},{9,8},{10,11... | collective-permute-start | bytes 73736 | tf_op jit(solution)/shard_map/ppermute | solution.py:344
  63.8 1.1 collective-permute-start.22
  65.8 1.7 %collective-permute-done.22.refs_3_ = f32[96,128]{1,0:T(8,128)S(1)} collective-permute-done((f32[96,128]{1,0:T(8,128)S(1)}, f32[96,128]{1,0:T(8,128)S(1)}, u32[]{:S(2)}, u32[]{:S(2)}) %collective-permute-start.22) | collective-permute-done | bytes 49184 | tf_op jit(solution)/shard_map/ppermute | solution.py:344
  67.5 1.8 %collective-permute-start.23 = (f32[192,128]{1,0:T(8,128)S(1)}, f32[192,128]{1,0:T(8,128)S(1)}, u32[]{:S(2)}, u32[]{:S(2)}) collective-permute-start(f32[192,128]{1,0:T(8,128)S(1)} %pad_maximum_fusion.7), channel_id=1, source_target_pairs={{0,5},{1,4},{2,7},{3,6},{4,1},{5,0},{6,3},{7,2},{8,13},{9,12},{10,... | collective-permute-start | bytes 294920 | tf_op jit(solution)/shard_map/ppermute | solution.py:344
  69.4 0.9 collective-permute-start.19
  70.3 3.2 %collective-permute-done.20.f_ref = f32[160,128]{1,0:T(8,128)S(1)} collective-permute-done((f32[160,128]{1,0:T(8,128)S(1)}, f32[160,128]{1,0:T(8,128)S(1)}, u32[]{:S(2)}, u32[]{:S(2)}) %collective-permute-start.20) | collective-permute-done | bytes 81952 | tf_op jit(solution)/shard_map/ppermute | solution.py:344
  73.6 3.4 %shard_map.119 = (f32[640,128]{1,0:T(8,128)S(1)}, f32[640,128]{1,0:T(8,128)S(1)}) custom-call(s32[4]{0:T(128)S(1)} %select_reduce_fusion.link_ref, s32[8]{0:T(128)S(1)} %fusion.9.order_ref, f32[640,128]{1,0:T(8,128)S(1)} %shard_map.117.y2_ref, f32[160,128]{1,0:T(8,128)S(1)} %collective-permute-done.19.e_ref, f32[160,128]{1,0:T(8,128)S(1)} %collective-permute-done.20.f_ref, ...), custom_call_target="tpu_custom_call" | custom-call | flops 838860800 | bytes 5275648 | tf_op jit(solution)/shard_map/pallas_call | solution.py:64
  77.5 1.8 %collective-permute-start.26 = (f32[160,128]{1,0:T(8,128)S(1)}, f32[160,128]{1,0:T(8,128)S(1)}, u32[]{:S(2)}, u32[]{:S(2)}) collective-permute-start(f32[160,128]{1,0:T(8,128)S(1)} %get-tuple-element.101), channel_id=1, source_target_pairs={{0,8},{1,9},{2,10},{3,11},{4,12},{5,13},{6,14},{7,15},{8,0},{9,1},... | collective-permute-start | bytes 245768 | tf_op jit(solution)/shard_map/ppermute | solution.py:344
  79.9 1.8 %collective-permute-done.26.r2 = f32[160,128]{1,0:T(8,128)S(1)} collective-permute-done((f32[160,128]{1,0:T(8,128)S(1)}, f32[160,128]{1,0:T(8,128)S(1)}, u32[]{:S(2)}, u32[]{:S(2)}) %collective-permute-start.26) | collective-permute-done | bytes 81952 | tf_op jit(solution)/shard_map/ppermute | solution.py:344
  81.8 1.7 %collective-permute-done.25.r1 = f32[160,128]{1,0:T(8,128)S(1)} collective-permute-done((f32[160,128]{1,0:T(8,128)S(1)}, f32[160,128]{1,0:T(8,128)S(1)}, u32[]{:S(2)}, u32[]{:S(2)}) %collective-permute-start.25) | collective-permute-done | bytes 81952 | tf_op jit(solution)/shard_map/ppermute | solution.py:344
  84.2 1.1 collective-permute-start.28
  85.3 2.4 %shard_map.121 = (f32[640,128]{1,0:T(8,128)S(1)}, f32[160,128]{1,0:T(8,128)S(1)}, f32[160,128]{1,0:T(8,128)S(1)}) custom-call(f32[640,128]{1,0:T(8,128)S(1)} %get-tuple-element.73.current_ref, bf16[1280,640]{1,0:T(8,128)(2,1)S(1)} %shard_map.107.inverse_ref, bf16[640,640]{1,0:T(8,128)(2,1)S(1)} %get-tuple-element.46.perm_ref, ...), custom_call_target="tpu_custom_call" | custom-call | flops 838860800 | bytes 3604480 | tf_op jit(solution)/shard_map/pallas_call | solution.py:64
  88.4 3.5 %collective-permute-done.29.g_ref.refs_2_ = f32[256,128]{1,0:T(8,128)S(1)} collective-permute-done((f32[256,128]{1,0:T(8,128)S(1)}, f32[256,128]{1,0:T(8,128)S(1)}, u32[]{:S(2)}, u32[]{:S(2)}) %collective-permute-start.29) | collective-permute-done | bytes 131104 | tf_op jit(solution)/shard_map/ppermute | solution.py:344
  92.0 3.2 %collective-permute-start.33 = (f32[48,128]{1,0:T(8,128)S(1)}, f32[48,128]{1,0:T(8,128)S(1)}, u32[]{:S(2)}, u32[]{:S(2)}) collective-permute-start(f32[48,128]{1,0:T(8,128)S(1)} %shard_map.123.refs_1_), channel_id=1, source_target_pairs={{0,1},{1,0},{2,3},{3,2},{4,5},{5,4},{6,7},{7,6},{8,9},{9,8},{10,11... | collective-permute-start | bytes 73736 | tf_op jit(solution)/shard_map/ppermute | solution.py:344
  96.1 1.0 collective-permute-start.34
  97.1 0.9 shard_map.122.y2_ref
  98.0 1.8 %collective-permute-done.34.refs_3_ = f32[96,128]{1,0:T(8,128)S(1)} collective-permute-done((f32[96,128]{1,0:T(8,128)S(1)}, f32[96,128]{1,0:T(8,128)S(1)}, u32[]{:S(2)}, u32[]{:S(2)}) %collective-permute-start.34) | collective-permute-done | bytes 49184 | tf_op jit(solution)/shard_map/ppermute | solution.py:344
  99.8 2.0 %collective-permute-start.35 = (f32[192,128]{1,0:T(8,128)S(1)}, f32[192,128]{1,0:T(8,128)S(1)}, u32[]{:S(2)}, u32[]{:S(2)}) collective-permute-start(f32[192,128]{1,0:T(8,128)S(1)} %pad_maximum_fusion.8), channel_id=1, source_target_pairs={{0,5},{1,4},{2,7},{3,6},{4,1},{5,0},{6,3},{7,2},{8,13},{9,12},{10,... | collective-permute-start | bytes 294920 | tf_op jit(solution)/shard_map/ppermute | solution.py:344
  102.5 3.7 %collective-permute-done.32.f_ref = f32[160,128]{1,0:T(8,128)S(1)} collective-permute-done((f32[160,128]{1,0:T(8,128)S(1)}, f32[160,128]{1,0:T(8,128)S(1)}, u32[]{:S(2)}, u32[]{:S(2)}) %collective-permute-start.32) | collective-permute-done | bytes 81952 | tf_op jit(solution)/shard_map/ppermute | solution.py:344
  106.1 3.4 %shard_map.124 = (f32[640,128]{1,0:T(8,128)S(1)}, f32[640,128]{1,0:T(8,128)S(1)}) custom-call(s32[4]{0:T(128)S(1)} %select_reduce_fusion.link_ref, s32[8]{0:T(128)S(1)} %fusion.9.order_ref, f32[640,128]{1,0:T(8,128)S(1)} %shard_map.122.y2_ref, f32[160,128]{1,0:T(8,128)S(1)} %collective-permute-done.31.e_ref, f32[160,128]{1,0:T(8,128)S(1)} %collective-permute-done.32.f_ref, ...), custom_call_target="tpu_custom_call" | custom-call | flops 838860800 | bytes 5275648 | tf_op jit(solution)/shard_map/pallas_call | solution.py:64
  110.0 1.0 collective-permute-start.38
  111.0 1.7 %collective-permute-start.37 = (f32[160,128]{1,0:T(8,128)S(1)}, f32[160,128]{1,0:T(8,128)S(1)}, u32[]{:S(2)}, u32[]{:S(2)}) collective-permute-start(f32[160,128]{1,0:T(8,128)S(1)} %get-tuple-element.96), channel_id=1, source_target_pairs={{0,8},{1,2},{2,1},{3,4},{4,3},{5,6},{6,5},{7,15},{8,0},{9,10},{10,... | collective-permute-start | bytes 245768 | tf_op jit(solution)/shard_map/ppermute | solution.py:344
  112.7 1.2 collective-permute-done.38.r2
  113.9 1.3 collective-permute-done.37.r1
  116.0 1.3 collective-permute-start.40
  117.3 2.2 %shard_map.126 = (f32[640,128]{1,0:T(8,128)S(1)}, f32[160,128]{1,0:T(8,128)S(1)}, f32[160,128]{1,0:T(8,128)S(1)}) custom-call(f32[640,128]{1,0:T(8,128)S(1)} %get-tuple-element.80.current_ref, bf16[1280,640]{1,0:T(8,128)(2,1)S(1)} %shard_map.107.inverse_ref, bf16[640,640]{1,0:T(8,128)(2,1)S(1)} %get-tuple-element.46.perm_ref, ...), custom_call_target="tpu_custom_call" | custom-call | flops 838860800 | bytes 3604480 | tf_op jit(solution)/shard_map/pallas_call | solution.py:64
  120.4 3.2 %collective-permute-done.41.g_ref.refs_2_ = f32[256,128]{1,0:T(8,128)S(1)} collective-permute-done((f32[256,128]{1,0:T(8,128)S(1)}, f32[256,128]{1,0:T(8,128)S(1)}, u32[]{:S(2)}, u32[]{:S(2)}) %collective-permute-start.41) | collective-permute-done | bytes 131104 | tf_op jit(solution)/shard_map/ppermute | solution.py:344
  123.7 3.3 %collective-permute-start.45 = (f32[48,128]{1,0:T(8,128)S(1)}, f32[48,128]{1,0:T(8,128)S(1)}, u32[]{:S(2)}, u32[]{:S(2)}) collective-permute-start(f32[48,128]{1,0:T(8,128)S(1)} %shard_map.128.refs_1_), channel_id=1, source_target_pairs={{0,1},{1,0},{2,3},{3,2},{4,5},{5,4},{6,7},{7,6},{8,9},{9,8},{10,11... | collective-permute-start | bytes 73736 | tf_op jit(solution)/shard_map/ppermute | solution.py:344
  127.9 1.1 collective-permute-start.46
  129.8 1.8 %collective-permute-done.46.refs_3_ = f32[96,128]{1,0:T(8,128)S(1)} collective-permute-done((f32[96,128]{1,0:T(8,128)S(1)}, f32[96,128]{1,0:T(8,128)S(1)}, u32[]{:S(2)}, u32[]{:S(2)}) %collective-permute-start.46) | collective-permute-done | bytes 49184 | tf_op jit(solution)/shard_map/ppermute | solution.py:344
  131.6 2.4 %collective-permute-start.47 = (f32[192,128]{1,0:T(8,128)S(1)}, f32[192,128]{1,0:T(8,128)S(1)}, u32[]{:S(2)}, u32[]{:S(2)}) collective-permute-start(f32[192,128]{1,0:T(8,128)S(1)} %pad_maximum_fusion.9), channel_id=1, source_target_pairs={{0,5},{1,4},{2,7},{3,6},{4,1},{5,0},{6,3},{7,2},{8,13},{9,12},{10,... | collective-permute-start | bytes 294920 | tf_op jit(solution)/shard_map/ppermute | solution.py:344
  134.7 3.6 %collective-permute-done.44.f_ref = f32[160,128]{1,0:T(8,128)S(1)} collective-permute-done((f32[160,128]{1,0:T(8,128)S(1)}, f32[160,128]{1,0:T(8,128)S(1)}, u32[]{:S(2)}, u32[]{:S(2)}) %collective-permute-start.44) | collective-permute-done | bytes 81952 | tf_op jit(solution)/shard_map/ppermute | solution.py:344
  138.3 3.4 %shard_map.129 = (f32[640,128]{1,0:T(8,128)}, f32[640,128]{1,0:T(8,128)S(1)}) custom-call(s32[4]{0:T(128)S(1)} %select_reduce_fusion.link_ref, s32[8]{0:T(128)S(1)} %fusion.9.order_ref, f32[640,128]{1,0:T(8,128)S(1)} %shard_map.127.y2_ref, f32[160,128]{1,0:T(8,128)S(1)} %collective-permute-done.43.e_ref, f32[160,128]{1,0:T(8,128)S(1)} %collective-permute-done.44.f_ref, ...), custom_call_target="tpu_custom_call" | custom-call | flops 838860800 | bytes 5275648 | tf_op jit(solution)/shard_map/pallas_call | solution.py:64
  142.9 1.2 collective-permute-start.49
  144.3 1.8 %collective-permute-done.50.r2 = f32[160,128]{1,0:T(8,128)S(1)} collective-permute-done((f32[160,128]{1,0:T(8,128)S(1)}, f32[160,128]{1,0:T(8,128)S(1)}, u32[]{:S(2)}, u32[]{:S(2)}) %collective-permute-start.50) | collective-permute-done | bytes 81952 | tf_op jit(solution)/shard_map/ppermute | solution.py:344
  146.1 1.0 collective-permute-done.49.r1
  147.1 1.7 %shard_map.130 = f32[640,128]{1,0:T(8,128)} custom-call(s32[4]{0:T(128)S(1)} %select_reduce_fusion.link_ref, f32[640,128]{1,0:T(8,128)S(1)} %get-tuple-element.87.f_ref, f32[160,128]{1,0:T(8,128)S(1)} %collective-permute-done.48.r0, f32[160,128]{1,0:T(8,128)S(1)} %collective-permute-done.49.r1, f32[160,128]{1,0:T(8,128)S(1)} %collective-permute-done.50.r2, ...), custom_call_target="tpu_custom_call" | custom-call | bytes 1802240 | tf_op jit(solution)/shard_map/pallas_call | solution.py:64
  (112 shorter events, 18.9 us)
Async XLA Ops:
  0.6 2.4 %copy-start.2 = (s32[1,1,640]{2,1,0:T(1,128)S(1)}, s32[1,1,640]{2,1,0:T(1,128)}, u32[]{:S(2)}) copy-start(s32[1,1,640]{2,1,0:T(1,128)} %param.12) | copy-start | bytes 7684
  0.6 3.7 %copy-start.3 = (f32[48,384]{1,0:T(8,128)S(1)}, f32[48,384]{1,0:T(8,128)}, u32[]{:S(2)}) copy-start(f32[48,384]{1,0:T(8,128)} %param.17) | copy-start | bytes 221188
  0.7 3.7 %copy-start.5 = (f32[1,48,48]{2,1,0:T(8,128)S(1)}, f32[1,48,48]{2,1,0:T(8,128)}, u32[]{:S(2)}) copy-start(f32[1,48,48]{2,1,0:T(8,128)} %param.16) | copy-start | bytes 27652
  0.7 3.7 %copy-start.4 = (f32[1,48,192]{2,1,0:T(8,128)S(1)}, f32[1,48,192]{2,1,0:T(8,128)}, u32[]{:S(2)}) copy-start(f32[1,48,192]{2,1,0:T(8,128)} %param.15) | copy-start | bytes 110596
  3.0 7.2 %copy-start = (f32[1,1,640,640]{3,2,1,0:T(8,128)S(1)}, f32[1,1,640,640]{3,2,1,0:T(8,128)}, u32[]{:S(2)}) copy-start(f32[1,1,640,640]{3,2,1,0:T(8,128)} %param.11) | copy-start | bytes 4915204
  5.5 6.2 %collective-permute-start.2 = (f32[336,128]{1,0:T(8,128)S(1)}, f32[336,128]{1,0:T(8,128)S(1)}, u32[]{:S(2)}, u32[]{:S(2)}) collective-permute-start(f32[336,128]{1,0:T(8,128)S(1)} %get-tuple-element.49), channel_id=1, source_target_pairs={{0,8},{1,9},{2,10},{3,11},{4,12},{5,13},{6,14},{7,15},{8,0},{9,1},... | collective-permute-start | bytes 516104 | tf_op jit(solution)/shard_map/ppermute | solution.py:344
  7.7 4.1 %collective-permute-start.3 = (f32[336,128]{1,0:T(8,128)S(1)}, f32[336,128]{1,0:T(8,128)S(1)}, u32[]{:S(2)}, u32[]{:S(2)}) collective-permute-start(f32[336,128]{1,0:T(8,128)S(1)} %get-tuple-element.50), channel_id=1, source_target_pairs={{0,1},{1,0},{2,3},{3,2},{4,5},{5,4},{6,7},{7,6},{8,16},{9,17},{10,... | collective-permute-start | bytes 516104 | tf_op jit(solution)/shard_map/ppermute | solution.py:344
  8.6 3.1 %collective-permute-start = (f32[384,128]{1,0:T(8,128)S(1)}, f32[384,128]{1,0:T(8,128)S(1)}, u32[]{:S(2)}, u32[]{:S(2)}) collective-permute-start(f32[384,128]{1,0:T(8,128)S(1)} %get-tuple-element.47), channel_id=1, source_target_pairs={{0,1},{1,0},{2,3},{3,2},{4,5},{5,4},{6,7},{7,6},{8,9},{9,8},{10,11... | collective-permute-start | bytes 589832 | tf_op jit(solution)/shard_map/ppermute | solution.py:344
  8.6 6.4 %collective-permute-start.1 = (f32[384,128]{1,0:T(8,128)S(1)}, f32[384,128]{1,0:T(8,128)S(1)}, u32[]{:S(2)}, u32[]{:S(2)}) collective-permute-start(f32[384,128]{1,0:T(8,128)S(1)} %get-tuple-element.48), channel_id=1, source_target_pairs={{0,8},{1,2},{2,1},{3,4},{4,3},{5,6},{6,5},{7,15},{8,0},{9,10},{10,... | collective-permute-start | bytes 589832 | tf_op jit(solution)/shard_map/ppermute | solution.py:344
  10.2 0.7 copy-start.6
  15.8 5.1 %collective-permute-start.4 = (f32[96,128]{1,0:T(8,128)S(1)}, f32[96,128]{1,0:T(8,128)S(1)}, u32[]{:S(2)}, u32[]{:S(2)}) collective-permute-start(f32[96,128]{1,0:T(8,128)S(1)} %pad_maximum_fusion.10), channel_id=1, source_target_pairs={{0,16},{1,17},{2,18},{3,19},{4,20},{5,21},{6,22},{7,23},{8,24},{9,... | collective-permute-start | bytes 147464 | tf_op jit(solution)/shard_map/ppermute | solution.py:344
  18.7 10.3 %copy-start.1 = (f32[1,1,640,640]{3,2,1,0:T(8,128)S(1)}, f32[1,1,640,640]{3,2,1,0:T(8,128)}, u32[]{:S(2)}) copy-start(f32[1,1,640,640]{3,2,1,0:T(8,128)} %param.10) | copy-start | bytes 4915204
  20.9 7.1 %collective-permute-start.5 = (f32[352,128]{1,0:T(8,128)S(1)}, f32[352,128]{1,0:T(8,128)S(1)}, u32[]{:S(2)}, u32[]{:S(2)}) collective-permute-start(f32[352,128]{1,0:T(8,128)S(1)} %pad_maximum_fusion.1), channel_id=1, source_target_pairs={{0,8},{1,9},{2,10},{3,11},{4,12},{5,13},{6,14},{7,15},{8,0},{9,1},... | collective-permute-start | bytes 540680 | tf_op jit(solution)/shard_map/ppermute | solution.py:344
  23.2 8.2 %collective-permute-start.6 = (f32[160,128]{1,0:T(8,128)S(1)}, f32[160,128]{1,0:T(8,128)S(1)}, u32[]{:S(2)}, u32[]{:S(2)}) collective-permute-start(f32[160,128]{1,0:T(8,128)S(1)} %get-tuple-element.58), channel_id=1, source_target_pairs={{0,1},{1,0},{2,3},{3,2},{4,5},{5,4},{6,7},{7,6},{8,16},{9,17},{10,... | collective-permute-start | bytes 245768 | tf_op jit(solution)/shard_map/ppermute | solution.py:344
  28.3 4.0 %collective-permute-start.9 = (f32[48,128]{1,0:T(8,128)S(1)}, f32[48,128]{1,0:T(8,128)S(1)}, u32[]{:S(2)}, u32[]{:S(2)}) collective-permute-start(f32[48,128]{1,0:T(8,128)S(1)} %shard_map.113.refs_0_), channel_id=1, source_target_pairs={{0,1},{1,0},{2,3},{3,2},{4,5},{5,4},{6,7},{7,6},{8,9},{9,8},{10,11... | collective-permute-start | bytes 73736 | tf_op jit(solution)/shard_map/ppermute | solution.py:344
  32.3 3.7 %collective-permute-start.10 = (f32[96,128]{1,0:T(8,128)S(1)}, f32[96,128]{1,0:T(8,128)S(1)}, u32[]{:S(2)}, u32[]{:S(2)}) collective-permute-start(f32[96,128]{1,0:T(8,128)S(1)} %pad_maximum_fusion.11), channel_id=1, source_target_pairs={{0,3},{1,2},{2,1},{3,0},{4,7},{5,6},{6,5},{7,4},{8,11},{9,10},{10,... | collective-permute-start | bytes 147464 | tf_op jit(solution)/shard_map/ppermute | solution.py:344
  33.4 4.7 %collective-permute-start.8 = (f32[160,128]{1,0:T(8,128)S(1)}, f32[160,128]{1,0:T(8,128)S(1)}, u32[]{:S(2)}, u32[]{:S(2)}) collective-permute-start(f32[160,128]{1,0:T(8,128)S(1)} %get-tuple-element.110), channel_id=1, source_target_pairs={{0,8},{1,2},{2,1},{3,4},{4,3},{5,6},{6,5},{7,15},{8,0},{9,10},{10,... | collective-permute-start | bytes 245768 | tf_op jit(solution)/shard_map/ppermute | solution.py:344
  34.2 3.8 %collective-permute-start.7 = (f32[160,128]{1,0:T(8,128)S(1)}, f32[160,128]{1,0:T(8,128)S(1)}, u32[]{:S(2)}, u32[]{:S(2)}) collective-permute-start(f32[160,128]{1,0:T(8,128)S(1)} %get-tuple-element.111), channel_id=1, source_target_pairs={{0,1},{1,0},{2,3},{3,2},{4,5},{5,4},{6,7},{7,6},{8,9},{9,8},{10,11... | collective-permute-start | bytes 245768 | tf_op jit(solution)/shard_map/ppermute | solution.py:344
  36.0 5.5 %collective-permute-start.11 = (f32[192,128]{1,0:T(8,128)S(1)}, f32[192,128]{1,0:T(8,128)S(1)}, u32[]{:S(2)}, u32[]{:S(2)}) collective-permute-start(f32[192,128]{1,0:T(8,128)S(1)} %pad_maximum_fusion.6), channel_id=1, source_target_pairs={{0,5},{1,4},{2,7},{3,6},{4,1},{5,0},{6,3},{7,2},{8,13},{9,12},{10,... | collective-permute-start | bytes 294920 | tf_op jit(solution)/shard_map/ppermute | solution.py:344
  44.9 2.9 %collective-permute-start.15 = (f32[160,128]{1,0:T(8,128)S(1)}, f32[160,128]{1,0:T(8,128)S(1)}, u32[]{:S(2)}, u32[]{:S(2)}) collective-permute-start(f32[160,128]{1,0:T(8,128)S(1)} %get-tuple-element.106), channel_id=1, source_target_pairs={{0,1},{1,0},{2,3},{3,2},{4,5},{5,4},{6,7},{7,6},{8,16},{9,17},{10,... | collective-permute-start | bytes 245768 | tf_op jit(solution)/shard_map/ppermute | solution.py:344
  45.5 3.9 %collective-permute-start.14 = (f32[160,128]{1,0:T(8,128)S(1)}, f32[160,128]{1,0:T(8,128)S(1)}, u32[]{:S(2)}, u32[]{:S(2)}) collective-permute-start(f32[160,128]{1,0:T(8,128)S(1)} %get-tuple-element.107), channel_id=1, source_target_pairs={{0,8},{1,9},{2,10},{3,11},{4,12},{5,13},{6,14},{7,15},{8,0},{9,1},... | collective-permute-start | bytes 245768 | tf_op jit(solution)/shard_map/ppermute | solution.py:344
  46.8 4.8 %collective-permute-start.13 = (f32[160,128]{1,0:T(8,128)S(1)}, f32[160,128]{1,0:T(8,128)S(1)}, u32[]{:S(2)}, u32[]{:S(2)}) collective-permute-start(f32[160,128]{1,0:T(8,128)S(1)} %get-tuple-element.108), channel_id=1, source_target_pairs={{0,8},{1,2},{2,1},{3,4},{4,3},{5,6},{6,5},{7,15},{8,0},{9,10},{10,... | collective-permute-start | bytes 245768 | tf_op jit(solution)/shard_map/ppermute | solution.py:344
  47.9 3.8 %collective-permute-start.12 = (f32[160,128]{1,0:T(8,128)S(1)}, f32[160,128]{1,0:T(8,128)S(1)}, u32[]{:S(2)}, u32[]{:S(2)}) collective-permute-start(f32[160,128]{1,0:T(8,128)S(1)} %get-tuple-element.109), channel_id=1, source_target_pairs={{0,1},{1,0},{2,3},{3,2},{4,5},{5,4},{6,7},{7,6},{8,9},{9,8},{10,11... | collective-permute-start | bytes 245768 | tf_op jit(solution)/shard_map/ppermute | solution.py:344
  52.4 3.8 %collective-permute-start.16 = (f32[48,128]{1,0:T(8,128)S(1)}, f32[48,128]{1,0:T(8,128)S(1)}, u32[]{:S(2)}, u32[]{:S(2)}) collective-permute-start(f32[48,128]{1,0:T(8,128)S(1)} %get-tuple-element.69.refs_0_), channel_id=1, source_target_pairs={{0,16},{1,17},{2,18},{3,19},{4,20},{5,21},{6,22},{7,23},{8,24},{9,... | collective-permute-start | bytes 73736 | tf_op jit(solution)/shard_map/ppermute | solution.py:344
  56.2 3.9 %collective-permute-start.17 = (f32[256,128]{1,0:T(8,128)S(1)}, f32[256,128]{1,0:T(8,128)S(1)}, u32[]{:S(2)}, u32[]{:S(2)}) collective-permute-start(f32[256,128]{1,0:T(8,128)S(1)} %pad_maximum_fusion.2), channel_id=1, source_target_pairs={{0,8},{1,9},{2,10},{3,11},{4,12},{5,13},{6,14},{7,15},{8,0},{9,1},... | collective-permute-start | bytes 393224 | tf_op jit(solution)/shard_map/ppermute | solution.py:344
  60.3 3.5 %collective-permute-start.21 = (f32[48,128]{1,0:T(8,128)S(1)}, f32[48,128]{1,0:T(8,128)S(1)}, u32[]{:S(2)}, u32[]{:S(2)}) collective-permute-start(f32[48,128]{1,0:T(8,128)S(1)} %shard_map.118.refs_1_), channel_id=1, source_target_pairs={{0,1},{1,0},{2,3},{3,2},{4,5},{5,4},{6,7},{7,6},{8,9},{9,8},{10,11... | collective-permute-start | bytes 73736 | tf_op jit(solution)/shard_map/ppermute | solution.py:344
  62.9 2.0 %collective-permute-start.18 = (f32[160,128]{1,0:T(8,128)S(1)}, f32[160,128]{1,0:T(8,128)S(1)}, u32[]{:S(2)}, u32[]{:S(2)}) collective-permute-start(f32[160,128]{1,0:T(8,128)S(1)} %get-tuple-element.70), channel_id=1, source_target_pairs={{0,1},{1,0},{2,3},{3,2},{4,5},{5,4},{6,7},{7,6},{8,16},{9,17},{10,... | collective-permute-start | bytes 245768 | tf_op jit(solution)/shard_map/ppermute | solution.py:344
  63.8 3.7 %collective-permute-start.22 = (f32[96,128]{1,0:T(8,128)S(1)}, f32[96,128]{1,0:T(8,128)S(1)}, u32[]{:S(2)}, u32[]{:S(2)}) collective-permute-start(f32[96,128]{1,0:T(8,128)S(1)} %pad_maximum_fusion.12), channel_id=1, source_target_pairs={{0,3},{1,2},{2,1},{3,0},{4,7},{5,6},{6,5},{7,4},{8,11},{9,10},{10,... | collective-permute-start | bytes 147464 | tf_op jit(solution)/shard_map/ppermute | solution.py:344
  67.5 6.1 %collective-permute-start.23 = (f32[192,128]{1,0:T(8,128)S(1)}, f32[192,128]{1,0:T(8,128)S(1)}, u32[]{:S(2)}, u32[]{:S(2)}) collective-permute-start(f32[192,128]{1,0:T(8,128)S(1)} %pad_maximum_fusion.7), channel_id=1, source_target_pairs={{0,5},{1,4},{2,7},{3,6},{4,1},{5,0},{6,3},{7,2},{8,13},{9,12},{10,... | collective-permute-start | bytes 294920 | tf_op jit(solution)/shard_map/ppermute | solution.py:344
  69.3 4.3 %collective-permute-start.20 = (f32[160,128]{1,0:T(8,128)S(1)}, f32[160,128]{1,0:T(8,128)S(1)}, u32[]{:S(2)}, u32[]{:S(2)}) collective-permute-start(f32[160,128]{1,0:T(8,128)S(1)} %get-tuple-element.104), channel_id=1, source_target_pairs={{0,8},{1,2},{2,1},{3,4},{4,3},{5,6},{6,5},{7,15},{8,0},{9,10},{10,... | collective-permute-start | bytes 245768 | tf_op jit(solution)/shard_map/ppermute | solution.py:344
  69.4 4.2 %collective-permute-start.19 = (f32[160,128]{1,0:T(8,128)S(1)}, f32[160,128]{1,0:T(8,128)S(1)}, u32[]{:S(2)}, u32[]{:S(2)}) collective-permute-start(f32[160,128]{1,0:T(8,128)S(1)} %get-tuple-element.105), channel_id=1, source_target_pairs={{0,1},{1,0},{2,3},{3,2},{4,5},{5,4},{6,7},{7,6},{8,9},{9,8},{10,11... | collective-permute-start | bytes 245768 | tf_op jit(solution)/shard_map/ppermute | solution.py:344
  77.0 2.9 %collective-permute-start.27 = (f32[160,128]{1,0:T(8,128)S(1)}, f32[160,128]{1,0:T(8,128)S(1)}, u32[]{:S(2)}, u32[]{:S(2)}) collective-permute-start(f32[160,128]{1,0:T(8,128)S(1)} %get-tuple-element.100), channel_id=1, source_target_pairs={{0,1},{1,0},{2,3},{3,2},{4,5},{5,4},{6,7},{7,6},{8,16},{9,17},{10,... | collective-permute-start | bytes 245768 | tf_op jit(solution)/shard_map/ppermute | solution.py:344
  77.5 4.3 %collective-permute-start.26 = (f32[160,128]{1,0:T(8,128)S(1)}, f32[160,128]{1,0:T(8,128)S(1)}, u32[]{:S(2)}, u32[]{:S(2)}) collective-permute-start(f32[160,128]{1,0:T(8,128)S(1)} %get-tuple-element.101), channel_id=1, source_target_pairs={{0,8},{1,9},{2,10},{3,11},{4,12},{5,13},{6,14},{7,15},{8,0},{9,1},... | collective-permute-start | bytes 245768 | tf_op jit(solution)/shard_map/ppermute | solution.py:344
  79.3 4.2 %collective-permute-start.25 = (f32[160,128]{1,0:T(8,128)S(1)}, f32[160,128]{1,0:T(8,128)S(1)}, u32[]{:S(2)}, u32[]{:S(2)}) collective-permute-start(f32[160,128]{1,0:T(8,128)S(1)} %get-tuple-element.102), channel_id=1, source_target_pairs={{0,8},{1,2},{2,1},{3,4},{4,3},{5,6},{6,5},{7,15},{8,0},{9,10},{10,... | collective-permute-start | bytes 245768 | tf_op jit(solution)/shard_map/ppermute | solution.py:344
  79.9 3.5 %collective-permute-start.24 = (f32[160,128]{1,0:T(8,128)S(1)}, f32[160,128]{1,0:T(8,128)S(1)}, u32[]{:S(2)}, u32[]{:S(2)}) collective-permute-start(f32[160,128]{1,0:T(8,128)S(1)} %get-tuple-element.103), channel_id=1, source_target_pairs={{0,1},{1,0},{2,3},{3,2},{4,5},{5,4},{6,7},{7,6},{8,9},{9,8},{10,11... | collective-permute-start | bytes 245768 | tf_op jit(solution)/shard_map/ppermute | solution.py:344
  84.2 3.7 %collective-permute-start.28 = (f32[48,128]{1,0:T(8,128)S(1)}, f32[48,128]{1,0:T(8,128)S(1)}, u32[]{:S(2)}, u32[]{:S(2)}) collective-permute-start(f32[48,128]{1,0:T(8,128)S(1)} %get-tuple-element.76.refs_0_), channel_id=1, source_target_pairs={{0,16},{1,17},{2,18},{3,19},{4,20},{5,21},{6,22},{7,23},{8,24},{9,... | collective-permute-start | bytes 73736 | tf_op jit(solution)/shard_map/ppermute | solution.py:344
  88.0 3.9 %collective-permute-start.29 = (f32[256,128]{1,0:T(8,128)S(1)}, f32[256,128]{1,0:T(8,128)S(1)}, u32[]{:S(2)}, u32[]{:S(2)}) collective-permute-start(f32[256,128]{1,0:T(8,128)S(1)} %pad_maximum_fusion.3), channel_id=1, source_target_pairs={{0,8},{1,9},{2,10},{3,11},{4,12},{5,13},{6,14},{7,15},{8,0},{9,1},... | collective-permute-start | bytes 393224 | tf_op jit(solution)/shard_map/ppermute | solution.py:344
  92.0 4.1 %collective-permute-start.33 = (f32[48,128]{1,0:T(8,128)S(1)}, f32[48,128]{1,0:T(8,128)S(1)}, u32[]{:S(2)}, u32[]{:S(2)}) collective-permute-start(f32[48,128]{1,0:T(8,128)S(1)} %shard_map.123.refs_1_), channel_id=1, source_target_pairs={{0,1},{1,0},{2,3},{3,2},{4,5},{5,4},{6,7},{7,6},{8,9},{9,8},{10,11... | collective-permute-start | bytes 73736 | tf_op jit(solution)/shard_map/ppermute | solution.py:344
  95.3 1.9 %collective-permute-start.30 = (f32[160,128]{1,0:T(8,128)S(1)}, f32[160,128]{1,0:T(8,128)S(1)}, u32[]{:S(2)}, u32[]{:S(2)}) collective-permute-start(f32[160,128]{1,0:T(8,128)S(1)} %get-tuple-element.77), channel_id=1, source_target_pairs={{0,1},{1,0},{2,3},{3,2},{4,5},{5,4},{6,7},{7,6},{8,16},{9,17},{10,... | collective-permute-start | bytes 245768 | tf_op jit(solution)/shard_map/ppermute | solution.py:344
  96.1 3.7 %collective-permute-start.34 = (f32[96,128]{1,0:T(8,128)S(1)}, f32[96,128]{1,0:T(8,128)S(1)}, u32[]{:S(2)}, u32[]{:S(2)}) collective-permute-start(f32[96,128]{1,0:T(8,128)S(1)} %pad_maximum_fusion.13), channel_id=1, source_target_pairs={{0,3},{1,2},{2,1},{3,0},{4,7},{5,6},{6,5},{7,4},{8,11},{9,10},{10,... | collective-permute-start | bytes 147464 | tf_op jit(solution)/shard_map/ppermute | solution.py:344
  99.8 6.3 %collective-permute-start.35 = (f32[192,128]{1,0:T(8,128)S(1)}, f32[192,128]{1,0:T(8,128)S(1)}, u32[]{:S(2)}, u32[]{:S(2)}) collective-permute-start(f32[192,128]{1,0:T(8,128)S(1)} %pad_maximum_fusion.8), channel_id=1, source_target_pairs={{0,5},{1,4},{2,7},{3,6},{4,1},{5,0},{6,3},{7,2},{8,13},{9,12},{10,... | collective-permute-start | bytes 294920 | tf_op jit(solution)/shard_map/ppermute | solution.py:344
  101.9 4.3 %collective-permute-start.32 = (f32[160,128]{1,0:T(8,128)S(1)}, f32[160,128]{1,0:T(8,128)S(1)}, u32[]{:S(2)}, u32[]{:S(2)}) collective-permute-start(f32[160,128]{1,0:T(8,128)S(1)} %get-tuple-element.98), channel_id=1, source_target_pairs={{0,8},{1,2},{2,1},{3,4},{4,3},{5,6},{6,5},{7,15},{8,0},{9,10},{10,... | collective-permute-start | bytes 245768 | tf_op jit(solution)/shard_map/ppermute | solution.py:344
  102.0 4.2 %collective-permute-start.31 = (f32[160,128]{1,0:T(8,128)S(1)}, f32[160,128]{1,0:T(8,128)S(1)}, u32[]{:S(2)}, u32[]{:S(2)}) collective-permute-start(f32[160,128]{1,0:T(8,128)S(1)} %get-tuple-element.99), channel_id=1, source_target_pairs={{0,1},{1,0},{2,3},{3,2},{4,5},{5,4},{6,7},{7,6},{8,9},{9,8},{10,11... | collective-permute-start | bytes 245768 | tf_op jit(solution)/shard_map/ppermute | solution.py:344
  109.6 3.2 %collective-permute-start.39 = (f32[160,128]{1,0:T(8,128)S(1)}, f32[160,128]{1,0:T(8,128)S(1)}, u32[]{:S(2)}, u32[]{:S(2)}) collective-permute-start(f32[160,128]{1,0:T(8,128)S(1)} %get-tuple-element.94), channel_id=1, source_target_pairs={{0,1},{1,0},{2,3},{3,2},{4,5},{5,4},{6,7},{7,6},{8,16},{9,17},{10,... | collective-permute-start | bytes 245768 | tf_op jit(solution)/shard_map/ppermute | solution.py:344
  110.0 3.9 %collective-permute-start.38 = (f32[160,128]{1,0:T(8,128)S(1)}, f32[160,128]{1,0:T(8,128)S(1)}, u32[]{:S(2)}, u32[]{:S(2)}) collective-permute-start(f32[160,128]{1,0:T(8,128)S(1)} %get-tuple-element.95), channel_id=1, source_target_pairs={{0,8},{1,9},{2,10},{3,11},{4,12},{5,13},{6,14},{7,15},{8,0},{9,1},... | collective-permute-start | bytes 245768 | tf_op jit(solution)/shard_map/ppermute | solution.py:344
  111.0 4.2 %collective-permute-start.37 = (f32[160,128]{1,0:T(8,128)S(1)}, f32[160,128]{1,0:T(8,128)S(1)}, u32[]{:S(2)}, u32[]{:S(2)}) collective-permute-start(f32[160,128]{1,0:T(8,128)S(1)} %get-tuple-element.96), channel_id=1, source_target_pairs={{0,8},{1,2},{2,1},{3,4},{4,3},{5,6},{6,5},{7,15},{8,0},{9,10},{10,... | collective-permute-start | bytes 245768 | tf_op jit(solution)/shard_map/ppermute | solution.py:344
  112.7 2.5 %collective-permute-start.36 = (f32[160,128]{1,0:T(8,128)S(1)}, f32[160,128]{1,0:T(8,128)S(1)}, u32[]{:S(2)}, u32[]{:S(2)}) collective-permute-start(f32[160,128]{1,0:T(8,128)S(1)} %get-tuple-element.97), channel_id=1, source_target_pairs={{0,1},{1,0},{2,3},{3,2},{4,5},{5,4},{6,7},{7,6},{8,9},{9,8},{10,11... | collective-permute-start | bytes 245768 | tf_op jit(solution)/shard_map/ppermute | solution.py:344
  116.0 3.6 %collective-permute-start.40 = (f32[48,128]{1,0:T(8,128)S(1)}, f32[48,128]{1,0:T(8,128)S(1)}, u32[]{:S(2)}, u32[]{:S(2)}) collective-permute-start(f32[48,128]{1,0:T(8,128)S(1)} %get-tuple-element.83.refs_0_), channel_id=1, source_target_pairs={{0,16},{1,17},{2,18},{3,19},{4,20},{5,21},{6,22},{7,23},{8,24},{9,... | collective-permute-start | bytes 73736 | tf_op jit(solution)/shard_map/ppermute | solution.py:344
  119.6 3.9 %collective-permute-start.41 = (f32[256,128]{1,0:T(8,128)S(1)}, f32[256,128]{1,0:T(8,128)S(1)}, u32[]{:S(2)}, u32[]{:S(2)}) collective-permute-start(f32[256,128]{1,0:T(8,128)S(1)} %pad_maximum_fusion.4), channel_id=1, source_target_pairs={{0,8},{1,9},{2,10},{3,11},{4,12},{5,13},{6,14},{7,15},{8,0},{9,1},... | collective-permute-start | bytes 393224 | tf_op jit(solution)/shard_map/ppermute | solution.py:344
  123.7 4.2 %collective-permute-start.45 = (f32[48,128]{1,0:T(8,128)S(1)}, f32[48,128]{1,0:T(8,128)S(1)}, u32[]{:S(2)}, u32[]{:S(2)}) collective-permute-start(f32[48,128]{1,0:T(8,128)S(1)} %shard_map.128.refs_1_), channel_id=1, source_target_pairs={{0,1},{1,0},{2,3},{3,2},{4,5},{5,4},{6,7},{7,6},{8,9},{9,8},{10,11... | collective-permute-start | bytes 73736 | tf_op jit(solution)/shard_map/ppermute | solution.py:344
  127.0 1.9 %collective-permute-start.42 = (f32[160,128]{1,0:T(8,128)S(1)}, f32[160,128]{1,0:T(8,128)S(1)}, u32[]{:S(2)}, u32[]{:S(2)}) collective-permute-start(f32[160,128]{1,0:T(8,128)S(1)} %get-tuple-element.84), channel_id=1, source_target_pairs={{0,1},{1,0},{2,3},{3,2},{4,5},{5,4},{6,7},{7,6},{8,16},{9,17},{10,... | collective-permute-start | bytes 245768 | tf_op jit(solution)/shard_map/ppermute | solution.py:344
  127.9 3.7 %collective-permute-start.46 = (f32[96,128]{1,0:T(8,128)S(1)}, f32[96,128]{1,0:T(8,128)S(1)}, u32[]{:S(2)}, u32[]{:S(2)}) collective-permute-start(f32[96,128]{1,0:T(8,128)S(1)} %pad_maximum_fusion.14), channel_id=1, source_target_pairs={{0,3},{1,2},{2,1},{3,0},{4,7},{5,6},{6,5},{7,4},{8,11},{9,10},{10,... | collective-permute-start | bytes 147464 | tf_op jit(solution)/shard_map/ppermute | solution.py:344
  131.6 6.7 %collective-permute-start.47 = (f32[192,128]{1,0:T(8,128)S(1)}, f32[192,128]{1,0:T(8,128)S(1)}, u32[]{:S(2)}, u32[]{:S(2)}) collective-permute-start(f32[192,128]{1,0:T(8,128)S(1)} %pad_maximum_fusion.9), channel_id=1, source_target_pairs={{0,5},{1,4},{2,7},{3,6},{4,1},{5,0},{6,3},{7,2},{8,13},{9,12},{10,... | collective-permute-start | bytes 294920 | tf_op jit(solution)/shard_map/ppermute | solution.py:344
  134.0 4.3 %collective-permute-start.44 = (f32[160,128]{1,0:T(8,128)S(1)}, f32[160,128]{1,0:T(8,128)S(1)}, u32[]{:S(2)}, u32[]{:S(2)}) collective-permute-start(f32[160,128]{1,0:T(8,128)S(1)} %get-tuple-element.92), channel_id=1, source_target_pairs={{0,8},{1,2},{2,1},{3,4},{4,3},{5,6},{6,5},{7,15},{8,0},{9,10},{10,... | collective-permute-start | bytes 245768 | tf_op jit(solution)/shard_map/ppermute | solution.py:344
  134.1 4.2 %collective-permute-start.43 = (f32[160,128]{1,0:T(8,128)S(1)}, f32[160,128]{1,0:T(8,128)S(1)}, u32[]{:S(2)}, u32[]{:S(2)}) collective-permute-start(f32[160,128]{1,0:T(8,128)S(1)} %get-tuple-element.93), channel_id=1, source_target_pairs={{0,1},{1,0},{2,3},{3,2},{4,5},{5,4},{6,7},{7,6},{8,9},{9,8},{10,11... | collective-permute-start | bytes 245768 | tf_op jit(solution)/shard_map/ppermute | solution.py:344
  141.7 2.6 %collective-permute-start.51 = (f32[160,128]{1,0:T(8,128)S(1)}, f32[160,128]{1,0:T(8,128)S(1)}, u32[]{:S(2)}, u32[]{:S(2)}) collective-permute-start(f32[160,128]{1,0:T(8,128)S(1)} %get-tuple-element.88), channel_id=1, source_target_pairs={{0,1},{1,0},{2,3},{3,2},{4,5},{5,4},{6,7},{7,6},{8,16},{9,17},{10,... | collective-permute-start | bytes 245768 | tf_op jit(solution)/shard_map/ppermute | solution.py:344
  142.2 3.9 %collective-permute-start.50 = (f32[160,128]{1,0:T(8,128)S(1)}, f32[160,128]{1,0:T(8,128)S(1)}, u32[]{:S(2)}, u32[]{:S(2)}) collective-permute-start(f32[160,128]{1,0:T(8,128)S(1)} %get-tuple-element.89), channel_id=1, source_target_pairs={{0,8},{1,9},{2,10},{3,11},{4,12},{5,13},{6,14},{7,15},{8,0},{9,1},... | collective-permute-start | bytes 245768 | tf_op jit(solution)/shard_map/ppermute | solution.py:344
  142.9 4.2 %collective-permute-start.49 = (f32[160,128]{1,0:T(8,128)S(1)}, f32[160,128]{1,0:T(8,128)S(1)}, u32[]{:S(2)}, u32[]{:S(2)}) collective-permute-start(f32[160,128]{1,0:T(8,128)S(1)} %get-tuple-element.90), channel_id=1, source_target_pairs={{0,8},{1,2},{2,1},{3,4},{4,3},{5,6},{6,5},{7,15},{8,0},{9,10},{10,... | collective-permute-start | bytes 245768 | tf_op jit(solution)/shard_map/ppermute | solution.py:344
  144.1 3.0 %collective-permute-start.48 = (f32[160,128]{1,0:T(8,128)S(1)}, f32[160,128]{1,0:T(8,128)S(1)}, u32[]{:S(2)}, u32[]{:S(2)}) collective-permute-start(f32[160,128]{1,0:T(8,128)S(1)} %get-tuple-element.91), channel_id=1, source_target_pairs={{0,1},{1,0},{2,3},{3,2},{4,5},{5,4},{6,7},{7,6},{8,9},{9,8},{10,11... | collective-permute-start | bytes 245768 | tf_op jit(solution)/shard_map/ppermute | solution.py:344

commit v4 on v3

--- a/solution.py
+++ b/solution.py
@@ -176,8 +176,17 @@
     map_t_ref[:, :coarse] = transposed(mapped, small_ref)
 
 
-def split_kernel(x_ref, o_ref):
-    o_ref[...] = stack_split(x_ref[...])
+def fold_kernel(perm_ref, x_ref, *refs):
+    rows = x_ref.shape[0]
+    for i, part in enumerate(split(x_ref[...], 2)):
+        part = dot(perm_ref[...], part).astype(BF16)
+        if len(refs) > 1:
+            part = dot(part, refs[0][...]).astype(BF16)
+        refs[-1][i * rows : (i + 1) * rows] = part
+
+
+def restore_kernel(x_ref, back_ref, out_ref):
+    out_ref[...] = permuted(back_ref[...], x_ref[...], 3)
 
 
 def level_kernel(
@@ -222,10 +231,10 @@
     c_ref[...] = product(basis_ref[...], current)
 
 
-def local_kernel(face, current_ref, inverse_ref, perm_ref, back_ref, y_ref, g_ref, h_ref):
+def local_kernel(face, current_ref, inverse_ref, back_ref, y_ref, g_ref, h_ref):
     n = current_ref.shape[1]
     moved = dot(back_ref[...], jnp.concatenate(split(current_ref[...], 2), axis=1)).astype(BF16)
-    y = permuted(perm_ref[...], product_parts(inverse_ref[...], [moved[:, :n], moved[:, n:]]))
+    y = product_parts(inverse_ref[...], [moved[:, :n], moved[:, n:]])
     y_ref[...] = y
     g_ref[...] = y[2 * face : 3 * face]
     h_ref[...] = y[3 * face :]
@@ -252,7 +261,7 @@
     refs[-1][...] = third
 
 
-def group_kernel(face, starts, coarse, link_ref, order_ref, y_ref, g_ref, h_ref, two_ref, *refs):
+def group_kernel(starts, coarse, order_ref, y_ref, two_ref, *refs):
     y2_ref, stack_ref = refs[len(starts) :]
     slot = 0
     for ref, spans in zip(refs, starts):
@@ -260,37 +269,26 @@
             offset = pl.multiple_of(order_ref[slot], 8)
             stack_ref[pl.ds(offset, coarse)] = ref[start : start + coarse]
             slot += 1
-    y = y_ref[...] + product(two_ref[...], stack_ref[...])
-    y2_ref[: 2 * face] = y[: 2 * face]
-    y2_ref[2 * face : 3 * face] = y[2 * face : 3 * face] + g_ref[:face] * link_ref[2].astype(F32)
-    y2_ref[3 * face :] = y[3 * face :] + h_ref[:face] * link_ref[3].astype(F32)
+    y2_ref[...] = y_ref[...] + product(two_ref[...], stack_ref[...])
 
 
 def update_kernel(
-    weight, first, face, starts, top, link_ref, order_ref, y2_ref, e_ref, f_ref, top_ref, perm_ref, back_ref, schur_ref, *refs
+    weight, first, face, top, link_ref, order_ref, y2_ref, r0, r1, r2, r3, top_ref, schur_ref, *refs
 ):
     if not first:
         old_ref, refs = refs[0], refs[1:]
-    x_ref, out_ref, stack_ref = refs[len(starts) :]
+    x_ref, out_ref, stack_ref = refs[-3:]
     slot = 0
-    for ref, first_row in zip(refs, starts):
-        for start in range(first_row, ref.shape[0], top):
+    for ref in refs[:-3]:
+        for start in range(0, ref.shape[0], top):
             stack_ref[pl.ds(pl.multiple_of(order_ref[slot], 8), top)] = ref[start : start + top]
             slot += 1
-    y2 = y2_ref[...] + product(top_ref[...], stack_ref[...])
-    update = jnp.concatenate(
-        [
-            y2[:face] + e_ref[:face] * link_ref[0].astype(F32),
-            y2[face : 2 * face] + f_ref[:face] * link_ref[1].astype(F32),
-            y2[2 * face :],
-        ],
-        axis=0,
-    )
-    x = weight * permuted(back_ref[...], update)
+    update = y2_ref[...] + received(face, link_ref, (r0, r1, r2, r3)) + product(top_ref[...], stack_ref[...])
+    x = weight * update
     if not first:
         x = old_ref[...] + x
     x_ref[...] = x
-    out_ref[...] = permuted(perm_ref[...], product(schur_ref[...], x))
+    out_ref[...] = product(schur_ref[...], x)
 
 
 def residual_kernel(face, link_ref, f_ref, r0, r1, r2, r3, asm_ref, back_ref, out_ref):
@@ -390,8 +388,12 @@
         flops=4 * size**2 * columns,
         scratch=[(size, LANES), (LANES, LANES)],
     )
-    schur2 = call(split_kernel, [((2 * size, size), BF16)], [], [schur[0, 0]])[0]
-    inverse2 = call(split_kernel, [((2 * size, size), BF16)], [], [local_inverse[0, 0]])[0]
+
+    def folded(x, *more):
+        return call(fold_kernel, [((2 * size, size), BF16)], [], [perm, x, *more], flops=4 * size**3)[0]
+
+    inverse2 = folded(local_inverse[0, 0])
+    schur2 = folded(schur[0, 0], back)
 
     got = exchange(sent)
     two2, top2 = call(
@@ -435,22 +437,20 @@
             functools.partial(local_kernel, face),
             [(n, F32), ((face, columns), F32), ((face, columns), F32)],
             [],
-            [current, inverse2, perm, back],
+            [current, inverse2, back],
             flops=2 * square,
         )
+        if row_pairs:
+            got = swap(jnp.concatenate([known, got_r]), lambda r, c: (r ^ 1, c))
+            more = known.shape[0]
+            pieces, starts = [coeffs, got_r, got], ((0,), (0,), (0, more))
+            map_starts, sources = ((0,), (coarse,), (coarse, more + coarse)), [map_t, got_r, got]
+        else:
+            pieces = [lax.all_gather(coeffs, "row", axis=0, tiled=True)]
+            starts = map_starts = (tuple(range(0, total, coarse)),)
+            sources = [lax.all_gather(map_t, "row", axis=0, tiled=True)] if first else None
+        got_g = swap_even_row(face_g)
         got_h = swap_odd_row(face_h)
-        if row_pairs:
-            got_g = swap_even_row(jnp.concatenate([face_g, known, got_r]))
-            more = face + known.shape[0]
-            pieces, starts = [coeffs, got_r, got_g], ((0,), (0,), (face, more))
-            map_starts = ((0,), (coarse,), (face + coarse, more + coarse))
-            sources = [map_t, got_r, got_g]
-        else:
-            got_g = swap_even_row(face_g)
-            spans = tuple(range(0, total, coarse))
-            pieces, starts = [lax.all_gather(coeffs, "row", axis=0, tiled=True)], (spans,)
-            map_starts = starts
-            sources = [lax.all_gather(map_t, "row", axis=0, tiled=True)] if first else None
         if first:
             maps = call(
                 functools.partial(maps_kernel, coarse, map_starts), [((2 * rows * top, coarse), BF16)], [], sources
@@ -460,10 +460,10 @@
         if doubling:
             more = swap(third, lambda r, c: (r, c ^ 1))
         y2 = call(
-            functools.partial(group_kernel, face, starts, coarse),
+            functools.partial(group_kernel, starts, coarse),
             [(n, F32)],
-            [link, row_order],
-            [y, got_g, got_h, two2] + pieces,
+            [row_order],
+            [y, two2] + pieces,
             scratch=[(total, columns)],
         )[0]
         got_f = swap_odd_col(y2[face : 2 * face])
@@ -478,15 +478,15 @@
                 bits *= 2
         else:
             tops = [lax.all_gather(third, "col", axis=0, tiled=True)]
-        starts = (0,) * len(tops)
         solution, field = call(
-            functools.partial(update_kernel, weight, first, face, starts, top),
+            functools.partial(update_kernel, weight, first, face, top),
             [(n, F32), (n, F32)],
             [link, col_order],
-            [y2, got_e, got_f, top2, perm, back, schur2] + ([] if first else [solution]) + tops,
+            [y2, got_e, got_f, got_g, got_h, top2, schur2] + ([] if first else [solution]) + tops,
             flops=2 * square,
             scratch=[(width, columns)],
         )
+    solution = call(restore_kernel, [(n, F32)], [], [solution, back], flops=square)[0]
     residual = call(
         functools.partial(residual_kernel, face),
         [(n, F32)],

time: 150 us -> 146 us (0.973)
  waiting for transfers between devices: 52.9 us -> 43.9 us
  starting transfers between devices: 54.9 us -> 63.1 us
  Pallas kernels: 36.7 us -> 34.5 us
    ppermute x52 -> x56, waiting for transfers between devices: 52.9 us -> 43.9 us  [swap(): return lax.ppermute(x, ('row', 'col'), swap_pairs(rows, cols, partner))]
    ppermute x52 -> x56, starting transfers between devices: 54.9 us -> 63.1 us  [swap(): return lax.ppermute(x, ('row', 'col'), swap_pairs(rows, cols, partner))]
    pallas_call x27 -> x28, Pallas kernels: 36.7 us -> 34.5 us  [call(): pl.pallas_call(body, out_shape=[jax.ShapeDtypeStruct(s, d) for s, d in ou...]
  transfers between devices with their start and end apart: 52 -> 56, of which waited for: 28 -> 26; matrix products, arithmetic and copies ran while one was open for 0% -> 0% of each run, Pallas kernels for 10% -> 12%
where the time goes in v4:
time: 146 us; the launch traced here: 145 us
  starting transfers between devices  63.1 us (43%)
  waiting for transfers between devices  43.9 us (30%)
  Pallas kernels  34.5 us (24%)
  other arithmetic  1.51 us (1%)
    ppermute x56, starting transfers between devices, swap(): return lax.ppermute(x, ('row', 'col'), swap_pairs(rows, cols, partner))  63.1 us
    ppermute x56, waiting for transfers between devices, swap(): return lax.ppermute(x, ('row', 'col'), swap_pairs(rows, cols, partner))  43.9 us
    pallas_call x28, Pallas kernels, call(): pl.pallas_call(body, out_shape=[jax.ShapeDtypeStruct(s, d) for s, d in ou...  34.5 us
  transfers between devices with their start and end apart: 56, of which 26 were waited for; matrix products, arithmetic and copies ran while one was open for 0% of the time, Pallas kernels for 12%

profile of v4, /device:TPU:1, one launch (start us, length us, event | category | flops | bytes accessed | tf_op | source)
XLA Modules:
  0.0 145.4 jit_solution(18025346525803943694)
XLA Ops:
  0.7 1.1 copy.12
  1.9 1.1 pad_maximum_fusion.load_ref.basis_ref
  3.0 1.3 shard_map.104
  4.5 1.0 shard_map.105
  5.5 2.2 %collective-permute-start.2 = (f32[336,128]{1,0:T(8,128)S(1)}, f32[336,128]{1,0:T(8,128)S(1)}, u32[]{:S(2)}, u32[]{:S(2)}) collective-permute-start(f32[336,128]{1,0:T(8,128)S(1)} %get-tuple-element.49), channel_id=1, source_target_pairs={{0,8},{1,9},{2,10},{3,11},{4,12},{5,13},{6,14},{7,15},{8,0},{9,1},... | collective-permute-start | bytes 516104 | tf_op jit(solution)/shard_map/ppermute | solution.py:342
  8.6 1.6 %collective-permute-start.1 = (f32[384,128]{1,0:T(8,128)S(1)}, f32[384,128]{1,0:T(8,128)S(1)}, u32[]{:S(2)}, u32[]{:S(2)}) collective-permute-start(f32[384,128]{1,0:T(8,128)S(1)} %get-tuple-element.48), channel_id=1, source_target_pairs={{0,8},{1,2},{2,1},{3,4},{4,3},{5,6},{6,5},{7,15},{8,0},{9,10},{10,... | collective-permute-start | bytes 589832 | tf_op jit(solution)/shard_map/ppermute | solution.py:342
  10.4 1.3 collective-permute-done.2.r2.g_ref
  11.8 3.3 %collective-permute-done.1.r1.f_ref = f32[384,128]{1,0:T(8,128)S(1)} collective-permute-done((f32[384,128]{1,0:T(8,128)S(1)}, f32[384,128]{1,0:T(8,128)S(1)}, u32[]{:S(2)}, u32[]{:S(2)}) %collective-permute-start.1) | collective-permute-done | bytes 196640 | tf_op jit(solution)/shard_map/ppermute | solution.py:342
  15.9 2.9 %collective-permute-start.4 = (f32[96,128]{1,0:T(8,128)S(1)}, f32[96,128]{1,0:T(8,128)S(1)}, u32[]{:S(2)}, u32[]{:S(2)}) collective-permute-start(f32[96,128]{1,0:T(8,128)S(1)} %pad_maximum_fusion.7), channel_id=1, source_target_pairs={{0,16},{1,17},{2,18},{3,19},{4,20},{5,21},{6,22},{7,23},{8,24},{9,... | collective-permute-start | bytes 147464 | tf_op jit(solution)/shard_map/ppermute | solution.py:342
  18.7 1.9 %collective-permute-done.4.refs_1_ = f32[96,128]{1,0:T(8,128)S(1)} collective-permute-done((f32[96,128]{1,0:T(8,128)S(1)}, f32[96,128]{1,0:T(8,128)S(1)}, u32[]{:S(2)}, u32[]{:S(2)}) %collective-permute-start.4) | collective-permute-done | bytes 49184 | tf_op jit(solution)/shard_map/ppermute | solution.py:342
  20.6 2.6 %collective-permute-start.5 = (f32[192,128]{1,0:T(8,128)S(1)}, f32[192,128]{1,0:T(8,128)S(1)}, u32[]{:S(2)}, u32[]{:S(2)}) collective-permute-start(f32[192,128]{1,0:T(8,128)S(1)} %pad_maximum_fusion.2), channel_id=1, source_target_pairs={{0,8},{1,9},{2,10},{3,11},{4,12},{5,13},{6,14},{7,15},{8,0},{9,1},... | collective-permute-start | bytes 294920 | tf_op jit(solution)/shard_map/ppermute | solution.py:342
  23.2 1.6 %shard_map.107.inverse_ref = bf16[1280,640]{1,0:T(8,128)(2,1)S(1)} custom-call(bf16[640,640]{1,0:T(8,128)(2,1)S(1)} %get-tuple-element.46.perm_ref, f32[640,640]{1,0:T(8,128)S(1)} %bitcast.13), custom_call_target="tpu_custom_call" | custom-call | flops 1048576000 | bytes 2457600 | tf_op jit(solution)/shard_map/pallas_call | solution.py:64
  24.8 1.5 %collective-permute-done.5.refs_2_ = f32[192,128]{1,0:T(8,128)S(1)} collective-permute-done((f32[192,128]{1,0:T(8,128)S(1)}, f32[192,128]{1,0:T(8,128)S(1)}, u32[]{:S(2)}, u32[]{:S(2)}) %collective-permute-start.5) | collective-permute-done | bytes 98336 | tf_op jit(solution)/shard_map/ppermute | solution.py:342
  27.2 1.4 shard_map.108
  28.7 1.5 %collective-permute-start.8 = (f32[160,128]{1,0:T(8,128)S(1)}, f32[160,128]{1,0:T(8,128)S(1)}, u32[]{:S(2)}, u32[]{:S(2)}) collective-permute-start(f32[160,128]{1,0:T(8,128)S(1)} %get-tuple-element.62), channel_id=1, source_target_pairs={{0,8},{1,9},{2,10},{3,11},{4,12},{5,13},{6,14},{7,15},{8,0},{9,1},... | collective-permute-start | bytes 245768 | tf_op jit(solution)/shard_map/ppermute | solution.py:342
  30.5 2.2 %shard_map.109 = (bf16[1280,192]{1,0:T(8,128)(2,1)S(1)}, bf16[1280,384]{1,0:T(8,128)(2,1)S(1)}) custom-call(s32[4]{0:T(128)S(1)} %select_reduce_fusion.link_ref, f32[640,48]{1,0:T(8,128)S(1)} %get-tuple-element.55.basis_ref, f32[48,192]{1,0:T(8,128)S(1)} %get-tuple-element.56.inverse_ref, f32[640,48]{1,0:T(8,128)S(1)} %get-tuple-element.57.coarse_ref, ...), custom_call_target="tpu_custom_call" | custom-call | bytes 1093632 | tf_op jit(solution)/shard_map/pallas_call | solution.py:64
  33.6 1.5 %collective-permute-start.11 = (f32[96,128]{1,0:T(8,128)S(1)}, f32[96,128]{1,0:T(8,128)S(1)}, u32[]{:S(2)}, u32[]{:S(2)}) collective-permute-start(f32[96,128]{1,0:T(8,128)S(1)} %pad_maximum_fusion.8), channel_id=1, source_target_pairs={{0,3},{1,2},{2,1},{3,0},{4,7},{5,6},{6,5},{7,4},{8,11},{9,10},{10,... | collective-permute-start | bytes 147464 | tf_op jit(solution)/shard_map/ppermute | solution.py:342
  37.2 3.4 %collective-permute-start.12 = (f32[192,128]{1,0:T(8,128)S(1)}, f32[192,128]{1,0:T(8,128)S(1)}, u32[]{:S(2)}, u32[]{:S(2)}) collective-permute-start(f32[192,128]{1,0:T(8,128)S(1)} %pad_maximum_fusion.3), channel_id=1, source_target_pairs={{0,5},{1,4},{2,7},{3,6},{4,1},{5,0},{6,3},{7,2},{8,13},{9,12},{10,... | collective-permute-start | bytes 294920 | tf_op jit(solution)/shard_map/ppermute | solution.py:342
  40.6 3.1 %shard_map.111.schur_ref = bf16[1280,640]{1,0:T(8,128)(2,1)S(1)} custom-call(bf16[640,640]{1,0:T(8,128)(2,1)S(1)} %get-tuple-element.46.perm_ref, f32[640,640]{1,0:T(8,128)S(1)} %bitcast.12, bf16[640,640]{1,0:T(8,128)(2,1)S(1)} %get-tuple-element.53.back_ref.refs_0_), custom_call_target="tpu_custom_call" | custom-call | flops 1048576000 | bytes 3276800 | tf_op jit(solution)/shard_map/pallas_call | solution.py:64
  44.0 2.2 %shard_map.114 = (f32[640,128]{1,0:T(8,128)S(1)}, f32[640,128]{1,0:T(8,128)S(1)}) custom-call(s32[4]{0:T(128)S(1)} %select_reduce_fusion.link_ref, s32[8]{0:T(128)S(1)} %fusion.9.order_ref, f32[640,128]{1,0:T(8,128)S(1)} %shard_map.110.y2_ref, f32[160,128]{1,0:T(8,128)S(1)} %collective-permute-done.6.r0, f32[160,128]{1,0:T(8,128)S(1)} %collective-permute-done.7.r1, ...), custom_call_target="tpu_custom_call" | custom-call | flops 838860800 | bytes 3473408 | tf_op jit(solution)/shard_map/pallas_call | solution.py:64
  48.9 1.7 %collective-permute-done.15.r2 = f32[160,128]{1,0:T(8,128)S(1)} collective-permute-done((f32[160,128]{1,0:T(8,128)S(1)}, f32[160,128]{1,0:T(8,128)S(1)}, u32[]{:S(2)}, u32[]{:S(2)}) %collective-permute-start.15) | collective-permute-done | bytes 81952 | tf_op jit(solution)/shard_map/ppermute | solution.py:342
  50.7 1.2 collective-permute-done.14.r1
  52.6 1.0 collective-permute-start.17
  53.7 2.6 %collective-permute-done.17.refs_1_ = f32[48,128]{1,0:T(8,128)S(1)} collective-permute-done((f32[48,128]{1,0:T(8,128)S(1)}, f32[48,128]{1,0:T(8,128)S(1)}, u32[]{:S(2)}, u32[]{:S(2)}) %collective-permute-start.17) | collective-permute-done | bytes 24608 | tf_op jit(solution)/shard_map/ppermute | solution.py:342
  57.2 2.0 %collective-permute-done.18.refs_2_ = f32[96,128]{1,0:T(8,128)S(1)} collective-permute-done((f32[96,128]{1,0:T(8,128)S(1)}, f32[96,128]{1,0:T(8,128)S(1)}, u32[]{:S(2)}, u32[]{:S(2)}) %collective-permute-start.18) | collective-permute-done | bytes 49184 | tf_op jit(solution)/shard_map/ppermute | solution.py:342
  59.4 3.5 %collective-permute-start.23 = (f32[48,128]{1,0:T(8,128)S(1)}, f32[48,128]{1,0:T(8,128)S(1)}, u32[]{:S(2)}, u32[]{:S(2)}) collective-permute-start(f32[48,128]{1,0:T(8,128)S(1)} %shard_map.118.refs_1_), channel_id=1, source_target_pairs={{0,1},{1,0},{2,3},{3,2},{4,5},{5,4},{6,7},{7,6},{8,9},{9,8},{10,11... | collective-permute-start | bytes 73736 | tf_op jit(solution)/shard_map/ppermute | solution.py:342
  63.8 1.4 shard_map.116
  67.5 1.7 %collective-permute-start.25 = (f32[192,128]{1,0:T(8,128)S(1)}, f32[192,128]{1,0:T(8,128)S(1)}, u32[]{:S(2)}, u32[]{:S(2)}) collective-permute-start(f32[192,128]{1,0:T(8,128)S(1)} %pad_maximum_fusion.4), channel_id=1, source_target_pairs={{0,5},{1,4},{2,7},{3,6},{4,1},{5,0},{6,3},{7,2},{8,13},{9,12},{10,... | collective-permute-start | bytes 294920 | tf_op jit(solution)/shard_map/ppermute | solution.py:342
  69.2 1.6 %collective-permute-start.20 = (f32[160,128]{1,0:T(8,128)S(1)}, f32[160,128]{1,0:T(8,128)S(1)}, u32[]{:S(2)}, u32[]{:S(2)}) collective-permute-start(f32[160,128]{1,0:T(8,128)S(1)} %get-tuple-element.104), channel_id=1, source_target_pairs={{0,8},{1,2},{2,1},{3,4},{4,3},{5,6},{6,5},{7,15},{8,0},{9,10},{10,... | collective-permute-start | bytes 245768 | tf_op jit(solution)/shard_map/ppermute | solution.py:342
  71.6 2.0 %collective-permute-done.20.r1 = f32[160,128]{1,0:T(8,128)S(1)} collective-permute-done((f32[160,128]{1,0:T(8,128)S(1)}, f32[160,128]{1,0:T(8,128)S(1)}, u32[]{:S(2)}, u32[]{:S(2)}) %collective-permute-start.20) | collective-permute-done | bytes 81952 | tf_op jit(solution)/shard_map/ppermute | solution.py:342
  73.6 2.3 %shard_map.119 = (f32[640,128]{1,0:T(8,128)S(1)}, f32[640,128]{1,0:T(8,128)S(1)}) custom-call(s32[4]{0:T(128)S(1)} %select_reduce_fusion.link_ref, s32[8]{0:T(128)S(1)} %fusion.9.order_ref, f32[640,128]{1,0:T(8,128)S(1)} %shard_map.117.y2_ref, f32[160,128]{1,0:T(8,128)S(1)} %collective-permute-done.19.r0, f32[160,128]{1,0:T(8,128)S(1)} %collective-permute-done.20.r1, ...), custom_call_target="tpu_custom_call" | custom-call | flops 838860800 | bytes 3801088 | tf_op jit(solution)/shard_map/pallas_call | solution.py:64
  76.4 1.7 %collective-permute-start.28 = (f32[160,128]{1,0:T(8,128)S(1)}, f32[160,128]{1,0:T(8,128)S(1)}, u32[]{:S(2)}, u32[]{:S(2)}) collective-permute-start(f32[160,128]{1,0:T(8,128)S(1)} %get-tuple-element.101), channel_id=1, source_target_pairs={{0,8},{1,9},{2,10},{3,11},{4,12},{5,13},{6,14},{7,15},{8,0},{9,1},... | collective-permute-start | bytes 245768 | tf_op jit(solution)/shard_map/ppermute | solution.py:342
  78.1 1.6 %collective-permute-start.27 = (f32[160,128]{1,0:T(8,128)S(1)}, f32[160,128]{1,0:T(8,128)S(1)}, u32[]{:S(2)}, u32[]{:S(2)}) collective-permute-start(f32[160,128]{1,0:T(8,128)S(1)} %get-tuple-element.102), channel_id=1, source_target_pairs={{0,8},{1,2},{2,1},{3,4},{4,3},{5,6},{6,5},{7,15},{8,0},{9,10},{10,... | collective-permute-start | bytes 245768 | tf_op jit(solution)/shard_map/ppermute | solution.py:342
  80.6 1.6 %collective-permute-done.27.r1 = f32[160,128]{1,0:T(8,128)S(1)} collective-permute-done((f32[160,128]{1,0:T(8,128)S(1)}, f32[160,128]{1,0:T(8,128)S(1)}, u32[]{:S(2)}, u32[]{:S(2)}) %collective-permute-start.27) | collective-permute-done | bytes 81952 | tf_op jit(solution)/shard_map/ppermute | solution.py:342
  84.0 2.7 %collective-permute-done.30.refs_1_ = f32[48,128]{1,0:T(8,128)S(1)} collective-permute-done((f32[48,128]{1,0:T(8,128)S(1)}, f32[48,128]{1,0:T(8,128)S(1)}, u32[]{:S(2)}, u32[]{:S(2)}) %collective-permute-start.30) | collective-permute-done | bytes 24608 | tf_op jit(solution)/shard_map/ppermute | solution.py:342
  86.7 2.9 %collective-permute-done.31.refs_2_ = f32[96,128]{1,0:T(8,128)S(1)} collective-permute-done((f32[96,128]{1,0:T(8,128)S(1)}, f32[96,128]{1,0:T(8,128)S(1)}, u32[]{:S(2)}, u32[]{:S(2)}) %collective-permute-start.31) | collective-permute-done | bytes 49184 | tf_op jit(solution)/shard_map/ppermute | solution.py:342
  89.8 3.2 %collective-permute-start.36 = (f32[48,128]{1,0:T(8,128)S(1)}, f32[48,128]{1,0:T(8,128)S(1)}, u32[]{:S(2)}, u32[]{:S(2)}) collective-permute-start(f32[48,128]{1,0:T(8,128)S(1)} %shard_map.123.refs_1_), channel_id=1, source_target_pairs={{0,1},{1,0},{2,3},{3,2},{4,5},{5,4},{6,7},{7,6},{8,9},{9,8},{10,11... | collective-permute-start | bytes 73736 | tf_op jit(solution)/shard_map/ppermute | solution.py:342
  93.9 1.2 collective-permute-start.37
  95.1 1.4 shard_map.121
  98.6 1.4 collective-permute-start.38
  100.0 1.0 collective-permute-start.33
  101.0 1.2 collective-permute-start.32
  102.2 2.3 %collective-permute-done.33.r1 = f32[160,128]{1,0:T(8,128)S(1)} collective-permute-done((f32[160,128]{1,0:T(8,128)S(1)}, f32[160,128]{1,0:T(8,128)S(1)}, u32[]{:S(2)}, u32[]{:S(2)}) %collective-permute-start.33) | collective-permute-done | bytes 81952 | tf_op jit(solution)/shard_map/ppermute | solution.py:342
  104.4 2.3 %shard_map.124 = (f32[640,128]{1,0:T(8,128)S(1)}, f32[640,128]{1,0:T(8,128)S(1)}) custom-call(s32[4]{0:T(128)S(1)} %select_reduce_fusion.link_ref, s32[8]{0:T(128)S(1)} %fusion.9.order_ref, f32[640,128]{1,0:T(8,128)S(1)} %shard_map.122.y2_ref, f32[160,128]{1,0:T(8,128)S(1)} %collective-permute-done.32.r0, f32[160,128]{1,0:T(8,128)S(1)} %collective-permute-done.33.r1, ...), custom_call_target="tpu_custom_call" | custom-call | flops 838860800 | bytes 3801088 | tf_op jit(solution)/shard_map/pallas_call | solution.py:64
  107.1 1.9 %collective-permute-start.41 = (f32[160,128]{1,0:T(8,128)S(1)}, f32[160,128]{1,0:T(8,128)S(1)}, u32[]{:S(2)}, u32[]{:S(2)}) collective-permute-start(f32[160,128]{1,0:T(8,128)S(1)} %get-tuple-element.95), channel_id=1, source_target_pairs={{0,8},{1,9},{2,10},{3,11},{4,12},{5,13},{6,14},{7,15},{8,0},{9,1},... | collective-permute-start | bytes 245768 | tf_op jit(solution)/shard_map/ppermute | solution.py:342
  109.0 1.3 collective-permute-start.40
  110.3 1.4 collective-permute-done.41.r2
  111.7 1.4 collective-permute-done.40.r1
  113.9 1.2 collective-permute-start.43
  115.1 2.7 %collective-permute-done.43.refs_1_ = f32[48,128]{1,0:T(8,128)S(1)} collective-permute-done((f32[48,128]{1,0:T(8,128)S(1)}, f32[48,128]{1,0:T(8,128)S(1)}, u32[]{:S(2)}, u32[]{:S(2)}) %collective-permute-start.43) | collective-permute-done | bytes 24608 | tf_op jit(solution)/shard_map/ppermute | solution.py:342
  117.8 2.9 %collective-permute-done.44.refs_2_ = f32[96,128]{1,0:T(8,128)S(1)} collective-permute-done((f32[96,128]{1,0:T(8,128)S(1)}, f32[96,128]{1,0:T(8,128)S(1)}, u32[]{:S(2)}, u32[]{:S(2)}) %collective-permute-start.44) | collective-permute-done | bytes 49184 | tf_op jit(solution)/shard_map/ppermute | solution.py:342
  120.9 2.7 %collective-permute-start.49 = (f32[48,128]{1,0:T(8,128)S(1)}, f32[48,128]{1,0:T(8,128)S(1)}, u32[]{:S(2)}, u32[]{:S(2)}) collective-permute-start(f32[48,128]{1,0:T(8,128)S(1)} %shard_map.128.refs_1_), channel_id=1, source_target_pairs={{0,1},{1,0},{2,3},{3,2},{4,5},{5,4},{6,7},{7,6},{8,9},{9,8},{10,11... | collective-permute-start | bytes 73736 | tf_op jit(solution)/shard_map/ppermute | solution.py:342
  124.5 1.2 collective-permute-start.50
  125.7 1.4 shard_map.126
  128.9 1.7 %collective-permute-start.51 = (f32[192,128]{1,0:T(8,128)S(1)}, f32[192,128]{1,0:T(8,128)S(1)}, u32[]{:S(2)}, u32[]{:S(2)}) collective-permute-start(f32[192,128]{1,0:T(8,128)S(1)} %pad_maximum_fusion.6), channel_id=1, source_target_pairs={{0,5},{1,4},{2,7},{3,6},{4,1},{5,0},{6,3},{7,2},{8,13},{9,12},{10,... | collective-permute-start | bytes 294920 | tf_op jit(solution)/shard_map/ppermute | solution.py:342
  130.6 1.0 collective-permute-start.46
  131.5 1.3 collective-permute-start.45
  132.9 2.0 %collective-permute-done.46.r1 = f32[160,128]{1,0:T(8,128)S(1)} collective-permute-done((f32[160,128]{1,0:T(8,128)S(1)}, f32[160,128]{1,0:T(8,128)S(1)}, u32[]{:S(2)}, u32[]{:S(2)}) %collective-permute-start.46) | collective-permute-done | bytes 81952 | tf_op jit(solution)/shard_map/ppermute | solution.py:342
  134.9 2.3 %shard_map.129 = (f32[640,128]{1,0:T(8,128)S(1)}, f32[640,128]{1,0:T(8,128)S(1)}) custom-call(s32[4]{0:T(128)S(1)} %select_reduce_fusion.link_ref, s32[8]{0:T(128)S(1)} %fusion.9.order_ref, f32[640,128]{1,0:T(8,128)S(1)} %shard_map.127.y2_ref, f32[160,128]{1,0:T(8,128)S(1)} %collective-permute-done.45.r0, f32[160,128]{1,0:T(8,128)S(1)} %collective-permute-done.46.r1, ...), custom_call_target="tpu_custom_call" | custom-call | flops 838860800 | bytes 3801088 | tf_op jit(solution)/shard_map/pallas_call | solution.py:64
  137.9 1.6 %collective-permute-start.54 = (f32[160,128]{1,0:T(8,128)S(1)}, f32[160,128]{1,0:T(8,128)S(1)}, u32[]{:S(2)}, u32[]{:S(2)}) collective-permute-start(f32[160,128]{1,0:T(8,128)S(1)} %get-tuple-element.89), channel_id=1, source_target_pairs={{0,8},{1,9},{2,10},{3,11},{4,12},{5,13},{6,14},{7,15},{8,0},{9,1},... | collective-permute-start | bytes 245768 | tf_op jit(solution)/shard_map/ppermute | solution.py:342
  139.5 1.3 collective-permute-start.53
  140.8 1.4 shard_map.130
  142.2 1.5 %collective-permute-done.53.r1 = f32[160,128]{1,0:T(8,128)S(1)} collective-permute-done((f32[160,128]{1,0:T(8,128)S(1)}, f32[160,128]{1,0:T(8,128)S(1)}, u32[]{:S(2)}, u32[]{:S(2)}) %collective-permute-start.53) | collective-permute-done | bytes 81952 | tf_op jit(solution)/shard_map/ppermute | solution.py:342
  143.7 1.7 %shard_map.131 = f32[640,128]{1,0:T(8,128)} custom-call(s32[4]{0:T(128)S(1)} %select_reduce_fusion.link_ref, f32[640,128]{1,0:T(8,128)S(1)} %get-tuple-element.87.f_ref, f32[160,128]{1,0:T(8,128)S(1)} %collective-permute-done.52.r0, f32[160,128]{1,0:T(8,128)S(1)} %collective-permute-done.53.r1, f32[160,128]{1,0:T(8,128)S(1)} %collective-permute-done.54.r2, ...), custom_call_target="tpu_custom_call" | custom-call | bytes 1802240 | tf_op jit(solution)/shard_map/pallas_call | solution.py:64
  (121 shorter events, 26.1 us)
Async XLA Ops:
  0.6 2.4 %copy-start.2 = (s32[1,1,640]{2,1,0:T(1,128)S(1)}, s32[1,1,640]{2,1,0:T(1,128)}, u32[]{:S(2)}) copy-start(s32[1,1,640]{2,1,0:T(1,128)} %param.12) | copy-start | bytes 7684
  0.6 3.7 %copy-start.3 = (f32[48,384]{1,0:T(8,128)S(1)}, f32[48,384]{1,0:T(8,128)}, u32[]{:S(2)}) copy-start(f32[48,384]{1,0:T(8,128)} %param.17) | copy-start | bytes 221188
  0.7 3.7 %copy-start.5 = (f32[1,48,48]{2,1,0:T(8,128)S(1)}, f32[1,48,48]{2,1,0:T(8,128)}, u32[]{:S(2)}) copy-start(f32[1,48,48]{2,1,0:T(8,128)} %param.16) | copy-start | bytes 27652
  0.7 3.7 %copy-start.4 = (f32[1,48,192]{2,1,0:T(8,128)S(1)}, f32[1,48,192]{2,1,0:T(8,128)}, u32[]{:S(2)}) copy-start(f32[1,48,192]{2,1,0:T(8,128)} %param.15) | copy-start | bytes 110596
  3.0 7.2 %copy-start.6 = (s32[1,1,4]{2,1,0:T(1,128)S(1)}, s32[1,1,4]{2,1,0:T(1,128)}, u32[]{:S(2)}) copy-start(s32[1,1,4]{2,1,0:T(1,128)} %param.13) | copy-start | bytes 52
  4.5 18.7 %copy-start.1 = (f32[1,1,640,640]{3,2,1,0:T(8,128)S(1)}, f32[1,1,640,640]{3,2,1,0:T(8,128)}, u32[]{:S(2)}) copy-start(f32[1,1,640,640]{3,2,1,0:T(8,128)} %param.11) | copy-start | bytes 4915204
  5.5 6.2 %collective-permute-start.2 = (f32[336,128]{1,0:T(8,128)S(1)}, f32[336,128]{1,0:T(8,128)S(1)}, u32[]{:S(2)}, u32[]{:S(2)}) collective-permute-start(f32[336,128]{1,0:T(8,128)S(1)} %get-tuple-element.49), channel_id=1, source_target_pairs={{0,8},{1,9},{2,10},{3,11},{4,12},{5,13},{6,14},{7,15},{8,0},{9,1},... | collective-permute-start | bytes 516104 | tf_op jit(solution)/shard_map/ppermute | solution.py:342
  7.7 4.1 %collective-permute-start.3 = (f32[336,128]{1,0:T(8,128)S(1)}, f32[336,128]{1,0:T(8,128)S(1)}, u32[]{:S(2)}, u32[]{:S(2)}) collective-permute-start(f32[336,128]{1,0:T(8,128)S(1)} %get-tuple-element.50), channel_id=1, source_target_pairs={{0,1},{1,0},{2,3},{3,2},{4,5},{5,4},{6,7},{7,6},{8,16},{9,17},{10,... | collective-permute-start | bytes 516104 | tf_op jit(solution)/shard_map/ppermute | solution.py:342
  8.6 3.1 %collective-permute-start = (f32[384,128]{1,0:T(8,128)S(1)}, f32[384,128]{1,0:T(8,128)S(1)}, u32[]{:S(2)}, u32[]{:S(2)}) collective-permute-start(f32[384,128]{1,0:T(8,128)S(1)} %get-tuple-element.47), channel_id=1, source_target_pairs={{0,1},{1,0},{2,3},{3,2},{4,5},{5,4},{6,7},{7,6},{8,9},{9,8},{10,11... | collective-permute-start | bytes 589832 | tf_op jit(solution)/shard_map/ppermute | solution.py:342
  8.6 6.4 %collective-permute-start.1 = (f32[384,128]{1,0:T(8,128)S(1)}, f32[384,128]{1,0:T(8,128)S(1)}, u32[]{:S(2)}, u32[]{:S(2)}) collective-permute-start(f32[384,128]{1,0:T(8,128)S(1)} %get-tuple-element.48), channel_id=1, source_target_pairs={{0,8},{1,2},{2,1},{3,4},{4,3},{5,6},{6,5},{7,15},{8,0},{9,10},{10,... | collective-permute-start | bytes 589832 | tf_op jit(solution)/shard_map/ppermute | solution.py:342
  15.9 4.8 %collective-permute-start.4 = (f32[96,128]{1,0:T(8,128)S(1)}, f32[96,128]{1,0:T(8,128)S(1)}, u32[]{:S(2)}, u32[]{:S(2)}) collective-permute-start(f32[96,128]{1,0:T(8,128)S(1)} %pad_maximum_fusion.7), channel_id=1, source_target_pairs={{0,16},{1,17},{2,18},{3,19},{4,20},{5,21},{6,22},{7,23},{8,24},{9,... | collective-permute-start | bytes 147464 | tf_op jit(solution)/shard_map/ppermute | solution.py:342
  20.6 5.7 %collective-permute-start.5 = (f32[192,128]{1,0:T(8,128)S(1)}, f32[192,128]{1,0:T(8,128)S(1)}, u32[]{:S(2)}, u32[]{:S(2)}) collective-permute-start(f32[192,128]{1,0:T(8,128)S(1)} %pad_maximum_fusion.2), channel_id=1, source_target_pairs={{0,8},{1,9},{2,10},{3,11},{4,12},{5,13},{6,14},{7,15},{8,0},{9,1},... | collective-permute-start | bytes 294920 | tf_op jit(solution)/shard_map/ppermute | solution.py:342
  26.6 7.0 %collective-permute-start.10 = (f32[48,128]{1,0:T(8,128)S(1)}, f32[48,128]{1,0:T(8,128)S(1)}, u32[]{:S(2)}, u32[]{:S(2)}) collective-permute-start(f32[48,128]{1,0:T(8,128)S(1)} %shard_map.113.refs_0_), channel_id=1, source_target_pairs={{0,1},{1,0},{2,3},{3,2},{4,5},{5,4},{6,7},{7,6},{8,9},{9,8},{10,11... | collective-permute-start | bytes 73736 | tf_op jit(solution)/shard_map/ppermute | solution.py:342
  28.7 15.0 %collective-permute-start.8 = (f32[160,128]{1,0:T(8,128)S(1)}, f32[160,128]{1,0:T(8,128)S(1)}, u32[]{:S(2)}, u32[]{:S(2)}) collective-permute-start(f32[160,128]{1,0:T(8,128)S(1)} %get-tuple-element.62), channel_id=1, source_target_pairs={{0,8},{1,9},{2,10},{3,11},{4,12},{5,13},{6,14},{7,15},{8,0},{9,1},... | collective-permute-start | bytes 245768 | tf_op jit(solution)/shard_map/ppermute | solution.py:342
  30.2 13.5 %collective-permute-start.9 = (f32[160,128]{1,0:T(8,128)S(1)}, f32[160,128]{1,0:T(8,128)S(1)}, u32[]{:S(2)}, u32[]{:S(2)}) collective-permute-start(f32[160,128]{1,0:T(8,128)S(1)} %get-tuple-element.63), channel_id=1, source_target_pairs={{0,1},{1,0},{2,3},{3,2},{4,5},{5,4},{6,7},{7,6},{8,16},{9,17},{10,... | collective-permute-start | bytes 245768 | tf_op jit(solution)/shard_map/ppermute | solution.py:342
  30.5 10.1 %copy-start = (f32[1,1,640,640]{3,2,1,0:T(8,128)S(1)}, f32[1,1,640,640]{3,2,1,0:T(8,128)}, u32[]{:S(2)}) copy-start(f32[1,1,640,640]{3,2,1,0:T(8,128)} %param.10) | copy-start | bytes 4915204
  33.6 3.6 %collective-permute-start.11 = (f32[96,128]{1,0:T(8,128)S(1)}, f32[96,128]{1,0:T(8,128)S(1)}, u32[]{:S(2)}, u32[]{:S(2)}) collective-permute-start(f32[96,128]{1,0:T(8,128)S(1)} %pad_maximum_fusion.8), channel_id=1, source_target_pairs={{0,3},{1,2},{2,1},{3,0},{4,7},{5,6},{6,5},{7,4},{8,11},{9,10},{10,... | collective-permute-start | bytes 147464 | tf_op jit(solution)/shard_map/ppermute | solution.py:342
  35.1 8.6 %collective-permute-start.7 = (f32[160,128]{1,0:T(8,128)S(1)}, f32[160,128]{1,0:T(8,128)S(1)}, u32[]{:S(2)}, u32[]{:S(2)}) collective-permute-start(f32[160,128]{1,0:T(8,128)S(1)} %get-tuple-element.110), channel_id=1, source_target_pairs={{0,8},{1,2},{2,1},{3,4},{4,3},{5,6},{6,5},{7,15},{8,0},{9,10},{10,... | collective-permute-start | bytes 245768 | tf_op jit(solution)/shard_map/ppermute | solution.py:342
  35.5 8.3 %collective-permute-start.6 = (f32[160,128]{1,0:T(8,128)S(1)}, f32[160,128]{1,0:T(8,128)S(1)}, u32[]{:S(2)}, u32[]{:S(2)}) collective-permute-start(f32[160,128]{1,0:T(8,128)S(1)} %get-tuple-element.111), channel_id=1, source_target_pairs={{0,1},{1,0},{2,3},{3,2},{4,5},{5,4},{6,7},{7,6},{8,9},{9,8},{10,11... | collective-permute-start | bytes 245768 | tf_op jit(solution)/shard_map/ppermute | solution.py:342
  37.2 6.8 %collective-permute-start.12 = (f32[192,128]{1,0:T(8,128)S(1)}, f32[192,128]{1,0:T(8,128)S(1)}, u32[]{:S(2)}, u32[]{:S(2)}) collective-permute-start(f32[192,128]{1,0:T(8,128)S(1)} %pad_maximum_fusion.3), channel_id=1, source_target_pairs={{0,5},{1,4},{2,7},{3,6},{4,1},{5,0},{6,3},{7,2},{8,13},{9,12},{10,... | collective-permute-start | bytes 294920 | tf_op jit(solution)/shard_map/ppermute | solution.py:342
  46.3 2.6 %collective-permute-start.16 = (f32[160,128]{1,0:T(8,128)S(1)}, f32[160,128]{1,0:T(8,128)S(1)}, u32[]{:S(2)}, u32[]{:S(2)}) collective-permute-start(f32[160,128]{1,0:T(8,128)S(1)} %get-tuple-element.106), channel_id=1, source_target_pairs={{0,1},{1,0},{2,3},{3,2},{4,5},{5,4},{6,7},{7,6},{8,16},{9,17},{10,... | collective-permute-start | bytes 245768 | tf_op jit(solution)/shard_map/ppermute | solution.py:342
  46.8 3.9 %collective-permute-start.15 = (f32[160,128]{1,0:T(8,128)S(1)}, f32[160,128]{1,0:T(8,128)S(1)}, u32[]{:S(2)}, u32[]{:S(2)}) collective-permute-start(f32[160,128]{1,0:T(8,128)S(1)} %get-tuple-element.107), channel_id=1, source_target_pairs={{0,8},{1,9},{2,10},{3,11},{4,12},{5,13},{6,14},{7,15},{8,0},{9,1},... | collective-permute-start | bytes 245768 | tf_op jit(solution)/shard_map/ppermute | solution.py:342
  47.6 4.2 %collective-permute-start.14 = (f32[160,128]{1,0:T(8,128)S(1)}, f32[160,128]{1,0:T(8,128)S(1)}, u32[]{:S(2)}, u32[]{:S(2)}) collective-permute-start(f32[160,128]{1,0:T(8,128)S(1)} %get-tuple-element.108), channel_id=1, source_target_pairs={{0,8},{1,2},{2,1},{3,4},{4,3},{5,6},{6,5},{7,15},{8,0},{9,10},{10,... | collective-permute-start | bytes 245768 | tf_op jit(solution)/shard_map/ppermute | solution.py:342
  48.2 3.7 %collective-permute-start.13 = (f32[160,128]{1,0:T(8,128)S(1)}, f32[160,128]{1,0:T(8,128)S(1)}, u32[]{:S(2)}, u32[]{:S(2)}) collective-permute-start(f32[160,128]{1,0:T(8,128)S(1)} %get-tuple-element.109), channel_id=1, source_target_pairs={{0,1},{1,0},{2,3},{3,2},{4,5},{5,4},{6,7},{7,6},{8,9},{9,8},{10,11... | collective-permute-start | bytes 245768 | tf_op jit(solution)/shard_map/ppermute | solution.py:342
  52.6 3.6 %collective-permute-start.17 = (f32[48,128]{1,0:T(8,128)S(1)}, f32[48,128]{1,0:T(8,128)S(1)}, u32[]{:S(2)}, u32[]{:S(2)}) collective-permute-start(f32[48,128]{1,0:T(8,128)S(1)} %get-tuple-element.68.refs_0_), channel_id=1, source_target_pairs={{0,16},{1,17},{2,18},{3,19},{4,20},{5,21},{6,22},{7,23},{8,24},{9,... | collective-permute-start | bytes 73736 | tf_op jit(solution)/shard_map/ppermute | solution.py:342
  56.3 2.9 %collective-permute-start.18 = (f32[96,128]{1,0:T(8,128)S(1)}, f32[96,128]{1,0:T(8,128)S(1)}, u32[]{:S(2)}, u32[]{:S(2)}) collective-permute-start(f32[96,128]{1,0:T(8,128)S(1)} %pad_maximum_fusion.9), channel_id=1, source_target_pairs={{0,8},{1,9},{2,10},{3,11},{4,12},{5,13},{6,14},{7,15},{8,0},{9,1},... | collective-permute-start | bytes 147464 | tf_op jit(solution)/shard_map/ppermute | solution.py:342
  59.4 4.4 %collective-permute-start.23 = (f32[48,128]{1,0:T(8,128)S(1)}, f32[48,128]{1,0:T(8,128)S(1)}, u32[]{:S(2)}, u32[]{:S(2)}) collective-permute-start(f32[48,128]{1,0:T(8,128)S(1)} %shard_map.118.refs_1_), channel_id=1, source_target_pairs={{0,1},{1,0},{2,3},{3,2},{4,5},{5,4},{6,7},{7,6},{8,9},{9,8},{10,11... | collective-permute-start | bytes 73736 | tf_op jit(solution)/shard_map/ppermute | solution.py:342
  63.8 3.7 %collective-permute-start.24 = (f32[96,128]{1,0:T(8,128)S(1)}, f32[96,128]{1,0:T(8,128)S(1)}, u32[]{:S(2)}, u32[]{:S(2)}) collective-permute-start(f32[96,128]{1,0:T(8,128)S(1)} %pad_maximum_fusion.10), channel_id=1, source_target_pairs={{0,3},{1,2},{2,1},{3,0},{4,7},{5,6},{6,5},{7,4},{8,11},{9,10},{10,... | collective-permute-start | bytes 147464 | tf_op jit(solution)/shard_map/ppermute | solution.py:342
  65.3 6.3 %collective-permute-start.21 = (f32[160,128]{1,0:T(8,128)S(1)}, f32[160,128]{1,0:T(8,128)S(1)}, u32[]{:S(2)}, u32[]{:S(2)}) collective-permute-start(f32[160,128]{1,0:T(8,128)S(1)} %get-tuple-element.69), channel_id=1, source_target_pairs={{0,8},{1,9},{2,10},{3,11},{4,12},{5,13},{6,14},{7,15},{8,0},{9,1},... | collective-permute-start | bytes 245768 | tf_op jit(solution)/shard_map/ppermute | solution.py:342
  65.9 5.7 %collective-permute-start.22 = (f32[160,128]{1,0:T(8,128)S(1)}, f32[160,128]{1,0:T(8,128)S(1)}, u32[]{:S(2)}, u32[]{:S(2)}) collective-permute-start(f32[160,128]{1,0:T(8,128)S(1)} %get-tuple-element.70), channel_id=1, source_target_pairs={{0,1},{1,0},{2,3},{3,2},{4,5},{5,4},{6,7},{7,6},{8,16},{9,17},{10,... | collective-permute-start | bytes 245768 | tf_op jit(solution)/shard_map/ppermute | solution.py:342
  67.5 6.1 %collective-permute-start.25 = (f32[192,128]{1,0:T(8,128)S(1)}, f32[192,128]{1,0:T(8,128)S(1)}, u32[]{:S(2)}, u32[]{:S(2)}) collective-permute-start(f32[192,128]{1,0:T(8,128)S(1)} %pad_maximum_fusion.4), channel_id=1, source_target_pairs={{0,5},{1,4},{2,7},{3,6},{4,1},{5,0},{6,3},{7,2},{8,13},{9,12},{10,... | collective-permute-start | bytes 294920 | tf_op jit(solution)/shard_map/ppermute | solution.py:342
  69.2 4.4 %collective-permute-start.20 = (f32[160,128]{1,0:T(8,128)S(1)}, f32[160,128]{1,0:T(8,128)S(1)}, u32[]{:S(2)}, u32[]{:S(2)}) collective-permute-start(f32[160,128]{1,0:T(8,128)S(1)} %get-tuple-element.104), channel_id=1, source_target_pairs={{0,8},{1,2},{2,1},{3,4},{4,3},{5,6},{6,5},{7,15},{8,0},{9,10},{10,... | collective-permute-start | bytes 245768 | tf_op jit(solution)/shard_map/ppermute | solution.py:342
  70.8 2.8 %collective-permute-start.19 = (f32[160,128]{1,0:T(8,128)S(1)}, f32[160,128]{1,0:T(8,128)S(1)}, u32[]{:S(2)}, u32[]{:S(2)}) collective-permute-start(f32[160,128]{1,0:T(8,128)S(1)} %get-tuple-element.105), channel_id=1, source_target_pairs={{0,1},{1,0},{2,3},{3,2},{4,5},{5,4},{6,7},{7,6},{8,9},{9,8},{10,11... | collective-permute-start | bytes 245768 | tf_op jit(solution)/shard_map/ppermute | solution.py:342
  75.9 3.8 %collective-permute-start.29 = (f32[160,128]{1,0:T(8,128)S(1)}, f32[160,128]{1,0:T(8,128)S(1)}, u32[]{:S(2)}, u32[]{:S(2)}) collective-permute-start(f32[160,128]{1,0:T(8,128)S(1)} %get-tuple-element.100), channel_id=1, source_target_pairs={{0,1},{1,0},{2,3},{3,2},{4,5},{5,4},{6,7},{7,6},{8,16},{9,17},{10,... | collective-permute-start | bytes 245768 | tf_op jit(solution)/shard_map/ppermute | solution.py:342
  76.4 4.2 %collective-permute-start.28 = (f32[160,128]{1,0:T(8,128)S(1)}, f32[160,128]{1,0:T(8,128)S(1)}, u32[]{:S(2)}, u32[]{:S(2)}) collective-permute-start(f32[160,128]{1,0:T(8,128)S(1)} %get-tuple-element.101), channel_id=1, source_target_pairs={{0,8},{1,9},{2,10},{3,11},{4,12},{5,13},{6,14},{7,15},{8,0},{9,1},... | collective-permute-start | bytes 245768 | tf_op jit(solution)/shard_map/ppermute | solution.py:342
  78.1 4.2 %collective-permute-start.27 = (f32[160,128]{1,0:T(8,128)S(1)}, f32[160,128]{1,0:T(8,128)S(1)}, u32[]{:S(2)}, u32[]{:S(2)}) collective-permute-start(f32[160,128]{1,0:T(8,128)S(1)} %get-tuple-element.102), channel_id=1, source_target_pairs={{0,8},{1,2},{2,1},{3,4},{4,3},{5,6},{6,5},{7,15},{8,0},{9,10},{10,... | collective-permute-start | bytes 245768 | tf_op jit(solution)/shard_map/ppermute | solution.py:342
  79.7 2.6 %collective-permute-start.26 = (f32[160,128]{1,0:T(8,128)S(1)}, f32[160,128]{1,0:T(8,128)S(1)}, u32[]{:S(2)}, u32[]{:S(2)}) collective-permute-start(f32[160,128]{1,0:T(8,128)S(1)} %get-tuple-element.103), channel_id=1, source_target_pairs={{0,1},{1,0},{2,3},{3,2},{4,5},{5,4},{6,7},{7,6},{8,9},{9,8},{10,11... | collective-permute-start | bytes 245768 | tf_op jit(solution)/shard_map/ppermute | solution.py:342
  83.1 3.6 %collective-permute-start.30 = (f32[48,128]{1,0:T(8,128)S(1)}, f32[48,128]{1,0:T(8,128)S(1)}, u32[]{:S(2)}, u32[]{:S(2)}) collective-permute-start(f32[48,128]{1,0:T(8,128)S(1)} %get-tuple-element.75.refs_0_), channel_id=1, source_target_pairs={{0,16},{1,17},{2,18},{3,19},{4,20},{5,21},{6,22},{7,23},{8,24},{9,... | collective-permute-start | bytes 73736 | tf_op jit(solution)/shard_map/ppermute | solution.py:342
  86.7 2.9 %collective-permute-start.31 = (f32[96,128]{1,0:T(8,128)S(1)}, f32[96,128]{1,0:T(8,128)S(1)}, u32[]{:S(2)}, u32[]{:S(2)}) collective-permute-start(f32[96,128]{1,0:T(8,128)S(1)} %pad_maximum_fusion.11), channel_id=1, source_target_pairs={{0,8},{1,9},{2,10},{3,11},{4,12},{5,13},{6,14},{7,15},{8,0},{9,1},... | collective-permute-start | bytes 147464 | tf_op jit(solution)/shard_map/ppermute | solution.py:342
  89.8 4.1 %collective-permute-start.36 = (f32[48,128]{1,0:T(8,128)S(1)}, f32[48,128]{1,0:T(8,128)S(1)}, u32[]{:S(2)}, u32[]{:S(2)}) collective-permute-start(f32[48,128]{1,0:T(8,128)S(1)} %shard_map.123.refs_1_), channel_id=1, source_target_pairs={{0,1},{1,0},{2,3},{3,2},{4,5},{5,4},{6,7},{7,6},{8,9},{9,8},{10,11... | collective-permute-start | bytes 73736 | tf_op jit(solution)/shard_map/ppermute | solution.py:342
  93.9 4.7 %collective-permute-start.37 = (f32[96,128]{1,0:T(8,128)S(1)}, f32[96,128]{1,0:T(8,128)S(1)}, u32[]{:S(2)}, u32[]{:S(2)}) collective-permute-start(f32[96,128]{1,0:T(8,128)S(1)} %pad_maximum_fusion.12), channel_id=1, source_target_pairs={{0,3},{1,2},{2,1},{3,0},{4,7},{5,6},{6,5},{7,4},{8,11},{9,10},{10,... | collective-permute-start | bytes 147464 | tf_op jit(solution)/shard_map/ppermute | solution.py:342
  96.6 5.6 %collective-permute-start.34 = (f32[160,128]{1,0:T(8,128)S(1)}, f32[160,128]{1,0:T(8,128)S(1)}, u32[]{:S(2)}, u32[]{:S(2)}) collective-permute-start(f32[160,128]{1,0:T(8,128)S(1)} %get-tuple-element.76), channel_id=1, source_target_pairs={{0,8},{1,9},{2,10},{3,11},{4,12},{5,13},{6,14},{7,15},{8,0},{9,1},... | collective-permute-start | bytes 245768 | tf_op jit(solution)/shard_map/ppermute | solution.py:342
  97.3 4.9 %collective-permute-start.35 = (f32[160,128]{1,0:T(8,128)S(1)}, f32[160,128]{1,0:T(8,128)S(1)}, u32[]{:S(2)}, u32[]{:S(2)}) collective-permute-start(f32[160,128]{1,0:T(8,128)S(1)} %get-tuple-element.77), channel_id=1, source_target_pairs={{0,1},{1,0},{2,3},{3,2},{4,5},{5,4},{6,7},{7,6},{8,16},{9,17},{10,... | collective-permute-start | bytes 245768 | tf_op jit(solution)/shard_map/ppermute | solution.py:342
  98.6 5.8 %collective-permute-start.38 = (f32[192,128]{1,0:T(8,128)S(1)}, f32[192,128]{1,0:T(8,128)S(1)}, u32[]{:S(2)}, u32[]{:S(2)}) collective-permute-start(f32[192,128]{1,0:T(8,128)S(1)} %pad_maximum_fusion.5), channel_id=1, source_target_pairs={{0,5},{1,4},{2,7},{3,6},{4,1},{5,0},{6,3},{7,2},{8,13},{9,12},{10,... | collective-permute-start | bytes 294920 | tf_op jit(solution)/shard_map/ppermute | solution.py:342
  100.0 4.4 %collective-permute-start.33 = (f32[160,128]{1,0:T(8,128)S(1)}, f32[160,128]{1,0:T(8,128)S(1)}, u32[]{:S(2)}, u32[]{:S(2)}) collective-permute-start(f32[160,128]{1,0:T(8,128)S(1)} %get-tuple-element.98), channel_id=1, source_target_pairs={{0,8},{1,2},{2,1},{3,4},{4,3},{5,6},{6,5},{7,15},{8,0},{9,10},{10,... | collective-permute-start | bytes 245768 | tf_op jit(solution)/shard_map/ppermute | solution.py:342
  101.0 3.4 %collective-permute-start.32 = (f32[160,128]{1,0:T(8,128)S(1)}, f32[160,128]{1,0:T(8,128)S(1)}, u32[]{:S(2)}, u32[]{:S(2)}) collective-permute-start(f32[160,128]{1,0:T(8,128)S(1)} %get-tuple-element.99), channel_id=1, source_target_pairs={{0,1},{1,0},{2,3},{3,2},{4,5},{5,4},{6,7},{7,6},{8,9},{9,8},{10,11... | collective-permute-start | bytes 245768 | tf_op jit(solution)/shard_map/ppermute | solution.py:342
  106.7 3.5 %collective-permute-start.42 = (f32[160,128]{1,0:T(8,128)S(1)}, f32[160,128]{1,0:T(8,128)S(1)}, u32[]{:S(2)}, u32[]{:S(2)}) collective-permute-start(f32[160,128]{1,0:T(8,128)S(1)} %get-tuple-element.94), channel_id=1, source_target_pairs={{0,1},{1,0},{2,3},{3,2},{4,5},{5,4},{6,7},{7,6},{8,16},{9,17},{10,... | collective-permute-start | bytes 245768 | tf_op jit(solution)/shard_map/ppermute | solution.py:342
  107.1 4.6 %collective-permute-start.41 = (f32[160,128]{1,0:T(8,128)S(1)}, f32[160,128]{1,0:T(8,128)S(1)}, u32[]{:S(2)}, u32[]{:S(2)}) collective-permute-start(f32[160,128]{1,0:T(8,128)S(1)} %get-tuple-element.95), channel_id=1, source_target_pairs={{0,8},{1,9},{2,10},{3,11},{4,12},{5,13},{6,14},{7,15},{8,0},{9,1},... | collective-permute-start | bytes 245768 | tf_op jit(solution)/shard_map/ppermute | solution.py:342
  109.0 4.2 %collective-permute-start.40 = (f32[160,128]{1,0:T(8,128)S(1)}, f32[160,128]{1,0:T(8,128)S(1)}, u32[]{:S(2)}, u32[]{:S(2)}) collective-permute-start(f32[160,128]{1,0:T(8,128)S(1)} %get-tuple-element.96), channel_id=1, source_target_pairs={{0,8},{1,2},{2,1},{3,4},{4,3},{5,6},{6,5},{7,15},{8,0},{9,10},{10,... | collective-permute-start | bytes 245768 | tf_op jit(solution)/shard_map/ppermute | solution.py:342
  110.3 2.9 %collective-permute-start.39 = (f32[160,128]{1,0:T(8,128)S(1)}, f32[160,128]{1,0:T(8,128)S(1)}, u32[]{:S(2)}, u32[]{:S(2)}) collective-permute-start(f32[160,128]{1,0:T(8,128)S(1)} %get-tuple-element.97), channel_id=1, source_target_pairs={{0,1},{1,0},{2,3},{3,2},{4,5},{5,4},{6,7},{7,6},{8,9},{9,8},{10,11... | collective-permute-start | bytes 245768 | tf_op jit(solution)/shard_map/ppermute | solution.py:342
  113.9 3.9 %collective-permute-start.43 = (f32[48,128]{1,0:T(8,128)S(1)}, f32[48,128]{1,0:T(8,128)S(1)}, u32[]{:S(2)}, u32[]{:S(2)}) collective-permute-start(f32[48,128]{1,0:T(8,128)S(1)} %get-tuple-element.82.refs_0_), channel_id=1, source_target_pairs={{0,16},{1,17},{2,18},{3,19},{4,20},{5,21},{6,22},{7,23},{8,24},{9,... | collective-permute-start | bytes 73736 | tf_op jit(solution)/shard_map/ppermute | solution.py:342
  117.8 2.9 %collective-permute-start.44 = (f32[96,128]{1,0:T(8,128)S(1)}, f32[96,128]{1,0:T(8,128)S(1)}, u32[]{:S(2)}, u32[]{:S(2)}) collective-permute-start(f32[96,128]{1,0:T(8,128)S(1)} %pad_maximum_fusion.13), channel_id=1, source_target_pairs={{0,8},{1,9},{2,10},{3,11},{4,12},{5,13},{6,14},{7,15},{8,0},{9,1},... | collective-permute-start | bytes 147464 | tf_op jit(solution)/shard_map/ppermute | solution.py:342
  120.9 3.6 %collective-permute-start.49 = (f32[48,128]{1,0:T(8,128)S(1)}, f32[48,128]{1,0:T(8,128)S(1)}, u32[]{:S(2)}, u32[]{:S(2)}) collective-permute-start(f32[48,128]{1,0:T(8,128)S(1)} %shard_map.128.refs_1_), channel_id=1, source_target_pairs={{0,1},{1,0},{2,3},{3,2},{4,5},{5,4},{6,7},{7,6},{8,9},{9,8},{10,11... | collective-permute-start | bytes 73736 | tf_op jit(solution)/shard_map/ppermute | solution.py:342
  124.5 4.3 %collective-permute-start.50 = (f32[96,128]{1,0:T(8,128)S(1)}, f32[96,128]{1,0:T(8,128)S(1)}, u32[]{:S(2)}, u32[]{:S(2)}) collective-permute-start(f32[96,128]{1,0:T(8,128)S(1)} %pad_maximum_fusion.14), channel_id=1, source_target_pairs={{0,3},{1,2},{2,1},{3,0},{4,7},{5,6},{6,5},{7,4},{8,11},{9,10},{10,... | collective-permute-start | bytes 147464 | tf_op jit(solution)/shard_map/ppermute | solution.py:342
  127.1 5.8 %collective-permute-start.47 = (f32[160,128]{1,0:T(8,128)S(1)}, f32[160,128]{1,0:T(8,128)S(1)}, u32[]{:S(2)}, u32[]{:S(2)}) collective-permute-start(f32[160,128]{1,0:T(8,128)S(1)} %get-tuple-element.83), channel_id=1, source_target_pairs={{0,8},{1,9},{2,10},{3,11},{4,12},{5,13},{6,14},{7,15},{8,0},{9,1},... | collective-permute-start | bytes 245768 | tf_op jit(solution)/shard_map/ppermute | solution.py:342
  127.5 5.4 %collective-permute-start.48 = (f32[160,128]{1,0:T(8,128)S(1)}, f32[160,128]{1,0:T(8,128)S(1)}, u32[]{:S(2)}, u32[]{:S(2)}) collective-permute-start(f32[160,128]{1,0:T(8,128)S(1)} %get-tuple-element.84), channel_id=1, source_target_pairs={{0,1},{1,0},{2,3},{3,2},{4,5},{5,4},{6,7},{7,6},{8,16},{9,17},{10,... | collective-permute-start | bytes 245768 | tf_op jit(solution)/shard_map/ppermute | solution.py:342
  128.9 6.1 %collective-permute-start.51 = (f32[192,128]{1,0:T(8,128)S(1)}, f32[192,128]{1,0:T(8,128)S(1)}, u32[]{:S(2)}, u32[]{:S(2)}) collective-permute-start(f32[192,128]{1,0:T(8,128)S(1)} %pad_maximum_fusion.6), channel_id=1, source_target_pairs={{0,5},{1,4},{2,7},{3,6},{4,1},{5,0},{6,3},{7,2},{8,13},{9,12},{10,... | collective-permute-start | bytes 294920 | tf_op jit(solution)/shard_map/ppermute | solution.py:342
  130.6 4.3 %collective-permute-start.46 = (f32[160,128]{1,0:T(8,128)S(1)}, f32[160,128]{1,0:T(8,128)S(1)}, u32[]{:S(2)}, u32[]{:S(2)}) collective-permute-start(f32[160,128]{1,0:T(8,128)S(1)} %get-tuple-element.92), channel_id=1, source_target_pairs={{0,8},{1,2},{2,1},{3,4},{4,3},{5,6},{6,5},{7,15},{8,0},{9,10},{10,... | collective-permute-start | bytes 245768 | tf_op jit(solution)/shard_map/ppermute | solution.py:342
  131.5 3.4 %collective-permute-start.45 = (f32[160,128]{1,0:T(8,128)S(1)}, f32[160,128]{1,0:T(8,128)S(1)}, u32[]{:S(2)}, u32[]{:S(2)}) collective-permute-start(f32[160,128]{1,0:T(8,128)S(1)} %get-tuple-element.93), channel_id=1, source_target_pairs={{0,1},{1,0},{2,3},{3,2},{4,5},{5,4},{6,7},{7,6},{8,9},{9,8},{10,11... | collective-permute-start | bytes 245768 | tf_op jit(solution)/shard_map/ppermute | solution.py:342
  137.2 5.0 %collective-permute-start.55 = (f32[160,128]{1,0:T(8,128)S(1)}, f32[160,128]{1,0:T(8,128)S(1)}, u32[]{:S(2)}, u32[]{:S(2)}) collective-permute-start(f32[160,128]{1,0:T(8,128)S(1)} %get-tuple-element.88), channel_id=1, source_target_pairs={{0,1},{1,0},{2,3},{3,2},{4,5},{5,4},{6,7},{7,6},{8,16},{9,17},{10,... | collective-permute-start | bytes 245768 | tf_op jit(solution)/shard_map/ppermute | solution.py:342
  137.9 4.3 %collective-permute-start.54 = (f32[160,128]{1,0:T(8,128)S(1)}, f32[160,128]{1,0:T(8,128)S(1)}, u32[]{:S(2)}, u32[]{:S(2)}) collective-permute-start(f32[160,128]{1,0:T(8,128)S(1)} %get-tuple-element.89), channel_id=1, source_target_pairs={{0,8},{1,9},{2,10},{3,11},{4,12},{5,13},{6,14},{7,15},{8,0},{9,1},... | collective-permute-start | bytes 245768 | tf_op jit(solution)/shard_map/ppermute | solution.py:342
  139.5 4.2 %collective-permute-start.53 = (f32[160,128]{1,0:T(8,128)S(1)}, f32[160,128]{1,0:T(8,128)S(1)}, u32[]{:S(2)}, u32[]{:S(2)}) collective-permute-start(f32[160,128]{1,0:T(8,128)S(1)} %get-tuple-element.90), channel_id=1, source_target_pairs={{0,8},{1,2},{2,1},{3,4},{4,3},{5,6},{6,5},{7,15},{8,0},{9,10},{10,... | collective-permute-start | bytes 245768 | tf_op jit(solution)/shard_map/ppermute | solution.py:342
  140.8 2.8 %collective-permute-start.52 = (f32[160,128]{1,0:T(8,128)S(1)}, f32[160,128]{1,0:T(8,128)S(1)}, u32[]{:S(2)}, u32[]{:S(2)}) collective-permute-start(f32[160,128]{1,0:T(8,128)S(1)} %get-tuple-element.91), channel_id=1, source_target_pairs={{0,1},{1,0},{2,3},{3,2},{4,5},{5,4},{6,7},{7,6},{8,9},{9,8},{10,11... | collective-permute-start | bytes 245768 | tf_op jit(solution)/shard_map/ppermute | solution.py:342

commit v5 on v4

--- a/solution.py
+++ b/solution.py
@@ -190,7 +190,7 @@
 
 
 def level_kernel(
-    face, link_ref, basis_ref, inverse_ref, coarse_ref, top_ref, e_ref, f_ref, g_ref, h_ref, two_ref, top_out_ref
+    face, link_ref, order_ref, basis_ref, inverse_ref, coarse_ref, top_ref, e_ref, f_ref, g_ref, h_ref, two_ref, own_ref, far_ref
 ):
     coarse, total = inverse_ref.shape
     top, width = top_ref.shape
@@ -212,7 +212,19 @@
         rows = slice(k * face, (k + 1) * face)
         near = stack_split(unpack_halves(ref, face, face, top) * link[k])
         outs.append(out[rows] + product(near, unpack(ref, start, top, width)))
-    top_out_ref[...] = stack_split(jnp.concatenate(outs + [out[2 * face :]], axis=0))
+    out = jnp.concatenate(outs + [out[2 * face :]], axis=0)
+    low, high = out[:, : width // 2], out[:, width // 2 :]
+    near = order_ref[0] < width // 2
+    own_ref[...] = stack_split(jnp.where(near, low, high))
+    far_ref[...] = stack_split(jnp.where(near, high, low))
+
+
+def cross_kernel(schur_ref, far_ref, out_ref):
+    rows = far_ref.shape[0] // 2
+    parts = [far_ref[:rows], far_ref[rows:]]
+    out_ref[:rows], out_ref[2 * rows : 3 * rows] = parts
+    hi, lo = split(product_parts(schur_ref[...], parts), 2)
+    out_ref[rows : 2 * rows], out_ref[3 * rows :] = hi, lo
 
 
 def received(face, link_ref, refs):
@@ -272,18 +284,46 @@
     y2_ref[...] = y_ref[...] + product(two_ref[...], stack_ref[...])
 
 
+def stacked(order_ref, slot, top, refs, stack_ref):
+    for ref in refs:
+        for start in range(0, ref.shape[0], top):
+            offset = lax.rem(order_ref[slot], stack_ref.shape[0])
+            stack_ref[pl.ds(pl.multiple_of(offset, 8), top)] = ref[start : start + top]
+            slot += 1
+    return stack_ref[...]
+
+
+def partial_kernel(weight, face, top, link_ref, order_ref, y2_ref, r0, r1, r2, r3, own_ref, schur_ref, old_ref, *refs):
+    x_ref, out_ref, stack_ref = refs[-3:]
+    known = stacked(order_ref, 0, top, refs[:-3], stack_ref)
+    update = y2_ref[...] + received(face, link_ref, (r0, r1, r2, r3)) + product(own_ref[...], known)
+    x = old_ref[...] + weight * update
+    x_ref[...] = x
+    out_ref[...] = product(schur_ref[...], x)
+
+
+def finish_kernel(weight, top, slot, order_ref, partial_ref, field_ref, cross_ref, more_ref, x_ref, out_ref, stack_ref):
+    rows = partial_ref.shape[0]
+    more = weight * product(cross_ref[...], stacked(order_ref, slot, top, [more_ref], stack_ref))
+    x_ref[...] = partial_ref[...] + more[:rows]
+    out_ref[...] = field_ref[...] + more[rows:]
+
+
 def update_kernel(
-    weight, first, face, top, link_ref, order_ref, y2_ref, r0, r1, r2, r3, top_ref, schur_ref, *refs
+    weight, first, face, top, link_ref, order_ref, y2_ref, r0, r1, r2, r3, own_ref, far_ref, schur_ref, *refs
 ):
     if not first:
         old_ref, refs = refs[0], refs[1:]
     x_ref, out_ref, stack_ref = refs[-3:]
-    slot = 0
+    slot, half = 0, stack_ref.shape[0] // 2
     for ref in refs[:-3]:
         for start in range(0, ref.shape[0], top):
-            stack_ref[pl.ds(pl.multiple_of(order_ref[slot], 8), top)] = ref[start : start + top]
+            side = slot * top // half * half
+            offset = side + lax.rem(order_ref[slot], half)
+            stack_ref[pl.ds(pl.multiple_of(offset, 8), top)] = ref[start : start + top]
             slot += 1
-    update = y2_ref[...] + received(face, link_ref, (r0, r1, r2, r3)) + product(top_ref[...], stack_ref[...])
+    update = y2_ref[...] + received(face, link_ref, (r0, r1, r2, r3))
+    update = update + product(own_ref[...], stack_ref[:half]) + product(far_ref[...], stack_ref[half:])
     x = weight * update
     if not first:
         x = old_ref[...] + x
@@ -396,19 +436,20 @@
     schur2 = folded(schur[0, 0], back)
 
     got = exchange(sent)
-    two2, top2 = call(
-        functools.partial(level_kernel, face),
-        [((2 * size, total), BF16), ((2 * size, width), BF16)],
-        [link],
-        [basis_f, inverse_rows, coarse_f, top_inverse] + got,
-    )
-
     doubling = cols & (cols - 1) == 0
     col_order = jnp.arange(cols, dtype=jnp.int32)
     if doubling:
         rest = sum((col_order >> i & 1) for i in range(1, cols.bit_length() - 1))
         col_order = col ^ col_order ^ (rest & 1)
     col_order = col_order * top
+    two2, own2, far2 = call(
+        functools.partial(level_kernel, face),
+        [((2 * size, total), BF16)] + [((2 * size, width // 2), BF16)] * 2,
+        [link, col_order],
+        [basis_f, inverse_rows, coarse_f, top_inverse] + got,
+    )
+    cross2 = call(cross_kernel, [((4 * size, width // 2), BF16)], [], [schur2, far2], flops=12 * size**2 * width)[0]
+
     row_order = jnp.arange(rows, dtype=jnp.int32)
     if row_pairs:
         row_order = row ^ ((row_order & 1) * 2 + row_order // 2)
@@ -478,14 +519,33 @@
                 bits *= 2
         else:
             tops = [lax.all_gather(third, "col", axis=0, tiled=True)]
-        solution, field = call(
-            functools.partial(update_kernel, weight, first, face, top),
-            [(n, F32), (n, F32)],
-            [link, col_order],
-            [y2, got_e, got_f, got_g, got_h, top2, schur2] + ([] if first else [solution]) + tops,
-            flops=2 * square,
-            scratch=[(width, columns)],
-        )
+        out = [y2, got_e, got_f, got_g, got_h]
+        if first or not doubling:
+            solution, field = call(
+                functools.partial(update_kernel, weight, first, face, top),
+                [(n, F32), (n, F32)],
+                [link, col_order],
+                out + [own2, far2, schur2] + ([] if first else [solution]) + tops,
+                flops=2 * square,
+                scratch=[(width, columns)],
+            )
+        else:
+            solution, field = call(
+                functools.partial(partial_kernel, weight, face, top),
+                [(n, F32), (n, F32)],
+                [link, col_order],
+                out + [own2, schur2, solution] + tops[:-1],
+                flops=2 * square,
+                scratch=[(width // 2, columns)],
+            )
+            solution, field = call(
+                functools.partial(finish_kernel, weight, top, cols // 2),
+                [(n, F32), (n, F32)],
+                [col_order],
+                [solution, field, cross2, tops[-1]],
+                flops=square,
+                scratch=[(width // 2, columns)],
+            )
     solution = call(restore_kernel, [(n, F32)], [], [solution, back], flops=square)[0]
     residual = call(
         functools.partial(residual_kernel, face),

time: 146 us -> 145 us (level)
  waiting for transfers between devices: 43.9 us -> 39.7 us
  Pallas kernels: 34.5 us -> 37.7 us
    ppermute x56, waiting for transfers between devices: 43.9 us -> 39.7 us  [swap(): return lax.ppermute(x, ('row', 'col'), swap_pairs(rows, cols, partner))]
    pallas_call x28 -> x32, Pallas kernels: 34.5 us -> 37.7 us  [call(): pl.pallas_call(body, out_shape=[jax.ShapeDtypeStruct(s, d) for s, d in ou...]
  transfers between devices with their start and end apart: 56 -> 56, of which waited for: 26 -> 27; matrix products, arithmetic and copies ran while one was open for 0% -> 0% of each run, Pallas kernels for 12% -> 17%
where the time goes in v5:
time: 145 us; the launch traced here: 143 us
  starting transfers between devices  62 us (43%)
  waiting for transfers between devices  39.7 us (27%)
  Pallas kernels  37.7 us (26%)
  other arithmetic  1.51 us (1%)
    ppermute x56, starting transfers between devices, swap(): return lax.ppermute(x, ('row', 'col'), swap_pairs(rows, cols, partner))  62 us
    ppermute x56, waiting for transfers between devices, swap(): return lax.ppermute(x, ('row', 'col'), swap_pairs(rows, cols, partner))  39.7 us
    pallas_call x32, Pallas kernels, call(): pl.pallas_call(body, out_shape=[jax.ShapeDtypeStruct(s, d) for s, d in ou...  37.7 us
  transfers between devices with their start and end apart: 56, of which 27 were waited for; matrix products, arithmetic and copies ran while one was open for 0% of the time, Pallas kernels for 17%

profile of v5, /device:TPU:1, one launch (start us, length us, event | category | flops | bytes accessed | tf_op | source)
XLA Modules:
  0.0 143.4 jit_solution(10615237875526417878)
XLA Ops:
  0.7 1.1 copy.12
  1.9 1.1 pad_maximum_fusion.load_ref.basis_ref
  3.0 1.3 shard_map.104
  4.5 1.0 shard_map.105
  5.6 2.7 %collective-permute-start.1 = (f32[384,128]{1,0:T(8,128)S(1)}, f32[384,128]{1,0:T(8,128)S(1)}, u32[]{:S(2)}, u32[]{:S(2)}) collective-permute-start(f32[384,128]{1,0:T(8,128)S(1)} %get-tuple-element.55), channel_id=1, source_target_pairs={{0,8},{1,2},{2,1},{3,4},{4,3},{5,6},{6,5},{7,15},{8,0},{9,10},{10,... | collective-permute-start | bytes 589832 | tf_op jit(solution)/shard_map/ppermute | solution.py:382
  8.2 1.3 collective-permute-start.2
  9.7 4.9 %collective-permute-done.2.r2.g_ref = f32[336,128]{1,0:T(8,128)S(1)} collective-permute-done((f32[336,128]{1,0:T(8,128)S(1)}, f32[336,128]{1,0:T(8,128)S(1)}, u32[]{:S(2)}, u32[]{:S(2)}) %collective-permute-start.2) | collective-permute-done | bytes 172064 | tf_op jit(solution)/shard_map/ppermute | solution.py:382
  15.4 3.6 %collective-permute-start.4 = (f32[96,128]{1,0:T(8,128)S(1)}, f32[96,128]{1,0:T(8,128)S(1)}, u32[]{:S(2)}, u32[]{:S(2)}) collective-permute-start(f32[96,128]{1,0:T(8,128)S(1)} %pad_maximum_fusion.7), channel_id=1, source_target_pairs={{0,16},{1,17},{2,18},{3,19},{4,20},{5,21},{6,22},{7,23},{8,24},{9,... | collective-permute-start | bytes 147464 | tf_op jit(solution)/shard_map/ppermute | solution.py:382
  19.0 1.5 %collective-permute-done.4.refs_1_ = f32[96,128]{1,0:T(8,128)S(1)} collective-permute-done((f32[96,128]{1,0:T(8,128)S(1)}, f32[96,128]{1,0:T(8,128)S(1)}, u32[]{:S(2)}, u32[]{:S(2)}) %collective-permute-start.4) | collective-permute-done | bytes 49184 | tf_op jit(solution)/shard_map/ppermute | solution.py:382
  20.5 1.1 collective-permute-start.5
  21.6 1.6 %shard_map.107.inverse_ref = bf16[1280,640]{1,0:T(8,128)(2,1)S(1)} custom-call(bf16[640,640]{1,0:T(8,128)(2,1)S(1)} %get-tuple-element.53.perm_ref, f32[640,640]{1,0:T(8,128)S(1)} %bitcast.13), custom_call_target="tpu_custom_call" | custom-call | flops 1048576000 | bytes 2457600 | tf_op jit(solution)/shard_map/pallas_call | solution.py:64
  24.2 3.1 %collective-permute-start.10 = (f32[48,128]{1,0:T(8,128)S(1)}, f32[48,128]{1,0:T(8,128)S(1)}, u32[]{:S(2)}, u32[]{:S(2)}) collective-permute-start(f32[48,128]{1,0:T(8,128)S(1)} %shard_map.113.refs_0_), channel_id=1, source_target_pairs={{0,1},{1,0},{2,3},{3,2},{4,5},{5,4},{6,7},{7,6},{8,9},{9,8},{10,11... | collective-permute-start | bytes 73736 | tf_op jit(solution)/shard_map/ppermute | solution.py:382
  27.4 1.4 shard_map.108
  28.8 1.3 collective-permute-start.8
  30.4 2.4 %shard_map.109 = (bf16[1280,192]{1,0:T(8,128)(2,1)S(1)}, bf16[1280,192]{1,0:T(8,128)(2,1)S(1)}, bf16[1280,192]{1,0:T(8,128)(2,1)S(1)}) custom-call(s32[4]{0:T(128)S(1)} %select_reduce_fusion.link_ref, s32[8]{0:T(128)S(1)} %fusion.9.order_ref, f32[640,48]{1,0:T(8,128)S(1)} %get-tuple-element.62.basis_ref, f32[48,192]{1,0:T(8,128)S(1)} %get-tuple-element.63.inverse_ref, ...), custom_call_target="tpu_custom_call" | custom-call | bytes 1093632 | tf_op jit(solution)/shard_map/pallas_call | solution.py:64
  35.9 1.5 %collective-permute-done.11.refs_2_ = f32[96,128]{1,0:T(8,128)S(1)} collective-permute-done((f32[96,128]{1,0:T(8,128)S(1)}, f32[96,128]{1,0:T(8,128)S(1)}, u32[]{:S(2)}, u32[]{:S(2)}) %collective-permute-start.11) | collective-permute-done | bytes 49184 | tf_op jit(solution)/shard_map/ppermute | solution.py:382
  37.4 1.1 collective-permute-start.12
  38.4 3.1 %shard_map.111.schur_ref = bf16[1280,640]{1,0:T(8,128)(2,1)S(1)} custom-call(bf16[640,640]{1,0:T(8,128)(2,1)S(1)} %get-tuple-element.53.perm_ref, f32[640,640]{1,0:T(8,128)S(1)} %bitcast.12, bf16[640,640]{1,0:T(8,128)(2,1)S(1)} %get-tuple-element.60.back_ref.refs_0_), custom_call_target="tpu_custom_call" | custom-call | flops 1048576000 | bytes 3276800 | tf_op jit(solution)/shard_map/pallas_call | solution.py:64
  42.1 2.0 %shard_map.114 = (f32[640,128]{1,0:T(8,128)S(1)}, f32[640,128]{1,0:T(8,128)S(1)}) custom-call(s32[4]{0:T(128)S(1)} %select_reduce_fusion.link_ref, s32[8]{0:T(128)S(1)} %fusion.9.order_ref, f32[640,128]{1,0:T(8,128)S(1)} %shard_map.110.y2_ref, f32[160,128]{1,0:T(8,128)S(1)} %collective-permute-done.6.r0, f32[160,128]{1,0:T(8,128)S(1)} %collective-permute-done.7.r1, ...), custom_call_target="tpu_custom_call" | custom-call | flops 838860800 | bytes 3473408 | tf_op jit(solution)/shard_map/pallas_call | solution.py:64
  45.3 3.3 %collective-permute-start.15 = (f32[160,128]{1,0:T(8,128)S(1)}, f32[160,128]{1,0:T(8,128)S(1)}, u32[]{:S(2)}, u32[]{:S(2)}) collective-permute-start(f32[160,128]{1,0:T(8,128)S(1)} %get-tuple-element.121), channel_id=1, source_target_pairs={{0,8},{1,9},{2,10},{3,11},{4,12},{5,13},{6,14},{7,15},{8,0},{9,1},... | collective-permute-start | bytes 245768 | tf_op jit(solution)/shard_map/ppermute | solution.py:382
  48.8 2.2 %collective-permute-done.15.r2 = f32[160,128]{1,0:T(8,128)S(1)} collective-permute-done((f32[160,128]{1,0:T(8,128)S(1)}, f32[160,128]{1,0:T(8,128)S(1)}, u32[]{:S(2)}, u32[]{:S(2)}) %collective-permute-start.15) | collective-permute-done | bytes 81952 | tf_op jit(solution)/shard_map/ppermute | solution.py:382
  51.8 1.8 %collective-permute-start.17 = (f32[48,128]{1,0:T(8,128)S(1)}, f32[48,128]{1,0:T(8,128)S(1)}, u32[]{:S(2)}, u32[]{:S(2)}) collective-permute-start(f32[48,128]{1,0:T(8,128)S(1)} %get-tuple-element.76.refs_0_), channel_id=1, source_target_pairs={{0,16},{1,17},{2,18},{3,19},{4,20},{5,21},{6,22},{7,23},{8,24},{9,... | collective-permute-start | bytes 73736 | tf_op jit(solution)/shard_map/ppermute | solution.py:382
  53.6 1.8 %collective-permute-done.17.refs_1_ = f32[48,128]{1,0:T(8,128)S(1)} collective-permute-done((f32[48,128]{1,0:T(8,128)S(1)}, f32[48,128]{1,0:T(8,128)S(1)}, u32[]{:S(2)}, u32[]{:S(2)}) %collective-permute-start.17) | collective-permute-done | bytes 24608 | tf_op jit(solution)/shard_map/ppermute | solution.py:382
  55.5 2.1 %collective-permute-start.18 = (f32[96,128]{1,0:T(8,128)S(1)}, f32[96,128]{1,0:T(8,128)S(1)}, u32[]{:S(2)}, u32[]{:S(2)}) collective-permute-start(f32[96,128]{1,0:T(8,128)S(1)} %pad_maximum_fusion.9), channel_id=1, source_target_pairs={{0,8},{1,9},{2,10},{3,11},{4,12},{5,13},{6,14},{7,15},{8,0},{9,1},... | collective-permute-start | bytes 147464 | tf_op jit(solution)/shard_map/ppermute | solution.py:382
  57.5 1.5 %collective-permute-done.18.refs_2_ = f32[96,128]{1,0:T(8,128)S(1)} collective-permute-done((f32[96,128]{1,0:T(8,128)S(1)}, f32[96,128]{1,0:T(8,128)S(1)}, u32[]{:S(2)}, u32[]{:S(2)}) %collective-permute-start.18) | collective-permute-done | bytes 49184 | tf_op jit(solution)/shard_map/ppermute | solution.py:382
  59.2 3.6 %collective-permute-start.23 = (f32[48,128]{1,0:T(8,128)S(1)}, f32[48,128]{1,0:T(8,128)S(1)}, u32[]{:S(2)}, u32[]{:S(2)}) collective-permute-start(f32[48,128]{1,0:T(8,128)S(1)} %shard_map.118.refs_0_), channel_id=1, source_target_pairs={{0,1},{1,0},{2,3},{3,2},{4,5},{5,4},{6,7},{7,6},{8,9},{9,8},{10,11... | collective-permute-start | bytes 73736 | tf_op jit(solution)/shard_map/ppermute | solution.py:382
  62.8 1.4 shard_map.116
  64.2 1.8 %collective-permute-start.21 = (f32[160,128]{1,0:T(8,128)S(1)}, f32[160,128]{1,0:T(8,128)S(1)}, u32[]{:S(2)}, u32[]{:S(2)}) collective-permute-start(f32[160,128]{1,0:T(8,128)S(1)} %get-tuple-element.77), channel_id=1, source_target_pairs={{0,8},{1,9},{2,10},{3,11},{4,12},{5,13},{6,14},{7,15},{8,0},{9,1},... | collective-permute-start | bytes 245768 | tf_op jit(solution)/shard_map/ppermute | solution.py:382
  67.6 1.7 %collective-permute-start.20 = (f32[160,128]{1,0:T(8,128)S(1)}, f32[160,128]{1,0:T(8,128)S(1)}, u32[]{:S(2)}, u32[]{:S(2)}) collective-permute-start(f32[160,128]{1,0:T(8,128)S(1)} %get-tuple-element.118), channel_id=1, source_target_pairs={{0,8},{1,2},{2,1},{3,4},{4,3},{5,6},{6,5},{7,15},{8,0},{9,10},{10,... | collective-permute-start | bytes 245768 | tf_op jit(solution)/shard_map/ppermute | solution.py:382
  69.4 1.8 %collective-permute-done.24.refs_2_ = f32[96,128]{1,0:T(8,128)S(1)} collective-permute-done((f32[96,128]{1,0:T(8,128)S(1)}, f32[96,128]{1,0:T(8,128)S(1)}, u32[]{:S(2)}, u32[]{:S(2)}) %collective-permute-start.24) | collective-permute-done | bytes 49184 | tf_op jit(solution)/shard_map/ppermute | solution.py:382
  71.3 1.3 shard_map.120.cross_ref
  72.7 1.8 %shard_map.119 = (f32[640,128]{1,0:T(8,128)S(1)}, f32[640,128]{1,0:T(8,128)S(1)}) custom-call(s32[4]{0:T(128)S(1)} %select_reduce_fusion.link_ref, s32[8]{0:T(128)S(1)} %fusion.9.order_ref, f32[640,128]{1,0:T(8,128)S(1)} %shard_map.117.y2_ref, f32[160,128]{1,0:T(8,128)S(1)} %collective-permute-done.19.r0, f32[160,128]{1,0:T(8,128)S(1)} %collective-permute-done.20.r1, ...), custom_call_target="tpu_custom_call" | custom-call | flops 838860800 | bytes 3211264 | tf_op jit(solution)/shard_map/pallas_call | solution.py:64
  74.5 1.0 collective-permute-done.25.more_ref
  75.6 1.1 shard_map.121
  76.7 1.2 collective-permute-start.27
  77.9 1.3 collective-permute-start.29
  79.3 2.5 %collective-permute-done.27.r1 = f32[160,128]{1,0:T(8,128)S(1)} collective-permute-done((f32[160,128]{1,0:T(8,128)S(1)}, f32[160,128]{1,0:T(8,128)S(1)}, u32[]{:S(2)}, u32[]{:S(2)}) %collective-permute-start.27) | collective-permute-done | bytes 81952 | tf_op jit(solution)/shard_map/ppermute | solution.py:382
  83.2 1.2 collective-permute-start.30
  84.4 2.4 %collective-permute-done.30.refs_1_ = f32[48,128]{1,0:T(8,128)S(1)} collective-permute-done((f32[48,128]{1,0:T(8,128)S(1)}, f32[48,128]{1,0:T(8,128)S(1)}, u32[]{:S(2)}, u32[]{:S(2)}) %collective-permute-start.30) | collective-permute-done | bytes 24608 | tf_op jit(solution)/shard_map/ppermute | solution.py:382
  87.8 2.0 %collective-permute-done.31.refs_2_ = f32[96,128]{1,0:T(8,128)S(1)} collective-permute-done((f32[96,128]{1,0:T(8,128)S(1)}, f32[96,128]{1,0:T(8,128)S(1)}, u32[]{:S(2)}, u32[]{:S(2)}) %collective-permute-start.31) | collective-permute-done | bytes 49184 | tf_op jit(solution)/shard_map/ppermute | solution.py:382
  90.0 3.4 %collective-permute-start.36 = (f32[48,128]{1,0:T(8,128)S(1)}, f32[48,128]{1,0:T(8,128)S(1)}, u32[]{:S(2)}, u32[]{:S(2)}) collective-permute-start(f32[48,128]{1,0:T(8,128)S(1)} %shard_map.125.refs_0_), channel_id=1, source_target_pairs={{0,1},{1,0},{2,3},{3,2},{4,5},{5,4},{6,7},{7,6},{8,9},{9,8},{10,11... | collective-permute-start | bytes 73736 | tf_op jit(solution)/shard_map/ppermute | solution.py:382
  93.4 1.4 shard_map.123
  99.0 1.5 %collective-permute-done.37.refs_2_ = f32[96,128]{1,0:T(8,128)S(1)} collective-permute-done((f32[96,128]{1,0:T(8,128)S(1)}, f32[96,128]{1,0:T(8,128)S(1)}, u32[]{:S(2)}, u32[]{:S(2)}) %collective-permute-start.37) | collective-permute-done | bytes 49184 | tf_op jit(solution)/shard_map/ppermute | solution.py:382
  100.6 1.9 %collective-permute-start.38 = (f32[192,128]{1,0:T(8,128)S(1)}, f32[192,128]{1,0:T(8,128)S(1)}, u32[]{:S(2)}, u32[]{:S(2)}) collective-permute-start(f32[192,128]{1,0:T(8,128)S(1)} %pad_maximum_fusion.5), channel_id=1, source_target_pairs={{0,5},{1,4},{2,7},{3,6},{4,1},{5,0},{6,3},{7,2},{8,13},{9,12},{10,... | collective-permute-start | bytes 294920 | tf_op jit(solution)/shard_map/ppermute | solution.py:382
  103.0 1.8 %shard_map.126 = (f32[640,128]{1,0:T(8,128)S(1)}, f32[640,128]{1,0:T(8,128)S(1)}) custom-call(s32[4]{0:T(128)S(1)} %select_reduce_fusion.link_ref, s32[8]{0:T(128)S(1)} %fusion.9.order_ref, f32[640,128]{1,0:T(8,128)S(1)} %shard_map.124.y2_ref, f32[160,128]{1,0:T(8,128)S(1)} %collective-permute-done.32.r0, f32[160,128]{1,0:T(8,128)S(1)} %collective-permute-done.33.r1, ...), custom_call_target="tpu_custom_call" | custom-call | flops 838860800 | bytes 3211264 | tf_op jit(solution)/shard_map/pallas_call | solution.py:64
  105.4 1.1 shard_map.127
  106.8 1.1 collective-permute-start.40
  109.1 2.0 %collective-permute-done.40.r1 = f32[160,128]{1,0:T(8,128)S(1)} collective-permute-done((f32[160,128]{1,0:T(8,128)S(1)}, f32[160,128]{1,0:T(8,128)S(1)}, u32[]{:S(2)}, u32[]{:S(2)}) %collective-permute-start.40) | collective-permute-done | bytes 81952 | tf_op jit(solution)/shard_map/ppermute | solution.py:382
  111.1 1.3 collective-permute-done.41.r2
  113.2 1.5 %collective-permute-start.43 = (f32[48,128]{1,0:T(8,128)S(1)}, f32[48,128]{1,0:T(8,128)S(1)}, u32[]{:S(2)}, u32[]{:S(2)}) collective-permute-start(f32[48,128]{1,0:T(8,128)S(1)} %get-tuple-element.94.refs_0_), channel_id=1, source_target_pairs={{0,16},{1,17},{2,18},{3,19},{4,20},{5,21},{6,22},{7,23},{8,24},{9,... | collective-permute-start | bytes 73736 | tf_op jit(solution)/shard_map/ppermute | solution.py:382
  114.7 2.2 %collective-permute-done.43.refs_1_ = f32[48,128]{1,0:T(8,128)S(1)} collective-permute-done((f32[48,128]{1,0:T(8,128)S(1)}, f32[48,128]{1,0:T(8,128)S(1)}, u32[]{:S(2)}, u32[]{:S(2)}) %collective-permute-start.43) | collective-permute-done | bytes 24608 | tf_op jit(solution)/shard_map/ppermute | solution.py:382
  117.5 2.4 %collective-permute-done.44.refs_2_ = f32[96,128]{1,0:T(8,128)S(1)} collective-permute-done((f32[96,128]{1,0:T(8,128)S(1)}, f32[96,128]{1,0:T(8,128)S(1)}, u32[]{:S(2)}, u32[]{:S(2)}) %collective-permute-start.44) | collective-permute-done | bytes 49184 | tf_op jit(solution)/shard_map/ppermute | solution.py:382
  120.0 3.2 %collective-permute-start.49 = (f32[48,128]{1,0:T(8,128)S(1)}, f32[48,128]{1,0:T(8,128)S(1)}, u32[]{:S(2)}, u32[]{:S(2)}) collective-permute-start(f32[48,128]{1,0:T(8,128)S(1)} %shard_map.131.refs_0_), channel_id=1, source_target_pairs={{0,1},{1,0},{2,3},{3,2},{4,5},{5,4},{6,7},{7,6},{8,9},{9,8},{10,11... | collective-permute-start | bytes 73736 | tf_op jit(solution)/shard_map/ppermute | solution.py:382
  123.2 1.4 shard_map.129
  124.6 1.2 collective-permute-start.47
  127.0 1.3 collective-permute-start.50
  129.1 1.5 %collective-permute-done.50.refs_2_ = f32[96,128]{1,0:T(8,128)S(1)} collective-permute-done((f32[96,128]{1,0:T(8,128)S(1)}, f32[96,128]{1,0:T(8,128)S(1)}, u32[]{:S(2)}, u32[]{:S(2)}) %collective-permute-start.50) | collective-permute-done | bytes 49184 | tf_op jit(solution)/shard_map/ppermute | solution.py:382
  130.7 1.6 %collective-permute-start.51 = (f32[192,128]{1,0:T(8,128)S(1)}, f32[192,128]{1,0:T(8,128)S(1)}, u32[]{:S(2)}, u32[]{:S(2)}) collective-permute-start(f32[192,128]{1,0:T(8,128)S(1)} %pad_maximum_fusion.6), channel_id=1, source_target_pairs={{0,5},{1,4},{2,7},{3,6},{4,1},{5,0},{6,3},{7,2},{8,13},{9,12},{10,... | collective-permute-start | bytes 294920 | tf_op jit(solution)/shard_map/ppermute | solution.py:382
  133.2 1.8 %shard_map.132 = (f32[640,128]{1,0:T(8,128)S(1)}, f32[640,128]{1,0:T(8,128)S(1)}) custom-call(s32[4]{0:T(128)S(1)} %select_reduce_fusion.link_ref, s32[8]{0:T(128)S(1)} %fusion.9.order_ref, f32[640,128]{1,0:T(8,128)S(1)} %shard_map.130.y2_ref, f32[160,128]{1,0:T(8,128)S(1)} %collective-permute-done.45.r0, f32[160,128]{1,0:T(8,128)S(1)} %collective-permute-done.46.r1, ...), custom_call_target="tpu_custom_call" | custom-call | flops 838860800 | bytes 3211264 | tf_op jit(solution)/shard_map/pallas_call | solution.py:64
  135.3 1.1 shard_map.133
  136.7 1.4 collective-permute-start.53
  138.1 1.1 collective-permute-start.54
  139.2 1.4 shard_map.134
  141.6 1.7 %shard_map.135 = f32[640,128]{1,0:T(8,128)} custom-call(s32[4]{0:T(128)S(1)} %select_reduce_fusion.link_ref, f32[640,128]{1,0:T(8,128)S(1)} %get-tuple-element.101.f_ref, f32[160,128]{1,0:T(8,128)S(1)} %collective-permute-done.52.r0, f32[160,128]{1,0:T(8,128)S(1)} %collective-permute-done.53.r1, f32[160,128]{1,0:T(8,128)S(1)} %collective-permute-done.54.r2, ...), custom_call_target="tpu_custom_call" | custom-call | bytes 1802240 | tf_op jit(solution)/shard_map/pallas_call | solution.py:64
  (125 shorter events, 25.9 us)
Async XLA Ops:
  0.6 2.4 %copy-start.2 = (s32[1,1,640]{2,1,0:T(1,128)S(1)}, s32[1,1,640]{2,1,0:T(1,128)}, u32[]{:S(2)}) copy-start(s32[1,1,640]{2,1,0:T(1,128)} %param.12) | copy-start | bytes 7684
  0.6 3.7 %copy-start.3 = (f32[48,384]{1,0:T(8,128)S(1)}, f32[48,384]{1,0:T(8,128)}, u32[]{:S(2)}) copy-start(f32[48,384]{1,0:T(8,128)} %param.17) | copy-start | bytes 221188
  0.7 3.7 %copy-start.5 = (f32[1,48,48]{2,1,0:T(8,128)S(1)}, f32[1,48,48]{2,1,0:T(8,128)}, u32[]{:S(2)}) copy-start(f32[1,48,48]{2,1,0:T(8,128)} %param.16) | copy-start | bytes 27652
  0.7 3.7 %copy-start.4 = (f32[1,48,192]{2,1,0:T(8,128)S(1)}, f32[1,48,192]{2,1,0:T(8,128)}, u32[]{:S(2)}) copy-start(f32[1,48,192]{2,1,0:T(8,128)} %param.15) | copy-start | bytes 110596
  2.9 6.6 %copy-start.6 = (s32[1,1,4]{2,1,0:T(1,128)S(1)}, s32[1,1,4]{2,1,0:T(1,128)}, u32[]{:S(2)}) copy-start(s32[1,1,4]{2,1,0:T(1,128)} %param.13) | copy-start | bytes 52
  4.5 17.1 %copy-start.1 = (f32[1,1,640,640]{3,2,1,0:T(8,128)S(1)}, f32[1,1,640,640]{3,2,1,0:T(8,128)}, u32[]{:S(2)}) copy-start(f32[1,1,640,640]{3,2,1,0:T(8,128)} %param.11) | copy-start | bytes 4915204
  5.5 9.1 %collective-permute-start = (f32[384,128]{1,0:T(8,128)S(1)}, f32[384,128]{1,0:T(8,128)S(1)}, u32[]{:S(2)}, u32[]{:S(2)}) collective-permute-start(f32[384,128]{1,0:T(8,128)S(1)} %get-tuple-element.54), channel_id=1, source_target_pairs={{0,1},{1,0},{2,3},{3,2},{4,5},{5,4},{6,7},{7,6},{8,9},{9,8},{10,11... | collective-permute-start | bytes 589832 | tf_op jit(solution)/shard_map/ppermute | solution.py:382
  5.6 9.1 %collective-permute-start.1 = (f32[384,128]{1,0:T(8,128)S(1)}, f32[384,128]{1,0:T(8,128)S(1)}, u32[]{:S(2)}, u32[]{:S(2)}) collective-permute-start(f32[384,128]{1,0:T(8,128)S(1)} %get-tuple-element.55), channel_id=1, source_target_pairs={{0,8},{1,2},{2,1},{3,4},{4,3},{5,6},{6,5},{7,15},{8,0},{9,10},{10,... | collective-permute-start | bytes 589832 | tf_op jit(solution)/shard_map/ppermute | solution.py:382
  8.2 6.4 %collective-permute-start.2 = (f32[336,128]{1,0:T(8,128)S(1)}, f32[336,128]{1,0:T(8,128)S(1)}, u32[]{:S(2)}, u32[]{:S(2)}) collective-permute-start(f32[336,128]{1,0:T(8,128)S(1)} %get-tuple-element.56), channel_id=1, source_target_pairs={{0,8},{1,9},{2,10},{3,11},{4,12},{5,13},{6,14},{7,15},{8,0},{9,1},... | collective-permute-start | bytes 516104 | tf_op jit(solution)/shard_map/ppermute | solution.py:382
  9.5 5.1 %collective-permute-start.3 = (f32[336,128]{1,0:T(8,128)S(1)}, f32[336,128]{1,0:T(8,128)S(1)}, u32[]{:S(2)}, u32[]{:S(2)}) collective-permute-start(f32[336,128]{1,0:T(8,128)S(1)} %get-tuple-element.57), channel_id=1, source_target_pairs={{0,1},{1,0},{2,3},{3,2},{4,5},{5,4},{6,7},{7,6},{8,16},{9,17},{10,... | collective-permute-start | bytes 516104 | tf_op jit(solution)/shard_map/ppermute | solution.py:382
  15.4 5.1 %collective-permute-start.4 = (f32[96,128]{1,0:T(8,128)S(1)}, f32[96,128]{1,0:T(8,128)S(1)}, u32[]{:S(2)}, u32[]{:S(2)}) collective-permute-start(f32[96,128]{1,0:T(8,128)S(1)} %pad_maximum_fusion.7), channel_id=1, source_target_pairs={{0,16},{1,17},{2,18},{3,19},{4,20},{5,21},{6,22},{7,23},{8,24},{9,... | collective-permute-start | bytes 147464 | tf_op jit(solution)/shard_map/ppermute | solution.py:382
  20.5 3.5 %collective-permute-start.5 = (f32[192,128]{1,0:T(8,128)S(1)}, f32[192,128]{1,0:T(8,128)S(1)}, u32[]{:S(2)}, u32[]{:S(2)}) collective-permute-start(f32[192,128]{1,0:T(8,128)S(1)} %pad_maximum_fusion.2), channel_id=1, source_target_pairs={{0,8},{1,9},{2,10},{3,11},{4,12},{5,13},{6,14},{7,15},{8,0},{9,1},... | collective-permute-start | bytes 294920 | tf_op jit(solution)/shard_map/ppermute | solution.py:382
  24.2 9.5 %collective-permute-start.10 = (f32[48,128]{1,0:T(8,128)S(1)}, f32[48,128]{1,0:T(8,128)S(1)}, u32[]{:S(2)}, u32[]{:S(2)}) collective-permute-start(f32[48,128]{1,0:T(8,128)S(1)} %shard_map.113.refs_0_), channel_id=1, source_target_pairs={{0,1},{1,0},{2,3},{3,2},{4,5},{5,4},{6,7},{7,6},{8,9},{9,8},{10,11... | collective-permute-start | bytes 73736 | tf_op jit(solution)/shard_map/ppermute | solution.py:382
  28.8 12.7 %collective-permute-start.8 = (f32[160,128]{1,0:T(8,128)S(1)}, f32[160,128]{1,0:T(8,128)S(1)}, u32[]{:S(2)}, u32[]{:S(2)}) collective-permute-start(f32[160,128]{1,0:T(8,128)S(1)} %get-tuple-element.69), channel_id=1, source_target_pairs={{0,8},{1,9},{2,10},{3,11},{4,12},{5,13},{6,14},{7,15},{8,0},{9,1},... | collective-permute-start | bytes 245768 | tf_op jit(solution)/shard_map/ppermute | solution.py:382
  30.1 11.4 %collective-permute-start.9 = (f32[160,128]{1,0:T(8,128)S(1)}, f32[160,128]{1,0:T(8,128)S(1)}, u32[]{:S(2)}, u32[]{:S(2)}) collective-permute-start(f32[160,128]{1,0:T(8,128)S(1)} %get-tuple-element.70), channel_id=1, source_target_pairs={{0,1},{1,0},{2,3},{3,2},{4,5},{5,4},{6,7},{7,6},{8,16},{9,17},{10,... | collective-permute-start | bytes 245768 | tf_op jit(solution)/shard_map/ppermute | solution.py:382
  30.4 8.0 %copy-start = (f32[1,1,640,640]{3,2,1,0:T(8,128)S(1)}, f32[1,1,640,640]{3,2,1,0:T(8,128)}, u32[]{:S(2)}) copy-start(f32[1,1,640,640]{3,2,1,0:T(8,128)} %param.10) | copy-start | bytes 4915204
  33.8 3.6 %collective-permute-start.11 = (f32[96,128]{1,0:T(8,128)S(1)}, f32[96,128]{1,0:T(8,128)S(1)}, u32[]{:S(2)}, u32[]{:S(2)}) collective-permute-start(f32[96,128]{1,0:T(8,128)S(1)} %pad_maximum_fusion.8), channel_id=1, source_target_pairs={{0,3},{1,2},{2,1},{3,0},{4,7},{5,6},{6,5},{7,4},{8,11},{9,10},{10,... | collective-permute-start | bytes 147464 | tf_op jit(solution)/shard_map/ppermute | solution.py:382
  34.6 6.9 %collective-permute-start.6 = (f32[160,128]{1,0:T(8,128)S(1)}, f32[160,128]{1,0:T(8,128)S(1)}, u32[]{:S(2)}, u32[]{:S(2)}) collective-permute-start(f32[160,128]{1,0:T(8,128)S(1)} %get-tuple-element.125), channel_id=1, source_target_pairs={{0,1},{1,0},{2,3},{3,2},{4,5},{5,4},{6,7},{7,6},{8,9},{9,8},{10,11... | collective-permute-start | bytes 245768 | tf_op jit(solution)/shard_map/ppermute | solution.py:382
  35.0 6.6 %collective-permute-start.7 = (f32[160,128]{1,0:T(8,128)S(1)}, f32[160,128]{1,0:T(8,128)S(1)}, u32[]{:S(2)}, u32[]{:S(2)}) collective-permute-start(f32[160,128]{1,0:T(8,128)S(1)} %get-tuple-element.124), channel_id=1, source_target_pairs={{0,8},{1,2},{2,1},{3,4},{4,3},{5,6},{6,5},{7,15},{8,0},{9,10},{10,... | collective-permute-start | bytes 245768 | tf_op jit(solution)/shard_map/ppermute | solution.py:382
  37.4 4.7 %collective-permute-start.12 = (f32[192,128]{1,0:T(8,128)S(1)}, f32[192,128]{1,0:T(8,128)S(1)}, u32[]{:S(2)}, u32[]{:S(2)}) collective-permute-start(f32[192,128]{1,0:T(8,128)S(1)} %pad_maximum_fusion.3), channel_id=1, source_target_pairs={{0,5},{1,4},{2,7},{3,6},{4,1},{5,0},{6,3},{7,2},{8,13},{9,12},{10,... | collective-permute-start | bytes 294920 | tf_op jit(solution)/shard_map/ppermute | solution.py:382
  44.1 4.5 %collective-permute-start.13 = (f32[160,128]{1,0:T(8,128)S(1)}, f32[160,128]{1,0:T(8,128)S(1)}, u32[]{:S(2)}, u32[]{:S(2)}) collective-permute-start(f32[160,128]{1,0:T(8,128)S(1)} %get-tuple-element.123), channel_id=1, source_target_pairs={{0,1},{1,0},{2,3},{3,2},{4,5},{5,4},{6,7},{7,6},{8,9},{9,8},{10,11... | collective-permute-start | bytes 245768 | tf_op jit(solution)/shard_map/ppermute | solution.py:382
  44.4 4.4 %collective-permute-start.14 = (f32[160,128]{1,0:T(8,128)S(1)}, f32[160,128]{1,0:T(8,128)S(1)}, u32[]{:S(2)}, u32[]{:S(2)}) collective-permute-start(f32[160,128]{1,0:T(8,128)S(1)} %get-tuple-element.122), channel_id=1, source_target_pairs={{0,8},{1,2},{2,1},{3,4},{4,3},{5,6},{6,5},{7,15},{8,0},{9,10},{10,... | collective-permute-start | bytes 245768 | tf_op jit(solution)/shard_map/ppermute | solution.py:382
  45.3 5.7 %collective-permute-start.15 = (f32[160,128]{1,0:T(8,128)S(1)}, f32[160,128]{1,0:T(8,128)S(1)}, u32[]{:S(2)}, u32[]{:S(2)}) collective-permute-start(f32[160,128]{1,0:T(8,128)S(1)} %get-tuple-element.121), channel_id=1, source_target_pairs={{0,8},{1,9},{2,10},{3,11},{4,12},{5,13},{6,14},{7,15},{8,0},{9,1},... | collective-permute-start | bytes 245768 | tf_op jit(solution)/shard_map/ppermute | solution.py:382
  48.6 2.4 %collective-permute-start.16 = (f32[160,128]{1,0:T(8,128)S(1)}, f32[160,128]{1,0:T(8,128)S(1)}, u32[]{:S(2)}, u32[]{:S(2)}) collective-permute-start(f32[160,128]{1,0:T(8,128)S(1)} %get-tuple-element.120), channel_id=1, source_target_pairs={{0,1},{1,0},{2,3},{3,2},{4,5},{5,4},{6,7},{7,6},{8,16},{9,17},{10,... | collective-permute-start | bytes 245768 | tf_op jit(solution)/shard_map/ppermute | solution.py:382
  51.8 3.6 %collective-permute-start.17 = (f32[48,128]{1,0:T(8,128)S(1)}, f32[48,128]{1,0:T(8,128)S(1)}, u32[]{:S(2)}, u32[]{:S(2)}) collective-permute-start(f32[48,128]{1,0:T(8,128)S(1)} %get-tuple-element.76.refs_0_), channel_id=1, source_target_pairs={{0,16},{1,17},{2,18},{3,19},{4,20},{5,21},{6,22},{7,23},{8,24},{9,... | collective-permute-start | bytes 73736 | tf_op jit(solution)/shard_map/ppermute | solution.py:382
  55.5 3.5 %collective-permute-start.18 = (f32[96,128]{1,0:T(8,128)S(1)}, f32[96,128]{1,0:T(8,128)S(1)}, u32[]{:S(2)}, u32[]{:S(2)}) collective-permute-start(f32[96,128]{1,0:T(8,128)S(1)} %pad_maximum_fusion.9), channel_id=1, source_target_pairs={{0,8},{1,9},{2,10},{3,11},{4,12},{5,13},{6,14},{7,15},{8,0},{9,1},... | collective-permute-start | bytes 147464 | tf_op jit(solution)/shard_map/ppermute | solution.py:382
  59.2 8.0 %collective-permute-start.23 = (f32[48,128]{1,0:T(8,128)S(1)}, f32[48,128]{1,0:T(8,128)S(1)}, u32[]{:S(2)}, u32[]{:S(2)}) collective-permute-start(f32[48,128]{1,0:T(8,128)S(1)} %shard_map.118.refs_0_), channel_id=1, source_target_pairs={{0,1},{1,0},{2,3},{3,2},{4,5},{5,4},{6,7},{7,6},{8,9},{9,8},{10,11... | collective-permute-start | bytes 73736 | tf_op jit(solution)/shard_map/ppermute | solution.py:382
  64.2 8.4 %collective-permute-start.21 = (f32[160,128]{1,0:T(8,128)S(1)}, f32[160,128]{1,0:T(8,128)S(1)}, u32[]{:S(2)}, u32[]{:S(2)}) collective-permute-start(f32[160,128]{1,0:T(8,128)S(1)} %get-tuple-element.77), channel_id=1, source_target_pairs={{0,8},{1,9},{2,10},{3,11},{4,12},{5,13},{6,14},{7,15},{8,0},{9,1},... | collective-permute-start | bytes 245768 | tf_op jit(solution)/shard_map/ppermute | solution.py:382
  66.1 6.6 %collective-permute-start.22 = (f32[160,128]{1,0:T(8,128)S(1)}, f32[160,128]{1,0:T(8,128)S(1)}, u32[]{:S(2)}, u32[]{:S(2)}) collective-permute-start(f32[160,128]{1,0:T(8,128)S(1)} %get-tuple-element.78), channel_id=1, source_target_pairs={{0,1},{1,0},{2,3},{3,2},{4,5},{5,4},{6,7},{7,6},{8,16},{9,17},{10,... | collective-permute-start | bytes 245768 | tf_op jit(solution)/shard_map/ppermute | solution.py:382
  67.3 3.9 %collective-permute-start.24 = (f32[96,128]{1,0:T(8,128)S(1)}, f32[96,128]{1,0:T(8,128)S(1)}, u32[]{:S(2)}, u32[]{:S(2)}) collective-permute-start(f32[96,128]{1,0:T(8,128)S(1)} %pad_maximum_fusion.10), channel_id=1, source_target_pairs={{0,3},{1,2},{2,1},{3,0},{4,7},{5,6},{6,5},{7,4},{8,11},{9,10},{10,... | collective-permute-start | bytes 147464 | tf_op jit(solution)/shard_map/ppermute | solution.py:382
  67.4 5.3 %collective-permute-start.19 = (f32[160,128]{1,0:T(8,128)S(1)}, f32[160,128]{1,0:T(8,128)S(1)}, u32[]{:S(2)}, u32[]{:S(2)}) collective-permute-start(f32[160,128]{1,0:T(8,128)S(1)} %get-tuple-element.119), channel_id=1, source_target_pairs={{0,1},{1,0},{2,3},{3,2},{4,5},{5,4},{6,7},{7,6},{8,9},{9,8},{10,11... | collective-permute-start | bytes 245768 | tf_op jit(solution)/shard_map/ppermute | solution.py:382
  67.6 5.1 %collective-permute-start.20 = (f32[160,128]{1,0:T(8,128)S(1)}, f32[160,128]{1,0:T(8,128)S(1)}, u32[]{:S(2)}, u32[]{:S(2)}) collective-permute-start(f32[160,128]{1,0:T(8,128)S(1)} %get-tuple-element.118), channel_id=1, source_target_pairs={{0,8},{1,2},{2,1},{3,4},{4,3},{5,6},{6,5},{7,15},{8,0},{9,10},{10,... | collective-permute-start | bytes 245768 | tf_op jit(solution)/shard_map/ppermute | solution.py:382
  71.2 4.4 %collective-permute-start.25 = (f32[192,128]{1,0:T(8,128)S(1)}, f32[192,128]{1,0:T(8,128)S(1)}, u32[]{:S(2)}, u32[]{:S(2)}) collective-permute-start(f32[192,128]{1,0:T(8,128)S(1)} %pad_maximum_fusion.4), channel_id=1, source_target_pairs={{0,5},{1,4},{2,7},{3,6},{4,1},{5,0},{6,3},{7,2},{8,13},{9,12},{10,... | collective-permute-start | bytes 294920 | tf_op jit(solution)/shard_map/ppermute | solution.py:382
  76.7 2.6 %collective-permute-start.26 = (f32[160,128]{1,0:T(8,128)S(1)}, f32[160,128]{1,0:T(8,128)S(1)}, u32[]{:S(2)}, u32[]{:S(2)}) collective-permute-start(f32[160,128]{1,0:T(8,128)S(1)} %get-tuple-element.117), channel_id=1, source_target_pairs={{0,1},{1,0},{2,3},{3,2},{4,5},{5,4},{6,7},{7,6},{8,9},{9,8},{10,11... | collective-permute-start | bytes 245768 | tf_op jit(solution)/shard_map/ppermute | solution.py:382
  76.7 5.0 %collective-permute-start.27 = (f32[160,128]{1,0:T(8,128)S(1)}, f32[160,128]{1,0:T(8,128)S(1)}, u32[]{:S(2)}, u32[]{:S(2)}) collective-permute-start(f32[160,128]{1,0:T(8,128)S(1)} %get-tuple-element.116), channel_id=1, source_target_pairs={{0,8},{1,2},{2,1},{3,4},{4,3},{5,6},{6,5},{7,15},{8,0},{9,10},{10,... | collective-permute-start | bytes 245768 | tf_op jit(solution)/shard_map/ppermute | solution.py:382
  77.9 4.5 %collective-permute-start.28 = (f32[160,128]{1,0:T(8,128)S(1)}, f32[160,128]{1,0:T(8,128)S(1)}, u32[]{:S(2)}, u32[]{:S(2)}) collective-permute-start(f32[160,128]{1,0:T(8,128)S(1)} %get-tuple-element.115), channel_id=1, source_target_pairs={{0,8},{1,9},{2,10},{3,11},{4,12},{5,13},{6,14},{7,15},{8,0},{9,1},... | collective-permute-start | bytes 245768 | tf_op jit(solution)/shard_map/ppermute | solution.py:382
  77.9 4.5 %collective-permute-start.29 = (f32[160,128]{1,0:T(8,128)S(1)}, f32[160,128]{1,0:T(8,128)S(1)}, u32[]{:S(2)}, u32[]{:S(2)}) collective-permute-start(f32[160,128]{1,0:T(8,128)S(1)} %get-tuple-element.114), channel_id=1, source_target_pairs={{0,1},{1,0},{2,3},{3,2},{4,5},{5,4},{6,7},{7,6},{8,16},{9,17},{10,... | collective-permute-start | bytes 245768 | tf_op jit(solution)/shard_map/ppermute | solution.py:382
  83.2 3.6 %collective-permute-start.30 = (f32[48,128]{1,0:T(8,128)S(1)}, f32[48,128]{1,0:T(8,128)S(1)}, u32[]{:S(2)}, u32[]{:S(2)}) collective-permute-start(f32[48,128]{1,0:T(8,128)S(1)} %get-tuple-element.85.refs_0_), channel_id=1, source_target_pairs={{0,16},{1,17},{2,18},{3,19},{4,20},{5,21},{6,22},{7,23},{8,24},{9,... | collective-permute-start | bytes 73736 | tf_op jit(solution)/shard_map/ppermute | solution.py:382
  86.8 2.9 %collective-permute-start.31 = (f32[96,128]{1,0:T(8,128)S(1)}, f32[96,128]{1,0:T(8,128)S(1)}, u32[]{:S(2)}, u32[]{:S(2)}) collective-permute-start(f32[96,128]{1,0:T(8,128)S(1)} %pad_maximum_fusion.11), channel_id=1, source_target_pairs={{0,8},{1,9},{2,10},{3,11},{4,12},{5,13},{6,14},{7,15},{8,0},{9,1},... | collective-permute-start | bytes 147464 | tf_op jit(solution)/shard_map/ppermute | solution.py:382
  90.0 6.9 %collective-permute-start.36 = (f32[48,128]{1,0:T(8,128)S(1)}, f32[48,128]{1,0:T(8,128)S(1)}, u32[]{:S(2)}, u32[]{:S(2)}) collective-permute-start(f32[48,128]{1,0:T(8,128)S(1)} %shard_map.125.refs_0_), channel_id=1, source_target_pairs={{0,1},{1,0},{2,3},{3,2},{4,5},{5,4},{6,7},{7,6},{8,9},{9,8},{10,11... | collective-permute-start | bytes 73736 | tf_op jit(solution)/shard_map/ppermute | solution.py:382
  94.8 7.6 %collective-permute-start.34 = (f32[160,128]{1,0:T(8,128)S(1)}, f32[160,128]{1,0:T(8,128)S(1)}, u32[]{:S(2)}, u32[]{:S(2)}) collective-permute-start(f32[160,128]{1,0:T(8,128)S(1)} %get-tuple-element.86), channel_id=1, source_target_pairs={{0,8},{1,9},{2,10},{3,11},{4,12},{5,13},{6,14},{7,15},{8,0},{9,1},... | collective-permute-start | bytes 245768 | tf_op jit(solution)/shard_map/ppermute | solution.py:382
  95.7 6.7 %collective-permute-start.35 = (f32[160,128]{1,0:T(8,128)S(1)}, f32[160,128]{1,0:T(8,128)S(1)}, u32[]{:S(2)}, u32[]{:S(2)}) collective-permute-start(f32[160,128]{1,0:T(8,128)S(1)} %get-tuple-element.87), channel_id=1, source_target_pairs={{0,1},{1,0},{2,3},{3,2},{4,5},{5,4},{6,7},{7,6},{8,16},{9,17},{10,... | collective-permute-start | bytes 245768 | tf_op jit(solution)/shard_map/ppermute | solution.py:382
  96.9 3.6 %collective-permute-start.37 = (f32[96,128]{1,0:T(8,128)S(1)}, f32[96,128]{1,0:T(8,128)S(1)}, u32[]{:S(2)}, u32[]{:S(2)}) collective-permute-start(f32[96,128]{1,0:T(8,128)S(1)} %pad_maximum_fusion.12), channel_id=1, source_target_pairs={{0,3},{1,2},{2,1},{3,0},{4,7},{5,6},{6,5},{7,4},{8,11},{9,10},{10,... | collective-permute-start | bytes 147464 | tf_op jit(solution)/shard_map/ppermute | solution.py:382
  97.9 4.5 %collective-permute-start.32 = (f32[160,128]{1,0:T(8,128)S(1)}, f32[160,128]{1,0:T(8,128)S(1)}, u32[]{:S(2)}, u32[]{:S(2)}) collective-permute-start(f32[160,128]{1,0:T(8,128)S(1)} %get-tuple-element.113), channel_id=1, source_target_pairs={{0,1},{1,0},{2,3},{3,2},{4,5},{5,4},{6,7},{7,6},{8,9},{9,8},{10,11... | collective-permute-start | bytes 245768 | tf_op jit(solution)/shard_map/ppermute | solution.py:382
  98.3 4.7 %collective-permute-start.33 = (f32[160,128]{1,0:T(8,128)S(1)}, f32[160,128]{1,0:T(8,128)S(1)}, u32[]{:S(2)}, u32[]{:S(2)}) collective-permute-start(f32[160,128]{1,0:T(8,128)S(1)} %get-tuple-element.112), channel_id=1, source_target_pairs={{0,8},{1,2},{2,1},{3,4},{4,3},{5,6},{6,5},{7,15},{8,0},{9,10},{10,... | collective-permute-start | bytes 245768 | tf_op jit(solution)/shard_map/ppermute | solution.py:382
  100.6 4.8 %collective-permute-start.38 = (f32[192,128]{1,0:T(8,128)S(1)}, f32[192,128]{1,0:T(8,128)S(1)}, u32[]{:S(2)}, u32[]{:S(2)}) collective-permute-start(f32[192,128]{1,0:T(8,128)S(1)} %pad_maximum_fusion.5), channel_id=1, source_target_pairs={{0,5},{1,4},{2,7},{3,6},{4,1},{5,0},{6,3},{7,2},{8,13},{9,12},{10,... | collective-permute-start | bytes 294920 | tf_op jit(solution)/shard_map/ppermute | solution.py:382
  106.5 2.6 %collective-permute-start.39 = (f32[160,128]{1,0:T(8,128)S(1)}, f32[160,128]{1,0:T(8,128)S(1)}, u32[]{:S(2)}, u32[]{:S(2)}) collective-permute-start(f32[160,128]{1,0:T(8,128)S(1)} %get-tuple-element.111), channel_id=1, source_target_pairs={{0,1},{1,0},{2,3},{3,2},{4,5},{5,4},{6,7},{7,6},{8,9},{9,8},{10,11... | collective-permute-start | bytes 245768 | tf_op jit(solution)/shard_map/ppermute | solution.py:382
  106.8 4.3 %collective-permute-start.40 = (f32[160,128]{1,0:T(8,128)S(1)}, f32[160,128]{1,0:T(8,128)S(1)}, u32[]{:S(2)}, u32[]{:S(2)}) collective-permute-start(f32[160,128]{1,0:T(8,128)S(1)} %get-tuple-element.110), channel_id=1, source_target_pairs={{0,8},{1,2},{2,1},{3,4},{4,3},{5,6},{6,5},{7,15},{8,0},{9,10},{10,... | collective-permute-start | bytes 245768 | tf_op jit(solution)/shard_map/ppermute | solution.py:382
  108.0 4.5 %collective-permute-start.41 = (f32[160,128]{1,0:T(8,128)S(1)}, f32[160,128]{1,0:T(8,128)S(1)}, u32[]{:S(2)}, u32[]{:S(2)}) collective-permute-start(f32[160,128]{1,0:T(8,128)S(1)} %get-tuple-element.109), channel_id=1, source_target_pairs={{0,8},{1,9},{2,10},{3,11},{4,12},{5,13},{6,14},{7,15},{8,0},{9,1},... | collective-permute-start | bytes 245768 | tf_op jit(solution)/shard_map/ppermute | solution.py:382
  108.5 3.9 %collective-permute-start.42 = (f32[160,128]{1,0:T(8,128)S(1)}, f32[160,128]{1,0:T(8,128)S(1)}, u32[]{:S(2)}, u32[]{:S(2)}) collective-permute-start(f32[160,128]{1,0:T(8,128)S(1)} %get-tuple-element.108), channel_id=1, source_target_pairs={{0,1},{1,0},{2,3},{3,2},{4,5},{5,4},{6,7},{7,6},{8,16},{9,17},{10,... | collective-permute-start | bytes 245768 | tf_op jit(solution)/shard_map/ppermute | solution.py:382
  113.2 3.6 %collective-permute-start.43 = (f32[48,128]{1,0:T(8,128)S(1)}, f32[48,128]{1,0:T(8,128)S(1)}, u32[]{:S(2)}, u32[]{:S(2)}) collective-permute-start(f32[48,128]{1,0:T(8,128)S(1)} %get-tuple-element.94.refs_0_), channel_id=1, source_target_pairs={{0,16},{1,17},{2,18},{3,19},{4,20},{5,21},{6,22},{7,23},{8,24},{9,... | collective-permute-start | bytes 73736 | tf_op jit(solution)/shard_map/ppermute | solution.py:382
  116.9 2.9 %collective-permute-start.44 = (f32[96,128]{1,0:T(8,128)S(1)}, f32[96,128]{1,0:T(8,128)S(1)}, u32[]{:S(2)}, u32[]{:S(2)}) collective-permute-start(f32[96,128]{1,0:T(8,128)S(1)} %pad_maximum_fusion.13), channel_id=1, source_target_pairs={{0,8},{1,9},{2,10},{3,11},{4,12},{5,13},{6,14},{7,15},{8,0},{9,1},... | collective-permute-start | bytes 147464 | tf_op jit(solution)/shard_map/ppermute | solution.py:382
  120.0 7.0 %collective-permute-start.49 = (f32[48,128]{1,0:T(8,128)S(1)}, f32[48,128]{1,0:T(8,128)S(1)}, u32[]{:S(2)}, u32[]{:S(2)}) collective-permute-start(f32[48,128]{1,0:T(8,128)S(1)} %shard_map.131.refs_0_), channel_id=1, source_target_pairs={{0,1},{1,0},{2,3},{3,2},{4,5},{5,4},{6,7},{7,6},{8,9},{9,8},{10,11... | collective-permute-start | bytes 73736 | tf_op jit(solution)/shard_map/ppermute | solution.py:382
  124.6 7.7 %collective-permute-start.47 = (f32[160,128]{1,0:T(8,128)S(1)}, f32[160,128]{1,0:T(8,128)S(1)}, u32[]{:S(2)}, u32[]{:S(2)}) collective-permute-start(f32[160,128]{1,0:T(8,128)S(1)} %get-tuple-element.95), channel_id=1, source_target_pairs={{0,8},{1,9},{2,10},{3,11},{4,12},{5,13},{6,14},{7,15},{8,0},{9,1},... | collective-permute-start | bytes 245768 | tf_op jit(solution)/shard_map/ppermute | solution.py:382
  125.8 6.4 %collective-permute-start.48 = (f32[160,128]{1,0:T(8,128)S(1)}, f32[160,128]{1,0:T(8,128)S(1)}, u32[]{:S(2)}, u32[]{:S(2)}) collective-permute-start(f32[160,128]{1,0:T(8,128)S(1)} %get-tuple-element.96), channel_id=1, source_target_pairs={{0,1},{1,0},{2,3},{3,2},{4,5},{5,4},{6,7},{7,6},{8,16},{9,17},{10,... | collective-permute-start | bytes 245768 | tf_op jit(solution)/shard_map/ppermute | solution.py:382
  127.0 3.6 %collective-permute-start.50 = (f32[96,128]{1,0:T(8,128)S(1)}, f32[96,128]{1,0:T(8,128)S(1)}, u32[]{:S(2)}, u32[]{:S(2)}) collective-permute-start(f32[96,128]{1,0:T(8,128)S(1)} %pad_maximum_fusion.14), channel_id=1, source_target_pairs={{0,3},{1,2},{2,1},{3,0},{4,7},{5,6},{6,5},{7,4},{8,11},{9,10},{10,... | collective-permute-start | bytes 147464 | tf_op jit(solution)/shard_map/ppermute | solution.py:382
  128.4 3.9 %collective-permute-start.45 = (f32[160,128]{1,0:T(8,128)S(1)}, f32[160,128]{1,0:T(8,128)S(1)}, u32[]{:S(2)}, u32[]{:S(2)}) collective-permute-start(f32[160,128]{1,0:T(8,128)S(1)} %get-tuple-element.107), channel_id=1, source_target_pairs={{0,1},{1,0},{2,3},{3,2},{4,5},{5,4},{6,7},{7,6},{8,9},{9,8},{10,11... | collective-permute-start | bytes 245768 | tf_op jit(solution)/shard_map/ppermute | solution.py:382
  128.7 4.4 %collective-permute-start.46 = (f32[160,128]{1,0:T(8,128)S(1)}, f32[160,128]{1,0:T(8,128)S(1)}, u32[]{:S(2)}, u32[]{:S(2)}) collective-permute-start(f32[160,128]{1,0:T(8,128)S(1)} %get-tuple-element.106), channel_id=1, source_target_pairs={{0,8},{1,2},{2,1},{3,4},{4,3},{5,6},{6,5},{7,15},{8,0},{9,10},{10,... | collective-permute-start | bytes 245768 | tf_op jit(solution)/shard_map/ppermute | solution.py:382
  130.7 4.7 %collective-permute-start.51 = (f32[192,128]{1,0:T(8,128)S(1)}, f32[192,128]{1,0:T(8,128)S(1)}, u32[]{:S(2)}, u32[]{:S(2)}) collective-permute-start(f32[192,128]{1,0:T(8,128)S(1)} %pad_maximum_fusion.6), channel_id=1, source_target_pairs={{0,5},{1,4},{2,7},{3,6},{4,1},{5,0},{6,3},{7,2},{8,13},{9,12},{10,... | collective-permute-start | bytes 294920 | tf_op jit(solution)/shard_map/ppermute | solution.py:382
  136.4 4.1 %collective-permute-start.52 = (f32[160,128]{1,0:T(8,128)S(1)}, f32[160,128]{1,0:T(8,128)S(1)}, u32[]{:S(2)}, u32[]{:S(2)}) collective-permute-start(f32[160,128]{1,0:T(8,128)S(1)} %get-tuple-element.105), channel_id=1, source_target_pairs={{0,1},{1,0},{2,3},{3,2},{4,5},{5,4},{6,7},{7,6},{8,9},{9,8},{10,11... | collective-permute-start | bytes 245768 | tf_op jit(solution)/shard_map/ppermute | solution.py:382
  136.7 4.2 %collective-permute-start.53 = (f32[160,128]{1,0:T(8,128)S(1)}, f32[160,128]{1,0:T(8,128)S(1)}, u32[]{:S(2)}, u32[]{:S(2)}) collective-permute-start(f32[160,128]{1,0:T(8,128)S(1)} %get-tuple-element.104), channel_id=1, source_target_pairs={{0,8},{1,2},{2,1},{3,4},{4,3},{5,6},{6,5},{7,15},{8,0},{9,10},{10,... | collective-permute-start | bytes 245768 | tf_op jit(solution)/shard_map/ppermute | solution.py:382
  138.1 3.5 %collective-permute-start.54 = (f32[160,128]{1,0:T(8,128)S(1)}, f32[160,128]{1,0:T(8,128)S(1)}, u32[]{:S(2)}, u32[]{:S(2)}) collective-permute-start(f32[160,128]{1,0:T(8,128)S(1)} %get-tuple-element.103), channel_id=1, source_target_pairs={{0,8},{1,9},{2,10},{3,11},{4,12},{5,13},{6,14},{7,15},{8,0},{9,1},... | collective-permute-start | bytes 245768 | tf_op jit(solution)/shard_map/ppermute | solution.py:382
  139.2 2.5 %collective-permute-start.55 = (f32[160,128]{1,0:T(8,128)S(1)}, f32[160,128]{1,0:T(8,128)S(1)}, u32[]{:S(2)}, u32[]{:S(2)}) collective-permute-start(f32[160,128]{1,0:T(8,128)S(1)} %get-tuple-element.102), channel_id=1, source_target_pairs={{0,1},{1,0},{2,3},{3,2},{4,5},{5,4},{6,7},{7,6},{8,16},{9,17},{10,... | collective-permute-start | bytes 245768 | tf_op jit(solution)/shard_map/ppermute | solution.py:382

commit v6 on v5

--- a/solution.py
+++ b/solution.py
@@ -39,9 +39,8 @@
 def product_parts(left2, right_parts):
     rows = left2.shape[0] // 2
     n = right_parts[0].shape[1]
-    out = dot(left2, jnp.concatenate(right_parts, axis=1))
-    out = out[:rows] + out[rows:]
-    return out[:, :n] + out[:, n:]
+    high = dot(left2[:rows], jnp.concatenate(right_parts, axis=1))
+    return high[:, :n] + (high[:, n:] + dot(left2[rows:], right_parts[0]))
 
 
 def product(left2, right):

time: 145 us -> 144 us (level)
  Pallas kernels: 37.7 us -> 35.8 us
    pallas_call x32, Pallas kernels: 37.7 us -> 35.8 us  [call(): pl.pallas_call(body, out_shape=[jax.ShapeDtypeStruct(s, d) for s, d in ou...]
  transfers between devices with their start and end apart: 56 -> 56, of which waited for: 27 -> 27; matrix products, arithmetic and copies ran while one was open for 0% -> 0% of each run, Pallas kernels for 17% -> 16%
where the time goes in v6:
time: 144 us; the launch traced here: 142 us
  starting transfers between devices  62 us (43%)
  waiting for transfers between devices  40.6 us (28%)
  Pallas kernels  35.8 us (25%)
  other arithmetic  1.51 us (1%)
    ppermute x56, starting transfers between devices, swap(): return lax.ppermute(x, ('row', 'col'), swap_pairs(rows, cols, partner))  62 us
    ppermute x56, waiting for transfers between devices, swap(): return lax.ppermute(x, ('row', 'col'), swap_pairs(rows, cols, partner))  40.6 us
    pallas_call x32, Pallas kernels, call(): pl.pallas_call(body, out_shape=[jax.ShapeDtypeStruct(s, d) for s, d in ou...  35.8 us
  transfers between devices with their start and end apart: 56, of which 27 were waited for; matrix products, arithmetic and copies ran while one was open for 0% of the time, Pallas kernels for 16%

profile of v6, /device:TPU:1, one launch (start us, length us, event | category | flops | bytes accessed | tf_op | source)
XLA Modules:
  0.0 142.5 jit_solution(476167836790898860)
XLA Ops:
  0.7 1.1 copy.12
  1.9 1.1 pad_maximum_fusion.load_ref.basis_ref
  3.0 1.3 shard_map.104
  4.5 1.1 shard_map.105
  5.7 2.6 %collective-permute-start.1 = (f32[384,128]{1,0:T(8,128)S(1)}, f32[384,128]{1,0:T(8,128)S(1)}, u32[]{:S(2)}, u32[]{:S(2)}) collective-permute-start(f32[384,128]{1,0:T(8,128)S(1)} %get-tuple-element.55), channel_id=1, source_target_pairs={{0,8},{1,2},{2,1},{3,4},{4,3},{5,6},{6,5},{7,15},{8,0},{9,10},{10,... | collective-permute-start | bytes 589832 | tf_op jit(solution)/shard_map/ppermute | solution.py:381
  8.3 1.3 collective-permute-start.2
  9.9 4.9 %collective-permute-done.2.r2.g_ref = f32[336,128]{1,0:T(8,128)S(1)} collective-permute-done((f32[336,128]{1,0:T(8,128)S(1)}, f32[336,128]{1,0:T(8,128)S(1)}, u32[]{:S(2)}, u32[]{:S(2)}) %collective-permute-start.2) | collective-permute-done | bytes 172064 | tf_op jit(solution)/shard_map/ppermute | solution.py:381
  15.5 3.6 %collective-permute-start.4 = (f32[96,128]{1,0:T(8,128)S(1)}, f32[96,128]{1,0:T(8,128)S(1)}, u32[]{:S(2)}, u32[]{:S(2)}) collective-permute-start(f32[96,128]{1,0:T(8,128)S(1)} %pad_maximum_fusion.7), channel_id=1, source_target_pairs={{0,16},{1,17},{2,18},{3,19},{4,20},{5,21},{6,22},{7,23},{8,24},{9,... | collective-permute-start | bytes 147464 | tf_op jit(solution)/shard_map/ppermute | solution.py:381
  19.1 1.5 %collective-permute-done.4.refs_1_ = f32[96,128]{1,0:T(8,128)S(1)} collective-permute-done((f32[96,128]{1,0:T(8,128)S(1)}, f32[96,128]{1,0:T(8,128)S(1)}, u32[]{:S(2)}, u32[]{:S(2)}) %collective-permute-start.4) | collective-permute-done | bytes 49184 | tf_op jit(solution)/shard_map/ppermute | solution.py:381
  20.6 1.1 collective-permute-start.5
  21.7 1.6 %shard_map.107.inverse_ref = bf16[1280,640]{1,0:T(8,128)(2,1)S(1)} custom-call(bf16[640,640]{1,0:T(8,128)(2,1)S(1)} %get-tuple-element.53.perm_ref, f32[640,640]{1,0:T(8,128)S(1)} %bitcast.13), custom_call_target="tpu_custom_call" | custom-call | flops 1048576000 | bytes 2457600 | tf_op jit(solution)/shard_map/pallas_call | solution.py:63
  24.4 3.1 %collective-permute-start.10 = (f32[48,128]{1,0:T(8,128)S(1)}, f32[48,128]{1,0:T(8,128)S(1)}, u32[]{:S(2)}, u32[]{:S(2)}) collective-permute-start(f32[48,128]{1,0:T(8,128)S(1)} %shard_map.113.refs_0_), channel_id=1, source_target_pairs={{0,1},{1,0},{2,3},{3,2},{4,5},{5,4},{6,7},{7,6},{8,9},{9,8},{10,11... | collective-permute-start | bytes 73736 | tf_op jit(solution)/shard_map/ppermute | solution.py:381
  27.5 1.3 shard_map.108
  28.8 1.3 collective-permute-start.8
  30.4 2.4 %shard_map.109 = (bf16[1280,192]{1,0:T(8,128)(2,1)S(1)}, bf16[1280,192]{1,0:T(8,128)(2,1)S(1)}, bf16[1280,192]{1,0:T(8,128)(2,1)S(1)}) custom-call(s32[4]{0:T(128)S(1)} %select_reduce_fusion.link_ref, s32[8]{0:T(128)S(1)} %fusion.9.order_ref, f32[640,48]{1,0:T(8,128)S(1)} %get-tuple-element.62.basis_ref, f32[48,192]{1,0:T(8,128)S(1)} %get-tuple-element.63.inverse_ref, ...), custom_call_target="tpu_custom_call" | custom-call | bytes 1093632 | tf_op jit(solution)/shard_map/pallas_call | solution.py:63
  35.7 1.5 %collective-permute-done.11.refs_2_ = f32[96,128]{1,0:T(8,128)S(1)} collective-permute-done((f32[96,128]{1,0:T(8,128)S(1)}, f32[96,128]{1,0:T(8,128)S(1)}, u32[]{:S(2)}, u32[]{:S(2)}) %collective-permute-start.11) | collective-permute-done | bytes 49184 | tf_op jit(solution)/shard_map/ppermute | solution.py:381
  37.3 1.1 collective-permute-start.12
  38.3 3.1 %shard_map.111.schur_ref = bf16[1280,640]{1,0:T(8,128)(2,1)S(1)} custom-call(bf16[640,640]{1,0:T(8,128)(2,1)S(1)} %get-tuple-element.53.perm_ref, f32[640,640]{1,0:T(8,128)S(1)} %bitcast.12, bf16[640,640]{1,0:T(8,128)(2,1)S(1)} %get-tuple-element.60.back_ref.refs_0_), custom_call_target="tpu_custom_call" | custom-call | flops 1048576000 | bytes 3276800 | tf_op jit(solution)/shard_map/pallas_call | solution.py:63
  42.0 1.7 %shard_map.114 = (f32[640,128]{1,0:T(8,128)S(1)}, f32[640,128]{1,0:T(8,128)S(1)}) custom-call(s32[4]{0:T(128)S(1)} %select_reduce_fusion.link_ref, s32[8]{0:T(128)S(1)} %fusion.9.order_ref, f32[640,128]{1,0:T(8,128)S(1)} %shard_map.110.y2_ref, f32[160,128]{1,0:T(8,128)S(1)} %collective-permute-done.6.r0, f32[160,128]{1,0:T(8,128)S(1)} %collective-permute-done.7.r1, ...), custom_call_target="tpu_custom_call" | custom-call | flops 838860800 | bytes 3473408 | tf_op jit(solution)/shard_map/pallas_call | solution.py:63
  44.9 3.3 %collective-permute-start.15 = (f32[160,128]{1,0:T(8,128)S(1)}, f32[160,128]{1,0:T(8,128)S(1)}, u32[]{:S(2)}, u32[]{:S(2)}) collective-permute-start(f32[160,128]{1,0:T(8,128)S(1)} %get-tuple-element.121), channel_id=1, source_target_pairs={{0,8},{1,9},{2,10},{3,11},{4,12},{5,13},{6,14},{7,15},{8,0},{9,1},... | collective-permute-start | bytes 245768 | tf_op jit(solution)/shard_map/ppermute | solution.py:381
  48.4 2.2 %collective-permute-done.15.r2 = f32[160,128]{1,0:T(8,128)S(1)} collective-permute-done((f32[160,128]{1,0:T(8,128)S(1)}, f32[160,128]{1,0:T(8,128)S(1)}, u32[]{:S(2)}, u32[]{:S(2)}) %collective-permute-start.15) | collective-permute-done | bytes 81952 | tf_op jit(solution)/shard_map/ppermute | solution.py:381
  51.4 1.8 %collective-permute-start.17 = (f32[48,128]{1,0:T(8,128)S(1)}, f32[48,128]{1,0:T(8,128)S(1)}, u32[]{:S(2)}, u32[]{:S(2)}) collective-permute-start(f32[48,128]{1,0:T(8,128)S(1)} %get-tuple-element.76.refs_0_), channel_id=1, source_target_pairs={{0,16},{1,17},{2,18},{3,19},{4,20},{5,21},{6,22},{7,23},{8,24},{9,... | collective-permute-start | bytes 73736 | tf_op jit(solution)/shard_map/ppermute | solution.py:381
  53.2 1.8 %collective-permute-done.17.refs_1_ = f32[48,128]{1,0:T(8,128)S(1)} collective-permute-done((f32[48,128]{1,0:T(8,128)S(1)}, f32[48,128]{1,0:T(8,128)S(1)}, u32[]{:S(2)}, u32[]{:S(2)}) %collective-permute-start.17) | collective-permute-done | bytes 24608 | tf_op jit(solution)/shard_map/ppermute | solution.py:381
  55.0 2.1 %collective-permute-start.18 = (f32[96,128]{1,0:T(8,128)S(1)}, f32[96,128]{1,0:T(8,128)S(1)}, u32[]{:S(2)}, u32[]{:S(2)}) collective-permute-start(f32[96,128]{1,0:T(8,128)S(1)} %pad_maximum_fusion.9), channel_id=1, source_target_pairs={{0,8},{1,9},{2,10},{3,11},{4,12},{5,13},{6,14},{7,15},{8,0},{9,1},... | collective-permute-start | bytes 147464 | tf_op jit(solution)/shard_map/ppermute | solution.py:381
  57.1 1.5 %collective-permute-done.18.refs_2_ = f32[96,128]{1,0:T(8,128)S(1)} collective-permute-done((f32[96,128]{1,0:T(8,128)S(1)}, f32[96,128]{1,0:T(8,128)S(1)}, u32[]{:S(2)}, u32[]{:S(2)}) %collective-permute-start.18) | collective-permute-done | bytes 49184 | tf_op jit(solution)/shard_map/ppermute | solution.py:381
  58.8 3.6 %collective-permute-start.23 = (f32[48,128]{1,0:T(8,128)S(1)}, f32[48,128]{1,0:T(8,128)S(1)}, u32[]{:S(2)}, u32[]{:S(2)}) collective-permute-start(f32[48,128]{1,0:T(8,128)S(1)} %shard_map.118.refs_0_), channel_id=1, source_target_pairs={{0,1},{1,0},{2,3},{3,2},{4,5},{5,4},{6,7},{7,6},{8,9},{9,8},{10,11... | collective-permute-start | bytes 73736 | tf_op jit(solution)/shard_map/ppermute | solution.py:381
  62.4 1.4 %shard_map.116 = (f32[640,128]{1,0:T(8,128)S(1)}, f32[160,128]{1,0:T(8,128)S(1)}, f32[160,128]{1,0:T(8,128)S(1)}) custom-call(f32[640,128]{1,0:T(8,128)S(1)} %get-tuple-element.74.current_ref, bf16[1280,640]{1,0:T(8,128)(2,1)S(1)} %shard_map.107.inverse_ref, bf16[640,640]{1,0:T(8,128)(2,1)S(1)} %get-tuple-element.60.back_ref.refs_0_), custom_call_target="tpu_custom_call" | custom-call | flops 838860800 | bytes 2785280 | tf_op jit(solution)/shard_map/pallas_call | solution.py:63
  63.8 1.8 %collective-permute-start.21 = (f32[160,128]{1,0:T(8,128)S(1)}, f32[160,128]{1,0:T(8,128)S(1)}, u32[]{:S(2)}, u32[]{:S(2)}) collective-permute-start(f32[160,128]{1,0:T(8,128)S(1)} %get-tuple-element.77), channel_id=1, source_target_pairs={{0,8},{1,9},{2,10},{3,11},{4,12},{5,13},{6,14},{7,15},{8,0},{9,1},... | collective-permute-start | bytes 245768 | tf_op jit(solution)/shard_map/ppermute | solution.py:381
  67.2 1.7 %collective-permute-start.20 = (f32[160,128]{1,0:T(8,128)S(1)}, f32[160,128]{1,0:T(8,128)S(1)}, u32[]{:S(2)}, u32[]{:S(2)}) collective-permute-start(f32[160,128]{1,0:T(8,128)S(1)} %get-tuple-element.118), channel_id=1, source_target_pairs={{0,8},{1,2},{2,1},{3,4},{4,3},{5,6},{6,5},{7,15},{8,0},{9,10},{10,... | collective-permute-start | bytes 245768 | tf_op jit(solution)/shard_map/ppermute | solution.py:381
  68.9 1.8 %collective-permute-done.24.refs_2_ = f32[96,128]{1,0:T(8,128)S(1)} collective-permute-done((f32[96,128]{1,0:T(8,128)S(1)}, f32[96,128]{1,0:T(8,128)S(1)}, u32[]{:S(2)}, u32[]{:S(2)}) %collective-permute-start.24) | collective-permute-done | bytes 49184 | tf_op jit(solution)/shard_map/ppermute | solution.py:381
  70.9 1.2 shard_map.120.cross_ref
  72.2 1.5 %shard_map.119 = (f32[640,128]{1,0:T(8,128)S(1)}, f32[640,128]{1,0:T(8,128)S(1)}) custom-call(s32[4]{0:T(128)S(1)} %select_reduce_fusion.link_ref, s32[8]{0:T(128)S(1)} %fusion.9.order_ref, f32[640,128]{1,0:T(8,128)S(1)} %shard_map.117.y2_ref, f32[160,128]{1,0:T(8,128)S(1)} %collective-permute-done.19.r0, f32[160,128]{1,0:T(8,128)S(1)} %collective-permute-done.20.r1, ...), custom_call_target="tpu_custom_call" | custom-call | flops 838860800 | bytes 3211264 | tf_op jit(solution)/shard_map/pallas_call | solution.py:63
  73.7 1.5 %collective-permute-done.25.more_ref = f32[192,128]{1,0:T(8,128)S(1)} collective-permute-done((f32[192,128]{1,0:T(8,128)S(1)}, f32[192,128]{1,0:T(8,128)S(1)}, u32[]{:S(2)}, u32[]{:S(2)}) %collective-permute-start.25) | collective-permute-done | bytes 98336 | tf_op jit(solution)/shard_map/ppermute | solution.py:381
  75.2 1.1 shard_map.121
  76.3 1.2 collective-permute-start.27
  77.5 1.3 collective-permute-start.29
  78.8 2.4 %collective-permute-done.27.r1 = f32[160,128]{1,0:T(8,128)S(1)} collective-permute-done((f32[160,128]{1,0:T(8,128)S(1)}, f32[160,128]{1,0:T(8,128)S(1)}, u32[]{:S(2)}, u32[]{:S(2)}) %collective-permute-start.27) | collective-permute-done | bytes 81952 | tf_op jit(solution)/shard_map/ppermute | solution.py:381
  83.8 2.6 %collective-permute-done.30.refs_1_ = f32[48,128]{1,0:T(8,128)S(1)} collective-permute-done((f32[48,128]{1,0:T(8,128)S(1)}, f32[48,128]{1,0:T(8,128)S(1)}, u32[]{:S(2)}, u32[]{:S(2)}) %collective-permute-start.30) | collective-permute-done | bytes 24608 | tf_op jit(solution)/shard_map/ppermute | solution.py:381
  87.2 2.2 %collective-permute-done.31.refs_2_ = f32[96,128]{1,0:T(8,128)S(1)} collective-permute-done((f32[96,128]{1,0:T(8,128)S(1)}, f32[96,128]{1,0:T(8,128)S(1)}, u32[]{:S(2)}, u32[]{:S(2)}) %collective-permute-start.31) | collective-permute-done | bytes 49184 | tf_op jit(solution)/shard_map/ppermute | solution.py:381
  89.5 3.4 %collective-permute-start.36 = (f32[48,128]{1,0:T(8,128)S(1)}, f32[48,128]{1,0:T(8,128)S(1)}, u32[]{:S(2)}, u32[]{:S(2)}) collective-permute-start(f32[48,128]{1,0:T(8,128)S(1)} %shard_map.125.refs_0_), channel_id=1, source_target_pairs={{0,1},{1,0},{2,3},{3,2},{4,5},{5,4},{6,7},{7,6},{8,9},{9,8},{10,11... | collective-permute-start | bytes 73736 | tf_op jit(solution)/shard_map/ppermute | solution.py:381
  93.0 1.3 shard_map.123
  98.4 1.5 %collective-permute-done.37.refs_2_ = f32[96,128]{1,0:T(8,128)S(1)} collective-permute-done((f32[96,128]{1,0:T(8,128)S(1)}, f32[96,128]{1,0:T(8,128)S(1)}, u32[]{:S(2)}, u32[]{:S(2)}) %collective-permute-start.37) | collective-permute-done | bytes 49184 | tf_op jit(solution)/shard_map/ppermute | solution.py:381
  100.0 1.9 %collective-permute-start.38 = (f32[192,128]{1,0:T(8,128)S(1)}, f32[192,128]{1,0:T(8,128)S(1)}, u32[]{:S(2)}, u32[]{:S(2)}) collective-permute-start(f32[192,128]{1,0:T(8,128)S(1)} %pad_maximum_fusion.5), channel_id=1, source_target_pairs={{0,5},{1,4},{2,7},{3,6},{4,1},{5,0},{6,3},{7,2},{8,13},{9,12},{10,... | collective-permute-start | bytes 294920 | tf_op jit(solution)/shard_map/ppermute | solution.py:381
  102.2 1.5 %shard_map.126 = (f32[640,128]{1,0:T(8,128)S(1)}, f32[640,128]{1,0:T(8,128)S(1)}) custom-call(s32[4]{0:T(128)S(1)} %select_reduce_fusion.link_ref, s32[8]{0:T(128)S(1)} %fusion.9.order_ref, f32[640,128]{1,0:T(8,128)S(1)} %shard_map.124.y2_ref, f32[160,128]{1,0:T(8,128)S(1)} %collective-permute-done.32.r0, f32[160,128]{1,0:T(8,128)S(1)} %collective-permute-done.33.r1, ...), custom_call_target="tpu_custom_call" | custom-call | flops 838860800 | bytes 3211264 | tf_op jit(solution)/shard_map/pallas_call | solution.py:63
  103.7 1.1 collective-permute-done.38.more_ref
  104.8 1.1 shard_map.127
  106.2 1.1 collective-permute-start.40
  108.5 2.0 %collective-permute-done.40.r1 = f32[160,128]{1,0:T(8,128)S(1)} collective-permute-done((f32[160,128]{1,0:T(8,128)S(1)}, f32[160,128]{1,0:T(8,128)S(1)}, u32[]{:S(2)}, u32[]{:S(2)}) %collective-permute-start.40) | collective-permute-done | bytes 81952 | tf_op jit(solution)/shard_map/ppermute | solution.py:381
  110.5 1.3 collective-permute-done.41.r2
  112.5 1.7 %collective-permute-start.43 = (f32[48,128]{1,0:T(8,128)S(1)}, f32[48,128]{1,0:T(8,128)S(1)}, u32[]{:S(2)}, u32[]{:S(2)}) collective-permute-start(f32[48,128]{1,0:T(8,128)S(1)} %get-tuple-element.94.refs_0_), channel_id=1, source_target_pairs={{0,16},{1,17},{2,18},{3,19},{4,20},{5,21},{6,22},{7,23},{8,24},{9,... | collective-permute-start | bytes 73736 | tf_op jit(solution)/shard_map/ppermute | solution.py:381
  114.3 1.9 %collective-permute-done.43.refs_1_ = f32[48,128]{1,0:T(8,128)S(1)} collective-permute-done((f32[48,128]{1,0:T(8,128)S(1)}, f32[48,128]{1,0:T(8,128)S(1)}, u32[]{:S(2)}, u32[]{:S(2)}) %collective-permute-start.43) | collective-permute-done | bytes 24608 | tf_op jit(solution)/shard_map/ppermute | solution.py:381
  116.8 2.3 %collective-permute-done.44.refs_2_ = f32[96,128]{1,0:T(8,128)S(1)} collective-permute-done((f32[96,128]{1,0:T(8,128)S(1)}, f32[96,128]{1,0:T(8,128)S(1)}, u32[]{:S(2)}, u32[]{:S(2)}) %collective-permute-start.44) | collective-permute-done | bytes 49184 | tf_op jit(solution)/shard_map/ppermute | solution.py:381
  119.3 3.2 %collective-permute-start.49 = (f32[48,128]{1,0:T(8,128)S(1)}, f32[48,128]{1,0:T(8,128)S(1)}, u32[]{:S(2)}, u32[]{:S(2)}) collective-permute-start(f32[48,128]{1,0:T(8,128)S(1)} %shard_map.131.refs_0_), channel_id=1, source_target_pairs={{0,1},{1,0},{2,3},{3,2},{4,5},{5,4},{6,7},{7,6},{8,9},{9,8},{10,11... | collective-permute-start | bytes 73736 | tf_op jit(solution)/shard_map/ppermute | solution.py:381
  122.6 1.3 shard_map.129
  123.9 1.0 collective-permute-start.47
  126.1 1.5 %collective-permute-start.50 = (f32[96,128]{1,0:T(8,128)S(1)}, f32[96,128]{1,0:T(8,128)S(1)}, u32[]{:S(2)}, u32[]{:S(2)}) collective-permute-start(f32[96,128]{1,0:T(8,128)S(1)} %pad_maximum_fusion.14), channel_id=1, source_target_pairs={{0,3},{1,2},{2,1},{3,0},{4,7},{5,6},{6,5},{7,4},{8,11},{9,10},{10,... | collective-permute-start | bytes 147464 | tf_op jit(solution)/shard_map/ppermute | solution.py:381
  128.2 1.5 %collective-permute-done.50.refs_2_ = f32[96,128]{1,0:T(8,128)S(1)} collective-permute-done((f32[96,128]{1,0:T(8,128)S(1)}, f32[96,128]{1,0:T(8,128)S(1)}, u32[]{:S(2)}, u32[]{:S(2)}) %collective-permute-start.50) | collective-permute-done | bytes 49184 | tf_op jit(solution)/shard_map/ppermute | solution.py:381
  129.7 1.6 %collective-permute-start.51 = (f32[192,128]{1,0:T(8,128)S(1)}, f32[192,128]{1,0:T(8,128)S(1)}, u32[]{:S(2)}, u32[]{:S(2)}) collective-permute-start(f32[192,128]{1,0:T(8,128)S(1)} %pad_maximum_fusion.6), channel_id=1, source_target_pairs={{0,5},{1,4},{2,7},{3,6},{4,1},{5,0},{6,3},{7,2},{8,13},{9,12},{10,... | collective-permute-start | bytes 294920 | tf_op jit(solution)/shard_map/ppermute | solution.py:381
  131.4 1.3 collective-permute-done.46.r1
  132.6 1.5 %shard_map.132 = (f32[640,128]{1,0:T(8,128)S(1)}, f32[640,128]{1,0:T(8,128)S(1)}) custom-call(s32[4]{0:T(128)S(1)} %select_reduce_fusion.link_ref, s32[8]{0:T(128)S(1)} %fusion.9.order_ref, f32[640,128]{1,0:T(8,128)S(1)} %shard_map.130.y2_ref, f32[160,128]{1,0:T(8,128)S(1)} %collective-permute-done.45.r0, f32[160,128]{1,0:T(8,128)S(1)} %collective-permute-done.46.r1, ...), custom_call_target="tpu_custom_call" | custom-call | flops 838860800 | bytes 3211264 | tf_op jit(solution)/shard_map/pallas_call | solution.py:63
  134.4 1.1 shard_map.133
  135.8 1.6 %collective-permute-start.53 = (f32[160,128]{1,0:T(8,128)S(1)}, f32[160,128]{1,0:T(8,128)S(1)}, u32[]{:S(2)}, u32[]{:S(2)}) collective-permute-start(f32[160,128]{1,0:T(8,128)S(1)} %get-tuple-element.104), channel_id=1, source_target_pairs={{0,8},{1,2},{2,1},{3,4},{4,3},{5,6},{6,5},{7,15},{8,0},{9,10},{10,... | collective-permute-start | bytes 245768 | tf_op jit(solution)/shard_map/ppermute | solution.py:381
  138.4 1.4 shard_map.134
  140.7 1.7 %shard_map.135 = f32[640,128]{1,0:T(8,128)} custom-call(s32[4]{0:T(128)S(1)} %select_reduce_fusion.link_ref, f32[640,128]{1,0:T(8,128)S(1)} %get-tuple-element.101.f_ref, f32[160,128]{1,0:T(8,128)S(1)} %collective-permute-done.52.r0, f32[160,128]{1,0:T(8,128)S(1)} %collective-permute-done.53.r1, f32[160,128]{1,0:T(8,128)S(1)} %collective-permute-done.54.r2, ...), custom_call_target="tpu_custom_call" | custom-call | bytes 1802240 | tf_op jit(solution)/shard_map/pallas_call | solution.py:63
  (125 shorter events, 25.9 us)
Async XLA Ops:
  0.6 2.4 %copy-start.2 = (s32[1,1,640]{2,1,0:T(1,128)S(1)}, s32[1,1,640]{2,1,0:T(1,128)}, u32[]{:S(2)}) copy-start(s32[1,1,640]{2,1,0:T(1,128)} %param.12) | copy-start | bytes 7684
  0.6 3.7 %copy-start.3 = (f32[48,384]{1,0:T(8,128)S(1)}, f32[48,384]{1,0:T(8,128)}, u32[]{:S(2)}) copy-start(f32[48,384]{1,0:T(8,128)} %param.17) | copy-start | bytes 221188
  0.7 3.7 %copy-start.5 = (f32[1,48,48]{2,1,0:T(8,128)S(1)}, f32[1,48,48]{2,1,0:T(8,128)}, u32[]{:S(2)}) copy-start(f32[1,48,48]{2,1,0:T(8,128)} %param.16) | copy-start | bytes 27652
  0.7 3.7 %copy-start.4 = (f32[1,48,192]{2,1,0:T(8,128)S(1)}, f32[1,48,192]{2,1,0:T(8,128)}, u32[]{:S(2)}) copy-start(f32[1,48,192]{2,1,0:T(8,128)} %param.15) | copy-start | bytes 110596
  2.9 6.7 %copy-start.6 = (s32[1,1,4]{2,1,0:T(1,128)S(1)}, s32[1,1,4]{2,1,0:T(1,128)}, u32[]{:S(2)}) copy-start(s32[1,1,4]{2,1,0:T(1,128)} %param.13) | copy-start | bytes 52
  4.5 17.2 %copy-start.1 = (f32[1,1,640,640]{3,2,1,0:T(8,128)S(1)}, f32[1,1,640,640]{3,2,1,0:T(8,128)}, u32[]{:S(2)}) copy-start(f32[1,1,640,640]{3,2,1,0:T(8,128)} %param.11) | copy-start | bytes 4915204
  5.6 9.1 %collective-permute-start = (f32[384,128]{1,0:T(8,128)S(1)}, f32[384,128]{1,0:T(8,128)S(1)}, u32[]{:S(2)}, u32[]{:S(2)}) collective-permute-start(f32[384,128]{1,0:T(8,128)S(1)} %get-tuple-element.54), channel_id=1, source_target_pairs={{0,1},{1,0},{2,3},{3,2},{4,5},{5,4},{6,7},{7,6},{8,9},{9,8},{10,11... | collective-permute-start | bytes 589832 | tf_op jit(solution)/shard_map/ppermute | solution.py:381
  5.7 9.1 %collective-permute-start.1 = (f32[384,128]{1,0:T(8,128)S(1)}, f32[384,128]{1,0:T(8,128)S(1)}, u32[]{:S(2)}, u32[]{:S(2)}) collective-permute-start(f32[384,128]{1,0:T(8,128)S(1)} %get-tuple-element.55), channel_id=1, source_target_pairs={{0,8},{1,2},{2,1},{3,4},{4,3},{5,6},{6,5},{7,15},{8,0},{9,10},{10,... | collective-permute-start | bytes 589832 | tf_op jit(solution)/shard_map/ppermute | solution.py:381
  8.3 6.4 %collective-permute-start.2 = (f32[336,128]{1,0:T(8,128)S(1)}, f32[336,128]{1,0:T(8,128)S(1)}, u32[]{:S(2)}, u32[]{:S(2)}) collective-permute-start(f32[336,128]{1,0:T(8,128)S(1)} %get-tuple-element.56), channel_id=1, source_target_pairs={{0,8},{1,9},{2,10},{3,11},{4,12},{5,13},{6,14},{7,15},{8,0},{9,1},... | collective-permute-start | bytes 516104 | tf_op jit(solution)/shard_map/ppermute | solution.py:381
  9.6 5.1 %collective-permute-start.3 = (f32[336,128]{1,0:T(8,128)S(1)}, f32[336,128]{1,0:T(8,128)S(1)}, u32[]{:S(2)}, u32[]{:S(2)}) collective-permute-start(f32[336,128]{1,0:T(8,128)S(1)} %get-tuple-element.57), channel_id=1, source_target_pairs={{0,1},{1,0},{2,3},{3,2},{4,5},{5,4},{6,7},{7,6},{8,16},{9,17},{10,... | collective-permute-start | bytes 516104 | tf_op jit(solution)/shard_map/ppermute | solution.py:381
  15.5 5.1 %collective-permute-start.4 = (f32[96,128]{1,0:T(8,128)S(1)}, f32[96,128]{1,0:T(8,128)S(1)}, u32[]{:S(2)}, u32[]{:S(2)}) collective-permute-start(f32[96,128]{1,0:T(8,128)S(1)} %pad_maximum_fusion.7), channel_id=1, source_target_pairs={{0,16},{1,17},{2,18},{3,19},{4,20},{5,21},{6,22},{7,23},{8,24},{9,... | collective-permute-start | bytes 147464 | tf_op jit(solution)/shard_map/ppermute | solution.py:381
  20.6 3.5 %collective-permute-start.5 = (f32[192,128]{1,0:T(8,128)S(1)}, f32[192,128]{1,0:T(8,128)S(1)}, u32[]{:S(2)}, u32[]{:S(2)}) collective-permute-start(f32[192,128]{1,0:T(8,128)S(1)} %pad_maximum_fusion.2), channel_id=1, source_target_pairs={{0,8},{1,9},{2,10},{3,11},{4,12},{5,13},{6,14},{7,15},{8,0},{9,1},... | collective-permute-start | bytes 294920 | tf_op jit(solution)/shard_map/ppermute | solution.py:381
  24.4 9.3 %collective-permute-start.10 = (f32[48,128]{1,0:T(8,128)S(1)}, f32[48,128]{1,0:T(8,128)S(1)}, u32[]{:S(2)}, u32[]{:S(2)}) collective-permute-start(f32[48,128]{1,0:T(8,128)S(1)} %shard_map.113.refs_0_), channel_id=1, source_target_pairs={{0,1},{1,0},{2,3},{3,2},{4,5},{5,4},{6,7},{7,6},{8,9},{9,8},{10,11... | collective-permute-start | bytes 73736 | tf_op jit(solution)/shard_map/ppermute | solution.py:381
  28.8 12.7 %collective-permute-start.8 = (f32[160,128]{1,0:T(8,128)S(1)}, f32[160,128]{1,0:T(8,128)S(1)}, u32[]{:S(2)}, u32[]{:S(2)}) collective-permute-start(f32[160,128]{1,0:T(8,128)S(1)} %get-tuple-element.69), channel_id=1, source_target_pairs={{0,8},{1,9},{2,10},{3,11},{4,12},{5,13},{6,14},{7,15},{8,0},{9,1},... | collective-permute-start | bytes 245768 | tf_op jit(solution)/shard_map/ppermute | solution.py:381
  30.1 11.4 %collective-permute-start.9 = (f32[160,128]{1,0:T(8,128)S(1)}, f32[160,128]{1,0:T(8,128)S(1)}, u32[]{:S(2)}, u32[]{:S(2)}) collective-permute-start(f32[160,128]{1,0:T(8,128)S(1)} %get-tuple-element.70), channel_id=1, source_target_pairs={{0,1},{1,0},{2,3},{3,2},{4,5},{5,4},{6,7},{7,6},{8,16},{9,17},{10,... | collective-permute-start | bytes 245768 | tf_op jit(solution)/shard_map/ppermute | solution.py:381
  30.4 8.0 %copy-start = (f32[1,1,640,640]{3,2,1,0:T(8,128)S(1)}, f32[1,1,640,640]{3,2,1,0:T(8,128)}, u32[]{:S(2)}) copy-start(f32[1,1,640,640]{3,2,1,0:T(8,128)} %param.10) | copy-start | bytes 4915204
  33.6 3.6 %collective-permute-start.11 = (f32[96,128]{1,0:T(8,128)S(1)}, f32[96,128]{1,0:T(8,128)S(1)}, u32[]{:S(2)}, u32[]{:S(2)}) collective-permute-start(f32[96,128]{1,0:T(8,128)S(1)} %pad_maximum_fusion.8), channel_id=1, source_target_pairs={{0,3},{1,2},{2,1},{3,0},{4,7},{5,6},{6,5},{7,4},{8,11},{9,10},{10,... | collective-permute-start | bytes 147464 | tf_op jit(solution)/shard_map/ppermute | solution.py:381
  34.5 6.9 %collective-permute-start.6 = (f32[160,128]{1,0:T(8,128)S(1)}, f32[160,128]{1,0:T(8,128)S(1)}, u32[]{:S(2)}, u32[]{:S(2)}) collective-permute-start(f32[160,128]{1,0:T(8,128)S(1)} %get-tuple-element.125), channel_id=1, source_target_pairs={{0,1},{1,0},{2,3},{3,2},{4,5},{5,4},{6,7},{7,6},{8,9},{9,8},{10,11... | collective-permute-start | bytes 245768 | tf_op jit(solution)/shard_map/ppermute | solution.py:381
  34.9 6.6 %collective-permute-start.7 = (f32[160,128]{1,0:T(8,128)S(1)}, f32[160,128]{1,0:T(8,128)S(1)}, u32[]{:S(2)}, u32[]{:S(2)}) collective-permute-start(f32[160,128]{1,0:T(8,128)S(1)} %get-tuple-element.124), channel_id=1, source_target_pairs={{0,8},{1,2},{2,1},{3,4},{4,3},{5,6},{6,5},{7,15},{8,0},{9,10},{10,... | collective-permute-start | bytes 245768 | tf_op jit(solution)/shard_map/ppermute | solution.py:381
  37.3 4.7 %collective-permute-start.12 = (f32[192,128]{1,0:T(8,128)S(1)}, f32[192,128]{1,0:T(8,128)S(1)}, u32[]{:S(2)}, u32[]{:S(2)}) collective-permute-start(f32[192,128]{1,0:T(8,128)S(1)} %pad_maximum_fusion.3), channel_id=1, source_target_pairs={{0,5},{1,4},{2,7},{3,6},{4,1},{5,0},{6,3},{7,2},{8,13},{9,12},{10,... | collective-permute-start | bytes 294920 | tf_op jit(solution)/shard_map/ppermute | solution.py:381
  43.7 4.5 %collective-permute-start.13 = (f32[160,128]{1,0:T(8,128)S(1)}, f32[160,128]{1,0:T(8,128)S(1)}, u32[]{:S(2)}, u32[]{:S(2)}) collective-permute-start(f32[160,128]{1,0:T(8,128)S(1)} %get-tuple-element.123), channel_id=1, source_target_pairs={{0,1},{1,0},{2,3},{3,2},{4,5},{5,4},{6,7},{7,6},{8,9},{9,8},{10,11... | collective-permute-start | bytes 245768 | tf_op jit(solution)/shard_map/ppermute | solution.py:381
  44.0 4.4 %collective-permute-start.14 = (f32[160,128]{1,0:T(8,128)S(1)}, f32[160,128]{1,0:T(8,128)S(1)}, u32[]{:S(2)}, u32[]{:S(2)}) collective-permute-start(f32[160,128]{1,0:T(8,128)S(1)} %get-tuple-element.122), channel_id=1, source_target_pairs={{0,8},{1,2},{2,1},{3,4},{4,3},{5,6},{6,5},{7,15},{8,0},{9,10},{10,... | collective-permute-start | bytes 245768 | tf_op jit(solution)/shard_map/ppermute | solution.py:381
  44.9 5.7 %collective-permute-start.15 = (f32[160,128]{1,0:T(8,128)S(1)}, f32[160,128]{1,0:T(8,128)S(1)}, u32[]{:S(2)}, u32[]{:S(2)}) collective-permute-start(f32[160,128]{1,0:T(8,128)S(1)} %get-tuple-element.121), channel_id=1, source_target_pairs={{0,8},{1,9},{2,10},{3,11},{4,12},{5,13},{6,14},{7,15},{8,0},{9,1},... | collective-permute-start | bytes 245768 | tf_op jit(solution)/shard_map/ppermute | solution.py:381
  48.2 2.4 %collective-permute-start.16 = (f32[160,128]{1,0:T(8,128)S(1)}, f32[160,128]{1,0:T(8,128)S(1)}, u32[]{:S(2)}, u32[]{:S(2)}) collective-permute-start(f32[160,128]{1,0:T(8,128)S(1)} %get-tuple-element.120), channel_id=1, source_target_pairs={{0,1},{1,0},{2,3},{3,2},{4,5},{5,4},{6,7},{7,6},{8,16},{9,17},{10,... | collective-permute-start | bytes 245768 | tf_op jit(solution)/shard_map/ppermute | solution.py:381
  51.4 3.6 %collective-permute-start.17 = (f32[48,128]{1,0:T(8,128)S(1)}, f32[48,128]{1,0:T(8,128)S(1)}, u32[]{:S(2)}, u32[]{:S(2)}) collective-permute-start(f32[48,128]{1,0:T(8,128)S(1)} %get-tuple-element.76.refs_0_), channel_id=1, source_target_pairs={{0,16},{1,17},{2,18},{3,19},{4,20},{5,21},{6,22},{7,23},{8,24},{9,... | collective-permute-start | bytes 73736 | tf_op jit(solution)/shard_map/ppermute | solution.py:381
  55.0 3.6 %collective-permute-start.18 = (f32[96,128]{1,0:T(8,128)S(1)}, f32[96,128]{1,0:T(8,128)S(1)}, u32[]{:S(2)}, u32[]{:S(2)}) collective-permute-start(f32[96,128]{1,0:T(8,128)S(1)} %pad_maximum_fusion.9), channel_id=1, source_target_pairs={{0,8},{1,9},{2,10},{3,11},{4,12},{5,13},{6,14},{7,15},{8,0},{9,1},... | collective-permute-start | bytes 147464 | tf_op jit(solution)/shard_map/ppermute | solution.py:381
  58.8 8.0 %collective-permute-start.23 = (f32[48,128]{1,0:T(8,128)S(1)}, f32[48,128]{1,0:T(8,128)S(1)}, u32[]{:S(2)}, u32[]{:S(2)}) collective-permute-start(f32[48,128]{1,0:T(8,128)S(1)} %shard_map.118.refs_0_), channel_id=1, source_target_pairs={{0,1},{1,0},{2,3},{3,2},{4,5},{5,4},{6,7},{7,6},{8,9},{9,8},{10,11... | collective-permute-start | bytes 73736 | tf_op jit(solution)/shard_map/ppermute | solution.py:381
  63.8 8.3 %collective-permute-start.21 = (f32[160,128]{1,0:T(8,128)S(1)}, f32[160,128]{1,0:T(8,128)S(1)}, u32[]{:S(2)}, u32[]{:S(2)}) collective-permute-start(f32[160,128]{1,0:T(8,128)S(1)} %get-tuple-element.77), channel_id=1, source_target_pairs={{0,8},{1,9},{2,10},{3,11},{4,12},{5,13},{6,14},{7,15},{8,0},{9,1},... | collective-permute-start | bytes 245768 | tf_op jit(solution)/shard_map/ppermute | solution.py:381
  65.6 6.5 %collective-permute-start.22 = (f32[160,128]{1,0:T(8,128)S(1)}, f32[160,128]{1,0:T(8,128)S(1)}, u32[]{:S(2)}, u32[]{:S(2)}) collective-permute-start(f32[160,128]{1,0:T(8,128)S(1)} %get-tuple-element.78), channel_id=1, source_target_pairs={{0,1},{1,0},{2,3},{3,2},{4,5},{5,4},{6,7},{7,6},{8,16},{9,17},{10,... | collective-permute-start | bytes 245768 | tf_op jit(solution)/shard_map/ppermute | solution.py:381
  66.8 3.9 %collective-permute-start.24 = (f32[96,128]{1,0:T(8,128)S(1)}, f32[96,128]{1,0:T(8,128)S(1)}, u32[]{:S(2)}, u32[]{:S(2)}) collective-permute-start(f32[96,128]{1,0:T(8,128)S(1)} %pad_maximum_fusion.10), channel_id=1, source_target_pairs={{0,3},{1,2},{2,1},{3,0},{4,7},{5,6},{6,5},{7,4},{8,11},{9,10},{10,... | collective-permute-start | bytes 147464 | tf_op jit(solution)/shard_map/ppermute | solution.py:381
  66.9 5.2 %collective-permute-start.19 = (f32[160,128]{1,0:T(8,128)S(1)}, f32[160,128]{1,0:T(8,128)S(1)}, u32[]{:S(2)}, u32[]{:S(2)}) collective-permute-start(f32[160,128]{1,0:T(8,128)S(1)} %get-tuple-element.119), channel_id=1, source_target_pairs={{0,1},{1,0},{2,3},{3,2},{4,5},{5,4},{6,7},{7,6},{8,9},{9,8},{10,11... | collective-permute-start | bytes 245768 | tf_op jit(solution)/shard_map/ppermute | solution.py:381
  67.2 5.0 %collective-permute-start.20 = (f32[160,128]{1,0:T(8,128)S(1)}, f32[160,128]{1,0:T(8,128)S(1)}, u32[]{:S(2)}, u32[]{:S(2)}) collective-permute-start(f32[160,128]{1,0:T(8,128)S(1)} %get-tuple-element.118), channel_id=1, source_target_pairs={{0,8},{1,2},{2,1},{3,4},{4,3},{5,6},{6,5},{7,15},{8,0},{9,10},{10,... | collective-permute-start | bytes 245768 | tf_op jit(solution)/shard_map/ppermute | solution.py:381
  70.8 4.4 %collective-permute-start.25 = (f32[192,128]{1,0:T(8,128)S(1)}, f32[192,128]{1,0:T(8,128)S(1)}, u32[]{:S(2)}, u32[]{:S(2)}) collective-permute-start(f32[192,128]{1,0:T(8,128)S(1)} %pad_maximum_fusion.4), channel_id=1, source_target_pairs={{0,5},{1,4},{2,7},{3,6},{4,1},{5,0},{6,3},{7,2},{8,13},{9,12},{10,... | collective-permute-start | bytes 294920 | tf_op jit(solution)/shard_map/ppermute | solution.py:381
  76.2 2.6 %collective-permute-start.26 = (f32[160,128]{1,0:T(8,128)S(1)}, f32[160,128]{1,0:T(8,128)S(1)}, u32[]{:S(2)}, u32[]{:S(2)}) collective-permute-start(f32[160,128]{1,0:T(8,128)S(1)} %get-tuple-element.117), channel_id=1, source_target_pairs={{0,1},{1,0},{2,3},{3,2},{4,5},{5,4},{6,7},{7,6},{8,9},{9,8},{10,11... | collective-permute-start | bytes 245768 | tf_op jit(solution)/shard_map/ppermute | solution.py:381
  76.3 4.9 %collective-permute-start.27 = (f32[160,128]{1,0:T(8,128)S(1)}, f32[160,128]{1,0:T(8,128)S(1)}, u32[]{:S(2)}, u32[]{:S(2)}) collective-permute-start(f32[160,128]{1,0:T(8,128)S(1)} %get-tuple-element.116), channel_id=1, source_target_pairs={{0,8},{1,2},{2,1},{3,4},{4,3},{5,6},{6,5},{7,15},{8,0},{9,10},{10,... | collective-permute-start | bytes 245768 | tf_op jit(solution)/shard_map/ppermute | solution.py:381
  77.5 4.5 %collective-permute-start.28 = (f32[160,128]{1,0:T(8,128)S(1)}, f32[160,128]{1,0:T(8,128)S(1)}, u32[]{:S(2)}, u32[]{:S(2)}) collective-permute-start(f32[160,128]{1,0:T(8,128)S(1)} %get-tuple-element.115), channel_id=1, source_target_pairs={{0,8},{1,9},{2,10},{3,11},{4,12},{5,13},{6,14},{7,15},{8,0},{9,1},... | collective-permute-start | bytes 245768 | tf_op jit(solution)/shard_map/ppermute | solution.py:381
  77.5 4.5 %collective-permute-start.29 = (f32[160,128]{1,0:T(8,128)S(1)}, f32[160,128]{1,0:T(8,128)S(1)}, u32[]{:S(2)}, u32[]{:S(2)}) collective-permute-start(f32[160,128]{1,0:T(8,128)S(1)} %get-tuple-element.114), channel_id=1, source_target_pairs={{0,1},{1,0},{2,3},{3,2},{4,5},{5,4},{6,7},{7,6},{8,16},{9,17},{10,... | collective-permute-start | bytes 245768 | tf_op jit(solution)/shard_map/ppermute | solution.py:381
  82.8 3.6 %collective-permute-start.30 = (f32[48,128]{1,0:T(8,128)S(1)}, f32[48,128]{1,0:T(8,128)S(1)}, u32[]{:S(2)}, u32[]{:S(2)}) collective-permute-start(f32[48,128]{1,0:T(8,128)S(1)} %get-tuple-element.85.refs_0_), channel_id=1, source_target_pairs={{0,16},{1,17},{2,18},{3,19},{4,20},{5,21},{6,22},{7,23},{8,24},{9,... | collective-permute-start | bytes 73736 | tf_op jit(solution)/shard_map/ppermute | solution.py:381
  86.4 2.9 %collective-permute-start.31 = (f32[96,128]{1,0:T(8,128)S(1)}, f32[96,128]{1,0:T(8,128)S(1)}, u32[]{:S(2)}, u32[]{:S(2)}) collective-permute-start(f32[96,128]{1,0:T(8,128)S(1)} %pad_maximum_fusion.11), channel_id=1, source_target_pairs={{0,8},{1,9},{2,10},{3,11},{4,12},{5,13},{6,14},{7,15},{8,0},{9,1},... | collective-permute-start | bytes 147464 | tf_op jit(solution)/shard_map/ppermute | solution.py:381
  89.5 6.7 %collective-permute-start.36 = (f32[48,128]{1,0:T(8,128)S(1)}, f32[48,128]{1,0:T(8,128)S(1)}, u32[]{:S(2)}, u32[]{:S(2)}) collective-permute-start(f32[48,128]{1,0:T(8,128)S(1)} %shard_map.125.refs_0_), channel_id=1, source_target_pairs={{0,1},{1,0},{2,3},{3,2},{4,5},{5,4},{6,7},{7,6},{8,9},{9,8},{10,11... | collective-permute-start | bytes 73736 | tf_op jit(solution)/shard_map/ppermute | solution.py:381
  94.2 7.6 %collective-permute-start.34 = (f32[160,128]{1,0:T(8,128)S(1)}, f32[160,128]{1,0:T(8,128)S(1)}, u32[]{:S(2)}, u32[]{:S(2)}) collective-permute-start(f32[160,128]{1,0:T(8,128)S(1)} %get-tuple-element.86), channel_id=1, source_target_pairs={{0,8},{1,9},{2,10},{3,11},{4,12},{5,13},{6,14},{7,15},{8,0},{9,1},... | collective-permute-start | bytes 245768 | tf_op jit(solution)/shard_map/ppermute | solution.py:381
  95.1 6.7 %collective-permute-start.35 = (f32[160,128]{1,0:T(8,128)S(1)}, f32[160,128]{1,0:T(8,128)S(1)}, u32[]{:S(2)}, u32[]{:S(2)}) collective-permute-start(f32[160,128]{1,0:T(8,128)S(1)} %get-tuple-element.87), channel_id=1, source_target_pairs={{0,1},{1,0},{2,3},{3,2},{4,5},{5,4},{6,7},{7,6},{8,16},{9,17},{10,... | collective-permute-start | bytes 245768 | tf_op jit(solution)/shard_map/ppermute | solution.py:381
  96.3 3.6 %collective-permute-start.37 = (f32[96,128]{1,0:T(8,128)S(1)}, f32[96,128]{1,0:T(8,128)S(1)}, u32[]{:S(2)}, u32[]{:S(2)}) collective-permute-start(f32[96,128]{1,0:T(8,128)S(1)} %pad_maximum_fusion.12), channel_id=1, source_target_pairs={{0,3},{1,2},{2,1},{3,0},{4,7},{5,6},{6,5},{7,4},{8,11},{9,10},{10,... | collective-permute-start | bytes 147464 | tf_op jit(solution)/shard_map/ppermute | solution.py:381
  97.2 4.6 %collective-permute-start.32 = (f32[160,128]{1,0:T(8,128)S(1)}, f32[160,128]{1,0:T(8,128)S(1)}, u32[]{:S(2)}, u32[]{:S(2)}) collective-permute-start(f32[160,128]{1,0:T(8,128)S(1)} %get-tuple-element.113), channel_id=1, source_target_pairs={{0,1},{1,0},{2,3},{3,2},{4,5},{5,4},{6,7},{7,6},{8,9},{9,8},{10,11... | collective-permute-start | bytes 245768 | tf_op jit(solution)/shard_map/ppermute | solution.py:381
  97.6 4.6 %collective-permute-start.33 = (f32[160,128]{1,0:T(8,128)S(1)}, f32[160,128]{1,0:T(8,128)S(1)}, u32[]{:S(2)}, u32[]{:S(2)}) collective-permute-start(f32[160,128]{1,0:T(8,128)S(1)} %get-tuple-element.112), channel_id=1, source_target_pairs={{0,8},{1,2},{2,1},{3,4},{4,3},{5,6},{6,5},{7,15},{8,0},{9,10},{10,... | collective-permute-start | bytes 245768 | tf_op jit(solution)/shard_map/ppermute | solution.py:381
  100.0 4.8 %collective-permute-start.38 = (f32[192,128]{1,0:T(8,128)S(1)}, f32[192,128]{1,0:T(8,128)S(1)}, u32[]{:S(2)}, u32[]{:S(2)}) collective-permute-start(f32[192,128]{1,0:T(8,128)S(1)} %pad_maximum_fusion.5), channel_id=1, source_target_pairs={{0,5},{1,4},{2,7},{3,6},{4,1},{5,0},{6,3},{7,2},{8,13},{9,12},{10,... | collective-permute-start | bytes 294920 | tf_op jit(solution)/shard_map/ppermute | solution.py:381
  105.9 2.6 %collective-permute-start.39 = (f32[160,128]{1,0:T(8,128)S(1)}, f32[160,128]{1,0:T(8,128)S(1)}, u32[]{:S(2)}, u32[]{:S(2)}) collective-permute-start(f32[160,128]{1,0:T(8,128)S(1)} %get-tuple-element.111), channel_id=1, source_target_pairs={{0,1},{1,0},{2,3},{3,2},{4,5},{5,4},{6,7},{7,6},{8,9},{9,8},{10,11... | collective-permute-start | bytes 245768 | tf_op jit(solution)/shard_map/ppermute | solution.py:381
  106.2 4.2 %collective-permute-start.40 = (f32[160,128]{1,0:T(8,128)S(1)}, f32[160,128]{1,0:T(8,128)S(1)}, u32[]{:S(2)}, u32[]{:S(2)}) collective-permute-start(f32[160,128]{1,0:T(8,128)S(1)} %get-tuple-element.110), channel_id=1, source_target_pairs={{0,8},{1,2},{2,1},{3,4},{4,3},{5,6},{6,5},{7,15},{8,0},{9,10},{10,... | collective-permute-start | bytes 245768 | tf_op jit(solution)/shard_map/ppermute | solution.py:381
  107.3 4.5 %collective-permute-start.41 = (f32[160,128]{1,0:T(8,128)S(1)}, f32[160,128]{1,0:T(8,128)S(1)}, u32[]{:S(2)}, u32[]{:S(2)}) collective-permute-start(f32[160,128]{1,0:T(8,128)S(1)} %get-tuple-element.109), channel_id=1, source_target_pairs={{0,8},{1,9},{2,10},{3,11},{4,12},{5,13},{6,14},{7,15},{8,0},{9,1},... | collective-permute-start | bytes 245768 | tf_op jit(solution)/shard_map/ppermute | solution.py:381
  107.9 3.8 %collective-permute-start.42 = (f32[160,128]{1,0:T(8,128)S(1)}, f32[160,128]{1,0:T(8,128)S(1)}, u32[]{:S(2)}, u32[]{:S(2)}) collective-permute-start(f32[160,128]{1,0:T(8,128)S(1)} %get-tuple-element.108), channel_id=1, source_target_pairs={{0,1},{1,0},{2,3},{3,2},{4,5},{5,4},{6,7},{7,6},{8,16},{9,17},{10,... | collective-permute-start | bytes 245768 | tf_op jit(solution)/shard_map/ppermute | solution.py:381
  112.5 3.6 %collective-permute-start.43 = (f32[48,128]{1,0:T(8,128)S(1)}, f32[48,128]{1,0:T(8,128)S(1)}, u32[]{:S(2)}, u32[]{:S(2)}) collective-permute-start(f32[48,128]{1,0:T(8,128)S(1)} %get-tuple-element.94.refs_0_), channel_id=1, source_target_pairs={{0,16},{1,17},{2,18},{3,19},{4,20},{5,21},{6,22},{7,23},{8,24},{9,... | collective-permute-start | bytes 73736 | tf_op jit(solution)/shard_map/ppermute | solution.py:381
  116.2 2.9 %collective-permute-start.44 = (f32[96,128]{1,0:T(8,128)S(1)}, f32[96,128]{1,0:T(8,128)S(1)}, u32[]{:S(2)}, u32[]{:S(2)}) collective-permute-start(f32[96,128]{1,0:T(8,128)S(1)} %pad_maximum_fusion.13), channel_id=1, source_target_pairs={{0,8},{1,9},{2,10},{3,11},{4,12},{5,13},{6,14},{7,15},{8,0},{9,1},... | collective-permute-start | bytes 147464 | tf_op jit(solution)/shard_map/ppermute | solution.py:381
  119.3 6.7 %collective-permute-start.49 = (f32[48,128]{1,0:T(8,128)S(1)}, f32[48,128]{1,0:T(8,128)S(1)}, u32[]{:S(2)}, u32[]{:S(2)}) collective-permute-start(f32[48,128]{1,0:T(8,128)S(1)} %shard_map.131.refs_0_), channel_id=1, source_target_pairs={{0,1},{1,0},{2,3},{3,2},{4,5},{5,4},{6,7},{7,6},{8,9},{9,8},{10,11... | collective-permute-start | bytes 73736 | tf_op jit(solution)/shard_map/ppermute | solution.py:381
  123.9 7.5 %collective-permute-start.47 = (f32[160,128]{1,0:T(8,128)S(1)}, f32[160,128]{1,0:T(8,128)S(1)}, u32[]{:S(2)}, u32[]{:S(2)}) collective-permute-start(f32[160,128]{1,0:T(8,128)S(1)} %get-tuple-element.95), channel_id=1, source_target_pairs={{0,8},{1,9},{2,10},{3,11},{4,12},{5,13},{6,14},{7,15},{8,0},{9,1},... | collective-permute-start | bytes 245768 | tf_op jit(solution)/shard_map/ppermute | solution.py:381
  124.9 6.5 %collective-permute-start.48 = (f32[160,128]{1,0:T(8,128)S(1)}, f32[160,128]{1,0:T(8,128)S(1)}, u32[]{:S(2)}, u32[]{:S(2)}) collective-permute-start(f32[160,128]{1,0:T(8,128)S(1)} %get-tuple-element.96), channel_id=1, source_target_pairs={{0,1},{1,0},{2,3},{3,2},{4,5},{5,4},{6,7},{7,6},{8,16},{9,17},{10,... | collective-permute-start | bytes 245768 | tf_op jit(solution)/shard_map/ppermute | solution.py:381
  126.1 3.6 %collective-permute-start.50 = (f32[96,128]{1,0:T(8,128)S(1)}, f32[96,128]{1,0:T(8,128)S(1)}, u32[]{:S(2)}, u32[]{:S(2)}) collective-permute-start(f32[96,128]{1,0:T(8,128)S(1)} %pad_maximum_fusion.14), channel_id=1, source_target_pairs={{0,3},{1,2},{2,1},{3,0},{4,7},{5,6},{6,5},{7,4},{8,11},{9,10},{10,... | collective-permute-start | bytes 147464 | tf_op jit(solution)/shard_map/ppermute | solution.py:381
  127.6 3.8 %collective-permute-start.45 = (f32[160,128]{1,0:T(8,128)S(1)}, f32[160,128]{1,0:T(8,128)S(1)}, u32[]{:S(2)}, u32[]{:S(2)}) collective-permute-start(f32[160,128]{1,0:T(8,128)S(1)} %get-tuple-element.107), channel_id=1, source_target_pairs={{0,1},{1,0},{2,3},{3,2},{4,5},{5,4},{6,7},{7,6},{8,9},{9,8},{10,11... | collective-permute-start | bytes 245768 | tf_op jit(solution)/shard_map/ppermute | solution.py:381
  127.9 4.7 %collective-permute-start.46 = (f32[160,128]{1,0:T(8,128)S(1)}, f32[160,128]{1,0:T(8,128)S(1)}, u32[]{:S(2)}, u32[]{:S(2)}) collective-permute-start(f32[160,128]{1,0:T(8,128)S(1)} %get-tuple-element.106), channel_id=1, source_target_pairs={{0,8},{1,2},{2,1},{3,4},{4,3},{5,6},{6,5},{7,15},{8,0},{9,10},{10,... | collective-permute-start | bytes 245768 | tf_op jit(solution)/shard_map/ppermute | solution.py:381
  129.7 4.7 %collective-permute-start.51 = (f32[192,128]{1,0:T(8,128)S(1)}, f32[192,128]{1,0:T(8,128)S(1)}, u32[]{:S(2)}, u32[]{:S(2)}) collective-permute-start(f32[192,128]{1,0:T(8,128)S(1)} %pad_maximum_fusion.6), channel_id=1, source_target_pairs={{0,5},{1,4},{2,7},{3,6},{4,1},{5,0},{6,3},{7,2},{8,13},{9,12},{10,... | collective-permute-start | bytes 294920 | tf_op jit(solution)/shard_map/ppermute | solution.py:381
  135.5 4.2 %collective-permute-start.52 = (f32[160,128]{1,0:T(8,128)S(1)}, f32[160,128]{1,0:T(8,128)S(1)}, u32[]{:S(2)}, u32[]{:S(2)}) collective-permute-start(f32[160,128]{1,0:T(8,128)S(1)} %get-tuple-element.105), channel_id=1, source_target_pairs={{0,1},{1,0},{2,3},{3,2},{4,5},{5,4},{6,7},{7,6},{8,9},{9,8},{10,11... | collective-permute-start | bytes 245768 | tf_op jit(solution)/shard_map/ppermute | solution.py:381
  135.8 4.2 %collective-permute-start.53 = (f32[160,128]{1,0:T(8,128)S(1)}, f32[160,128]{1,0:T(8,128)S(1)}, u32[]{:S(2)}, u32[]{:S(2)}) collective-permute-start(f32[160,128]{1,0:T(8,128)S(1)} %get-tuple-element.104), channel_id=1, source_target_pairs={{0,8},{1,2},{2,1},{3,4},{4,3},{5,6},{6,5},{7,15},{8,0},{9,10},{10,... | collective-permute-start | bytes 245768 | tf_op jit(solution)/shard_map/ppermute | solution.py:381
  137.4 3.3 %collective-permute-start.54 = (f32[160,128]{1,0:T(8,128)S(1)}, f32[160,128]{1,0:T(8,128)S(1)}, u32[]{:S(2)}, u32[]{:S(2)}) collective-permute-start(f32[160,128]{1,0:T(8,128)S(1)} %get-tuple-element.103), channel_id=1, source_target_pairs={{0,8},{1,9},{2,10},{3,11},{4,12},{5,13},{6,14},{7,15},{8,0},{9,1},... | collective-permute-start | bytes 245768 | tf_op jit(solution)/shard_map/ppermute | solution.py:381
  138.4 2.3 %collective-permute-start.55 = (f32[160,128]{1,0:T(8,128)S(1)}, f32[160,128]{1,0:T(8,128)S(1)}, u32[]{:S(2)}, u32[]{:S(2)}) collective-permute-start(f32[160,128]{1,0:T(8,128)S(1)} %get-tuple-element.102), channel_id=1, source_target_pairs={{0,1},{1,0},{2,3},{3,2},{4,5},{5,4},{6,7},{7,6},{8,16},{9,17},{10,... | collective-permute-start | bytes 245768 | tf_op jit(solution)/shard_map/ppermute | solution.py:381
